TPU v7x, 32 devices: a whole 2x2x4 slice. The times are simulated.
32 devices in a mesh: head: 4 (over x, core), blk: 8 (over z, y).
Axes of the slice: x: 2, y: 2, z: 4, core: 2. Of those that a mesh axis runs over, the one named last changes fastest.
Arguments:
- tokens: bfloat16 [4096, 2048], P(('blk', 'head')), may hold values from -6 to 6
- cotangent: bfloat16 [4096, 2048], P(('blk', 'head')), may hold values from -6 to 6
- segments: int32 [2, 2048], replicated, may hold values from 0 to 3, never falling along the last dimension, each value on 1 to 1024 neighbouring positions
- pair_order: int32 [8], replicated, may hold values from 0 to 7, each once
- norm_in: bfloat16 [2048], P(('head', 'blk')), may hold values from 0.25 to 1.75
- w_query: bfloat16 [2048, 2048], P(('head', 'blk')), may hold values from -0.1875 to 0.1875
- key_weight: bfloat16 [2048, 1024], P(('head', 'blk')), may hold values from -0.125 to 0.125
- value_weight: bfloat16 [2048, 1024], P(('head', 'blk')), may hold values from -0.125 to 0.125
- w_out: bfloat16 [2048, 2048], P(('head', 'blk')), may hold values from -0.75 to 0.75
- norm_mid: bfloat16 [2048], P(('head', 'blk')), may hold values from 0.25 to 1.75
- w_gate: bfloat16 [2048, 8192], P('blk', 'head'), may hold values from -0.125 to 0.125
- w_up: bfloat16 [2048, 8192], P('blk', 'head'), may hold values from -0.125 to 0.125
- w_down: bfloat16 [2048, 8192], P('blk', 'head'), may hold values from -0.125 to 0.125
Outputs:
- layer_out: bfloat16 [4096, 2048], P(('blk', 'head'))
- grad_tokens: float32 [4096, 2048], P(('blk', 'head'))
- grad_norm_in: float32 [2048], P(('head', 'blk'))
- grad_query: float32 [2048, 2048], P(('head', 'blk'))
- grad_key: float32 [2048, 1024], P(('head', 'blk'))
- grad_value: float32 [2048, 1024], P(('head', 'blk'))
- grad_out: float32 [2048, 2048], P(('head', 'blk'))
- grad_norm_mid: float32 [2048], P(('head', 'blk'))
- grad_gate: float32 [2048, 8192], P('blk', 'head')
- grad_up: float32 [2048, 8192], P('blk', 'head')
- grad_down: float32 [2048, 8192], P('blk', 'head')
Inputs may be any that keep to these rules, and one draw needn't show every extreme that they name: `segments`: along each sequence the ids never fall; each id names one run of consecutive positions, and all four ids occur. `pair_order`: each pair number occurs once.
All inputs are finite; a program needn't handle non-finite values.
Results may differ from a plain program's by a relative error of at most 0.03.
Values may be sent and summed in bfloat16 or wider, within the bound.
No kernel may reach another device: no remote copies, remote signals or barrier semaphores. Data moves between devices by JAX's collectives and lax.ppermute only.
A program may use at most 448 MiB of HBM per device.

v0:
```python
import jax
import jax.numpy as jnp
from jax import lax
from jax.sharding import PartitionSpec as P

QUERY_HEAD_COUNT = 8
KEY_VALUE_HEADS = 4
HEAD_WIDTH = 256
SEQS = 2
BLOCK = 256


EPS = 1e-06
THETA = 1000042.0
NEGATIVE = -1e30
CONTRACT_ROWS = (((0,), (0,)), ((), ()))
CONTRACT_COLS = (((1,), (1,)), ((), ()))


def shifted(x, axis, by):
    size = lax.axis_size(axis)
    return lax.ppermute(x, axis, [(i, (i + by) % size) for i in range(size)])


def frequencies(head_size):
    return 1.0 / THETA ** (jnp.arange(0, head_size, 2, dtype=jnp.float32) / head_size)


def apply_rotary(values_in, cosine_table, sine_lookup):
    half_size = values_in.shape[-1] // 2
    first_half = values_in[..., :half_size]
    second_half = values_in[..., half_size:]
    return jnp.concatenate(
        [
            first_half * cosine_table - second_half * sine_lookup,
            second_half * cosine_table + first_half * sine_lookup,
        ],
        axis=-1,
    )


def key_layout(row_ids, pair_order, groups, group_rows):
    group_id = row_ids // group_rows
    chosen = group_id[:, None] == jnp.arange(groups, dtype=jnp.int32)[None, :]
    pair_id = jnp.sum(jnp.where(chosen, pair_order[None, :], 0), axis=1)
    per_seq = groups // SEQS
    seq_id = pair_id // per_seq
    first_span = pair_id % per_seq
    span_rows = group_rows // 2
    local_row = row_ids % group_rows
    span_id = jnp.where(local_row < span_rows, first_span, 2 * per_seq - 1 - first_span)
    return (seq_id, span_id * span_rows + local_row % span_rows)


def fetch_attention(norm_in, w_query, key_weight, value_weight, w_out, norm_mid):
    return (
        lax.all_gather(norm_in, ("head", "blk"), axis=0, tiled=True),
        lax.all_gather(w_query, ("head", "blk"), axis=0, tiled=True),
        lax.all_gather(key_weight, ("head", "blk"), axis=0, tiled=True),
        lax.all_gather(value_weight, ("head", "blk"), axis=0, tiled=True),
        lax.all_gather(w_out, ("head", "blk"), axis=0, tiled=True),
        lax.all_gather(norm_mid, ("head", "blk"), axis=0, tiled=True),
    )


def fetch_ffn(w_gate, w_up, w_down):
    return (
        lax.all_gather(w_gate, "blk", axis=0, tiled=True),
        lax.all_gather(w_up, "blk", axis=0, tiled=True),
        lax.all_gather(w_down, "blk", axis=0, tiled=True),
    )


def group_gather(local_rows):
    return lax.all_gather(local_rows, "head", axis=0, tiled=True)


def group_sum(partial_value):
    return lax.psum_scatter(partial_value, "head", scatter_dimension=0, tiled=True)


def pass_keys(key_cur, value_cur):
    return shifted((key_cur, value_cur), "blk", 1)


def rms_back(grad_norm, normed, inv_rms, gain):
    scaled = grad_norm * gain
    return inv_rms * (scaled - normed * jnp.mean(scaled * normed, axis=-1, keepdims=True))


def local(
    tokens,
    cotangent,
    segments,
    pair_order,
    norm_in,
    w_query,
    key_weight,
    value_weight,
    w_out,
    norm_mid,
    w_gate,
    w_up,
    w_down,
):
    head_dimension = lax.axis_size("head")
    groups = lax.axis_size("blk")
    group_index = lax.axis_index("blk")
    head_index = lax.axis_index("head")
    token_rows = tokens.shape[0]
    group_rows = token_rows * head_dimension
    seq_len = segments.shape[1]
    seg_flat = segments.reshape(-1)
    key_value_local = KEY_VALUE_HEADS // head_dimension
    query_local = QUERY_HEAD_COUNT // head_dimension
    queries_per_key_value = QUERY_HEAD_COUNT // KEY_VALUE_HEADS
    score_scale = HEAD_WIDTH ** (-0.5)
    query_cols = QUERY_HEAD_COUNT * HEAD_WIDTH
    key_cols = KEY_VALUE_HEADS * HEAD_WIDTH
    query_ids = group_index * group_rows + jnp.arange(group_rows, dtype=jnp.int32)
    query_seq, query_pos = key_layout(query_ids, pair_order, groups, group_rows)
    query_seg = seg_flat[query_seq * seq_len + query_pos]
    query_block_slice = query_pos // BLOCK
    own_pos = lax.dynamic_slice_in_dim(query_pos, head_index * token_rows, token_rows, 0)
    angles = own_pos.astype(jnp.float32)[:, None] * frequencies(HEAD_WIDTH)[None, :]
    cosine_table = jnp.cos(angles)[:, None, :]
    sine_lookup = jnp.sin(angles)[:, None, :]

    def visible_from(first_row_index, row_count):
        key_ids = first_row_index + jnp.arange(row_count, dtype=jnp.int32)
        key_seq, key_pos = key_layout(key_ids, pair_order, groups, group_rows)
        key_seg = seg_flat[key_seq * seq_len + key_pos]
        return (
            (query_seq[:, None] == key_seq[None, :])
            & (query_seg[:, None] == key_seg[None, :])
            & (key_pos[None, :] // BLOCK <= query_block_slice[:, None])
        )

    tokens_f = tokens.astype(jnp.float32)
    gathered = fetch_attention(norm_in, w_query, key_weight, value_weight, w_out, norm_mid)
    gain_in = gathered[0].astype(jnp.float32)
    gain_mid = gathered[5].astype(jnp.float32)
    inv_in = lax.rsqrt(jnp.mean(tokens_f * tokens_f, axis=-1, keepdims=True) + EPS)
    normed_in = tokens_f * inv_in
    input_low = (normed_in * gain_in).astype(jnp.bfloat16)
    query_lin = jnp.dot(input_low, gathered[1], preferred_element_type=jnp.float32)
    key_linear = jnp.dot(input_low, gathered[2], preferred_element_type=jnp.float32)
    value_linear = jnp.dot(input_low, gathered[3], preferred_element_type=jnp.float32)
    query_matrix = (
        apply_rotary(
            query_lin.reshape(token_rows, QUERY_HEAD_COUNT, HEAD_WIDTH), cosine_table, sine_lookup
        )
        .reshape(token_rows, query_cols)
        .astype(jnp.bfloat16)
    )
    rotated_keys = (
        apply_rotary(
            key_linear.reshape(token_rows, KEY_VALUE_HEADS, HEAD_WIDTH), cosine_table, sine_lookup
        )
        .reshape(token_rows, key_cols)
        .astype(jnp.bfloat16)
    )
    reduced_values = value_linear.astype(jnp.bfloat16)
    query_heads, key_heads, value_heads = (
        lax.all_to_all(query_matrix, "head", split_axis=1, concat_axis=0, tiled=True),
        lax.all_to_all(rotated_keys, "head", split_axis=1, concat_axis=0, tiled=True),
        lax.all_to_all(reduced_values, "head", split_axis=1, concat_axis=0, tiled=True),
    )
    query_four = query_heads.reshape(group_rows, key_value_local, queries_per_key_value, HEAD_WIDTH)

    def attend_block(fold_state, members, first_row_index):
        key_piece, value_piece = members
        row_count = key_piece.shape[0]
        visible = visible_from(first_row_index, row_count)
        row_max, row_total, weighted = fold_state
        scores = (
            jnp.einsum(
                "qkgd,skd->kgqs",
                query_four,
                key_piece.reshape(row_count, key_value_local, HEAD_WIDTH),
                preferred_element_type=jnp.float32,
            )
            * score_scale
        )
        scores = jnp.where(visible, scores, NEGATIVE)
        new_max = jnp.maximum(row_max, jnp.max(scores, axis=-1))
        weights = jnp.where(visible, jnp.exp(scores - new_max[..., None]), 0.0)
        factor = jnp.exp(row_max - new_max)
        new_total = row_total * factor + jnp.sum(weights, axis=-1)
        new_weighted = weighted * factor[..., None] + jnp.einsum(
            "kgqs,skd->kgqd",
            weights.astype(jnp.bfloat16),
            value_piece.reshape(row_count, key_value_local, HEAD_WIDTH),
            preferred_element_type=jnp.float32,
        )
        return (new_max, new_total, new_weighted)

    def forward_step(step_id, forward_state):
        key_cur, value_cur, row_max, row_total, weighted = forward_state
        source = (group_index - step_id) % groups
        row_max, row_total, weighted = attend_block(
            (row_max, row_total, weighted), (key_cur, value_cur), source * group_rows
        )
        key_next, value_next = pass_keys(key_cur, value_cur)
        return (key_next, value_next, row_max, row_total, weighted)

    forward_init = (
        key_heads,
        value_heads,
        jnp.full((key_value_local, queries_per_key_value, group_rows), NEGATIVE, jnp.float32),
        jnp.zeros((key_value_local, queries_per_key_value, group_rows), jnp.float32),
        jnp.zeros((key_value_local, queries_per_key_value, group_rows, HEAD_WIDTH), jnp.float32),
    )
    forward_final = lax.fori_loop(0, groups, forward_step, forward_init)
    row_max, row_total, weighted = (forward_final[2], forward_final[3], forward_final[4])
    attention_f = weighted / row_total[..., None]
    log_total = row_max + jnp.log(row_total)
    attention_rows = jnp.transpose(attention_f, (2, 0, 1, 3)).reshape(
        group_rows, query_local * HEAD_WIDTH
    )
    attention_low = attention_rows.astype(jnp.bfloat16)
    attention_tok = lax.all_to_all(attention_low, "head", split_axis=0, concat_axis=1, tiled=True)
    branch = lax.dot_general(
        attention_tok, gathered[4], CONTRACT_COLS, preferred_element_type=jnp.float32
    )
    middle = tokens_f + branch
    inv_mid = lax.rsqrt(jnp.mean(middle * middle, axis=-1, keepdims=True) + EPS)
    normed_mid = middle * inv_mid
    mid_low = (normed_mid * gain_mid).astype(jnp.bfloat16)
    ffn_params = fetch_ffn(w_gate, w_up, w_down)
    mid_group = group_gather(mid_low)
    gate_lin = jnp.dot(mid_group, ffn_params[0], preferred_element_type=jnp.float32)
    up_proj = jnp.dot(mid_group, ffn_params[1], preferred_element_type=jnp.float32)
    gate_sig = jax.nn.sigmoid(gate_lin)
    gate_silu = gate_lin * gate_sig
    hidden_act = (gate_silu * up_proj).astype(jnp.bfloat16)
    ffn_partial = lax.dot_general(
        hidden_act, ffn_params[2], CONTRACT_COLS, preferred_element_type=jnp.float32
    )
    ffn_out = group_sum(ffn_partial)
    layer_out = (middle + ffn_out).astype(jnp.bfloat16)
    grad_y = cotangent.astype(jnp.float32)
    ffn_params = fetch_ffn(w_gate, w_up, w_down)
    grad_group = group_gather(cotangent)
    grad_hidden = jnp.dot(grad_group, ffn_params[2], preferred_element_type=jnp.float32)
    grad_gate_lin = (grad_hidden * up_proj * gate_sig * (1.0 + gate_lin * (1.0 - gate_sig))).astype(
        jnp.bfloat16
    )
    grad_up_proj = (grad_hidden * gate_silu).astype(jnp.bfloat16)
    ff_local = w_gate.shape[1]
    ffn_summed = lax.psum_scatter(
        jnp.concatenate(
            [
                lax.dot_general(
                    mid_group, grad_gate_lin, CONTRACT_ROWS, preferred_element_type=jnp.float32
                ),
                lax.dot_general(
                    mid_group, grad_up_proj, CONTRACT_ROWS, preferred_element_type=jnp.float32
                ),
                lax.dot_general(
                    grad_group, hidden_act, CONTRACT_ROWS, preferred_element_type=jnp.float32
                ),
            ],
            axis=1,
        ),
        "blk",
        scatter_dimension=0,
        tiled=True,
    )
    grad_gate_w = ffn_summed[:, :ff_local]
    grad_up_w = ffn_summed[:, ff_local : 2 * ff_local]
    grad_down_w = ffn_summed[:, 2 * ff_local :]
    mid_partial = lax.dot_general(
        grad_gate_lin, ffn_params[0], CONTRACT_COLS, preferred_element_type=jnp.float32
    ) + lax.dot_general(
        grad_up_proj, ffn_params[1], CONTRACT_COLS, preferred_element_type=jnp.float32
    )
    grad_mid = group_sum(mid_partial)
    gain_mid_term = jnp.sum(grad_mid * normed_mid, axis=0)
    grad_middle = grad_y + rms_back(grad_mid, normed_mid, inv_mid, gain_mid)
    grad_branch = grad_middle.astype(jnp.bfloat16)
    gathered = fetch_attention(norm_in, w_query, key_weight, value_weight, w_out, norm_mid)
    grad_attention_tok = jnp.dot(
        grad_branch, gathered[4], preferred_element_type=jnp.float32
    ).astype(jnp.bfloat16)
    grad_attention = lax.all_to_all(
        grad_attention_tok, "head", split_axis=1, concat_axis=0, tiled=True
    )
    grad_four = grad_attention.reshape(
        group_rows, key_value_local, queries_per_key_value, HEAD_WIDTH
    )
    row_delta = jnp.transpose(
        jnp.sum(grad_four.astype(jnp.float32) * jnp.transpose(attention_f, (2, 0, 1, 3)), axis=-1),
        (1, 2, 0),
    )

    def cycle_step(step_id, cycle_state):
        key_cur, value_cur, grad_key, grad_value, grad_query = cycle_state
        source = (group_index - step_id) % groups
        visible = visible_from(source * group_rows, group_rows)
        partials = (grad_key, grad_value, grad_query)
        grad_key_in, grad_value_in, grad_query_in = partials
        key_three = key_cur.reshape(group_rows, key_value_local, HEAD_WIDTH)
        value_three = value_cur.reshape(group_rows, key_value_local, HEAD_WIDTH)
        scores = (
            jnp.einsum("qkgd,skd->kgqs", query_four, key_three, preferred_element_type=jnp.float32)
            * score_scale
        )
        probabilities = jnp.where(visible, jnp.exp(scores - log_total[..., None]), 0.0)
        grad_value_out = grad_value_in + jnp.einsum(
            "kgqs,qkgd->skd",
            probabilities.astype(jnp.bfloat16),
            grad_four,
            preferred_element_type=jnp.float32,
        )
        grad_probs = jnp.einsum(
            "qkgd,skd->kgqs", grad_four, value_three, preferred_element_type=jnp.float32
        )
        grad_scores = (probabilities * (grad_probs - row_delta[..., None])).astype(jnp.bfloat16)
        grad_query_out = (
            grad_query_in
            + jnp.einsum(
                "kgqs,skd->kgqd", grad_scores, key_three, preferred_element_type=jnp.float32
            )
            * score_scale
        )
        grad_key_out = (
            grad_key_in
            + jnp.einsum(
                "kgqs,qkgd->skd", grad_scores, query_four, preferred_element_type=jnp.float32
            )
            * score_scale
        )
        partials = (grad_key_out, grad_value_out, grad_query_out)
        key_next, value_next = pass_keys(key_cur, value_cur)
        grad_key_next, grad_value_next = shifted((partials[0], partials[1]), "blk", 1)
        return (key_next, value_next, grad_key_next, grad_value_next, partials[2])

    def cycle_pair(pair_id, cycle_state):
        return cycle_step(2 * pair_id + 1, cycle_step(2 * pair_id, cycle_state))

    zero_grad = jnp.zeros((group_rows, key_value_local, HEAD_WIDTH), jnp.float32)
    cycle_init = (
        key_heads,
        value_heads,
        zero_grad,
        zero_grad,
        jnp.zeros((key_value_local, queries_per_key_value, group_rows, HEAD_WIDTH), jnp.float32),
    )
    cycle_final = lax.fori_loop(0, groups // 2, cycle_pair, cycle_init)
    grad_query_rows = (
        jnp.transpose(cycle_final[4], (2, 0, 1, 3))
        .reshape(group_rows, query_local * HEAD_WIDTH)
        .astype(jnp.bfloat16)
    )
    grad_key_rows = (
        cycle_final[2].reshape(group_rows, key_value_local * HEAD_WIDTH).astype(jnp.bfloat16)
    )
    grad_value_rows = (
        cycle_final[3].reshape(group_rows, key_value_local * HEAD_WIDTH).astype(jnp.bfloat16)
    )
    grad_q_tok, grad_key_tokens, grad_v_tok = (
        lax.all_to_all(grad_query_rows, "head", split_axis=0, concat_axis=1, tiled=True),
        lax.all_to_all(grad_key_rows, "head", split_axis=0, concat_axis=1, tiled=True),
        lax.all_to_all(grad_value_rows, "head", split_axis=0, concat_axis=1, tiled=True),
    )
    grad_q_lin = (
        apply_rotary(
            grad_q_tok.astype(jnp.float32).reshape(token_rows, QUERY_HEAD_COUNT, HEAD_WIDTH),
            cosine_table,
            -sine_lookup,
        )
        .reshape(token_rows, query_cols)
        .astype(jnp.bfloat16)
    )
    grad_k_lin = (
        apply_rotary(
            grad_key_tokens.astype(jnp.float32).reshape(token_rows, KEY_VALUE_HEADS, HEAD_WIDTH),
            cosine_table,
            -sine_lookup,
        )
        .reshape(token_rows, key_cols)
        .astype(jnp.bfloat16)
    )
    grad_in = (
        lax.dot_general(grad_q_lin, gathered[1], CONTRACT_COLS, preferred_element_type=jnp.float32)
        + lax.dot_general(
            grad_k_lin, gathered[2], CONTRACT_COLS, preferred_element_type=jnp.float32
        )
        + lax.dot_general(
            grad_v_tok, gathered[3], CONTRACT_COLS, preferred_element_type=jnp.float32
        )
    )
    gain_in_term = jnp.sum(grad_in * normed_in, axis=0)
    grad_tokens = grad_middle + rms_back(grad_in, normed_in, inv_in, gain_in)
    summed_all = lax.psum_scatter(
        jnp.concatenate(
            [
                gain_in_term[:, None],
                lax.dot_general(
                    input_low, grad_q_lin, CONTRACT_ROWS, preferred_element_type=jnp.float32
                ),
                lax.dot_general(
                    input_low, grad_k_lin, CONTRACT_ROWS, preferred_element_type=jnp.float32
                ),
                lax.dot_general(
                    input_low, grad_v_tok, CONTRACT_ROWS, preferred_element_type=jnp.float32
                ),
                lax.dot_general(
                    grad_branch, attention_tok, CONTRACT_ROWS, preferred_element_type=jnp.float32
                ),
                gain_mid_term[:, None],
            ],
            axis=1,
        ),
        ("head", "blk"),
        scatter_dimension=0,
        tiled=True,
    )
    first_key = 1 + query_cols
    first_value = first_key + key_cols
    first_out = first_value + key_cols
    first_gain = first_out + query_cols
    attention_grads = (
        summed_all[:, 0],
        summed_all[:, 1:first_key],
        summed_all[:, first_key:first_value],
        summed_all[:, first_value:first_out],
        summed_all[:, first_out:first_gain],
        summed_all[:, first_gain],
    )
    return (
        layer_out,
        grad_tokens,
        attention_grads[0],
        attention_grads[1],
        attention_grads[2],
        attention_grads[3],
        attention_grads[4],
        attention_grads[5],
        grad_gate_w,
        grad_up_w,
        grad_down_w,
    )


def solution(mesh):
    placed = (
        P(("blk", "head"), None),
        P(("blk", "head"), None),
        P(),
        P(),
        P(("head", "blk")),
        P(("head", "blk"), None),
        P(("head", "blk"), None),
        P(("head", "blk"), None),
        P(("head", "blk"), None),
        P(("head", "blk")),
        P("blk", "head"),
        P("blk", "head"),
        P("blk", "head"),
    )
    return jax.shard_map(
        local,
        mesh=mesh,
        in_specs=placed,
        out_specs=(
            P(("blk", "head"), None),
            P(("blk", "head"), None),
            P(("head", "blk")),
            P(("head", "blk"), None),
            P(("head", "blk"), None),
            P(("head", "blk"), None),
            P(("head", "blk"), None),
            P(("head", "blk")),
            P("blk", "head"),
            P("blk", "head"),
            P("blk", "head"),
        ),
        check_vma=False,
    )
```

profile of v0, /device:TPU:0, one launch (start us, length us, event | category | flops | bytes accessed | tf_op | source)
XLA Modules:
  0.0 3059.3 jit_solution(17103852280913465050)
XLA Ops:
  11.7 42.2 %all-reduce.2 = (bf16[2048]{0:T(1024)(128)(2,1)S(1)}, bf16[2048]{0:T(1024)(128)(2,1)S(1)}) all-reduce(bf16[2048]{0:T(1024)(128)(2,1)S(1)} %dynamic-update-slice, bf16[2048]{0:T(1024)(128)(2,1)S(1)} %dynamic-update-slice.1), channel_id=1, replica_groups=mesh['head'=4,'blk'=8] {'head','blk'}, use_global_device_ids=true, to_apply=%add | all-reduce | flops 4096 | bytes 16384
  57.0 19.0 all-gather.10.cloned.1.call-done
  84.5 55.2 %all-gather.12.cloned.1.call-done = bf16[2048,1024]{1,0:T(8,128)(2,1)} async-done(((bf16[64,1024]{1,0:T(8,128)(2,1)}), bf16[2048,1024]{1,0:T(8,128)(2,1)}) %all-gather.12.cloned.1.call-update) | async-done | bytes 4194320 | tf_op jit(solution)/shard_map/all_gather | solution.py:60
  143.4 75.3 %all-gather.14.cloned.1.call-done = bf16[2048,2048]{1,0:T(8,128)(2,1)} async-done(((bf16[64,2048]{1,0:T(8,128)(2,1)}), bf16[2048,2048]{1,0:T(8,128)(2,1)}) %all-gather.14.cloned.1.call-update) | async-done | bytes 8388624 | tf_op jit(solution)/shard_map/all_gather | solution.py:58
  249.0 189.3 %while.50 = (s32[]{:T(128)}, bf16[512,256]{1,0:T(8,128)(2,1)S(1)}, bf16[512,256]{1,0:T(8,128)(2,1)S(1)}, f32[1,2,512]{2,1,0:T(2,128)S(1)}, f32[1,2,512]{2,1,0:T(...) while((s32[]{:T(128)}, bf16[512,256]{1,0:T(8,128)(2,1)S(1)}, ...), condition=%wide.region_6.7_spmd.clone, body=%wide.region_2.6_spmd.clone.sunk | while | flops 545869312 | bytes 13738418 | solution.py:214
  258.1 8.5 collective-permute-done
  266.5 8.7 collective-permute-done.1
  281.5 10.1 collective-permute-done
  291.6 9.8 collective-permute-done.1
  307.6 11.4 collective-permute-done
  347.3 11.4 collective-permute-done
  358.7 9.6 collective-permute-done.1
  374.5 11.4 collective-permute-done
  385.9 9.4 collective-permute-done.1
  419.1 10.8 collective-permute-done
  429.9 8.4 collective-permute-done.1
  442.6 8.4 all-to-all-start.3
  451.0 8.8 all-to-all-done.3
  470.2 17.2 all-gather.20.cloned.1.call-done
  487.4 24.8 all-gather.18.cloned.1.call-done
  512.2 10.7 fusion.144
  522.8 116.4 %all-gather.22.cloned.1.call-done = bf16[2048,2048]{1,0:T(8,128)(2,1)} async-done(((bf16[256,2048]{1,0:T(8,128)(2,1)}), bf16[2048,2048]{1,0:T(8,128)(2,1)}) %all-gather.22.cloned.1.call-update) | async-done | bytes 8388624 | tf_op jit(solution)/shard_map/all_gather | solution.py:69
  639.3 10.5 fusion.145
  649.8 11.9 all-gather.26.cloned.1.call-done
  661.6 127.1 %all-gather.24.cloned.1.call-done = bf16[2048,2048]{1,0:T(8,128)(2,1)} async-done(((bf16[256,2048]{1,0:T(8,128)(2,1)}), bf16[2048,2048]{1,0:T(8,128)(2,1)}) %all-gather.24.cloned.1.call-update) | async-done | bytes 8388624 | tf_op jit(solution)/shard_map/all_gather | solution.py:70
  788.8 13.5 multiply_convert_fusion
  802.3 9.1 fusion.147
  817.7 10.9 fusion.146
  828.9 12.7 fusion.150
  841.6 8.3 fusion.149
  849.9 8.2 convolution_bitcast_fusion.5
  858.2 37.0 %pad_maximum_fusion = f32[2048,6144]{0,1:T(8,128)} fusion(f32[2048,2048]{0,1:T(8,128)} %convolution_bitcast_fusion.5, f32[2048,2048]{0,1:T(8,128)} %fusion.150, f32[2048,2048]{0,1:T(8,128)} %fusion.149), kind=kLoop, calls=%fused_computation.240 | loop fusion | flops 25165824 | bytes 100663296 | tf_op jit(solution)/shard_map/concatenate | solution.py:252
  896.9 10.8 reduce-scatter.7.cloned.1.call-done
  919.9 8.8 all-to-all-done.4
  932.7 574.4 %while.51 = (s32[]{:T(128)}, bf16[512,256]{1,0:T(8,128)(2,1)S(1)}, bf16[512,256]{1,0:T(8,128)(2,1)}, f32[512,1,256]{2,0,1:T(8,128)}, f32[512,1,256]{2,0,1:T(8,12...) while((s32[]{:T(128)}, bf16[512,256]{1,0:T(8,128)(2,1)S(1)}, ...), condition=%wide.region_15.16_spmd.clone, body=%wide.region_12.15_spmd.clone.sunk | while | flops 2696571904 | bytes 55143388 | solution.py:350
  953.1 8.4 collective-permute-done.4
  963.0 21.1 collective-permute-done.6
  985.6 20.9 collective-permute-done.8
  1009.7 11.6 collective-permute-start.5
  1022.8 39.8 %collective-permute-done.3 = bf16[512,256]{1,0:T(8,128)(2,1)S(1)} collective-permute-done((bf16[512,256]{1,0:T(8,128)(2,1)}, bf16[512,256]{1,0:T(8,128)(2,1)S(1)}, u32[]{:S(2)}, u32[]{:S(2)}) %collective-permute-start.3) | collective-permute-done | bytes 262176 | tf_op jit(solution)/shard_map/while/body/eval_jaxpr/ppermute | solution.py:22
  1062.6 10.9 collective-permute-done.5
  1087.1 18.1 collective-permute-start.6
  1113.0 12.9 collective-permute-done.6
  1133.9 14.5 collective-permute-done.8
  1161.0 9.2 collective-permute-start.5
  1171.6 32.9 %collective-permute-done.3 = bf16[512,256]{1,0:T(8,128)(2,1)S(1)} collective-permute-done((bf16[512,256]{1,0:T(8,128)(2,1)}, bf16[512,256]{1,0:T(8,128)(2,1)S(1)}, u32[]{:S(2)}, u32[]{:S(2)}) %collective-permute-start.3) | collective-permute-done | bytes 262176 | tf_op jit(solution)/shard_map/while/body/eval_jaxpr/ppermute | solution.py:22
  1204.6 10.6 collective-permute-done.5
  1237.3 15.5 collective-permute-start.6
  1268.9 12.8 collective-permute-start.7
  1291.4 12.8 collective-permute-start.9
  1317.5 28.4 collective-permute-done.3
  1345.9 10.4 collective-permute-done.5
  1357.3 12.9 collective-permute-start.2
  1385.1 15.0 collective-permute-start.6
  1415.7 13.2 collective-permute-start.7
  1437.7 13.7 collective-permute-start.9
  1455.6 10.4 collective-permute-start.5
  1467.5 29.6 collective-permute-done.3
  1497.1 9.0 collective-permute-done.5
  1512.2 10.0 fusion.111
  1565.2 132.6 %concatenate.26 = f32[2048,6146]{0,1:T(8,128)} concatenate(f32[2048,1]{0,1:T(1,128)S(1)} %bitcast.427, f32[2048,2048]{0,1:T(8,128)} %fusion.128, f32[2048,1024]{0,1:T(8,128)} %fusion.130, f32[2048,1024]{0,1:T(8,128)} %fusion.132, f32[2048,2048]{0,1:T(8,128)} %fusion.111, f32[2048,1]{0,1:T(1,128)S(1)} %bitcast.426), dimensions={1} | concatenate | bytes 100696064 | tf_op jit(solution)/shard_map/concatenate | solution.py:397
  1697.8 50.2 %copy.178 = f32[2048,6146]{1,0:T(8,128)} copy(f32[2048,6146]{0,1:T(8,128)} %concatenate.26) | data formatting | bytes 100696064
  1750.7 217.1 %reduce-scatter.11.cloned.1.call-done = f32[256,6144]{0,1:T(8,128)} async-done(((f32[2048,6144]{0,1:T(8,128)}), f32[256,6144]{0,1:T(8,128)}) %reduce-scatter.11.cloned.1.call-update) | async-done | bytes 6291472 | tf_op jit(solution)/shard_map/reduce_scatter | solution.py:251
  1981.0 1064.7 %reduce-scatter.13.cloned.1.call-done = f32[64,6146]{1,0:T(8,128)} async-done(((f32[2048,6146]{1,0:T(8,128)}), f32[64,6146]{1,0:T(8,128)}) %reduce-scatter.13.cloned.1.call-update) | async-done | bytes 1573392
  (497 shorter events, 416.7 us)
Async XLA Ops:
  7.2 68.8 %all-gather.10.cloned.1.call-start = ((), (), s32[]{:S(2)}) async-start(), calls=%async_computation.12 | async-start | bytes 4325376 | tf_op jit(solution)/shard_map/all_gather | solution.py:59
  7.9 131.8 %all-gather.12.cloned.1.call-start = ((), (), s32[]{:S(2)}) async-start(), calls=%async_computation.13 | async-start | bytes 4325376 | tf_op jit(solution)/shard_map/all_gather | solution.py:60
  8.7 210.0 %all-gather.14.cloned.1.call-start = ((), (), s32[]{:S(2)}) async-start(), calls=%async_computation.14 | async-start | bytes 8650752 | tf_op jit(solution)/shard_map/all_gather | solution.py:58
  9.4 450.7 %all-gather.16.cloned.1.call-start = ((), (), s32[]{:S(2)}) async-start(), calls=%async_computation.15 | async-start | bytes 8650752 | tf_op jit(solution)/shard_map/all_gather | solution.py:61
  81.1 144.4 %all-to-all-start = ((bf16[128,4,256]{2,0,1:T(8,128)(2,1)}), bf16[128,4,256]{2,0,1:T(8,128)(2,1)S(1)}, u32[]{:S(2)}, u32[]{:S(2)}) async-start(bf16[128,4,256]{2,0,1:T(8,128)(2,1)} %copy.151), calls=%async_computation | async-start | bytes 524288 | tf_op jit(solution)/shard_map/all_to_all | solution.py:166
  239.7 247.7 %all-gather.20.cloned.1.call-start = ((), (), s32[]{:S(2)}) async-start(), calls=%async_computation.17 | async-start | bytes 9437184 | tf_op jit(solution)/shard_map/all_gather | solution.py:68
  249.0 17.5 collective-permute-start
  250.6 24.7 collective-permute-start.1
  275.3 16.4 collective-permute-start
  275.4 26.1 collective-permute-start.1
  301.5 17.6 collective-permute-start
  301.6 23.9 collective-permute-start.1
  325.5 15.6 collective-permute-start.1
  341.2 17.5 collective-permute-start
  341.2 27.1 collective-permute-start.1
  368.3 17.5 collective-permute-start
  368.4 26.8 collective-permute-start.1
  395.4 17.6 collective-permute-start.1
  413.0 16.9 collective-permute-start
  413.1 25.2 collective-permute-start.1
  442.6 17.3 all-to-all-start.3
  451.0 61.2 %all-gather.18.cloned.1.call-start = ((), (), s32[]{:S(2)}) async-start(), calls=%async_computation.16 | async-start | bytes 2621440 | tf_op jit(solution)/shard_map/all_gather | solution.py:75
  467.7 171.6 %all-gather.22.cloned.1.call-start = ((), (), s32[]{:S(2)}) async-start(), calls=%async_computation.18 | async-start | bytes 9437184 | tf_op jit(solution)/shard_map/all_gather | solution.py:69
  468.4 193.2 %all-gather.26.cloned.1.call-start = ((), (), s32[]{:S(2)}) async-start(), calls=%async_computation.21 | async-start | bytes 2621440 | tf_op jit(solution)/shard_map/all_gather | solution.py:75
  469.2 319.6 %all-gather.24.cloned.1.call-start = ((), (), s32[]{:S(2)}) async-start(), calls=%async_computation.19 | async-start | bytes 9437184 | tf_op jit(solution)/shard_map/all_gather | solution.py:70
  469.9 425.3 %reduce-scatter.9.cloned.1.call-start = ((), (), s32[]{:S(2)}) async-start(), calls=%async_computation.22 | async-start | bytes 5242880 | tf_op jit(solution)/shard_map/reduce_scatter | solution.py:79
  817.7 90.1 %reduce-scatter.7.cloned.1.call-start = ((), (), s32[]{:S(2)}) async-start(), calls=%async_computation.20 | async-start | bytes 5242880 | tf_op jit(solution)/shard_map/reduce_scatter | solution.py:79
  828.6 1139.1 %reduce-scatter.11.cloned.1.call-start = ((), (), s32[]{:S(2)}) async-start(), calls=%async_computation.23 | async-start | bytes 56623104 | tf_op jit(solution)/shard_map/reduce_scatter | solution.py:251
  916.1 12.5 all-to-all-start.4
  932.7 18.6 collective-permute-start.2
  934.2 27.4 collective-permute-start.4
  947.2 36.9 %collective-permute-start.6 = (f32[512,1,256]{2,0,1:T(8,128)}, f32[512,1,256]{2,0,1:T(8,128)}, u32[]{:S(2)}, u32[]{:S(2)}) collective-permute-start(f32[512,1,256]{2,0,1:T(8,128)} %fusion.253), channel_id=1, source_target_pairs={{0,1},{1,2},{2,3},{3,4},{4,5},{5,6},{6,7},{7,0},{8,9},{9,10},{10,1... | collective-permute-start | bytes 1572872 | tf_op jit(solution)/shard_map/while/body/eval_jaxpr/ppermute | solution.py:22
  949.9 56.6 %collective-permute-start.8 = (f32[512,1,256]{2,0,1:T(8,128)}, f32[512,1,256]{2,0,1:T(8,128)}, u32[]{:S(2)}, u32[]{:S(2)}) collective-permute-start(f32[512,1,256]{2,0,1:T(8,128)} %fusion.257), channel_id=1, source_target_pairs={{0,1},{1,2},{2,3},{3,4},{4,5},{5,6},{6,7},{7,0},{8,9},{9,10},{10,1... | collective-permute-start | bytes 1572872 | tf_op jit(solution)/shard_map/while/body/eval_jaxpr/ppermute | solution.py:22
  985.6 87.9 %collective-permute-start.7 = (f32[512,1,256]{2,0,1:T(8,128)S(1)}, f32[512,1,256]{2,0,1:T(8,128)S(1)}, u32[]{:S(2)}, u32[]{:S(2)}) collective-permute-start(f32[512,1,256]{2,0,1:T(8,128)S(1)} %fusion.256), channel_id=1, source_target_pairs={{0,1},{1,2},{2,3},{3,4},{4,5},{5,6},{6,7},{7,0},{8,9},{9,10},{10,1... | collective-permute-start | bytes 1572872 | tf_op jit(solution)/shard_map/while/body/eval_jaxpr/ppermute | solution.py:22
  1008.0 65.5 %collective-permute-start.9 = (f32[512,1,256]{2,0,1:T(8,128)S(1)}, f32[512,1,256]{2,0,1:T(8,128)S(1)}, u32[]{:S(2)}, u32[]{:S(2)}) collective-permute-start(f32[512,1,256]{2,0,1:T(8,128)S(1)} %fusion.258), channel_id=1, source_target_pairs={{0,1},{1,2},{2,3},{3,4},{4,5},{5,6},{6,7},{7,0},{8,9},{9,10},{10,1... | collective-permute-start | bytes 1572872 | tf_op jit(solution)/shard_map/while/body/eval_jaxpr/ppermute | solution.py:22
  1008.6 54.0 %collective-permute-start.3 = (bf16[512,256]{1,0:T(8,128)(2,1)}, bf16[512,256]{1,0:T(8,128)(2,1)S(1)}, u32[]{:S(2)}, u32[]{:S(2)}) collective-permute-start(bf16[512,256]{1,0:T(8,128)(2,1)} %collective-permute-done.2), channel_id=1, source_target_pairs={{0,1},{1,2},{2,3},{3,4},{4,5},{5,6},{6,7},{7,0},{8,9},{9,10},{10,1... | collective-permute-start | bytes 786440 | tf_op jit(solution)/shard_map/while/body/eval_jaxpr/ppermute | solution.py:22
  1009.7 63.8 %collective-permute-start.5 = (bf16[512,256]{1,0:T(8,128)(2,1)}, bf16[512,256]{1,0:T(8,128)(2,1)}, u32[]{:S(2)}, u32[]{:S(2)}) collective-permute-start(bf16[512,256]{1,0:T(8,128)(2,1)} %collective-permute-done.4), channel_id=1, source_target_pairs={{0,1},{1,2},{2,3},{3,4},{4,5},{5,6},{6,7},{7,0},{8,9},{9,10},{10,1... | collective-permute-start | bytes 786440 | tf_op jit(solution)/shard_map/while/body/eval_jaxpr/ppermute | solution.py:22
  1074.5 35.3 %collective-permute-start.2 = (bf16[512,256]{1,0:T(8,128)(2,1)S(1)}, bf16[512,256]{1,0:T(8,128)(2,1)}, u32[]{:S(2)}, u32[]{:S(2)}) collective-permute-start(bf16[512,256]{1,0:T(8,128)(2,1)S(1)} %get-tuple-element.1530), channel_id=1, source_target_pairs={{0,1},{1,2},{2,3},{3,4},{4,5},{5,6},{6,7},{7,0},{8,9},{9,10},{10,1... | collective-permute-start | bytes 786440 | tf_op jit(solution)/shard_map/while/body/eval_jaxpr/ppermute | solution.py:22
  1074.5 37.1 %collective-permute-start.4 = (bf16[512,256]{1,0:T(8,128)(2,1)}, bf16[512,256]{1,0:T(8,128)(2,1)}, u32[]{:S(2)}, u32[]{:S(2)}) collective-permute-start(bf16[512,256]{1,0:T(8,128)(2,1)} %get-tuple-element.1531), channel_id=1, source_target_pairs={{0,1},{1,2},{2,3},{3,4},{4,5},{5,6},{6,7},{7,0},{8,9},{9,10},{10,1... | collective-permute-start | bytes 786440 | tf_op jit(solution)/shard_map/while/body/eval_jaxpr/ppermute | solution.py:22
  1087.1 38.9 %collective-permute-start.6 = (f32[512,1,256]{2,0,1:T(8,128)}, f32[512,1,256]{2,0,1:T(8,128)}, u32[]{:S(2)}, u32[]{:S(2)}) collective-permute-start(f32[512,1,256]{2,0,1:T(8,128)} %fusion.253), channel_id=1, source_target_pairs={{0,1},{1,2},{2,3},{3,4},{4,5},{5,6},{6,7},{7,0},{8,9},{9,10},{10,1... | collective-permute-start | bytes 1572872 | tf_op jit(solution)/shard_map/while/body/eval_jaxpr/ppermute | solution.py:22
  1106.4 42.0 %collective-permute-start.8 = (f32[512,1,256]{2,0,1:T(8,128)}, f32[512,1,256]{2,0,1:T(8,128)}, u32[]{:S(2)}, u32[]{:S(2)}) collective-permute-start(f32[512,1,256]{2,0,1:T(8,128)} %fusion.257), channel_id=1, source_target_pairs={{0,1},{1,2},{2,3},{3,4},{4,5},{5,6},{6,7},{7,0},{8,9},{9,10},{10,1... | collective-permute-start | bytes 1572872 | tf_op jit(solution)/shard_map/while/body/eval_jaxpr/ppermute | solution.py:22
  1127.4 87.7 %collective-permute-start.7 = (f32[512,1,256]{2,0,1:T(8,128)S(1)}, f32[512,1,256]{2,0,1:T(8,128)S(1)}, u32[]{:S(2)}, u32[]{:S(2)}) collective-permute-start(f32[512,1,256]{2,0,1:T(8,128)S(1)} %fusion.256), channel_id=1, source_target_pairs={{0,1},{1,2},{2,3},{3,4},{4,5},{5,6},{6,7},{7,0},{8,9},{9,10},{10,1... | collective-permute-start | bytes 1572872 | tf_op jit(solution)/shard_map/while/body/eval_jaxpr/ppermute | solution.py:22
  1149.9 65.2 %collective-permute-start.9 = (f32[512,1,256]{2,0,1:T(8,128)S(1)}, f32[512,1,256]{2,0,1:T(8,128)S(1)}, u32[]{:S(2)}, u32[]{:S(2)}) collective-permute-start(f32[512,1,256]{2,0,1:T(8,128)S(1)} %fusion.258), channel_id=1, source_target_pairs={{0,1},{1,2},{2,3},{3,4},{4,5},{5,6},{6,7},{7,0},{8,9},{9,10},{10,1... | collective-permute-start | bytes 1572872 | tf_op jit(solution)/shard_map/while/body/eval_jaxpr/ppermute | solution.py:22
  1156.9 47.6 %collective-permute-start.3 = (bf16[512,256]{1,0:T(8,128)(2,1)}, bf16[512,256]{1,0:T(8,128)(2,1)S(1)}, u32[]{:S(2)}, u32[]{:S(2)}) collective-permute-start(bf16[512,256]{1,0:T(8,128)(2,1)} %collective-permute-done.2), channel_id=1, source_target_pairs={{0,1},{1,2},{2,3},{3,4},{4,5},{5,6},{6,7},{7,0},{8,9},{9,10},{10,1... | collective-permute-start | bytes 786440 | tf_op jit(solution)/shard_map/while/body/eval_jaxpr/ppermute | solution.py:22
  1161.0 54.1 %collective-permute-start.5 = (bf16[512,256]{1,0:T(8,128)(2,1)}, bf16[512,256]{1,0:T(8,128)(2,1)}, u32[]{:S(2)}, u32[]{:S(2)}) collective-permute-start(bf16[512,256]{1,0:T(8,128)(2,1)} %collective-permute-done.4), channel_id=1, source_target_pairs={{0,1},{1,2},{2,3},{3,4},{4,5},{5,6},{6,7},{7,0},{8,9},{9,10},{10,1... | collective-permute-start | bytes 786440 | tf_op jit(solution)/shard_map/while/body/eval_jaxpr/ppermute | solution.py:22
  1216.1 41.2 %collective-permute-start.2 = (bf16[512,256]{1,0:T(8,128)(2,1)S(1)}, bf16[512,256]{1,0:T(8,128)(2,1)}, u32[]{:S(2)}, u32[]{:S(2)}) collective-permute-start(bf16[512,256]{1,0:T(8,128)(2,1)S(1)} %get-tuple-element.1530), channel_id=1, source_target_pairs={{0,1},{1,2},{2,3},{3,4},{4,5},{5,6},{6,7},{7,0},{8,9},{9,10},{10,1... | collective-permute-start | bytes 786440 | tf_op jit(solution)/shard_map/while/body/eval_jaxpr/ppermute | solution.py:22
  1222.4 36.7 %collective-permute-start.4 = (bf16[512,256]{1,0:T(8,128)(2,1)}, bf16[512,256]{1,0:T(8,128)(2,1)}, u32[]{:S(2)}, u32[]{:S(2)}) collective-permute-start(bf16[512,256]{1,0:T(8,128)(2,1)} %get-tuple-element.1531), channel_id=1, source_target_pairs={{0,1},{1,2},{2,3},{3,4},{4,5},{5,6},{6,7},{7,0},{8,9},{9,10},{10,1... | collective-permute-start | bytes 786440 | tf_op jit(solution)/shard_map/while/body/eval_jaxpr/ppermute | solution.py:22
  1237.3 30.1 collective-permute-start.6
  1254.0 35.9 %collective-permute-start.8 = (f32[512,1,256]{2,0,1:T(8,128)}, f32[512,1,256]{2,0,1:T(8,128)}, u32[]{:S(2)}, u32[]{:S(2)}) collective-permute-start(f32[512,1,256]{2,0,1:T(8,128)} %fusion.257), channel_id=1, source_target_pairs={{0,1},{1,2},{2,3},{3,4},{4,5},{5,6},{6,7},{7,0},{8,9},{9,10},{10,1... | collective-permute-start | bytes 1572872 | tf_op jit(solution)/shard_map/while/body/eval_jaxpr/ppermute | solution.py:22
  1268.9 87.5 %collective-permute-start.7 = (f32[512,1,256]{2,0,1:T(8,128)S(1)}, f32[512,1,256]{2,0,1:T(8,128)S(1)}, u32[]{:S(2)}, u32[]{:S(2)}) collective-permute-start(f32[512,1,256]{2,0,1:T(8,128)S(1)} %fusion.256), channel_id=1, source_target_pairs={{0,1},{1,2},{2,3},{3,4},{4,5},{5,6},{6,7},{7,0},{8,9},{9,10},{10,1... | collective-permute-start | bytes 1572872 | tf_op jit(solution)/shard_map/while/body/eval_jaxpr/ppermute | solution.py:22
  1291.4 65.0 %collective-permute-start.9 = (f32[512,1,256]{2,0,1:T(8,128)S(1)}, f32[512,1,256]{2,0,1:T(8,128)S(1)}, u32[]{:S(2)}, u32[]{:S(2)}) collective-permute-start(f32[512,1,256]{2,0,1:T(8,128)S(1)} %fusion.258), channel_id=1, source_target_pairs={{0,1},{1,2},{2,3},{3,4},{4,5},{5,6},{6,7},{7,0},{8,9},{9,10},{10,1... | collective-permute-start | bytes 1572872 | tf_op jit(solution)/shard_map/while/body/eval_jaxpr/ppermute | solution.py:22
  1304.7 41.3 %collective-permute-start.3 = (bf16[512,256]{1,0:T(8,128)(2,1)}, bf16[512,256]{1,0:T(8,128)(2,1)S(1)}, u32[]{:S(2)}, u32[]{:S(2)}) collective-permute-start(bf16[512,256]{1,0:T(8,128)(2,1)} %collective-permute-done.2), channel_id=1, source_target_pairs={{0,1},{1,2},{2,3},{3,4},{4,5},{5,6},{6,7},{7,0},{8,9},{9,10},{10,1... | collective-permute-start | bytes 786440 | tf_op jit(solution)/shard_map/while/body/eval_jaxpr/ppermute | solution.py:22
  1308.1 48.3 %collective-permute-start.5 = (bf16[512,256]{1,0:T(8,128)(2,1)}, bf16[512,256]{1,0:T(8,128)(2,1)}, u32[]{:S(2)}, u32[]{:S(2)}) collective-permute-start(bf16[512,256]{1,0:T(8,128)(2,1)} %collective-permute-done.4), channel_id=1, source_target_pairs={{0,1},{1,2},{2,3},{3,4},{4,5},{5,6},{6,7},{7,0},{8,9},{9,10},{10,1... | collective-permute-start | bytes 786440 | tf_op jit(solution)/shard_map/while/body/eval_jaxpr/ppermute | solution.py:22
  1357.3 47.4 %collective-permute-start.2 = (bf16[512,256]{1,0:T(8,128)(2,1)S(1)}, bf16[512,256]{1,0:T(8,128)(2,1)}, u32[]{:S(2)}, u32[]{:S(2)}) collective-permute-start(bf16[512,256]{1,0:T(8,128)(2,1)S(1)} %get-tuple-element.1530), channel_id=1, source_target_pairs={{0,1},{1,2},{2,3},{3,4},{4,5},{5,6},{6,7},{7,0},{8,9},{9,10},{10,1... | collective-permute-start | bytes 786440 | tf_op jit(solution)/shard_map/while/body/eval_jaxpr/ppermute | solution.py:22
  1370.3 36.2 %collective-permute-start.4 = (bf16[512,256]{1,0:T(8,128)(2,1)}, bf16[512,256]{1,0:T(8,128)(2,1)}, u32[]{:S(2)}, u32[]{:S(2)}) collective-permute-start(bf16[512,256]{1,0:T(8,128)(2,1)} %get-tuple-element.1531), channel_id=1, source_target_pairs={{0,1},{1,2},{2,3},{3,4},{4,5},{5,6},{6,7},{7,0},{8,9},{9,10},{10,1... | collective-permute-start | bytes 786440 | tf_op jit(solution)/shard_map/while/body/eval_jaxpr/ppermute | solution.py:22
  1385.1 29.1 collective-permute-start.6
  1401.4 34.8 %collective-permute-start.8 = (f32[512,1,256]{2,0,1:T(8,128)}, f32[512,1,256]{2,0,1:T(8,128)}, u32[]{:S(2)}, u32[]{:S(2)}) collective-permute-start(f32[512,1,256]{2,0,1:T(8,128)} %fusion.257), channel_id=1, source_target_pairs={{0,1},{1,2},{2,3},{3,4},{4,5},{5,6},{6,7},{7,0},{8,9},{9,10},{10,1... | collective-permute-start | bytes 1572872 | tf_op jit(solution)/shard_map/while/body/eval_jaxpr/ppermute | solution.py:22
  1415.7 90.4 %collective-permute-start.7 = (f32[512,1,256]{2,0,1:T(8,128)S(1)}, f32[512,1,256]{2,0,1:T(8,128)S(1)}, u32[]{:S(2)}, u32[]{:S(2)}) collective-permute-start(f32[512,1,256]{2,0,1:T(8,128)S(1)} %fusion.256), channel_id=1, source_target_pairs={{0,1},{1,2},{2,3},{3,4},{4,5},{5,6},{6,7},{7,0},{8,9},{9,10},{10,1... | collective-permute-start | bytes 1572872 | tf_op jit(solution)/shard_map/while/body/eval_jaxpr/ppermute | solution.py:22
  1437.7 68.4 %collective-permute-start.9 = (f32[512,1,256]{2,0,1:T(8,128)S(1)}, f32[512,1,256]{2,0,1:T(8,128)S(1)}, u32[]{:S(2)}, u32[]{:S(2)}) collective-permute-start(f32[512,1,256]{2,0,1:T(8,128)S(1)} %fusion.258), channel_id=1, source_target_pairs={{0,1},{1,2},{2,3},{3,4},{4,5},{5,6},{6,7},{7,0},{8,9},{9,10},{10,1... | collective-permute-start | bytes 1572872 | tf_op jit(solution)/shard_map/while/body/eval_jaxpr/ppermute | solution.py:22
  1451.8 45.3 %collective-permute-start.3 = (bf16[512,256]{1,0:T(8,128)(2,1)}, bf16[512,256]{1,0:T(8,128)(2,1)S(1)}, u32[]{:S(2)}, u32[]{:S(2)}) collective-permute-start(bf16[512,256]{1,0:T(8,128)(2,1)} %collective-permute-done.2), channel_id=1, source_target_pairs={{0,1},{1,2},{2,3},{3,4},{4,5},{5,6},{6,7},{7,0},{8,9},{9,10},{10,1... | collective-permute-start | bytes 786440 | tf_op jit(solution)/shard_map/while/body/eval_jaxpr/ppermute | solution.py:22
  1455.6 50.5 %collective-permute-start.5 = (bf16[512,256]{1,0:T(8,128)(2,1)}, bf16[512,256]{1,0:T(8,128)(2,1)}, u32[]{:S(2)}, u32[]{:S(2)}) collective-permute-start(bf16[512,256]{1,0:T(8,128)(2,1)} %collective-permute-done.4), channel_id=1, source_target_pairs={{0,1},{1,2},{2,3},{3,4},{4,5},{5,6},{6,7},{7,0},{8,9},{9,10},{10,1... | collective-permute-start | bytes 786440 | tf_op jit(solution)/shard_map/while/body/eval_jaxpr/ppermute | solution.py:22
  1508.8 14.2 all-to-all-start.7
  1532.4 13.4 all-to-all-start.5
  1535.9 1509.8 %reduce-scatter.13.cloned.1.call-start = ((), (), s32[]{:S(2)}) async-start(), calls=%async_computation.24 | async-start | bytes 52985856
  (57 other events, 922.6 us)
Sparse Core Ops, SparseCore 0:
  11.1 64.8 all-gather.9
  79.1 60.6 all-gather.11
  142.7 75.9 all-gather.13
  221.5 96.6 all-gather.15
  320.1 167.2 all-gather.19
  489.4 22.7 all-gather.17
  514.3 124.9 all-gather.21
  640.8 20.7 all-gather.25
  663.8 124.9 all-gather.23
  817.8 42.7 reduce-scatter.8
  863.3 44.4 reduce-scatter.6
  911.5 1056.1 reduce-scatter.10
  1970.2 1075.4 reduce-scatter.12
where the time goes:
time: 3070 us; the launch traced here: 3060 us
  waiting for transfers between devices  2190 us (71%)
  local copies, waits for them, and re-layouts  274 us (9%)
  starting transfers between devices  248 us (8%)
  matrix products  217 us (7%)
  other arithmetic  71 us (2%)
  blocking collectives  42.2 us (1%)
    unnamed x14, waiting for transfers between devices  1070 us
    ppermute x48, waiting for transfers between devices, shifted(): return lax.ppermute(x, axis, [(i, (i + by) % size) for i in range(size)])  415 us
    reduce_scatter x1, waiting for transfers between devices, local(): lax.psum_scatter(jnp.concatenate([lax.dot_general(mid_group, grad_gate_li...  217 us
    ppermute x48, starting transfers between devices, shifted(): return lax.ppermute(x, axis, [(i, (i + by) % size) for i in range(size)])  213 us
    concatenate x1, local copies, waits for them, and re-layouts, local(): jnp.concatenate([gain_in_term[:, None], lax.dot_general(input_low, grad_q...  133 us
    all_gather x1, waiting for transfers between devices, fetch_ffn(): lax.all_gather(w_down, 'blk', axis=0, tiled=True)  127 us
    all_gather x1, waiting for transfers between devices, fetch_ffn(): lax.all_gather(w_up, 'blk', axis=0, tiled=True)  116 us
    all_gather x1, waiting for transfers between devices, fetch_attention(): lax.all_gather(w_query, ('head', 'blk'), axis=0, tiled=True)  75.3 us
  transfers between devices with their start and end apart: 69, of which 49 were waited for; matrix products, arithmetic and copies ran while one was open for 17% of the time, Pallas kernels for 0%

commit v1 on v0

v1 whole, which is shorter than its diff:
```python
import functools

import jax
import jax.numpy as jnp
from jax import lax
from jax.experimental import pallas as pl
from jax.experimental.pallas import tpu as pltpu
from jax.sharding import PartitionSpec as P

QUERY_HEAD_COUNT = 8
KEY_VALUE_HEADS = 4
HEAD_WIDTH = 256
SEQS = 2
BLOCK = 256

EPS = 1e-06
THETA = 1000042.0
NEGATIVE = -1e30
ROWS = (((0,), (0,)), ((), ()))
COLS = (((1,), (1,)), ((), ()))
BF16 = jnp.bfloat16
F32 = jnp.float32

CORE, CROSS, TURN = 1, 2, 2


def frequencies(head_size):
    return 1.0 / THETA ** (jnp.arange(0, head_size, 2, dtype=F32) / head_size)


def rotate(values, cosine, sine):
    half = HEAD_WIDTH // 2
    parts = []
    for first in range(0, values.shape[-1], HEAD_WIDTH):
        a = values[:, first : first + half]
        b = values[:, first + half : first + HEAD_WIDTH]
        parts += [a * cosine - b * sine, b * cosine + a * sine]
    return jnp.concatenate(parts, axis=-1)


def swap(value, head_mask, blk_mask):
    groups = lax.axis_size("blk")
    count = lax.axis_size("head") * groups
    mask = head_mask * groups + blk_mask
    return lax.ppermute(value, ("head", "blk"), [(i, i ^ mask) for i in range(count)])


def masks_of(size):
    out, bit = [], size >> 1
    while bit:
        out.append(bit)
        bit >>= 1
    return out


def add(a, b, dtype):
    return (a.astype(F32) + b.astype(F32)).astype(dtype)


def spread(piece, masks):
    have = {0: piece}
    for mask in masks:
        for key, value in list(have.items()):
            have[key ^ mask] = swap(value, 0, mask)
    return have


def fold(pieces, masks):
    have = dict(pieces)
    for mask in masks:
        for key in sorted(k for k in have if k & mask):
            received = swap(have.pop(key), 0, mask)
            left = key ^ mask
            have[left] = add(have[left], received, F32 if mask == masks[-1] else BF16)
    return have[0]


def span_of(pair_ref, group, late, per_seq):
    pair = pair_ref[group]
    seq = pair // per_seq
    first = pair - seq * per_seq
    return seq, jnp.where(late == 0, first, 2 * per_seq - 1 - first)


def tile_visible(place_ref, pair_ref, seg_ref, step, part, per_seq, seq_len):
    group, cross = place_ref[0], place_ref[1]
    seq_k, span_k = span_of(pair_ref, group ^ (step // 2), cross ^ (step % 2), per_seq)
    seq_q, span_q = span_of(pair_ref, group, cross ^ part, per_seq)
    last_k = seg_ref[seq_k * seq_len + span_k * BLOCK + BLOCK - 1]
    first_q = seg_ref[seq_q * seq_len + span_q * BLOCK]
    visible = (seq_k == seq_q) & (span_k <= span_q) & (last_k >= first_q)
    spans = 2 * per_seq
    return visible, seq_k * spans + span_k, seq_q * spans + span_q


def tile_mask(seg_row_ref, seg_col_ref, place_k, place_q):
    lanes = lax.broadcasted_iota(jnp.int32, seg_col_ref.shape, 1)
    column = jnp.sum(jnp.where(lanes == place_k, seg_col_ref[...], 0), axis=1, keepdims=True)
    row = seg_row_ref[pl.ds(place_q, 1), :]
    row = jnp.concatenate([row, row], axis=1)
    return column == row


def stack_heads(ref, part):
    rows = pl.ds(part * BLOCK, BLOCK)
    return jnp.concatenate([ref[rows, :HEAD_WIDTH], ref[rows, HEAD_WIDTH:]], axis=0)


def forward_kernel(
    per_seq, place_ref, pair_ref, seg_ref, q_ref, kv_ref, row_ref, col_ref,
    low_ref, out_ref, lse_ref, max_ref, sum_ref, acc_ref,
):
    step = pl.program_id(0)
    seq_len = 2 * per_seq * BLOCK

    @pl.when(step == 0)
    def _():
        max_ref[...] = jnp.full(max_ref.shape, NEGATIVE, F32)
        sum_ref[...] = jnp.zeros(sum_ref.shape, F32)
        acc_ref[...] = jnp.zeros(acc_ref.shape, F32)

    for part in range(2):
        visible, place_k, place_q = tile_visible(
            place_ref, pair_ref, seg_ref, step, part, per_seq, seq_len
        )

        @pl.when(visible)
        def _():
            keys = kv_ref[:, :HEAD_WIDTH]
            values = kv_ref[:, HEAD_WIDTH:]
            queries = stack_heads(q_ref, part)
            scores = lax.dot_general(keys, queries, COLS, preferred_element_type=F32)
            mask = tile_mask(row_ref, col_ref, place_k, place_q)
            scores = jnp.where(mask, scores, NEGATIVE)
            old_max = max_ref[part]
            new_max = jnp.maximum(old_max, jnp.max(scores, axis=0, keepdims=True))
            weights = jnp.where(mask, jnp.exp(scores - new_max), 0.0)
            factor = jnp.exp(old_max - new_max)
            max_ref[part] = new_max
            sum_ref[part] = sum_ref[part] * factor + jnp.sum(weights, axis=0, keepdims=True)
            acc_ref[part] = acc_ref[part] * factor + lax.dot_general(
                values, weights.astype(BF16), ROWS, preferred_element_type=F32
            )

    @pl.when(step == pl.num_programs(0) - 1)
    def _():
        for part in range(2):
            total = sum_ref[part]
            attended = (acc_ref[part] / total).T
            rows = pl.ds(part * BLOCK, BLOCK)
            for head in range(2):
                one = attended[head * BLOCK : (head + 1) * BLOCK]
                cols = pl.ds(head * HEAD_WIDTH, HEAD_WIDTH)
                out_ref[rows, cols] = one
                low_ref[rows, cols] = one.astype(BF16)
            lse_ref[part] = max_ref[part] + jnp.log(total)


def backward_kernel(
    per_seq, place_ref, pair_ref, seg_ref, q_ref, kv_ref, row_ref, col_ref, lse_ref, out_ref, do_ref,
    dq_ref, dkv_ref, delta_ref, dq_acc, dk_acc, dv_acc,
):
    step = pl.program_id(0)
    seq_len = 2 * per_seq * BLOCK

    @pl.when(step == 0)
    def _():
        dq_acc[...] = jnp.zeros(dq_acc.shape, F32)
        for part in range(2):
            product = stack_heads(out_ref, part) * stack_heads(do_ref, part).astype(F32)
            delta_ref[part] = jnp.sum(product.T, axis=0, keepdims=True)

    dk_acc[...] = jnp.zeros(dk_acc.shape, F32)
    dv_acc[...] = jnp.zeros(dv_acc.shape, F32)
    for part in range(2):
        visible, place_k, place_q = tile_visible(
            place_ref, pair_ref, seg_ref, step, part, per_seq, seq_len
        )

        @pl.when(visible)
        def _():
            keys = kv_ref[:, :HEAD_WIDTH]
            values = kv_ref[:, HEAD_WIDTH:]
            queries = stack_heads(q_ref, part)
            grads = stack_heads(do_ref, part)
            scores = lax.dot_general(keys, queries, COLS, preferred_element_type=F32)
            mask = tile_mask(row_ref, col_ref, place_k, place_q)
            probs = jnp.where(mask, jnp.exp(scores - lse_ref[part]), 0.0)
            grad_probs = lax.dot_general(values, grads, COLS, preferred_element_type=F32)
            grad_scores = (probs * (grad_probs - delta_ref[part])).astype(BF16)
            dv_acc[...] += jnp.dot(probs.astype(BF16), grads, preferred_element_type=F32)
            dk_acc[...] += jnp.dot(grad_scores, queries, preferred_element_type=F32)
            dq_acc[part] += lax.dot_general(
                grad_scores, keys, ROWS, preferred_element_type=F32
            )

    dkv_ref[:, :HEAD_WIDTH] = dk_acc[...].astype(BF16)
    dkv_ref[:, HEAD_WIDTH:] = dv_acc[...].astype(BF16)

    @pl.when(step == pl.num_programs(0) - 1)
    def _():
        for part in range(2):
            rows = pl.ds(part * BLOCK, BLOCK)
            for head in range(2):
                one = dq_acc[part, head * BLOCK : (head + 1) * BLOCK]
                dq_ref[rows, pl.ds(head * HEAD_WIDTH, HEAD_WIDTH)] = (
                    one * HEAD_WIDTH ** (-0.5)
                ).astype(BF16)


def whole(shape):
    return pl.BlockSpec(shape, lambda step, *refs: (0,) * len(shape))


def attend(place, pair_order, seg_flat, queries, keys_values, seg_row, seg_col, per_seq):
    steps = keys_values.shape[0] // BLOCK
    rows, width = queries.shape
    return pl.pallas_call(
        functools.partial(forward_kernel, per_seq),
        grid_spec=pltpu.PrefetchScalarGridSpec(
            num_scalar_prefetch=3,
            grid=(steps,),
            in_specs=[
                whole(queries.shape),
                pl.BlockSpec((BLOCK, 2 * HEAD_WIDTH), lambda step, *refs: (step, 0)),
                whole(seg_row.shape),
                whole(seg_col.shape),
            ],
            out_specs=[whole((rows, width)), whole((rows, width)), whole((2, 1, rows))],
            scratch_shapes=[
                pltpu.VMEM((2, 1, rows), F32),
                pltpu.VMEM((2, 1, rows), F32),
                pltpu.VMEM((2, HEAD_WIDTH, rows), F32),
            ],
        ),
        out_shape=[
            jax.ShapeDtypeStruct((rows, width), BF16),
            jax.ShapeDtypeStruct((rows, width), F32),
            jax.ShapeDtypeStruct((2, 1, rows), F32),
        ],
        compiler_params=pltpu.CompilerParams(dimension_semantics=("arbitrary",)),
        cost_estimate=pl.CostEstimate(
            flops=6_000_000_000, bytes_accessed=6_000_000, transcendentals=2_000_000
        ),
        name="attend",
    )(place, pair_order, seg_flat, queries, keys_values, seg_row, seg_col)


def attend_back(
    place, pair_order, seg_flat, queries, keys_values, seg_row, seg_col, lse, out, grads, per_seq
):
    steps = keys_values.shape[0] // BLOCK
    rows, width = queries.shape
    return pl.pallas_call(
        functools.partial(backward_kernel, per_seq),
        grid_spec=pltpu.PrefetchScalarGridSpec(
            num_scalar_prefetch=3,
            grid=(steps,),
            in_specs=[
                whole(queries.shape),
                pl.BlockSpec((BLOCK, 2 * HEAD_WIDTH), lambda step, *refs: (step, 0)),
                whole(seg_row.shape),
                whole(seg_col.shape),
                whole(lse.shape),
                whole(out.shape),
                whole(grads.shape),
            ],
            out_specs=[
                whole((rows, width)),
                pl.BlockSpec((BLOCK, 2 * HEAD_WIDTH), lambda step, *refs: (step, 0)),
            ],
            scratch_shapes=[
                pltpu.VMEM((2, 1, rows), F32),
                pltpu.VMEM((2, rows, HEAD_WIDTH), F32),
                pltpu.VMEM((BLOCK, HEAD_WIDTH), F32),
                pltpu.VMEM((BLOCK, HEAD_WIDTH), F32),
            ],
        ),
        out_shape=[
            jax.ShapeDtypeStruct((rows, width), BF16),
            jax.ShapeDtypeStruct(keys_values.shape, BF16),
        ],
        compiler_params=pltpu.CompilerParams(dimension_semantics=("arbitrary",)),
        cost_estimate=pl.CostEstimate(
            flops=16_000_000_000, bytes_accessed=12_000_000, transcendentals=2_000_000
        ),
        name="attend_back",
    )(place, pair_order, seg_flat, queries, keys_values, seg_row, seg_col, lse, out, grads)


def gather_four(own):
    beside = swap(own, CORE, 0)
    across = swap(own, CROSS, 0)
    both = swap(across, CORE, 0)
    return jnp.concatenate([own, beside, across, both], axis=0)


def fold_four(partial_sum):
    rows = partial_sum.shape[0] // 4
    four = partial_sum.reshape(2, 2, rows, -1)
    across = add(four[1, 0], swap(four[1, 1], CORE, 0), BF16)
    own = add(four[0, 0], swap(four[0, 1], CORE, 0), F32)
    return own + swap(across, CROSS, 0).astype(F32)


def gather_eight(own):
    half = own.shape[1] // 2
    left, right = own[:, :half], own[:, half:]
    left_x = swap(left, CROSS, 0)
    right_t = swap(right, 0, TURN)
    left_t = swap(left, 0, TURN)
    right_x = swap(right, CROSS, 0)
    left_xt = swap(left_x, 0, TURN)
    right_xt = swap(right_t, CROSS, 0)
    four = jnp.concatenate(
        [
            jnp.concatenate([left, left_t, left_x, left_xt], axis=0),
            jnp.concatenate([right, right_t, right_x, right_xt], axis=0),
        ],
        axis=1,
    )
    return jnp.concatenate([four, swap(four, CORE, 0)], axis=0)


def fold_eight(partial_sum):
    rows, width = partial_sum.shape[0] // 8, partial_sum.shape[1]
    eight = partial_sum.reshape(2, 2, 2, rows, width)
    four = add(eight[0], swap(eight[1], CORE, 0), BF16)
    left, right = four[..., : width // 2], four[..., width // 2 :]
    left = add(left[:, 0], swap(left[:, 1], 0, TURN), BF16)
    right = add(right[0], swap(right[1], CROSS, 0), BF16)
    left = add(left[0], swap(left[1], CROSS, 0), F32)
    right = add(right[0], swap(right[1], 0, TURN), F32)
    return jnp.concatenate([left, right], axis=-1)


def rms_back(grad_norm, normed, inv_rms, gain):
    scaled = grad_norm * gain
    return inv_rms * (scaled - normed * jnp.mean(scaled * normed, axis=-1, keepdims=True))


def local(
    tokens,
    cotangent,
    segments,
    pair_order,
    norm_in,
    w_query,
    key_weight,
    value_weight,
    w_out,
    norm_mid,
    w_gate,
    w_up,
    w_down,
):
    heads = lax.axis_size("head")
    groups = lax.axis_size("blk")
    group = lax.axis_index("blk")
    head = lax.axis_index("head")
    cross, core = head // 2, head % 2
    turn = (group // TURN) % 2
    high, low = group // 4, group % 2
    token_rows, width = tokens.shape
    group_rows = token_rows * heads
    per_seq = groups // SEQS
    seq_len = segments.shape[1]
    shard = norm_in.shape[0]
    blk_masks = masks_of(groups)
    far_masks = [mask for mask in blk_masks if mask != TURN]
    key_local = HEAD_WIDTH
    query_local = w_query.shape[1] // heads

    rows = jnp.arange(group_rows, dtype=jnp.int32)
    local_row = (head ^ (rows // token_rows)) * token_rows + rows % token_rows
    pair = lax.dynamic_index_in_dim(pair_order, group, keepdims=False)
    first_span = pair % per_seq
    span = jnp.where(local_row < BLOCK, first_span, 2 * per_seq - 1 - first_span)
    positions = span * BLOCK + local_row % BLOCK
    angles = positions.astype(F32)[:, None] * frequencies(HEAD_WIDTH)[None, :]
    cosine, sine = jnp.cos(angles), jnp.sin(angles)
    seg_halves = segments.reshape(-1, 2, BLOCK // 2)
    seg_row = jnp.where(core == 0, seg_halves, seg_halves[:, ::-1]).reshape(-1, BLOCK)
    seg_col = seg_row.T
    seg_flat = segments.reshape(-1)
    place = jnp.stack([group, cross]).astype(jnp.int32)

    gains = jnp.zeros((2, heads * groups, shard), BF16)
    gains = lax.dynamic_update_slice(
        gains, jnp.stack([norm_in, norm_mid])[:, None], (0, head * groups + group, 0)
    )
    for mask in (CROSS, CORE):
        gains = gains + swap(gains, mask, 0)
    for mask in blk_masks:
        gains = gains + swap(gains, 0, mask)
    gains = gains.reshape(2, width).astype(F32)
    gain_in, gain_mid = gains[0], gains[1]

    def by_head(weight):
        return weight.reshape(shard, heads, -1).transpose(1, 0, 2)

    def gather_rows(local_cols):
        cols = local_cols.shape[-1]
        mine = lax.all_to_all(local_cols, "head", split_axis=0, concat_axis=0, tiled=True)
        full = jnp.zeros((heads, groups, shard, cols), BF16)
        for mask, piece in spread(mine, blk_masks).items():
            full = lax.dynamic_update_slice(full, piece[:, None], (0, group ^ mask, 0, 0))
        return full.reshape(width, cols)

    weight_in = gather_rows(
        jnp.concatenate([by_head(w_query), by_head(key_weight), by_head(value_weight)], axis=-1)
    )
    weight_out = gather_rows(by_head(w_out))

    token_group = gather_four(tokens).astype(F32)
    inv_group = lax.rsqrt(jnp.mean(token_group * token_group, axis=-1, keepdims=True) + EPS)
    input_low = (token_group * inv_group * gain_in).astype(BF16)
    lin = jnp.dot(input_low, weight_in, preferred_element_type=F32)
    keys_values = jnp.concatenate(
        [
            rotate(lin[:, query_local : query_local + key_local], cosine, sine).astype(BF16),
            lin[:, query_local + key_local :].astype(BF16),
        ],
        axis=-1,
    )
    queries = rotate(lin[:, :query_local], cosine, sine).astype(BF16)
    queries = queries * jnp.asarray(HEAD_WIDTH ** (-0.5), BF16)
    kv_pieces = spread(keys_values, blk_masks)
    kv_all = jnp.concatenate([kv_pieces[mask] for mask in range(groups)], axis=0)
    attention_low, attention_f, lse = attend(
        place, pair_order, seg_flat, queries, kv_all, seg_row, seg_col, per_seq
    )
    branch = fold_four(
        lax.dot_general(attention_low, weight_out, COLS, preferred_element_type=F32).astype(BF16)
    )
    tokens_f = tokens.astype(F32)
    middle = tokens_f + branch
    inv_mid = lax.rsqrt(jnp.mean(middle * middle, axis=-1, keepdims=True) + EPS)
    normed_mid = middle * inv_mid
    mid_low = (normed_mid * gain_mid).astype(BF16)

    ff_rows, ff_cols = w_gate.shape
    ff_own = ff_cols // 2

    def gather_ffn(weight):
        mine = lax.dynamic_slice_in_dim(weight, turn * ff_own, ff_own, 1)
        other = lax.dynamic_slice_in_dim(weight, (1 - turn) * ff_own, ff_own, 1)
        received = swap(other, 0, TURN)
        both = jnp.stack(
            [jnp.where(turn == 0, mine, received), jnp.where(turn == 0, received, mine)]
        )
        full = jnp.zeros((groups // 4, 2, 2, ff_rows, ff_own), BF16)
        for mask, piece in spread(both, far_masks).items():
            full = lax.dynamic_update_slice(
                full, piece[None, :, None], (high ^ (mask // 4), 0, low ^ (mask % 2), 0, 0)
            )
        return full.reshape(width, ff_own)

    down = gather_ffn(w_down)
    gate = gather_ffn(w_gate)
    up = gather_ffn(w_up)
    grad_group = gather_eight(cotangent)
    grad_hidden = jnp.dot(grad_group, down, preferred_element_type=F32)
    mid_group = gather_eight(mid_low)
    gate_lin = jnp.dot(mid_group, gate, preferred_element_type=F32)
    up_proj = jnp.dot(mid_group, up, preferred_element_type=F32)
    gate_sig = jax.nn.sigmoid(gate_lin)
    gate_silu = gate_lin * gate_sig
    hidden_act = (gate_silu * up_proj).astype(BF16)
    grad_gate_lin = (
        grad_hidden * up_proj * gate_sig * (1.0 + gate_lin * (1.0 - gate_sig))
    ).astype(BF16)
    grad_up_proj = (grad_hidden * gate_silu).astype(BF16)
    mid_partial = lax.dot_general(
        grad_gate_lin, gate, COLS, preferred_element_type=F32
    ) + lax.dot_general(grad_up_proj, up, COLS, preferred_element_type=F32)
    grad_mid = fold_eight(mid_partial.astype(BF16))
    ffn_partial = lax.dot_general(hidden_act, down, COLS, preferred_element_type=F32)
    ffn_out = fold_eight(ffn_partial.astype(BF16))
    layer_out = (middle + ffn_out).astype(BF16)

    def fold_ffn(lhs, rhs):
        partial_sum = lax.dot_general(lhs, rhs, ROWS, preferred_element_type=F32).astype(BF16)
        partial_sum = partial_sum.reshape(groups // 4, 2, 2, ff_rows, ff_own)
        pieces = {}
        for mask in range(groups):
            if mask & TURN:
                continue
            piece = lax.dynamic_slice(
                partial_sum,
                (high ^ (mask // 4), 0, low ^ (mask % 2), 0, 0),
                (1, 2, 1, ff_rows, ff_own),
            )
            pieces[mask] = piece.reshape(2, ff_rows, ff_own)
        total = fold(pieces, far_masks[::-1])
        mine = lax.dynamic_index_in_dim(total, turn, 0, keepdims=False)
        other = lax.dynamic_index_in_dim(total, 1 - turn, 0, keepdims=False).astype(BF16)
        received = swap(other, 0, TURN).astype(F32)
        return jnp.concatenate(
            [jnp.where(turn == 0, mine, received), jnp.where(turn == 0, received, mine)], axis=1
        )

    grad_down_w = fold_ffn(grad_group, hidden_act)
    grad_gate_w = fold_ffn(mid_group, grad_gate_lin)
    grad_up_w = fold_ffn(mid_group, grad_up_proj)

    def everywhere(vector):
        for mask in (CORE, CROSS):
            vector = vector + swap(vector, mask, 0)
        for mask in blk_masks:
            vector = vector + swap(vector, 0, mask)
        return lax.dynamic_slice_in_dim(vector, (head * groups + group) * shard, shard, 0)

    grad_norm_mid = everywhere(jnp.sum(grad_mid * normed_mid, axis=0))
    grad_y = cotangent.astype(F32)
    grad_middle = grad_y + rms_back(grad_mid, normed_mid, inv_mid, gain_mid)
    branch_group = gather_four(grad_middle.astype(BF16))

    def fold_rows(lhs, rhs):
        partial_sum = lax.dot_general(lhs, rhs, ROWS, preferred_element_type=F32).astype(BF16)
        cols = partial_sum.shape[1]
        partial_sum = partial_sum.reshape(heads, groups, shard, cols)
        pieces = {
            mask: lax.dynamic_index_in_dim(partial_sum, group ^ mask, 1, keepdims=False)
            for mask in range(groups)
        }
        total = fold(pieces, blk_masks[::-1]).astype(BF16)
        total = lax.all_to_all(total, "head", split_axis=0, concat_axis=0, tiled=True)
        return total.astype(F32)

    def full_cols(by_heads):
        return by_heads.transpose(1, 0, 2).reshape(shard, -1)

    grad_attention = jnp.dot(branch_group, weight_out, preferred_element_type=F32).astype(BF16)
    grad_out_w = full_cols(fold_rows(branch_group, attention_low))
    grad_queries, grad_kv = attend_back(
        place, pair_order, seg_flat, queries, kv_all, seg_row, seg_col,
        lse, attention_f, grad_attention, per_seq,
    )
    grad_kv = grad_kv.reshape(groups, group_rows, 2 * HEAD_WIDTH)
    kv_total = fold({mask: grad_kv[mask] for mask in range(groups)}, blk_masks[::-1])
    kv_low = kv_total.astype(BF16)
    grad_lin = jnp.concatenate(
        [
            rotate(grad_queries.astype(F32), cosine, -sine).astype(BF16),
            rotate(kv_low[:, :HEAD_WIDTH].astype(F32), cosine, -sine).astype(BF16),
            kv_low[:, HEAD_WIDTH:],
        ],
        axis=-1,
    )
    grad_in = fold_four(
        lax.dot_general(grad_lin, weight_in, COLS, preferred_element_type=F32).astype(BF16)
    )
    in_grads = fold_rows(input_low, grad_lin)
    inv_in = inv_group[:token_rows]
    normed_in = tokens_f * inv_in
    grad_norm_in = everywhere(jnp.sum(grad_in * normed_in, axis=0))
    grad_tokens = grad_middle + rms_back(grad_in, normed_in, inv_in, gain_in)
    first_value = query_local + key_local
    return (
        layer_out,
        grad_tokens,
        grad_norm_in,
        full_cols(in_grads[..., :query_local]),
        full_cols(in_grads[..., query_local:first_value]),
        full_cols(in_grads[..., first_value:]),
        grad_out_w,
        grad_norm_mid,
        grad_gate_w,
        grad_up_w,
        grad_down_w,
    )


def solution(mesh):
    rows = P(("blk", "head"), None)
    shards = P(("head", "blk"), None)
    vector = P(("head", "blk"))
    hidden = P("blk", "head")
    return jax.shard_map(
        local,
        mesh=mesh,
        in_specs=(
            rows, rows, P(), P(), vector, shards, shards, shards, shards, vector, hidden, hidden, hidden,
        ),
        out_specs=(
            rows, rows, vector, shards, shards, shards, shards, vector, hidden, hidden, hidden,
        ),
        check_vma=False,
    )
```

time: 3070 us -> 961 us (0.31)
  waiting for transfers between devices: 2190 us -> 583 us
  local copies, waits for them, and re-layouts: 274 us -> 44.7 us
  matrix products: 217 us -> 75 us
  starting transfers between devices: 248 us -> 131 us
  blocking collectives: 42.2 us -> 0 us
    unnamed x14 -> x0, waiting for transfers between devices: 1070 us -> none
    all_gather x9 -> x0, waiting for transfers between devices: 447 us -> none  [the longest x1 127 us: fetch_ffn(): lax.all_gather(w_down, 'blk', axis=0, tiled=True)]
    reduce_scatter x3 -> x0, waiting for transfers between devices: 228 us -> none  [the longest x1 217 us: local(): lax.psum_scatter(jnp.concatenate([lax.dot_general(mid_group, grad_gate_li...]
    ppermute x48 -> x117, waiting for transfers between devices: 415 us -> 572 us  [swap(): lax.ppermute(value, ('head', 'blk'), [(i, i ^ mask) for i in range(count)])]
    concatenate x2 -> x3, local copies, waits for them, and re-layouts: 133 us -> 1.01 us  [the longest x1 0.95 us: local(): jnp.concatenate([by_head(w_query), by_head(key_weight), by_head(value_wei...]
    dot_general x75 -> x15, matrix products: 206 us -> 75 us  [the longest x3 17.2 us: fold_ffn(): lax.dot_general(lhs, rhs, ROWS, preferred_element_type=F32).astype(BF16)]
    ppermute x48 -> x117, starting transfers between devices: 213 us -> 117 us  [swap(): lax.ppermute(value, ('head', 'blk'), [(i, i ^ mask) for i in range(count)])]
    unnamed x88 -> x161, local copies, waits for them, and re-layouts: 64.3 us -> 4.84 us
  transfers between devices with their start and end apart: 69 -> 121, of which waited for: 49 -> 50; matrix products, arithmetic and copies ran while one was open for 17% -> 16% of each run, Pallas kernels for 0% -> 3%
where the time goes in v1:
time: 961 us; the launch traced here: 951 us
  waiting for transfers between devices  583 us (61%)
  starting transfers between devices  131 us (14%)
  other arithmetic  84.3 us (9%)
  matrix products  75 us (8%)
  local copies, waits for them, and re-layouts  44.7 us (5%)
  Pallas kernels  28.4 us (3%)
    ppermute x117, waiting for transfers between devices, swap(): lax.ppermute(value, ('head', 'blk'), [(i, i ^ mask) for i in range(count)])  572 us
    ppermute x117, starting transfers between devices, swap(): lax.ppermute(value, ('head', 'blk'), [(i, i ^ mask) for i in range(count)])  117 us
    concatenate x2, other arithmetic, gather_eight(): jnp.concatenate([jnp.concatenate([left, left_t, left_x, left_xt], axis=0)...  26.7 us
  transfers between devices with their start and end apart: 121, of which 50 were waited for; matrix products, arithmetic and copies ran while one was open for 16% of the time, Pallas kernels for 3%

profile of v1, /device:TPU:0, one launch (start us, length us, event | category | flops | bytes accessed | tf_op | source)
XLA Modules:
  0.0 951.4 jit_solution(7036125397121895767)
XLA Ops:
  2.7 3.0 collective-permute-start.43
  12.2 3.4 all-to-all-start.1
  28.8 3.6 collective-permute-start.6
  38.5 3.5 all-to-all-start
  45.6 5.2 all-to-all-done
  51.4 6.8 collective-permute-done.22
  64.0 3.4 collective-permute-done.59
  75.5 3.1 collective-permute-done.58
  79.1 7.3 collective-permute-done.61
  87.3 13.4 %maximum_maximum_fusion.1 = bf16[512,2048]{1,0:T(8,128)(2,1)} fusion(bf16[128,1024]{1,0:T(8,128)(2,1)S(1)} %collective-permute-done.61, bf16[128,1024]{1,0:T(8,128)(2,1)S(1)} %collective-permute-done.60, bf16[128,1024]{1,0:T(8,128)(2,1)S(1)} %collective-permute-done.59, bf16[128,1024]{1,0:T(8,128)(2,1)S(1)} %copy-done.23, ...), kind=kLoop, calls=%fused_computation.27 | loop fusion | flops 16777216 | bytes 4194304 | tf_op jit(solution)/shard_map/concatenate | solution.py:315
  104.1 6.6 collective-permute-done.8
  111.3 10.6 %collective-permute-done.9 = bf16[4,64,1024]{2,1,0:T(8,128)(2,1)S(1)} collective-permute-done((bf16[4,64,1024]{2,1,0:T(8,128)(2,1)S(1)}, bf16[4,64,1024]{2,1,0:T(8,128)(2,1)S(1)}, u32[]{:S(2)}, u32[]{:S(2)}) %collective-permute-start.9) | collective-permute-done | bytes 524320 | tf_op jit(solution)/shard_map/ppermute | solution.py:45
  125.0 11.6 %collective-permute-done.10 = bf16[4,64,1024]{2,1,0:T(8,128)(2,1)S(1)} collective-permute-done((bf16[4,64,1024]{2,1,0:T(8,128)(2,1)S(1)}, bf16[4,64,1024]{2,1,0:T(8,128)(2,1)S(1)}, u32[]{:S(2)}, u32[]{:S(2)}) %collective-permute-start.10) | collective-permute-done | bytes 524320 | tf_op jit(solution)/shard_map/ppermute | solution.py:45
  139.5 12.0 %collective-permute-done.13 = bf16[4,64,1024]{2,1,0:T(8,128)(2,1)S(1)} collective-permute-done((bf16[4,64,1024]{2,1,0:T(8,128)(2,1)S(1)}, bf16[4,64,1024]{2,1,0:T(8,128)(2,1)S(1)}, u32[]{:S(2)}, u32[]{:S(2)}) %collective-permute-start.13) | collective-permute-done | bytes 524320 | tf_op jit(solution)/shard_map/ppermute | solution.py:45
  152.1 10.7 %collective-permute-done.14 = bf16[4,64,1024]{2,1,0:T(8,128)(2,1)S(1)} collective-permute-done((bf16[4,64,1024]{2,1,0:T(8,128)(2,1)S(1)}, bf16[4,64,1024]{2,1,0:T(8,128)(2,1)S(1)}, u32[]{:S(2)}, u32[]{:S(2)}) %collective-permute-start.14) | collective-permute-done | bytes 524320 | tf_op jit(solution)/shard_map/ppermute | solution.py:45
  174.1 54.2 %collective-permute-done.18 = bf16[512,512]{1,0:T(8,128)(2,1)S(1)} collective-permute-done((bf16[512,512]{1,0:T(8,128)(2,1)S(1)}, bf16[512,512]{1,0:T(8,128)(2,1)S(1)}, u32[]{:S(2)}, u32[]{:S(2)}) %collective-permute-start.18) | collective-permute-done | bytes 524320 | tf_op jit(solution)/shard_map/ppermute | solution.py:45
  233.3 8.2 collective-permute-done.20
  246.5 8.7 collective-permute-done.19
  255.8 33.1 %collective-permute-done.21 = bf16[512,512]{1,0:T(8,128)(2,1)S(1)} collective-permute-done((bf16[512,512]{1,0:T(8,128)(2,1)S(1)}, bf16[512,512]{1,0:T(8,128)(2,1)S(1)}, u32[]{:S(2)}, u32[]{:S(2)}) %collective-permute-start.21) | collective-permute-done | bytes 524320 | tf_op jit(solution)/shard_map/ppermute | solution.py:45
  290.9 13.3 %attend.1 = (bf16[512,512]{1,0:T(8,128)(2,1)}, f32[512,512]{1,0:T(8,128)}, f32[2,1,512]{2,1,0:T(1,128)}) custom-call(s32[2]{0:T(128)} %pad_add_fusion.place_ref, s32[8]{0:T(128)} %pair_ref.3, s32[4096]{0:T(1024)} %bitcast.438, bf16[512,512]{1,0:T(8,128)(2,1)} %maximum_multiply_fusion.q_ref, bf16[4096,512]{1,0:T(8,128)(2,1)} %copy-done.57, ...), custom_call_target="tpu_custom_call" | custom-call | flops 6000000000 | bytes 6000000 | tf_op jit(solution)/shard_map/attend/pallas_call | solution.py:218
  304.2 3.1 convolution_convert_fusion.7
  308.7 5.0 collective-permute-start.40
  319.9 9.7 %collective-permute-done.31 = bf16[128,2048]{1,0:T(8,128)(2,1)S(1)} collective-permute-done((bf16[128,2048]{1,0:T(8,128)(2,1)S(1)}, bf16[128,2048]{1,0:T(8,128)(2,1)S(1)}, u32[]{:S(2)}, u32[]{:S(2)}) %collective-permute-start.31) | collective-permute-done | bytes 524320 | tf_op jit(solution)/shard_map/ppermute | solution.py:45
  332.0 26.5 %collective-permute-done.40 = bf16[2,256,1024]{2,1,0:T(8,128)(2,1)S(1)} collective-permute-done((bf16[2,256,1024]{2,1,0:T(8,128)(2,1)S(1)}, bf16[2,256,1024]{2,1,0:T(8,128)(2,1)S(1)}, u32[]{:S(2)}, u32[]{:S(2)}) %collective-permute-start.40) | collective-permute-done | bytes 1048608 | tf_op jit(solution)/shard_map/ppermute | solution.py:45
  360.7 11.7 %collective-permute-done.35 = bf16[128,1024]{1,0:T(8,128)(2,1)S(1)} collective-permute-done((bf16[128,1024]{1,0:T(8,128)(2,1)S(1)}, bf16[128,1024]{1,0:T(8,128)(2,1)S(1)}, u32[]{:S(2)}, u32[]{:S(2)}) %collective-permute-start.35) | collective-permute-done | bytes 262176 | tf_op jit(solution)/shard_map/ppermute | solution.py:45
  373.7 6.2 collective-permute-done.36
  381.7 5.2 collective-permute-done.37
  386.9 13.3 %maximum_maximum_fusion = bf16[512,2048]{1,0:T(8,128)(2,1)S(1)} fusion(bf16[128,1024]{1,0:T(8,128)(2,1)S(1)} %collective-permute-done.37, bf16[128,1024]{1,0:T(8,128)(2,1)S(1)} %collective-permute-done.36, bf16[128,1024]{1,0:T(8,128)(2,1)S(1)} %collective-permute-done.35, bf16[128,1024]{1,0:T(8,128)(2,1)S(1)} %get-tuple-element.94, ...), kind=kLoop, calls=%fused_computation.26 | loop fusion | flops 16777216 | bytes 4194304 | tf_op jit(solution)/shard_map/concatenate | solution.py:315
  400.5 10.5 %collective-permute-done.42 = bf16[2,256,1024]{2,1,0:T(8,128)(2,1)S(1)} collective-permute-done((bf16[2,256,1024]{2,1,0:T(8,128)(2,1)S(1)}, bf16[2,256,1024]{2,1,0:T(8,128)(2,1)S(1)}, u32[]{:S(2)}, u32[]{:S(2)}) %collective-permute-start.42) | collective-permute-done | bytes 1048608 | tf_op jit(solution)/shard_map/ppermute | solution.py:45
  411.2 7.9 fusion.114
  419.1 2.8 pad_maximum_fusion
  421.9 4.5 fusion.121
  426.5 7.7 multiply_convert_fusion.1
  434.2 5.2 convolution_convert_fusion.2
  439.4 6.9 fusion.122
  446.3 4.8 convolution_convert_fusion.4
  451.1 7.0 convolution_convert_fusion.1
  464.5 5.0 convolution_convert_fusion.3
  471.0 12.0 %add_convert_fusion = bf16[1024,2048]{1,0:T(8,128)(2,1)} fusion(f32[1024,2048]{1,0:T(8,128)} %fusion.122, bf16[1024,1024]{1,0:T(8,128)(2,1)} %get-tuple-element.31, bf16[2048,1024]{1,0:T(8,128)(2,1)} %bitcast.400), kind=kOutput, calls=%fused_computation | convolution fusion | flops 4299161600 | bytes 18874368 | tf_op jit(solution)/shard_map/dot_general | solution.py:474
  483.0 2.7 collective-permute-done.114
  491.8 38.8 %collective-permute-done.110 = bf16[2,256,1024]{2,1,0:T(8,128)(2,1)} collective-permute-done((bf16[2,256,1024]{2,1,0:T(8,128)(2,1)}, bf16[2,256,1024]{2,1,0:T(8,128)(2,1)}, u32[]{:S(2)}, u32[]{:S(2)}) %collective-permute-start.110) | collective-permute-done | bytes 1048608 | tf_op jit(solution)/shard_map/ppermute | solution.py:45
  532.6 43.0 %collective-permute-done.106 = bf16[2,256,1024]{2,1,0:T(8,128)(2,1)} collective-permute-done((bf16[2,256,1024]{2,1,0:T(8,128)(2,1)}, bf16[2,256,1024]{2,1,0:T(8,128)(2,1)}, u32[]{:S(2)}, u32[]{:S(2)}) %collective-permute-start.106) | collective-permute-done | bytes 1048608 | tf_op jit(solution)/shard_map/ppermute | solution.py:45
  584.4 61.4 %collective-permute-done.111 = bf16[2,256,1024]{2,1,0:T(8,128)(2,1)} collective-permute-done((bf16[2,256,1024]{2,1,0:T(8,128)(2,1)S(1)}, bf16[2,256,1024]{2,1,0:T(8,128)(2,1)}, u32[]{:S(2)}, u32[]{:S(2)}) %collective-permute-start.111) | collective-permute-done | bytes 1048608 | tf_op jit(solution)/shard_map/ppermute | solution.py:45
  650.1 18.1 %collective-permute-done.107 = bf16[2,256,1024]{2,1,0:T(8,128)(2,1)S(1)} collective-permute-done((bf16[2,256,1024]{2,1,0:T(8,128)(2,1)S(1)}, bf16[2,256,1024]{2,1,0:T(8,128)(2,1)S(1)}, u32[]{:S(2)}, u32[]{:S(2)}) %collective-permute-start.107) | collective-permute-done | bytes 1048608 | tf_op jit(solution)/shard_map/ppermute | solution.py:45
  675.3 37.8 %collective-permute-done.64 = bf16[2,128,1024]{2,1,0:T(8,128)(2,1)S(1)} collective-permute-done((bf16[2,128,1024]{2,1,0:T(8,128)(2,1)S(1)}, bf16[2,128,1024]{2,1,0:T(8,128)(2,1)S(1)}, u32[]{:S(2)}, u32[]{:S(2)}) %collective-permute-start.64) | collective-permute-done | bytes 524320 | tf_op jit(solution)/shard_map/ppermute | solution.py:45
  714.6 12.3 %collective-permute-done.52 = bf16[2,128,1024]{2,1,0:T(8,128)(2,1)S(1)} collective-permute-done((bf16[2,128,1024]{2,1,0:T(8,128)(2,1)S(1)}, bf16[2,128,1024]{2,1,0:T(8,128)(2,1)S(1)}, u32[]{:S(2)}, u32[]{:S(2)}) %collective-permute-start.52) | collective-permute-done | bytes 524320 | tf_op jit(solution)/shard_map/ppermute | solution.py:45
  729.2 5.2 collective-permute-done.65
  736.6 4.2 collective-permute-done.53
  746.6 7.5 collective-permute-done.69
  761.9 15.1 %attend_back.1 = (bf16[512,512]{1,0:T(8,128)(2,1)}, bf16[4096,512]{1,0:T(8,128)(2,1)}) custom-call(s32[2]{0:T(128)} %pad_add_fusion.place_ref, s32[8]{0:T(128)} %pair_ref.3, s32[4096]{0:T(1024)} %bitcast.439, bf16[512,512]{1,0:T(8,128)(2,1)} %maximum_multiply_fusion.q_ref, bf16[4096,512]{1,0:T(8,128)(2,1)} %copy-done.57, s32[16,256]{1,0:T(8,128)} %copy.149.row_ref, ...), custom_call_target="tpu_custom_call" | custom-call | flops 16000000000 | bytes 12000000 | tf_op jit(solution)/shard_map/attend_back/pallas_call | solution.py:254
  784.3 9.6 %collective-permute-done.72 = bf16[512,512]{1,0:T(8,128)(2,1)S(1)} collective-permute-done((bf16[512,512]{1,0:T(8,128)(2,1)S(1)}, bf16[512,512]{1,0:T(8,128)(2,1)S(1)}, u32[]{:S(2)}, u32[]{:S(2)}) %collective-permute-start.72) | collective-permute-done | bytes 524320 | tf_op jit(solution)/shard_map/ppermute | solution.py:45
  793.9 11.2 %collective-permute-done.75 = bf16[512,512]{1,0:T(8,128)(2,1)S(1)} collective-permute-done((bf16[512,512]{1,0:T(8,128)(2,1)S(1)}, bf16[512,512]{1,0:T(8,128)(2,1)S(1)}, u32[]{:S(2)}, u32[]{:S(2)}) %collective-permute-start.75) | collective-permute-done | bytes 524320 | tf_op jit(solution)/shard_map/ppermute | solution.py:45
  813.0 3.4 collective-permute-done.74
  817.4 4.4 collective-permute-start.77
  828.1 10.7 %collective-permute-done.71 = bf16[512,512]{1,0:T(8,128)(2,1)S(1)} collective-permute-done((bf16[512,512]{1,0:T(8,128)(2,1)S(1)}, bf16[512,512]{1,0:T(8,128)(2,1)S(1)}, u32[]{:S(2)}, u32[]{:S(2)}) %collective-permute-start.71) | collective-permute-done | bytes 524320 | tf_op jit(solution)/shard_map/ppermute | solution.py:45
  848.1 2.9 convolution_convert_fusion
  857.2 9.8 %collective-permute-done.87 = bf16[4,64,1024]{2,1,0:T(8,128)(2,1)S(1)} collective-permute-done((bf16[4,64,1024]{2,1,0:T(8,128)(2,1)S(1)}, bf16[4,64,1024]{2,1,0:T(8,128)(2,1)S(1)}, u32[]{:S(2)}, u32[]{:S(2)}) %collective-permute-start.87) | collective-permute-done | bytes 524320 | tf_op jit(solution)/shard_map/ppermute | solution.py:45
  869.4 8.4 collective-permute-done.90
  886.7 3.4 all-to-all-start.3
  890.6 6.0 collective-permute-done.80
  900.9 4.2 collective-permute-start.92
  909.7 19.8 %collective-permute-done.83 = f32[2048]{0:T(1024)S(1)} collective-permute-done((f32[2048]{0:T(1024)S(1)}, f32[2048]{0:T(1024)S(1)}, u32[]{:S(2)}, u32[]{:S(2)}) %collective-permute-start.83) | collective-permute-done | bytes 8224 | tf_op jit(solution)/shard_map/ppermute | solution.py:45
  936.1 3.5 all-to-all-start.2
  942.8 5.6 all-to-all-done.2
  (521 shorter events, 220.8 us)
Async XLA Ops:
  2.7 66.3 %collective-permute-start.43 = (bf16[256,1024]{1,0:T(8,128)(2,1)}, bf16[256,1024]{1,0:T(8,128)(2,1)}, u32[]{:S(2)}, u32[]{:S(2)}) collective-permute-start(bf16[256,1024]{1,0:T(8,128)(2,1)} %constant_dynamic-slice_fusion.1), channel_id=1, source_target_pairs={{0,2},{1,3},{2,0},{3,1},{4,6},{5,7},{6,4},{7,5},{8,10},{9,11},{10,... | collective-permute-start | bytes 1572872 | tf_op jit(solution)/shard_map/ppermute | solution.py:45
  7.6 61.5 %collective-permute-start.47 = (bf16[256,1024]{1,0:T(8,128)(2,1)}, bf16[256,1024]{1,0:T(8,128)(2,1)}, u32[]{:S(2)}, u32[]{:S(2)}) collective-permute-start(bf16[256,1024]{1,0:T(8,128)(2,1)} %constant_dynamic-slice_fusion), channel_id=1, source_target_pairs={{0,2},{1,3},{2,0},{3,1},{4,6},{5,7},{6,4},{7,5},{8,10},{9,11},{10,... | collective-permute-start | bytes 1572872 | tf_op jit(solution)/shard_map/ppermute | solution.py:45
  12.2 26.3 %all-to-all-start.1 = ((bf16[4,64,512]{2,1,0:T(8,128)(2,1)}), bf16[4,64,512]{2,1,0:T(8,128)(2,1)S(1)}, u32[]{:S(2)}, u32[]{:S(2)}) async-start(bf16[4,64,512]{2,1,0:T(8,128)(2,1)} %copy.150), calls=%async_computation.1 | async-start | bytes 524288 | tf_op jit(solution)/shard_map/all_to_all | solution.py:404
  17.5 44.7 %collective-permute-start.57 = (bf16[128,1024]{1,0:T(8,128)(2,1)}, bf16[128,1024]{1,0:T(8,128)(2,1)}, u32[]{:S(2)}, u32[]{:S(2)}) collective-permute-start(bf16[128,1024]{1,0:T(8,128)(2,1)} %get-tuple-element.91), channel_id=1, source_target_pairs={{0,16},{1,17},{2,18},{3,19},{4,20},{5,21},{6,22},{7,23},{8,24},{9,... | collective-permute-start | bytes 786440 | tf_op jit(solution)/shard_map/ppermute | solution.py:45
  67.4 33.3 %collective-permute-start.1 = (bf16[128,2048]{1,0:T(8,128)(2,1)S(1)}, bf16[128,2048]{1,0:T(8,128)(2,1)S(1)}, u32[]{:S(2)}, u32[]{:S(2)}) collective-permute-start(bf16[128,2048]{1,0:T(8,128)(2,1)S(1)} %copy-done), channel_id=1, source_target_pairs={{0,16},{1,17},{2,18},{3,19},{4,20},{5,21},{6,22},{7,23},{8,24},{9,... | collective-permute-start | bytes 1572872 | tf_op jit(solution)/shard_map/ppermute | solution.py:45
  73.0 29.5 %collective-permute-start.39 = (bf16[256,1024]{1,0:T(8,128)(2,1)S(1)}, bf16[256,1024]{1,0:T(8,128)(2,1)S(1)}, u32[]{:S(2)}, u32[]{:S(2)}) collective-permute-start(bf16[256,1024]{1,0:T(8,128)(2,1)S(1)} %copy-done.37), channel_id=1, source_target_pairs={{0,2},{1,3},{2,0},{3,1},{4,6},{5,7},{6,4},{7,5},{8,10},{9,11},{10,... | collective-permute-start | bytes 1572872 | tf_op jit(solution)/shard_map/ppermute | solution.py:45
  75.5 46.5 %collective-permute-start = (bf16[128,2048]{1,0:T(8,128)(2,1)S(1)}, bf16[128,2048]{1,0:T(8,128)(2,1)S(1)}, u32[]{:S(2)}, u32[]{:S(2)}) collective-permute-start(bf16[128,2048]{1,0:T(8,128)(2,1)S(1)} %copy-done), channel_id=1, source_target_pairs={{0,8},{1,9},{2,10},{3,11},{4,12},{5,13},{6,14},{7,15},{8,0},{9,1},... | collective-permute-start | bytes 1572872 | tf_op jit(solution)/shard_map/ppermute | solution.py:45
  78.6 91.8 %collective-permute-start.25 = (bf16[4,64,512]{2,1,0:T(8,128)(2,1)S(1)}, bf16[4,64,512]{2,1,0:T(8,128)(2,1)S(1)}, u32[]{:S(2)}, u32[]{:S(2)}) collective-permute-start(bf16[4,64,512]{2,1,0:T(8,128)(2,1)S(1)} %all-to-all-done.1), channel_id=1, source_target_pairs={{0,1},{1,0},{2,3},{3,2},{4,5},{5,4},{6,7},{7,6},{8,9},{9,8},{10,11... | collective-permute-start | bytes 786440 | tf_op jit(solution)/shard_map/ppermute | solution.py:45
  86.5 24.3 %collective-permute-start.8 = (bf16[4,64,1024]{2,1,0:T(8,128)(2,1)S(1)}, bf16[4,64,1024]{2,1,0:T(8,128)(2,1)S(1)}, u32[]{:S(2)}, u32[]{:S(2)}) collective-permute-start(bf16[4,64,1024]{2,1,0:T(8,128)(2,1)S(1)} %all-to-all-done), channel_id=1, source_target_pairs={{0,4},{1,5},{2,6},{3,7},{4,0},{5,1},{6,2},{7,3},{8,12},{9,13},{10,... | collective-permute-start | bytes 1572872 | tf_op jit(solution)/shard_map/ppermute | solution.py:45
  102.5 21.5 %collective-permute-start.2 = (bf16[128,2048]{1,0:T(8,128)(2,1)S(1)}, bf16[128,2048]{1,0:T(8,128)(2,1)S(1)}, u32[]{:S(2)}, u32[]{:S(2)}) collective-permute-start(bf16[128,2048]{1,0:T(8,128)(2,1)S(1)} %collective-permute-done.1), channel_id=1, source_target_pairs={{0,8},{1,9},{2,10},{3,11},{4,12},{5,13},{6,14},{7,15},{8,0},{9,1},... | collective-permute-start | bytes 1572872 | tf_op jit(solution)/shard_map/ppermute | solution.py:45
  110.7 26.5 %collective-permute-start.11 = (bf16[4,64,1024]{2,1,0:T(8,128)(2,1)S(1)}, bf16[4,64,1024]{2,1,0:T(8,128)(2,1)S(1)}, u32[]{:S(2)}, u32[]{:S(2)}) collective-permute-start(bf16[4,64,1024]{2,1,0:T(8,128)(2,1)S(1)} %all-to-all-done), channel_id=1, source_target_pairs={{0,1},{1,0},{2,3},{3,2},{4,5},{5,4},{6,7},{7,6},{8,9},{9,8},{10,11... | collective-permute-start | bytes 1572872 | tf_op jit(solution)/shard_map/ppermute | solution.py:45
  121.9 45.2 %collective-permute-start.24 = (bf16[4,64,512]{2,1,0:T(8,128)(2,1)}, bf16[4,64,512]{2,1,0:T(8,128)(2,1)S(1)}, u32[]{:S(2)}, u32[]{:S(2)}) collective-permute-start(bf16[4,64,512]{2,1,0:T(8,128)(2,1)} %collective-permute-done.22), channel_id=1, source_target_pairs={{0,2},{1,3},{2,0},{3,1},{4,6},{5,7},{6,4},{7,5},{8,10},{9,11},{10,... | collective-permute-start | bytes 786440 | tf_op jit(solution)/shard_map/ppermute | solution.py:45
  137.2 25.5 %collective-permute-start.14 = (bf16[4,64,1024]{2,1,0:T(8,128)(2,1)S(1)}, bf16[4,64,1024]{2,1,0:T(8,128)(2,1)S(1)}, u32[]{:S(2)}, u32[]{:S(2)}) collective-permute-start(bf16[4,64,1024]{2,1,0:T(8,128)(2,1)S(1)} %collective-permute-done.10), channel_id=1, source_target_pairs={{0,1},{1,0},{2,3},{3,2},{4,5},{5,4},{6,7},{7,6},{8,9},{9,8},{10,11... | collective-permute-start | bytes 1572872 | tf_op jit(solution)/shard_map/ppermute | solution.py:45
  138.8 32.3 %collective-permute-start.26 = (bf16[4,64,512]{2,1,0:T(8,128)(2,1)}, bf16[4,64,512]{2,1,0:T(8,128)(2,1)S(1)}, u32[]{:S(2)}, u32[]{:S(2)}) collective-permute-start(bf16[4,64,512]{2,1,0:T(8,128)(2,1)} %collective-permute-done.22), channel_id=1, source_target_pairs={{0,1},{1,0},{2,3},{3,2},{4,5},{5,4},{6,7},{7,6},{8,9},{9,8},{10,11... | collective-permute-start | bytes 786440 | tf_op jit(solution)/shard_map/ppermute | solution.py:45
  151.5 22.1 %collective-permute-start.27 = (bf16[4,64,512]{2,1,0:T(8,128)(2,1)}, bf16[4,64,512]{2,1,0:T(8,128)(2,1)S(1)}, u32[]{:S(2)}, u32[]{:S(2)}) collective-permute-start(bf16[4,64,512]{2,1,0:T(8,128)(2,1)} %collective-permute-done.23), channel_id=1, source_target_pairs={{0,1},{1,0},{2,3},{3,2},{4,5},{5,4},{6,7},{7,6},{8,9},{9,8},{10,11... | collective-permute-start | bytes 786440 | tf_op jit(solution)/shard_map/ppermute | solution.py:45
  162.7 146.0 %collective-permute-start.44 = (bf16[2,256,1024]{2,1,0:T(8,128)(2,1)}, bf16[2,256,1024]{2,1,0:T(8,128)(2,1)}, u32[]{:S(2)}, u32[]{:S(2)}) collective-permute-start(bf16[2,256,1024]{2,1,0:T(8,128)(2,1)} %pad_maximum_fusion.8), channel_id=1, source_target_pairs={{0,4},{1,5},{2,6},{3,7},{4,0},{5,1},{6,2},{7,3},{8,12},{9,13},{10,... | collective-permute-start | bytes 3145736 | tf_op jit(solution)/shard_map/ppermute | solution.py:45
  167.1 61.2 %collective-permute-start.18 = (bf16[512,512]{1,0:T(8,128)(2,1)S(1)}, bf16[512,512]{1,0:T(8,128)(2,1)S(1)}, u32[]{:S(2)}, u32[]{:S(2)}) collective-permute-start(bf16[512,512]{1,0:T(8,128)(2,1)S(1)} %get-tuple-element.95), channel_id=1, source_target_pairs={{0,4},{1,5},{2,6},{3,7},{4,0},{5,1},{6,2},{7,3},{8,12},{9,13},{10,... | collective-permute-start | bytes 1572872 | tf_op jit(solution)/shard_map/ppermute | solution.py:45
  170.4 58.7 %collective-permute-start.16 = (bf16[512,512]{1,0:T(8,128)(2,1)S(1)}, bf16[512,512]{1,0:T(8,128)(2,1)S(1)}, u32[]{:S(2)}, u32[]{:S(2)}) collective-permute-start(bf16[512,512]{1,0:T(8,128)(2,1)S(1)} %get-tuple-element.95), channel_id=1, source_target_pairs={{0,2},{1,3},{2,0},{3,1},{4,6},{5,7},{6,4},{7,5},{8,10},{9,11},{10,... | collective-permute-start | bytes 1572872 | tf_op jit(solution)/shard_map/ppermute | solution.py:45
  171.1 58.5 %collective-permute-start.28 = (bf16[4,64,512]{2,1,0:T(8,128)(2,1)S(1)}, bf16[4,64,512]{2,1,0:T(8,128)(2,1)S(1)}, u32[]{:S(2)}, u32[]{:S(2)}) collective-permute-start(bf16[4,64,512]{2,1,0:T(8,128)(2,1)S(1)} %collective-permute-done.24), channel_id=1, source_target_pairs={{0,1},{1,0},{2,3},{3,2},{4,5},{5,4},{6,7},{7,6},{8,9},{9,8},{10,11... | collective-permute-start | bytes 786440 | tf_op jit(solution)/shard_map/ppermute | solution.py:45
  173.6 59.1 %collective-permute-start.15 = (bf16[512,512]{1,0:T(8,128)(2,1)S(1)}, bf16[512,512]{1,0:T(8,128)(2,1)S(1)}, u32[]{:S(2)}, u32[]{:S(2)}) collective-permute-start(bf16[512,512]{1,0:T(8,128)(2,1)S(1)} %get-tuple-element.95), channel_id=1, source_target_pairs={{0,1},{1,0},{2,3},{3,2},{4,5},{5,4},{6,7},{7,6},{8,9},{9,8},{10,11... | collective-permute-start | bytes 1572872 | tf_op jit(solution)/shard_map/ppermute | solution.py:45
  230.3 24.9 %collective-permute-start.19 = (bf16[512,512]{1,0:T(8,128)(2,1)S(1)}, bf16[512,512]{1,0:T(8,128)(2,1)S(1)}, u32[]{:S(2)}, u32[]{:S(2)}) collective-permute-start(bf16[512,512]{1,0:T(8,128)(2,1)S(1)} %collective-permute-done.18), channel_id=1, source_target_pairs={{0,1},{1,0},{2,3},{3,2},{4,5},{5,4},{6,7},{7,6},{8,9},{9,8},{10,11... | collective-permute-start | bytes 1572872 | tf_op jit(solution)/shard_map/ppermute | solution.py:45
  232.7 85.7 %collective-permute-start.45 = (bf16[2,256,1024]{2,1,0:T(8,128)(2,1)}, bf16[2,256,1024]{2,1,0:T(8,128)(2,1)}, u32[]{:S(2)}, u32[]{:S(2)}) collective-permute-start(bf16[2,256,1024]{2,1,0:T(8,128)(2,1)} %pad_maximum_fusion.8), channel_id=1, source_target_pairs={{0,1},{1,0},{2,3},{3,2},{4,5},{5,4},{6,7},{7,6},{8,9},{9,8},{10,11... | collective-permute-start | bytes 3145736 | tf_op jit(solution)/shard_map/ppermute | solution.py:45
  241.5 47.4 %collective-permute-start.21 = (bf16[512,512]{1,0:T(8,128)(2,1)S(1)}, bf16[512,512]{1,0:T(8,128)(2,1)S(1)}, u32[]{:S(2)}, u32[]{:S(2)}) collective-permute-start(bf16[512,512]{1,0:T(8,128)(2,1)S(1)} %collective-permute-done.20), channel_id=1, source_target_pairs={{0,1},{1,0},{2,3},{3,2},{4,5},{5,4},{6,7},{7,6},{8,9},{9,8},{10,11... | collective-permute-start | bytes 1572872 | tf_op jit(solution)/shard_map/ppermute | solution.py:45
  243.9 71.5 %collective-permute-start.48 = (bf16[2,256,1024]{2,1,0:T(8,128)(2,1)}, bf16[2,256,1024]{2,1,0:T(8,128)(2,1)}, u32[]{:S(2)}, u32[]{:S(2)}) collective-permute-start(bf16[2,256,1024]{2,1,0:T(8,128)(2,1)} %pad_maximum_fusion.9), channel_id=1, source_target_pairs={{0,4},{1,5},{2,6},{3,7},{4,0},{5,1},{6,2},{7,3},{8,12},{9,13},{10,... | collective-permute-start | bytes 3145736 | tf_op jit(solution)/shard_map/ppermute | solution.py:45
  255.2 75.2 %collective-permute-start.49 = (bf16[2,256,1024]{2,1,0:T(8,128)(2,1)}, bf16[2,256,1024]{2,1,0:T(8,128)(2,1)S(1)}, u32[]{:S(2)}, u32[]{:S(2)}) collective-permute-start(bf16[2,256,1024]{2,1,0:T(8,128)(2,1)} %pad_maximum_fusion.9), channel_id=1, source_target_pairs={{0,1},{1,0},{2,3},{3,2},{4,5},{5,4},{6,7},{7,6},{8,9},{9,8},{10,11... | collective-permute-start | bytes 3145736 | tf_op jit(solution)/shard_map/ppermute | solution.py:45
  308.7 49.8 %collective-permute-start.40 = (bf16[2,256,1024]{2,1,0:T(8,128)(2,1)S(1)}, bf16[2,256,1024]{2,1,0:T(8,128)(2,1)S(1)}, u32[]{:S(2)}, u32[]{:S(2)}) collective-permute-start(bf16[2,256,1024]{2,1,0:T(8,128)(2,1)S(1)} %pad_maximum_fusion.7), channel_id=1, source_target_pairs={{0,4},{1,5},{2,6},{3,7},{4,0},{5,1},{6,2},{7,3},{8,12},{9,13},{10,... | collective-permute-start | bytes 3145736 | tf_op jit(solution)/shard_map/ppermute | solution.py:45
  318.4 40.1 %collective-permute-start.41 = (bf16[2,256,1024]{2,1,0:T(8,128)(2,1)S(1)}, bf16[2,256,1024]{2,1,0:T(8,128)(2,1)S(1)}, u32[]{:S(2)}, u32[]{:S(2)}) collective-permute-start(bf16[2,256,1024]{2,1,0:T(8,128)(2,1)S(1)} %pad_maximum_fusion.7), channel_id=1, source_target_pairs={{0,1},{1,0},{2,3},{3,2},{4,5},{5,4},{6,7},{7,6},{8,9},{9,8},{10,11... | collective-permute-start | bytes 3145736 | tf_op jit(solution)/shard_map/ppermute | solution.py:45
  319.9 91.3 %collective-permute-start.62 = (bf16[512,2048]{1,0:T(8,128)(2,1)S(1)}, bf16[512,2048]{1,0:T(8,128)(2,1)S(1)}, u32[]{:S(2)}, u32[]{:S(2)}) collective-permute-start(bf16[512,2048]{1,0:T(8,128)(2,1)S(1)} %copy-done.20), channel_id=1, source_target_pairs={{0,8},{1,9},{2,10},{3,11},{4,12},{5,13},{6,14},{7,15},{8,0},{9,1},... | collective-permute-start | bytes 6291464 | tf_op jit(solution)/shard_map/ppermute | solution.py:45
  329.7 70.6 %collective-permute-start.46 = (bf16[2,256,1024]{2,1,0:T(8,128)(2,1)}, bf16[2,256,1024]{2,1,0:T(8,128)(2,1)S(1)}, u32[]{:S(2)}, u32[]{:S(2)}) collective-permute-start(bf16[2,256,1024]{2,1,0:T(8,128)(2,1)} %collective-permute-done.44), channel_id=1, source_target_pairs={{0,1},{1,0},{2,3},{3,2},{4,5},{5,4},{6,7},{7,6},{8,9},{9,8},{10,11... | collective-permute-start | bytes 3145736 | tf_op jit(solution)/shard_map/ppermute | solution.py:45
  330.4 30.2 %collective-permute-start.33 = (bf16[128,1024]{1,0:T(8,128)(2,1)S(1)}, bf16[128,1024]{1,0:T(8,128)(2,1)S(1)}, u32[]{:S(2)}, u32[]{:S(2)}) collective-permute-start(bf16[128,1024]{1,0:T(8,128)(2,1)S(1)} %get-tuple-element.93), channel_id=1, source_target_pairs={{0,16},{1,17},{2,18},{3,19},{4,20},{5,21},{6,22},{7,23},{8,24},{9,... | collective-permute-start | bytes 786440 | tf_op jit(solution)/shard_map/ppermute | solution.py:45
  360.6 39.8 %collective-permute-start.50 = (bf16[2,256,1024]{2,1,0:T(8,128)(2,1)}, bf16[2,256,1024]{2,1,0:T(8,128)(2,1)S(1)}, u32[]{:S(2)}, u32[]{:S(2)}) collective-permute-start(bf16[2,256,1024]{2,1,0:T(8,128)(2,1)} %collective-permute-done.48), channel_id=1, source_target_pairs={{0,1},{1,0},{2,3},{3,2},{4,5},{5,4},{6,7},{7,6},{8,9},{9,8},{10,11... | collective-permute-start | bytes 3145736 | tf_op jit(solution)/shard_map/ppermute | solution.py:45
  379.9 31.1 %collective-permute-start.42 = (bf16[2,256,1024]{2,1,0:T(8,128)(2,1)S(1)}, bf16[2,256,1024]{2,1,0:T(8,128)(2,1)S(1)}, u32[]{:S(2)}, u32[]{:S(2)}) collective-permute-start(bf16[2,256,1024]{2,1,0:T(8,128)(2,1)S(1)} %collective-permute-done.40), channel_id=1, source_target_pairs={{0,1},{1,0},{2,3},{3,2},{4,5},{5,4},{6,7},{7,6},{8,9},{9,8},{10,11... | collective-permute-start | bytes 3145736 | tf_op jit(solution)/shard_map/ppermute | solution.py:45
  459.3 26.4 %collective-permute-start.114 = (bf16[2,256,1024]{2,1,0:T(8,128)(2,1)}, bf16[2,256,1024]{2,1,0:T(8,128)(2,1)}, u32[]{:S(2)}, u32[]{:S(2)}) collective-permute-start(bf16[2,256,1024]{2,1,0:T(8,128)(2,1)} %get-tuple-element.35), channel_id=1, source_target_pairs={{0,1},{1,0},{2,3},{3,2},{4,5},{5,4},{6,7},{7,6},{8,9},{9,8},{10,11... | collective-permute-start | bytes 3145736 | tf_op jit(solution)/shard_map/ppermute | solution.py:45
  459.6 117.6 %collective-permute-start.113 = (bf16[2,256,1024]{2,1,0:T(8,128)(2,1)S(1)}, bf16[2,256,1024]{2,1,0:T(8,128)(2,1)}, u32[]{:S(2)}, u32[]{:S(2)}) collective-permute-start(bf16[2,256,1024]{2,1,0:T(8,128)(2,1)S(1)} %get-tuple-element.34), channel_id=1, source_target_pairs={{0,1},{1,0},{2,3},{3,2},{4,5},{5,4},{6,7},{7,6},{8,9},{9,8},{10,11... | collective-permute-start | bytes 3145736 | tf_op jit(solution)/shard_map/ppermute | solution.py:45
  462.5 68.2 %collective-permute-start.110 = (bf16[2,256,1024]{2,1,0:T(8,128)(2,1)}, bf16[2,256,1024]{2,1,0:T(8,128)(2,1)}, u32[]{:S(2)}, u32[]{:S(2)}) collective-permute-start(bf16[2,256,1024]{2,1,0:T(8,128)(2,1)} %get-tuple-element.37), channel_id=1, source_target_pairs={{0,1},{1,0},{2,3},{3,2},{4,5},{5,4},{6,7},{7,6},{8,9},{9,8},{10,11... | collective-permute-start | bytes 3145736 | tf_op jit(solution)/shard_map/ppermute | solution.py:45
  462.8 121.5 %collective-permute-start.109 = (bf16[2,256,1024]{2,1,0:T(8,128)(2,1)S(1)}, bf16[2,256,1024]{2,1,0:T(8,128)(2,1)}, u32[]{:S(2)}, u32[]{:S(2)}) collective-permute-start(bf16[2,256,1024]{2,1,0:T(8,128)(2,1)S(1)} %get-tuple-element.36), channel_id=1, source_target_pairs={{0,1},{1,0},{2,3},{3,2},{4,5},{5,4},{6,7},{7,6},{8,9},{9,8},{10,11... | collective-permute-start | bytes 3145736 | tf_op jit(solution)/shard_map/ppermute | solution.py:45
  470.7 104.9 %collective-permute-start.106 = (bf16[2,256,1024]{2,1,0:T(8,128)(2,1)}, bf16[2,256,1024]{2,1,0:T(8,128)(2,1)}, u32[]{:S(2)}, u32[]{:S(2)}) collective-permute-start(bf16[2,256,1024]{2,1,0:T(8,128)(2,1)} %get-tuple-element.39), channel_id=1, source_target_pairs={{0,1},{1,0},{2,3},{3,2},{4,5},{5,4},{6,7},{7,6},{8,9},{9,8},{10,11... | collective-permute-start | bytes 3145736 | tf_op jit(solution)/shard_map/ppermute | solution.py:45
  487.4 91.6 %collective-permute-start.115 = (bf16[2,256,1024]{2,1,0:T(8,128)(2,1)S(1)}, bf16[2,256,1024]{2,1,0:T(8,128)(2,1)S(1)}, u32[]{:S(2)}, u32[]{:S(2)}) collective-permute-start(bf16[2,256,1024]{2,1,0:T(8,128)(2,1)S(1)} %fusion.6), channel_id=1, source_target_pairs={{0,4},{1,5},{2,6},{3,7},{4,0},{5,1},{6,2},{7,3},{8,12},{9,13},{10,... | collective-permute-start | bytes 3145736 | tf_op jit(solution)/shard_map/ppermute | solution.py:45
  530.7 117.4 %collective-permute-start.105 = (bf16[2,256,1024]{2,1,0:T(8,128)(2,1)S(1)}, bf16[2,256,1024]{2,1,0:T(8,128)(2,1)}, u32[]{:S(2)}, u32[]{:S(2)}) collective-permute-start(bf16[2,256,1024]{2,1,0:T(8,128)(2,1)S(1)} %get-tuple-element.38), channel_id=1, source_target_pairs={{0,1},{1,0},{2,3},{3,2},{4,5},{5,4},{6,7},{7,6},{8,9},{9,8},{10,11... | collective-permute-start | bytes 3145736 | tf_op jit(solution)/shard_map/ppermute | solution.py:45
  575.6 94.6 %collective-permute-start.63 = (bf16[2,2,128,2048]{3,2,1,0:T(8,128)(2,1)S(1)}, bf16[2,2,128,2048]{3,2,1,0:T(8,128)(2,1)S(1)}, u32[]{:S(2)}, u32[]{:S(2)}) collective-permute-start(bf16[2,2,128,2048]{3,2,1,0:T(8,128)(2,1)S(1)} %bitcast.424), channel_id=1, source_target_pairs={{0,8},{1,9},{2,10},{3,11},{4,12},{5,13},{6,14},{7,15},{8,0},{9,1},... | collective-permute-start | bytes 6291464 | tf_op jit(solution)/shard_map/ppermute | solution.py:45
  577.2 68.6 %collective-permute-start.111 = (bf16[2,256,1024]{2,1,0:T(8,128)(2,1)S(1)}, bf16[2,256,1024]{2,1,0:T(8,128)(2,1)}, u32[]{:S(2)}, u32[]{:S(2)}) collective-permute-start(bf16[2,256,1024]{2,1,0:T(8,128)(2,1)S(1)} %fusion.8), channel_id=1, source_target_pairs={{0,4},{1,5},{2,6},{3,7},{4,0},{5,1},{6,2},{7,3},{8,12},{9,13},{10,... | collective-permute-start | bytes 3145736 | tf_op jit(solution)/shard_map/ppermute | solution.py:45
  580.0 88.3 %collective-permute-start.107 = (bf16[2,256,1024]{2,1,0:T(8,128)(2,1)S(1)}, bf16[2,256,1024]{2,1,0:T(8,128)(2,1)S(1)}, u32[]{:S(2)}, u32[]{:S(2)}) collective-permute-start(bf16[2,256,1024]{2,1,0:T(8,128)(2,1)S(1)} %fusion.10), channel_id=1, source_target_pairs={{0,4},{1,5},{2,6},{3,7},{4,0},{5,1},{6,2},{7,3},{8,12},{9,13},{10,... | collective-permute-start | bytes 3145736 | tf_op jit(solution)/shard_map/ppermute | solution.py:45
  584.3 88.9 %collective-permute-start.51 = (bf16[2,2,128,2048]{3,2,1,0:T(8,128)(2,1)S(1)}, bf16[2,2,128,2048]{3,2,1,0:T(8,128)(2,1)S(1)}, u32[]{:S(2)}, u32[]{:S(2)}) collective-permute-start(bf16[2,2,128,2048]{3,2,1,0:T(8,128)(2,1)S(1)} %bitcast.425), channel_id=1, source_target_pairs={{0,8},{1,9},{2,10},{3,11},{4,12},{5,13},{6,14},{7,15},{8,0},{9,1},... | collective-permute-start | bytes 6291464 | tf_op jit(solution)/shard_map/ppermute | solution.py:45
  645.8 98.3 %collective-permute-start.116 = (bf16[256,1024]{1,0:T(8,128)(2,1)S(1)}, bf16[256,1024]{1,0:T(8,128)(2,1)S(1)}, u32[]{:S(2)}, u32[]{:S(2)}) collective-permute-start(bf16[256,1024]{1,0:T(8,128)(2,1)S(1)} %fusion.38), channel_id=1, source_target_pairs={{0,2},{1,3},{2,0},{3,1},{4,6},{5,7},{6,4},{7,5},{8,10},{9,11},{10,... | collective-permute-start | bytes 1572872 | tf_op jit(solution)/shard_map/ppermute | solution.py:45
  648.0 96.4 %collective-permute-start.112 = (bf16[256,1024]{1,0:T(8,128)(2,1)S(1)}, bf16[256,1024]{1,0:T(8,128)(2,1)S(1)}, u32[]{:S(2)}, u32[]{:S(2)}) collective-permute-start(bf16[256,1024]{1,0:T(8,128)(2,1)S(1)} %fusion.37), channel_id=1, source_target_pairs={{0,2},{1,3},{2,0},{3,1},{4,6},{5,7},{6,4},{7,5},{8,10},{9,11},{10,... | collective-permute-start | bytes 1572872 | tf_op jit(solution)/shard_map/ppermute | solution.py:45
  670.1 84.0 %collective-permute-start.108 = (bf16[256,1024]{1,0:T(8,128)(2,1)S(1)}, bf16[256,1024]{1,0:T(8,128)(2,1)S(1)}, u32[]{:S(2)}, u32[]{:S(2)}) collective-permute-start(bf16[256,1024]{1,0:T(8,128)(2,1)S(1)} %fusion.36), channel_id=1, source_target_pairs={{0,2},{1,3},{2,0},{3,1},{4,6},{5,7},{6,4},{7,5},{8,10},{9,11},{10,... | collective-permute-start | bytes 1572872 | tf_op jit(solution)/shard_map/ppermute | solution.py:45
  671.1 42.0 %collective-permute-start.64 = (bf16[2,128,1024]{2,1,0:T(8,128)(2,1)S(1)}, bf16[2,128,1024]{2,1,0:T(8,128)(2,1)S(1)}, u32[]{:S(2)}, u32[]{:S(2)}) collective-permute-start(bf16[2,128,1024]{2,1,0:T(8,128)(2,1)S(1)} %slice_bitcast_fusion.7), channel_id=1, source_target_pairs={{0,2},{1,3},{2,0},{3,1},{4,6},{5,7},{6,4},{7,5},{8,10},{9,11},{10,... | collective-permute-start | bytes 1572872 | tf_op jit(solution)/shard_map/ppermute | solution.py:45
  673.2 39.9 %collective-permute-start.66 = (bf16[2,128,1024]{2,1,0:T(8,128)(2,1)S(1)}, bf16[2,128,1024]{2,1,0:T(8,128)(2,1)S(1)}, u32[]{:S(2)}, u32[]{:S(2)}) collective-permute-start(bf16[2,128,1024]{2,1,0:T(8,128)(2,1)S(1)} %slice_bitcast_fusion.5), channel_id=1, source_target_pairs={{0,16},{1,17},{2,18},{3,19},{4,20},{5,21},{6,22},{7,23},{8,24},{9,... | collective-permute-start | bytes 1572872 | tf_op jit(solution)/shard_map/ppermute | solution.py:45
  759.1 23.4 %collective-permute-start.102 = (f32[2048]{0:T(1024)S(1)}, f32[2048]{0:T(1024)S(1)}, u32[]{:S(2)}, u32[]{:S(2)}) collective-permute-start(f32[2048]{0:T(1024)S(1)} %add.535), channel_id=1, source_target_pairs={{0,4},{1,5},{2,6},{3,7},{4,0},{5,1},{6,2},{7,3},{8,12},{9,13},{10,... | collective-permute-start | bytes 24584 | tf_op jit(solution)/shard_map/ppermute | solution.py:45
  779.3 25.8 %collective-permute-start.75 = (bf16[512,512]{1,0:T(8,128)(2,1)S(1)}, bf16[512,512]{1,0:T(8,128)(2,1)S(1)}, u32[]{:S(2)}, u32[]{:S(2)}) collective-permute-start(bf16[512,512]{1,0:T(8,128)(2,1)S(1)} %get-tuple-element.47), channel_id=1, source_target_pairs={{0,1},{1,0},{2,3},{3,2},{4,5},{5,4},{6,7},{7,6},{8,9},{9,8},{10,11... | collective-permute-start | bytes 1572872 | tf_op jit(solution)/shard_map/ppermute | solution.py:45
  782.5 33.8 %collective-permute-start.74 = (bf16[512,512]{1,0:T(8,128)(2,1)S(1)}, bf16[512,512]{1,0:T(8,128)(2,1)S(1)}, u32[]{:S(2)}, u32[]{:S(2)}) collective-permute-start(bf16[512,512]{1,0:T(8,128)(2,1)S(1)} %get-tuple-element.48), channel_id=1, source_target_pairs={{0,1},{1,0},{2,3},{3,2},{4,5},{5,4},{6,7},{7,6},{8,9},{9,8},{10,11... | collective-permute-start | bytes 1572872 | tf_op jit(solution)/shard_map/ppermute | solution.py:45
  808.5 30.3 %collective-permute-start.71 = (bf16[512,512]{1,0:T(8,128)(2,1)S(1)}, bf16[512,512]{1,0:T(8,128)(2,1)S(1)}, u32[]{:S(2)}, u32[]{:S(2)}) collective-permute-start(bf16[512,512]{1,0:T(8,128)(2,1)S(1)} %get-tuple-element.46), channel_id=1, source_target_pairs={{0,1},{1,0},{2,3},{3,2},{4,5},{5,4},{6,7},{7,6},{8,9},{9,8},{10,11... | collective-permute-start | bytes 1572872 | tf_op jit(solution)/shard_map/ppermute | solution.py:45
  816.3 22.8 %collective-permute-start.73 = (bf16[512,512]{1,0:T(8,128)(2,1)S(1)}, bf16[512,512]{1,0:T(8,128)(2,1)S(1)}, u32[]{:S(2)}, u32[]{:S(2)}) collective-permute-start(bf16[512,512]{1,0:T(8,128)(2,1)S(1)} %get-tuple-element.50), channel_id=1, source_target_pairs={{0,2},{1,3},{2,0},{3,1},{4,6},{5,7},{6,4},{7,5},{8,10},{9,11},{10,... | collective-permute-start | bytes 1572872 | tf_op jit(solution)/shard_map/ppermute | solution.py:45
  817.4 24.2 %collective-permute-start.77 = (bf16[512,512]{1,0:T(8,128)(2,1)S(1)}, bf16[512,512]{1,0:T(8,128)(2,1)S(1)}, u32[]{:S(2)}, u32[]{:S(2)}) collective-permute-start(bf16[512,512]{1,0:T(8,128)(2,1)S(1)} %add_convert_fusion.5), channel_id=1, source_target_pairs={{0,4},{1,5},{2,6},{3,7},{4,0},{5,1},{6,2},{7,3},{8,12},{9,13},{10,... | collective-permute-start | bytes 1572872 | tf_op jit(solution)/shard_map/ppermute | solution.py:45
  824.1 55.4 %collective-permute-start.103 = (f32[2048]{0:T(1024)S(1)}, f32[2048]{0:T(1024)S(1)}, u32[]{:S(2)}, u32[]{:S(2)}) collective-permute-start(f32[2048]{0:T(1024)S(1)} %add.536), channel_id=1, source_target_pairs={{0,2},{1,3},{2,0},{3,1},{4,6},{5,7},{6,4},{7,5},{8,10},{9,11},{10,... | collective-permute-start | bytes 24584 | tf_op jit(solution)/shard_map/ppermute | solution.py:45
  827.6 24.7 %collective-permute-start.96 = (bf16[4,64,512]{2,1,0:T(8,128)(2,1)S(1)}, bf16[4,64,512]{2,1,0:T(8,128)(2,1)S(1)}, u32[]{:S(2)}, u32[]{:S(2)}) collective-permute-start(bf16[4,64,512]{2,1,0:T(8,128)(2,1)S(1)} %get-tuple-element.69), channel_id=1, source_target_pairs={{0,1},{1,0},{2,3},{3,2},{4,5},{5,4},{6,7},{7,6},{8,9},{9,8},{10,11... | collective-permute-start | bytes 786440 | tf_op jit(solution)/shard_map/ppermute | solution.py:45
  838.8 40.7 %collective-permute-start.93 = (bf16[4,64,512]{2,1,0:T(8,128)(2,1)S(1)}, bf16[4,64,512]{2,1,0:T(8,128)(2,1)S(1)}, u32[]{:S(2)}, u32[]{:S(2)}) collective-permute-start(bf16[4,64,512]{2,1,0:T(8,128)(2,1)S(1)} %get-tuple-element.68), channel_id=1, source_target_pairs={{0,1},{1,0},{2,3},{3,2},{4,5},{5,4},{6,7},{7,6},{8,9},{9,8},{10,11... | collective-permute-start | bytes 786440 | tf_op jit(solution)/shard_map/ppermute | solution.py:45
  852.3 25.4 %collective-permute-start.90 = (bf16[4,64,1024]{2,1,0:T(8,128)(2,1)S(1)}, bf16[4,64,1024]{2,1,0:T(8,128)(2,1)S(1)}, u32[]{:S(2)}, u32[]{:S(2)}) collective-permute-start(bf16[4,64,1024]{2,1,0:T(8,128)(2,1)S(1)} %get-tuple-element.43), channel_id=1, source_target_pairs={{0,1},{1,0},{2,3},{3,2},{4,5},{5,4},{6,7},{7,6},{8,9},{9,8},{10,11... | collective-permute-start | bytes 1572872 | tf_op jit(solution)/shard_map/ppermute | solution.py:45
  854.4 27.1 %collective-permute-start.95 = (bf16[4,64,512]{2,1,0:T(8,128)(2,1)S(1)}, bf16[4,64,512]{2,1,0:T(8,128)(2,1)S(1)}, u32[]{:S(2)}, u32[]{:S(2)}) collective-permute-start(bf16[4,64,512]{2,1,0:T(8,128)(2,1)S(1)} %get-tuple-element.72), channel_id=1, source_target_pairs={{0,2},{1,3},{2,0},{3,1},{4,6},{5,7},{6,4},{7,5},{8,10},{9,11},{10,... | collective-permute-start | bytes 786440 | tf_op jit(solution)/shard_map/ppermute | solution.py:45
  884.2 22.1 %collective-permute-start.104 = (f32[2048]{0:T(1024)S(1)}, f32[2048]{0:T(1024)S(1)}, u32[]{:S(2)}, u32[]{:S(2)}) collective-permute-start(f32[2048]{0:T(1024)S(1)} %add.537), channel_id=1, source_target_pairs={{0,1},{1,0},{2,3},{3,2},{4,5},{5,4},{6,7},{7,6},{8,9},{9,8},{10,11... | collective-permute-start | bytes 24584 | tf_op jit(solution)/shard_map/ppermute | solution.py:45
  886.7 22.2 %all-to-all-start.3 = ((bf16[4,64,512]{2,1,0:T(8,128)(2,1)}), bf16[4,64,512]{2,1,0:T(8,128)(2,1)S(1)}, u32[]{:S(2)}, u32[]{:S(2)}) async-start(bf16[4,64,512]{2,1,0:T(8,128)(2,1)} %add_convert_fusion.11), calls=%async_computation.3 | async-start | bytes 524288 | tf_op jit(solution)/shard_map/all_to_all | solution.py:528
  890.1 43.4 %collective-permute-start.86 = (bf16[4,64,1024]{2,1,0:T(8,128)(2,1)}, bf16[4,64,1024]{2,1,0:T(8,128)(2,1)}, u32[]{:S(2)}, u32[]{:S(2)}) collective-permute-start(bf16[4,64,1024]{2,1,0:T(8,128)(2,1)} %get-tuple-element.40), channel_id=1, source_target_pairs={{0,1},{1,0},{2,3},{3,2},{4,5},{5,4},{6,7},{7,6},{8,9},{9,8},{10,11... | collective-permute-start | bytes 1572872 | tf_op jit(solution)/shard_map/ppermute | solution.py:45
  896.6 36.9 %collective-permute-start.88 = (bf16[4,64,1024]{2,1,0:T(8,128)(2,1)}, bf16[4,64,1024]{2,1,0:T(8,128)(2,1)}, u32[]{:S(2)}, u32[]{:S(2)}) collective-permute-start(bf16[4,64,1024]{2,1,0:T(8,128)(2,1)} %get-tuple-element.44), channel_id=1, source_target_pairs={{0,2},{1,3},{2,0},{3,1},{4,6},{5,7},{6,4},{7,5},{8,10},{9,11},{10,... | collective-permute-start | bytes 1572872 | tf_op jit(solution)/shard_map/ppermute | solution.py:45
  900.9 32.6 %collective-permute-start.92 = (bf16[4,64,1024]{2,1,0:T(8,128)(2,1)}, bf16[4,64,1024]{2,1,0:T(8,128)(2,1)}, u32[]{:S(2)}, u32[]{:S(2)}) collective-permute-start(bf16[4,64,1024]{2,1,0:T(8,128)(2,1)} %add_convert_fusion.2), channel_id=1, source_target_pairs={{0,4},{1,5},{2,6},{3,7},{4,0},{5,1},{6,2},{7,3},{8,12},{9,13},{10,... | collective-permute-start | bytes 1572872 | tf_op jit(solution)/shard_map/ppermute | solution.py:45
  (133 other events, 2287.2 us)

commit v2 on v1

v2 whole, which is shorter than its diff:
```python
import functools

import jax
import jax.numpy as jnp
from jax import lax
from jax.experimental import pallas as pl
from jax.experimental.layout import Layout, with_layout_constraint
from jax.experimental.pallas import tpu as pltpu
from jax.sharding import PartitionSpec as P

QUERY_HEAD_COUNT = 8
KEY_VALUE_HEADS = 4
HEAD_WIDTH = 256
SEQS = 2
BLOCK = 256

EPS = 1e-06
THETA = 1000042.0
NEGATIVE = -1e30
ROWS = (((0,), (0,)), ((), ()))
COLS = (((1,), (1,)), ((), ()))
BF16 = jnp.bfloat16
F32 = jnp.float32

CORE, CROSS, TURN = 1, 2, 2


def frequencies(head_size):
    return 1.0 / THETA ** (jnp.arange(0, head_size, 2, dtype=F32) / head_size)


def rotate(values, cosine, sine):
    half = HEAD_WIDTH // 2
    parts = []
    for first in range(0, values.shape[-1], HEAD_WIDTH):
        a = values[:, first : first + half]
        b = values[:, first + half : first + HEAD_WIDTH]
        parts += [a * cosine - b * sine, b * cosine + a * sine]
    return jnp.concatenate(parts, axis=-1)


def row_major(value):
    return with_layout_constraint(value, Layout(tuple(range(value.ndim))))


def swap(value, head_mask, blk_mask):
    groups = lax.axis_size("blk")
    count = lax.axis_size("head") * groups
    mask = head_mask * groups + blk_mask
    pairs = [(i, i ^ mask) for i in range(count)]
    return row_major(lax.ppermute(row_major(value), ("head", "blk"), pairs))


def masks_of(size):
    out, bit = [], size >> 1
    while bit:
        out.append(bit)
        bit >>= 1
    return out


def add(a, b, dtype):
    return (a.astype(F32) + b.astype(F32)).astype(dtype)


def pair(own, received, bit, axis):
    first = jnp.where(bit == 0, own, received)
    second = jnp.where(bit == 0, received, own)
    return jnp.stack([first, second], axis=axis)


def after(value, *others):
    return lax.optimization_barrier((value, *others))[0]


def assemble_kernel(places, *refs):
    parts, out, sems = refs[:-2], refs[-2], refs[-1]
    copies = [
        pltpu.make_async_copy(
            part,
            out.at[pl.ds(row, part.shape[0]), pl.ds(col, part.shape[1])],
            sems.at[i],
        )
        for i, (part, (row, col)) in enumerate(zip(parts, places))
    ]
    for copy in copies:
        copy.start()
    for copy in copies:
        copy.wait()


def assemble(parts, places):
    rows = max(row + part.shape[0] for part, (row, _) in zip(parts, places))
    cols = max(col + part.shape[1] for part, (_, col) in zip(parts, places))
    return pl.pallas_call(
        functools.partial(assemble_kernel, places),
        in_specs=[pl.BlockSpec(memory_space=pl.ANY)] * len(parts),
        out_specs=pl.BlockSpec(memory_space=pltpu.VMEM),
        out_shape=jax.ShapeDtypeStruct((rows, cols), parts[0].dtype),
        scratch_shapes=[pltpu.SemaphoreType.DMA((len(parts),))],
        cost_estimate=pl.CostEstimate(
            flops=0, bytes_accessed=4 * rows * cols, transcendentals=0
        ),
        name="assemble",
    )(*parts)


def stack_rows(parts):
    places, row = [], 0
    for part in parts:
        places.append((row, 0))
        row += part.shape[0]
    return assemble(parts, places)


class Sent:
    value = None


class Flow:
    def __init__(self):
        self.batch, self.before = [], []

    def send(self, value, head_mask, blk_mask):
        sent = Sent()
        self.batch.append((sent, value, head_mask, blk_mask))
        return sent

    def go(self):
        if not self.batch:
            return
        values = tuple(entry[1] for entry in self.batch)
        held = lax.optimization_barrier(values + tuple(sent.value for sent in self.before))
        arrived = [
            swap(value, head_mask, blk_mask)
            for (_, _, head_mask, blk_mask), value in zip(self.batch, held)
        ]
        for (sent, *_), value in zip(self.batch, lax.optimization_barrier(tuple(arrived))):
            sent.value = value
        self.before = [entry[0] for entry in self.batch]
        self.batch = []


    def join(self, value):
        return after(value, *(sent.value for sent in self.before))


class Spread:
    def __init__(self, own, masks):
        self.masks, self.have = masks, {0: own}
        self.sents = {}

    def wave(self, flow, count):
        self.settle()
        for key in sorted(self.have):
            if bin(key).count("1") == count:
                for mask in self.masks:
                    if key == 0 or mask < (key & -key):
                        self.sents[key ^ mask] = flow.send(
                            self.have[key], CROSS if mask == 1 else 0, mask & ~1
                        )

    def settle(self):
        for key, sent in list(self.sents.items()):
            self.have[key] = sent.value
            del self.sents[key]


class Chain:
    def __init__(self, own, masks):
        self.blocks, self.masks, self.sent = own[None], list(masks), None

    def advance(self, flow):
        self.settle()
        if self.masks:
            mask = self.masks.pop(0)
            self.sent = flow.send(self.blocks, CROSS if mask == 1 else 0, mask & ~1)

    def settle(self):
        if self.sent is not None:
            self.blocks = jnp.concatenate([self.blocks, self.sent.value], axis=0)
            self.sent = None


class Fold:
    def __init__(self, blocks, masks):
        self.blocks, self.masks, self.sent = blocks, list(masks), None

    def advance(self, flow):
        if self.sent is not None:
            self.blocks = add(self.keep, self.sent.value, BF16 if self.masks else F32)
            self.sent = None
        if not self.masks:
            return False
        mask = self.masks.pop(0)
        half = self.blocks.shape[0] // 2
        self.keep = self.blocks[:half]
        self.sent = flow.send(self.blocks[half:], CROSS if mask == 1 else 0, mask & ~1)
        return True


class Bulk:
    def __init__(self, masks, count):
        self.masks = masks
        self.pieces, self.sents, self.done = {}, [], {}
        keys = [0]
        self.order = {}
        for mask in masks:
            self.order[mask] = [(key, which) for key in keys for which in range(count)]
            keys = keys + [key ^ mask for key in keys]

    def settle(self):
        waiting = []
        for name, sent in self.sents:
            if sent.value is None:
                waiting.append((name, sent))
            else:
                self.pieces.setdefault(name, []).append(sent.value)
        self.sents = waiting

    def take(self, flow, mask, rows, limit):
        self.limit = limit
        self.settle()
        for name in self.order[mask]:
            piece, offset, total = self.done.get((mask, name), (0, 0, 0))
            have = self.pieces.get(name, [])
            if total == limit or piece >= len(have):
                continue
            value = have[piece][offset : offset + rows]
            offset += value.shape[0]
            total += value.shape[0]
            if offset == have[piece].shape[0]:
                piece, offset = piece + 1, 0
            self.done[mask, name] = (piece, offset, total)
            self.sents.append(((name[0] ^ mask, name[1]), flow.send(value, 0, mask)))
            return True
        return False

    def left(self, mask, which):
        return any(
            self.done.get((m, name), (0, 0, 0))[2] < self.limit
            for m in self.masks
            if mask in (None, m)
            for name in self.order[m]
            if name[1] == which
        )

    def parts(self, which):
        self.settle()
        return {key: parts for (key, place), parts in self.pieces.items() if place == which}


class FfnFold:
    def __init__(self, total, masks, turn):
        count = 1 << len(masks)
        blocks = total.reshape(count, -1, total.shape[1])
        self.blocks = [blocks[i] for i in range(count)]
        self.rows, self.turn = blocks.shape[1], turn
        self.missing, self.tasks, self.sent_rows = [len(masks)] + [0] * (count - 1), {}, {}
        for stage, mask in enumerate(masks):
            half = count >> (stage + 1)
            self.tasks[mask] = [(block, half) for block in range(2 * half - 1, half - 1, -1)]
            for block in range(half, 2 * half):
                self.missing[block] = stage
        self.got, self.sents, self.turning = {}, [], None

    def settle(self):
        waiting = []
        for block, half, sent in self.sents:
            if sent.value is None:
                waiting.append((block, half, sent))
                continue
            parts = self.got.setdefault(block, [])
            parts.append(sent.value)
            if sum(part.shape[0] for part in parts) == self.rows:
                into = block - half
                self.missing[into] -= 1
                received = jnp.concatenate(parts, axis=0)
                self.blocks[into] = add(self.blocks[into], received, BF16 if into else F32)
        self.sents = waiting

    def take(self, flow, mask, rows):
        self.settle()
        for block, half in self.tasks[mask]:
            if self.missing[block]:
                continue
            first = self.sent_rows.get(block, 0)
            piece = self.blocks[block][first : first + rows]
            self.sent_rows[block] = first + piece.shape[0]
            if self.sent_rows[block] == self.rows:
                self.tasks[mask].remove((block, half))
            self.sents.append((block, half, flow.send(piece, 0, mask)))
            return True
        return False

    def take_turn(self, flow):
        self.settle()
        if self.missing[0] or self.turning is not None:
            return False
        total = self.blocks[0].reshape(2, self.rows // 2, -1)
        self.mine = lax.dynamic_index_in_dim(total, self.turn, 0, keepdims=False)
        other = lax.dynamic_index_in_dim(total, 1 - self.turn, 0, keepdims=False)
        self.turning = flow.send(other.astype(BF16), 0, TURN)
        return True

    def result(self):
        rows, cols = self.mine.shape
        out = jnp.zeros((rows, 2 * cols), F32)
        out = lax.dynamic_update_slice(out, self.mine, (0, self.turn * cols))
        received = self.turning.value.astype(F32)
        return lax.dynamic_update_slice(out, received, (0, (1 - self.turn) * cols))


def span_of(pair_ref, group, late, per_seq):
    pair = pair_ref[group]
    seq = pair // per_seq
    first = pair - seq * per_seq
    return seq, jnp.where(late == 0, first, 2 * per_seq - 1 - first)


def tile_visible(place_ref, pair_ref, seg_ref, step, part, per_seq, seq_len):
    group, cross = place_ref[0], place_ref[1]
    piece, low = step // 2, step % 2
    key, count = 0, SEQS * per_seq
    bits = count.bit_length() - 1
    for bit in range(bits):
        key = key + ((piece >> bit) & 1) * (1 << (bits - 1 - bit))
    seq_k, span_k = span_of(
        pair_ref, group ^ (key - key % 2 + low), cross ^ (key % 2), per_seq
    )
    seq_q, span_q = span_of(pair_ref, group ^ part, cross, per_seq)
    last_k = seg_ref[seq_k * seq_len + span_k * BLOCK + BLOCK - 1]
    first_q = seg_ref[seq_q * seq_len + span_q * BLOCK]
    visible = (seq_k == seq_q) & (span_k <= span_q) & (last_k >= first_q)
    spans = 2 * per_seq
    return visible, seq_k * spans + span_k, seq_q * spans + span_q


def tile_mask(seg_row_ref, seg_col_ref, place_k, place_q):
    lanes = lax.broadcasted_iota(jnp.int32, seg_col_ref.shape, 1)
    column = jnp.sum(jnp.where(lanes == place_k, seg_col_ref[...], 0), axis=1, keepdims=True)
    row = seg_row_ref[pl.ds(place_q, 1), :]
    row = jnp.concatenate([row, row], axis=1)
    return column == row


def stack_heads(ref, part):
    rows = pl.ds(part * BLOCK, BLOCK)
    return jnp.concatenate([ref[rows, :HEAD_WIDTH], ref[rows, HEAD_WIDTH:]], axis=0)


def forward_kernel(
    per_seq, place_ref, pair_ref, seg_ref, q_ref, kv_ref, row_ref, col_ref,
    low_ref, out_ref, lse_ref, max_ref, sum_ref, acc_ref,
):
    step = pl.program_id(0)
    seq_len = 2 * per_seq * BLOCK

    @pl.when(step == 0)
    def _():
        max_ref[...] = jnp.full(max_ref.shape, NEGATIVE, F32)
        sum_ref[...] = jnp.zeros(sum_ref.shape, F32)
        acc_ref[...] = jnp.zeros(acc_ref.shape, F32)

    for part in range(2):
        visible, place_k, place_q = tile_visible(
            place_ref, pair_ref, seg_ref, step, part, per_seq, seq_len
        )

        @pl.when(visible)
        def _():
            keys = kv_ref[:, :HEAD_WIDTH]
            values = kv_ref[:, HEAD_WIDTH:]
            queries = stack_heads(q_ref, part)
            scores = lax.dot_general(keys, queries, COLS, preferred_element_type=F32)
            mask = tile_mask(row_ref, col_ref, place_k, place_q)
            scores = jnp.where(mask, scores, NEGATIVE)
            old_max = max_ref[part]
            new_max = jnp.maximum(old_max, jnp.max(scores, axis=0, keepdims=True))
            weights = jnp.where(mask, jnp.exp(scores - new_max), 0.0)
            factor = jnp.exp(old_max - new_max)
            max_ref[part] = new_max
            sum_ref[part] = sum_ref[part] * factor + jnp.sum(weights, axis=0, keepdims=True)
            acc_ref[part] = acc_ref[part] * factor + lax.dot_general(
                values, weights.astype(BF16), ROWS, preferred_element_type=F32
            )

    @pl.when(step == pl.num_programs(0) - 1)
    def _():
        for part in range(2):
            total = sum_ref[part]
            attended = (acc_ref[part] / total).T
            rows = pl.ds(part * BLOCK, BLOCK)
            for head in range(2):
                one = attended[head * BLOCK : (head + 1) * BLOCK]
                cols = pl.ds(head * HEAD_WIDTH, HEAD_WIDTH)
                out_ref[rows, cols] = one
                low_ref[rows, cols] = one.astype(BF16)
            lse_ref[part] = max_ref[part] + jnp.log(total)


def backward_kernel(
    per_seq, place_ref, pair_ref, seg_ref, q_ref, kv_ref, row_ref, col_ref, lse_ref, out_ref, do_ref,
    dq_ref, dk_ref, dv_ref, delta_ref, dq_acc, dk_acc, dv_acc,
):
    step = pl.program_id(0)
    seq_len = 2 * per_seq * BLOCK

    @pl.when(step == 0)
    def _():
        dq_acc[...] = jnp.zeros(dq_acc.shape, F32)
        for part in range(2):
            product = stack_heads(out_ref, part) * stack_heads(do_ref, part).astype(F32)
            delta_ref[part] = jnp.sum(product.T, axis=0, keepdims=True)

    dk_acc[...] = jnp.zeros(dk_acc.shape, F32)
    dv_acc[...] = jnp.zeros(dv_acc.shape, F32)
    for part in range(2):
        visible, place_k, place_q = tile_visible(
            place_ref, pair_ref, seg_ref, step, part, per_seq, seq_len
        )

        @pl.when(visible)
        def _():
            keys = kv_ref[:, :HEAD_WIDTH]
            values = kv_ref[:, HEAD_WIDTH:]
            queries = stack_heads(q_ref, part)
            grads = stack_heads(do_ref, part)
            scores = lax.dot_general(keys, queries, COLS, preferred_element_type=F32)
            mask = tile_mask(row_ref, col_ref, place_k, place_q)
            probs = jnp.where(mask, jnp.exp(scores - lse_ref[part]), 0.0)
            grad_probs = lax.dot_general(values, grads, COLS, preferred_element_type=F32)
            grad_scores = (probs * (grad_probs - delta_ref[part])).astype(BF16)
            dv_acc[...] += jnp.dot(probs.astype(BF16), grads, preferred_element_type=F32)
            dk_acc[...] += jnp.dot(grad_scores, queries, preferred_element_type=F32)
            dq_acc[part] += lax.dot_general(
                grad_scores, keys, ROWS, preferred_element_type=F32
            )

    dk_ref[...] = dk_acc[...].astype(BF16)
    dv_ref[...] = dv_acc[...].astype(BF16)

    @pl.when(step == pl.num_programs(0) - 1)
    def _():
        for part in range(2):
            rows = pl.ds(part * BLOCK, BLOCK)
            for head in range(2):
                one = dq_acc[part, head * BLOCK : (head + 1) * BLOCK]
                dq_ref[rows, pl.ds(head * HEAD_WIDTH, HEAD_WIDTH)] = (
                    one * HEAD_WIDTH ** (-0.5)
                ).astype(BF16)


def whole(shape):
    return pl.BlockSpec(shape, lambda step, *refs: (0,) * len(shape))


def attend(place, pair_order, seg_flat, queries, keys_values, seg_row, seg_col, per_seq):
    steps = keys_values.shape[0] // BLOCK
    rows, width = queries.shape
    return pl.pallas_call(
        functools.partial(forward_kernel, per_seq),
        grid_spec=pltpu.PrefetchScalarGridSpec(
            num_scalar_prefetch=3,
            grid=(steps,),
            in_specs=[
                whole(queries.shape),
                pl.BlockSpec((BLOCK, 2 * HEAD_WIDTH), lambda step, *refs: (step, 0)),
                whole(seg_row.shape),
                whole(seg_col.shape),
            ],
            out_specs=[whole((rows, width)), whole((rows, width)), whole((2, 1, rows))],
            scratch_shapes=[
                pltpu.VMEM((2, 1, rows), F32),
                pltpu.VMEM((2, 1, rows), F32),
                pltpu.VMEM((2, HEAD_WIDTH, rows), F32),
            ],
        ),
        out_shape=[
            jax.ShapeDtypeStruct((rows, width), BF16),
            jax.ShapeDtypeStruct((rows, width), F32),
            jax.ShapeDtypeStruct((2, 1, rows), F32),
        ],
        compiler_params=pltpu.CompilerParams(dimension_semantics=("arbitrary",)),
        cost_estimate=pl.CostEstimate(
            flops=6_000_000_000, bytes_accessed=6_000_000, transcendentals=2_000_000
        ),
        name="attend",
    )(place, pair_order, seg_flat, queries, keys_values, seg_row, seg_col)


def attend_back(
    place, pair_order, seg_flat, queries, keys_values, seg_row, seg_col, lse, out, grads, per_seq
):
    steps = keys_values.shape[0] // BLOCK
    rows, width = queries.shape
    return pl.pallas_call(
        functools.partial(backward_kernel, per_seq),
        grid_spec=pltpu.PrefetchScalarGridSpec(
            num_scalar_prefetch=3,
            grid=(steps,),
            in_specs=[
                whole(queries.shape),
                pl.BlockSpec((BLOCK, 2 * HEAD_WIDTH), lambda step, *refs: (step, 0)),
                whole(seg_row.shape),
                whole(seg_col.shape),
                whole(lse.shape),
                whole(out.shape),
                whole(grads.shape),
            ],
            out_specs=[
                whole((rows, width)),
                pl.BlockSpec((BLOCK, HEAD_WIDTH), lambda step, *refs: (step, 0)),
                pl.BlockSpec((BLOCK, HEAD_WIDTH), lambda step, *refs: (step, 0)),
            ],
            scratch_shapes=[
                pltpu.VMEM((2, 1, rows), F32),
                pltpu.VMEM((2, rows, HEAD_WIDTH), F32),
                pltpu.VMEM((BLOCK, HEAD_WIDTH), F32),
                pltpu.VMEM((BLOCK, HEAD_WIDTH), F32),
            ],
        ),
        out_shape=[
            jax.ShapeDtypeStruct((rows, width), BF16),
            jax.ShapeDtypeStruct((keys_values.shape[0], HEAD_WIDTH), BF16),
            jax.ShapeDtypeStruct((keys_values.shape[0], HEAD_WIDTH), BF16),
        ],
        compiler_params=pltpu.CompilerParams(dimension_semantics=("arbitrary",)),
        cost_estimate=pl.CostEstimate(
            flops=16_000_000_000, bytes_accessed=12_000_000, transcendentals=2_000_000
        ),
        name="attend_back",
    )(place, pair_order, seg_flat, queries, keys_values, seg_row, seg_col, lse, out, grads)


def rms_back(scaled, normed, inv_rms):
    return inv_rms * (scaled - normed * jnp.mean(scaled * normed, axis=-1, keepdims=True))


def bits_of(number, count):
    return [(number >> (count - 1 - i)) & 1 for i in range(count)]


def flip(value, bits, axes):
    for bit, axis in zip(bits, axes):
        value = jnp.where(bit == 0, value, jnp.flip(value, axis))
    return value


def local(
    tokens,
    cotangent,
    segments,
    pair_order,
    norm_in,
    w_query,
    key_weight,
    value_weight,
    w_out,
    norm_mid,
    w_gate,
    w_up,
    w_down,
):
    heads = lax.axis_size("head")
    groups = lax.axis_size("blk")
    group = lax.axis_index("blk")
    head = lax.axis_index("head")
    cross, core = head // 2, head % 2
    turn = (group // TURN) % 2
    low = group % 2
    depth = groups.bit_length() - 1
    token_rows, width = tokens.shape
    group_rows = token_rows * heads
    per_seq = groups // SEQS
    shard = norm_in.shape[0]
    blk_masks = masks_of(groups)
    wide_masks = blk_masks[:-1] + [1]
    far_masks = [mask for mask in blk_masks if mask != TURN]
    key_local = HEAD_WIDTH
    query_local = w_query.shape[1] // heads
    in_cols = query_local + 2 * key_local
    ff_rows, ff_cols = w_gate.shape
    ff_own = ff_cols // 2
    group_bits = bits_of(group, depth)

    wide_axes = [-depth - 2] + [-depth + i for i in range(depth - 1)]
    wide_bits = [cross] + group_bits[:-1]

    def to_wide(value):
        lead = value.shape[:-1]
        value = value.reshape(lead + (2, 2) + (2,) * (depth - 1) + (2 * shard,))
        value = flip(value, wide_bits, wide_axes)
        base = len(lead)
        order = [base] + [base + 2 + i for i in range(depth - 2, -1, -1)]
        order += [base + 1, base + depth + 1]
        return value.transpose(*range(base), *order).reshape(lead + (width,))

    def from_wide(value):
        lead = value.shape[:-1]
        value = value.reshape(lead + (2,) + (2,) * (depth - 1) + (2, 2 * shard))
        base = len(lead)
        order = [base, base + depth] + [base + 1 + i for i in range(depth - 2, -1, -1)]
        order += [base + depth + 1]
        value = value.transpose(*range(base), *order)
        return flip(value, wide_bits, wide_axes).reshape(lead + (width,))

    far_axes = [-depth - 1 + i for i in range(depth - 2)] + [-2]
    far_bits = group_bits[: depth - 2] + [low]

    def to_far(value):
        lead = value.shape[:-1]
        value = value.reshape(lead + (2,) * depth + (ff_rows,))
        value = flip(value, far_bits, far_axes)
        base = len(lead)
        order = [base + depth - 1] + [base + i for i in range(depth - 3, -1, -1)]
        order += [base + depth - 2, base + depth]
        return value.transpose(*range(base), *order).reshape(lead + (width,))

    def from_far(value):
        lead = value.shape[:-1]
        value = value.reshape(lead + (2,) * depth + (ff_rows,))
        base = len(lead)
        order = [base + 1 + i for i in range(depth - 3, -1, -1)]
        order += [base + depth - 1, base, base + depth]
        value = value.transpose(*range(base), *order)
        return flip(value, far_bits, far_axes).reshape(lead + (width,))

    def reversed_key(place, masks):
        bits = [(place >> (len(masks) - 1 - i)) & 1 for i in range(len(masks))]
        return sum(mask for bit, mask in zip(bits, masks[::-1]) if bit)

    def in_fold_order(have, masks):
        return [have[reversed_key(place, masks)] for place in range(1 << len(masks))]

    rows = jnp.arange(group_rows, dtype=jnp.int32)
    part_rows = 2 * token_rows
    local_row = cross * part_rows + (core ^ (rows % part_rows // token_rows)) * token_rows
    local_row = local_row + rows % token_rows
    pairs = [lax.dynamic_index_in_dim(pair_order, group ^ part, keepdims=False) for part in (0, 1)]
    first_span = jnp.where(rows < part_rows, pairs[0], pairs[1]) % per_seq
    span = jnp.where(local_row < BLOCK, first_span, 2 * per_seq - 1 - first_span)
    positions = span * BLOCK + local_row % BLOCK
    angles = positions.astype(F32)[:, None] * frequencies(HEAD_WIDTH)[None, :]
    cosine, sine = jnp.cos(angles), jnp.sin(angles)
    seg_halves = segments.reshape(-1, 2, BLOCK // 2)
    seg_row = jnp.where(core == 0, seg_halves, seg_halves[:, ::-1]).reshape(-1, BLOCK)
    seg_col = seg_row.T
    seg_flat = segments.reshape(-1)
    place = jnp.stack([group, cross]).astype(jnp.int32)

    flow = Flow()

    gains = jnp.zeros((2, heads * groups, shard), BF16)
    gains = lax.dynamic_update_slice(
        gains, jnp.stack([norm_in, norm_mid])[:, None], (0, head * groups + group, 0)
    )
    hops = [blk_masks[:1], blk_masks[-1:], blk_masks[1:-1], [None]]

    def hop():
        nonlocal gains, gain_sent
        if gain_sent is not None:
            gains = gains + gain_sent.value
            gain_sent = None
        if hops:
            *direct, last = hops.pop(0)
            for mask in direct:
                gains = gains + swap(gains, 0, mask)
            gain_sent = flow.send(gains, *((CROSS, 0) if last is None else (0, last)))

    gain_sent = None

    def column_half(weights, bit):
        return jnp.concatenate(
            [
                lax.dynamic_slice_in_dim(weight, bit * (weight.shape[1] // 2), weight.shape[1] // 2, 1)
                for weight in weights
            ],
            axis=1,
        )

    def core_half(value, bit):
        parts, first = [], 0
        for count in (2 * query_local, 2 * key_local, 2 * key_local, 2 * query_local):
            parts.append(
                lax.dynamic_slice_in_dim(value, first + bit * (count // 2), count // 2, 2)
            )
            first += count
        return jnp.concatenate(parts, axis=2)

    attention_weights = (w_query, key_weight, value_weight, w_out)

    def index(value, place):
        return lax.dynamic_index_in_dim(value, place, 0, keepdims=False)

    def halves(weight, bit):
        return lax.dynamic_slice_in_dim(weight, bit * ff_own, ff_own, 1)

    ffn_weights = (w_down, w_gate, w_up)
    bulk, block_rows = Bulk(far_masks, 3), 2 * ff_rows

    def send_turn(which):
        return flow.send(halves(ffn_weights[which], 1 - turn), 0, TURN)

    def end_turn(which, sent):
        own = pair(halves(ffn_weights[which], turn), sent.value, turn, 0)
        bulk.pieces[0, which] = [own.reshape(block_rows, -1)]

    def near(rows):
        return bulk.take(flow, 1, rows, block_rows)

    def high(rows):
        return any([bulk.take(flow, mask, rows, block_rows) for mask in far_masks[:-1]])

    weights_low = flow.send(column_half(attention_weights, 1 - low), 0, 1)
    turned = send_turn(0)
    cot_far = to_far(cotangent)
    cot_x = flow.send(cot_far, CROSS, 0)
    hop()
    flow.go()
    end_turn(0, turned)
    both = pair(column_half(attention_weights, low), weights_low.value, low, 0)
    weights_core = flow.send(core_half(both, 1 - core), CORE, 0)
    hop()
    flow.go()
    own_cols = pair(core_half(both, core), weights_core.value, core, 0).reshape(4 * shard, -1)
    spread_in = Spread(own_cols[:, :in_cols], wide_masks)
    chain_out = Chain(own_cols[:, in_cols:], wide_masks)
    spread_in.wave(flow, 0)
    token_x = to_wide(tokens)
    token_low = flow.send(token_x, 0, 1)
    hop()
    flow.go()
    token_group = jnp.concatenate(
        [token_x, swap(token_x, CORE, 0), token_low.value, swap(token_low.value, CORE, 0)], axis=0
    ).astype(F32)
    spread_in.wave(flow, 1)
    near(block_rows)
    high(ff_rows)
    flow.go()
    for count in range(2, depth):
        if count > 2:
            flow.go()
        spread_in.wave(flow, count)
    chain_out.advance(flow)
    turned = send_turn(1)
    hop()
    flow.go()
    end_turn(1, turned)
    hop()
    spread_in.settle()
    weight_in = jnp.concatenate(in_fold_order(spread_in.have, wide_masks), axis=0)
    gains = gains + swap(gains, CORE, 0)
    gains = gains.reshape(2, width).astype(F32)
    gain_in, gain_mid = to_wide(gains[:1]), gains[1:]
    turned = send_turn(2)
    near(ff_rows)
    high(ff_rows)
    flow.go()
    end_turn(2, turned)

    inv_group = lax.rsqrt(jnp.mean(token_group * token_group, axis=-1, keepdims=True) + EPS)
    input_low = (token_group * inv_group * gain_in).astype(BF16)
    lin = flow.join(jnp.dot(input_low, weight_in, preferred_element_type=F32))
    keys_values = jnp.concatenate(
        [
            rotate(lin[:, query_local : query_local + key_local], cosine, sine).astype(BF16),
            lin[:, query_local + key_local :].astype(BF16),
        ],
        axis=-1,
    )
    queries = rotate(lin[:, :query_local], cosine, sine).astype(BF16)
    queries = queries * jnp.asarray(HEAD_WIDTH ** (-0.5), BF16)

    spread_kv = Spread(keys_values, wide_masks)
    spread_kv.wave(flow, 0)
    near(ff_rows)
    near(ff_rows)
    flow.go()
    spread_kv.wave(flow, 1)
    near(ff_rows)
    high(ff_rows)
    flow.go()
    for count in range(2, depth):
        if count > 2:
            flow.go()
        spread_kv.wave(flow, count)
    chain_out.advance(flow)
    high(ff_rows)
    near(ff_rows)
    flow.go()
    spread_kv.settle()
    kv_all = jnp.concatenate(in_fold_order(spread_kv.have, wide_masks), axis=0)
    while chain_out.masks:
        chain_out.advance(flow)
        if not chain_out.masks:
            high(ff_rows)
            near(ff_rows)
            cot_t = flow.send(cot_far, 0, TURN)
        flow.go()
    attention_low, attention_f, lse = attend(
        place, pair_order, seg_flat, queries, kv_all, seg_row, seg_col, per_seq
    )
    attention_low = flow.join(attention_low)
    chain_out.settle()
    weight_out = chain_out.blocks.reshape(width, -1)
    branch = lax.dot_general(attention_low, weight_out, COLS, preferred_element_type=F32)
    branch = row_major(branch.astype(BF16)).reshape(2, 2, token_rows, width)
    branch_across = add(branch[1, 0], swap(branch[1, 1], CORE, 0), BF16)
    branch_own = add(branch[0, 0], swap(branch[0, 1], CORE, 0), F32)
    branch_sent = flow.send(branch_across, 0, 1)
    cot_xt = flow.send(cot_t.value, CROSS, 0)
    high(ff_rows // 2)
    flow.go()
    branch = branch_own + branch_sent.value.astype(F32)

    tokens_f = tokens.astype(F32)
    middle = tokens_f + from_wide(branch)
    inv_mid = lax.rsqrt(jnp.mean(middle * middle, axis=-1, keepdims=True) + EPS)
    normed_mid = middle * inv_mid
    mid_low = to_far((normed_mid * gain_mid).astype(BF16))

    half = width // 2
    left, right = mid_low[:, :half], mid_low[:, half:]
    left_x = flow.send(left, CROSS, 0)
    right_t = flow.send(right, 0, TURN)
    near(ff_rows)
    high(ff_rows // 2)
    flow.go()
    left_t = flow.send(left, 0, TURN)
    right_x = flow.send(right, CROSS, 0)
    left_xt = flow.send(left_x.value, 0, TURN)
    right_xt = flow.send(right_t.value, CROSS, 0)
    high(ff_rows)
    flow.go()
    def four_rows(parts, first_col):
        return [(part, (i * token_rows, first_col)) for i, part in enumerate(parts)]

    placed = four_rows([left, left_t.value, left_x.value, left_xt.value], 0)
    placed += four_rows([right, right_t.value, right_x.value, right_xt.value], half)
    mid_four = assemble([part for part, _ in placed], [where for _, where in placed])
    early = [near(block_rows) for _ in range(2)] + [high(block_rows)]
    flow.go()

    def eight(four):
        return stack_rows([four, swap(four, CORE, 0)])

    mid_group = eight(mid_four)
    cot_four = jnp.concatenate([cot_far, cot_t.value, cot_x.value, cot_xt.value], axis=0)
    grad_group = jnp.concatenate([cot_four, swap(cot_four, CORE, 0)], axis=0)

    def weight_of(which):
        have = bulk.parts(which)
        return jnp.concatenate(
            [part for parts in in_fold_order(have, far_masks) for part in parts], axis=0
        )

    while bulk.left(None, 0):
        near(block_rows), high(block_rows)
        flow.go()
    down = weight_of(0)
    grad_hidden = flow.join(jnp.dot(grad_group, down, preferred_element_type=F32))
    while bulk.left(1, 1):
        near(block_rows), high(block_rows)
        flow.go()
    while True:
        more = [near(block_rows) for _ in range(4)] + [high(block_rows)]
        flow.go()
        if not bulk.left(None, 2):
            break
    gate = weight_of(1)
    gate_lin = flow.join(jnp.dot(mid_group, gate, preferred_element_type=F32))
    up = weight_of(2)
    up_proj = jnp.dot(mid_group, up, preferred_element_type=F32)
    gate_sig = jax.nn.sigmoid(gate_lin)
    gate_silu = gate_lin * gate_sig
    hidden_act = (gate_silu * up_proj).astype(BF16)
    grad_gate_lin = (
        grad_hidden * up_proj * gate_sig * (1.0 + gate_lin * (1.0 - gate_sig))
    ).astype(BF16)
    grad_up_proj = (grad_hidden * gate_silu).astype(BF16)

    def ffn_fold(lhs, rhs):
        total = lax.dot_general(lhs, rhs, ROWS, preferred_element_type=F32)
        total = row_major(total.astype(BF16))
        return FfnFold(total, far_masks[::-1], turn)

    down_fold = ffn_fold(grad_group, hidden_act)
    ffn_folds = [down_fold]

    def near(rows):
        found = [
            (-block, i)
            for i, fold in enumerate(ffn_folds)
            for block, _ in fold.tasks[1][:1]
            if not fold.missing[block]
        ]
        return bool(found) and ffn_folds[min(found)[1]].take(flow, 1, rows)

    def high(rows):
        found = False
        for mask in far_masks[:-1][::-1]:
            found = any(fold.take(flow, mask, rows) for fold in ffn_folds) or found
        return found

    near(ff_rows)
    flow.go()
    mid_partial = lax.dot_general(
        grad_gate_lin, gate, COLS, preferred_element_type=F32
    ) + lax.dot_general(grad_up_proj, up, COLS, preferred_element_type=F32)
    mid_partial = flow.join(row_major(mid_partial.astype(BF16))).reshape(2, 2, 2, token_rows, width)
    four = add(mid_partial[0], swap(mid_partial[1], CORE, 0), BF16)
    left, right = four[..., :half], four[..., half:]
    left_sent = flow.send(left[:, 1], 0, TURN)
    right_sent = flow.send(right[1], CROSS, 0)
    near(ff_rows)
    flow.go()
    gate_fold = ffn_fold(mid_group, grad_gate_lin)
    ffn_partial = lax.dot_general(hidden_act, down, COLS, preferred_element_type=F32)
    ffn_partial = row_major(ffn_partial.astype(BF16)).reshape(2, 2, 2, token_rows, width)
    out_four = add(ffn_partial[0], swap(ffn_partial[1], CORE, 0), BF16)
    left = add(left[:, 0], left_sent.value, BF16)
    right = add(right[0], right_sent.value, BF16)
    left_sent = flow.send(left[1], CROSS, 0)
    right_sent = flow.send(right[1], 0, TURN)
    high(ff_rows // 2)
    flow.go()
    ffn_folds.append(gate_fold)
    grad_mid = jnp.concatenate(
        [add(left[0], left_sent.value, F32), add(right[0], right_sent.value, F32)], axis=-1
    )
    grad_mid = from_far(grad_mid)
    norm_mid_sum = jnp.sum(grad_mid * normed_mid, axis=0)
    grad_y = cotangent.astype(F32)
    grad_middle = grad_y + rms_back(grad_mid * gain_mid, normed_mid, inv_mid)
    grad_branch = to_wide(grad_middle.astype(BF16))
    branch_low = flow.send(grad_branch, 0, 1)
    high(ff_rows // 2)
    out_parts = [flow.send(out_four[1, 0], CROSS, 0)]
    flow.go()
    up_fold = ffn_fold(mid_group, grad_up_proj)
    ffn_folds.append(up_fold)
    branch_group = jnp.concatenate(
        [grad_branch, swap(grad_branch, CORE, 0), branch_low.value, swap(branch_low.value, CORE, 0)],
        axis=0,
    )
    grad_attention = jnp.dot(branch_group, weight_out, preferred_element_type=F32).astype(BF16)

    def weight_fold(lhs, rhs, extra=None):
        total = lax.dot_general(lhs, rhs, ROWS, preferred_element_type=F32)
        if extra is not None:
            column = jnp.broadcast_to(to_wide(extra[None])[0][:, None], (width, 128))
            total = jnp.concatenate([total, column], axis=1)
        total = row_major(total.astype(BF16))
        return Fold(total.reshape(groups, 4 * shard, -1), wide_masks[::-1])

    out_fold = weight_fold(branch_group, attention_low, norm_mid_sum)
    out_fold.advance(flow)
    near(block_rows)
    high(ff_rows)
    flow.go()
    grad_queries, grad_keys, grad_values = attend_back(
        place, pair_order, seg_flat, queries, kv_all, seg_row, seg_col,
        lse, attention_f, grad_attention, per_seq,
    )
    grad_queries = flow.join(grad_queries)
    grad_keys = flow.join(grad_keys)
    key_fold = Fold(grad_keys.reshape(groups, group_rows, -1), wide_masks[::-1])
    value_fold = Fold(grad_values.reshape(groups, group_rows, -1), wide_masks[::-1])
    key_fold.advance(flow)
    near(block_rows)
    high(ff_rows)
    flow.go()
    key_fold.advance(flow)
    value_fold.advance(flow)
    near(block_rows)
    high(ff_rows)
    flow.go()
    query_lin = rotate(grad_queries.astype(F32), cosine, -sine).astype(BF16)
    query_fold = weight_fold(input_low, query_lin)
    turns = [down_fold, gate_fold, up_fold]

    def take_turn():
        for fold in turns:
            if fold.take_turn(flow):
                turns.remove(fold)
                return

    while True:
        running = [fold.advance(flow) for fold in (key_fold, value_fold)]
        if not any(running):
            break
        query_fold.advance(flow)
        if all(running):
            high(ff_rows // 2)
            near(block_rows)
        else:
            near(ff_rows)
            if len(out_parts) == 1:
                out_parts.append(flow.send(out_four[1, 1], CROSS, 0))
        flow.go()
    high(ff_rows // 2)
    take_turn()
    flow.go()
    keys_low, values_low = key_fold.blocks[0].astype(BF16), value_fold.blocks[0].astype(BF16)
    kv_lin = jnp.concatenate(
        [rotate(keys_low.astype(F32), cosine, -sine).astype(BF16), values_low], axis=-1
    )
    grad_lin = jnp.concatenate([query_lin, kv_lin], axis=-1)
    grad_in = lax.dot_general(grad_lin, weight_in, COLS, preferred_element_type=F32)
    grad_in = row_major(grad_in.astype(BF16)).reshape(2, 2, token_rows, width)
    in_across = add(grad_in[1, 0], swap(grad_in[1, 1], CORE, 0), BF16)
    in_own = add(grad_in[0, 0], swap(grad_in[0, 1], CORE, 0), F32)
    in_sent = flow.send(in_across, 0, 1)
    kv_fold = weight_fold(input_low, kv_lin)
    kv_fold.advance(flow)
    query_fold.advance(flow)
    out_fold.advance(flow)
    high(ff_rows // 2)
    near(ff_rows)
    flow.go()
    kv_fold.advance(flow)
    query_fold.advance(flow)
    high(ff_rows // 2)
    near(ff_rows)
    flow.go()
    kv_fold.advance(flow)
    out_fold.advance(flow)
    high(ff_rows)
    near(block_rows)
    take_turn()
    flow.go()
    out_two = [add(out_four[0, i], sent.value, BF16) for i, sent in enumerate(out_parts)]
    while True:
        running = [fold.advance(flow) for fold in (kv_fold, query_fold, out_fold)]
        if not any(running):
            break
        near(block_rows), high(block_rows)
        flow.go()

    total = jnp.concatenate(
        [fold.blocks[0] for fold in (query_fold, kv_fold, out_fold)], axis=-1
    ).reshape(2, 2, shard, -1)
    total_core = flow.send(index(total, 1 - core).astype(BF16), CORE, 0)
    out_sent = flow.send(out_two[1], 0, TURN)
    flow.go()
    total = pair(index(total, core), total_core.value.astype(F32), core, 1)
    total_low = flow.send(index(total, 1 - low).astype(BF16), 0, 1)
    while True:
        near(block_rows), high(block_rows)
        for fold in list(turns):
            if fold.take_turn(flow):
                turns.remove(fold)
        if not flow.batch:
            break
        flow.go()
    total = pair(index(total, low), total_low.value.astype(F32), low, 0).reshape(4, shard, -1)
    layer_out = (middle + from_far(add(out_two[0], out_sent.value, F32))).astype(BF16)
    scaled = in_own + in_sent.value.astype(F32)
    tokens_f = tokens.astype(F32)
    inv_in = inv_group[:token_rows]
    normed_in = tokens_f * inv_in
    grad_tokens = grad_middle + rms_back(from_wide(scaled * gain_in), normed_in, inv_in)

    def columns(first, count):
        return total[..., first : first + count].transpose(1, 0, 2).reshape(shard, -1)

    in_grads = [
        columns(0, query_local),
        columns(query_local, key_local),
        columns(query_local + key_local, key_local),
    ]
    grad_norm_in = sum(
        jnp.sum(grad * weight.astype(F32), axis=1)
        for grad, weight in zip(in_grads, attention_weights)
    ) / norm_in.astype(F32)
    grad_norm_mid = jnp.sum(total[..., in_cols + query_local], axis=0)
    return (
        layer_out,
        grad_tokens,
        grad_norm_in,
        *in_grads,
        columns(in_cols, query_local),
        grad_norm_mid,
        gate_fold.result(),
        up_fold.result(),
        down_fold.result(),
    )


def solution(mesh):
    rows = P(("blk", "head"), None)
    shards = P(("head", "blk"), None)
    vector = P(("head", "blk"))
    hidden = P("blk", "head")
    return jax.shard_map(
        local,
        mesh=mesh,
        in_specs=(
            rows, rows, P(), P(), vector, shards, shards, shards, shards, vector, hidden, hidden, hidden,
        ),
        out_specs=(
            rows, rows, vector, shards, shards, shards, shards, vector, hidden, hidden, hidden,
        ),
        check_vma=False,
    )
```

time: 961 us -> 816 us (0.85)
  waiting for transfers between devices: 583 us -> 354 us
  local copies, waits for them, and re-layouts: 44.7 us -> 121 us
    ppermute x117 -> x115, waiting for transfers between devices: 572 us -> 354 us  [swap(): return row_major(lax.ppermute(row_major(value), ('head', 'blk'), pairs))]
    unnamed x161 -> x322, local copies, waits for them, and re-layouts: 4.84 us -> 55 us
    concatenate x7 -> x10, other arithmetic: 34.1 us -> 9.51 us  [the longest x3 3.68 us: settle(): self.blocks = jnp.concatenate([self.blocks, self.sent.value], axis=0)]
    ppermute x117 -> x115, starting transfers between devices: 117 us -> 139 us  [swap(): return row_major(lax.ppermute(row_major(value), ('head', 'blk'), pairs))]
    reshape x11 -> x25, local copies, waits for them, and re-layouts: 8.1 us -> 22.9 us  [the longest x2 5.13 us: from_far(): return flip(value, far_bits, far_axes).reshape(lead + (width,))]
    all_to_all x4 -> x0, starting transfers between devices: 13.8 us -> none  [the longest x2 6.88 us: gather_rows(): lax.all_to_all(local_cols, 'head', split_axis=0, concat_axis=0, tiled=True)]
    select_n x3 -> x23, other arithmetic: 3.23 us -> 15.8 us  [the longest x20 10.4 us: flip(): value = jnp.where(bit == 0, value, jnp.flip(value, axis))]
    all_to_all x4 -> x0, waiting for transfers between devices: 10.7 us -> none  [the longest x2 5.58 us: fold_rows(): lax.all_to_all(total, 'head', split_axis=0, concat_axis=0, tiled=True)]
  transfers between devices with their start and end apart: 121 -> 115, of which waited for: 50 -> 67; matrix products, arithmetic and copies ran while one was open for 16% -> 19% of each run, Pallas kernels for 3% -> 4%
where the time goes in v2:
time: 816 us; the launch traced here: 809 us
  waiting for transfers between devices  354 us (43%)
  starting transfers between devices  139 us (17%)
  local copies, waits for them, and re-layouts  121 us (15%)
  other arithmetic  82.5 us (10%)
  matrix products  76.1 us (9%)
  Pallas kernels  33.3 us (4%)
    ppermute x115, waiting for transfers between devices, swap(): return row_major(lax.ppermute(row_major(value), ('head', 'blk'), pairs))  354 us
    ppermute x115, starting transfers between devices, swap(): return row_major(lax.ppermute(row_major(value), ('head', 'blk'), pairs))  139 us
    unnamed x322, local copies, waits for them, and re-layouts  55 us
  transfers between devices with their start and end apart: 115, of which 67 were waited for; matrix products, arithmetic and copies ran while one was open for 19% of the time, Pallas kernels for 4%

profile of v2, /device:TPU:0, one launch (start us, length us, event | category | flops | bytes accessed | tf_op | source)
XLA Modules:
  0.0 809.0 jit_solution(7762331046482782072)
XLA Ops:
  8.6 3.0 collective-permute-start.2
  18.7 4.6 collective-permute-done.4
  45.8 14.8 %collective-permute-done.11 = bf16[2,32,64]{2,1,0:T(8,128)(2,1)S(1)} collective-permute-done((bf16[2,32,64]{2,1,0:T(8,128)(2,1)S(1)}, bf16[2,32,64]{2,1,0:T(8,128)(2,1)S(1)}, u32[]{:S(2)}, u32[]{:S(2)}) %collective-permute-start.11) | collective-permute-done | bytes 8224 | tf_op jit(solution)/shard_map/ppermute | solution.py:51
  78.7 5.5 collective-permute-done.13
  84.2 10.4 %collective-permute-done.14 = bf16[256,1024]{1,0:T(8,128)(2,1)S(1)} collective-permute-done((bf16[256,1024]{1,0:T(8,128)(2,1)}, bf16[256,1024]{1,0:T(8,128)(2,1)S(1)}, u32[]{:S(2)}, u32[]{:S(2)}) %collective-permute-start.14) | collective-permute-done | bytes 524320 | tf_op jit(solution)/shard_map/ppermute | solution.py:51
  94.6 3.6 collective-permute-done.17
  102.6 5.0 collective-permute-done.21
  107.6 5.9 collective-permute-done.19
  120.0 5.3 fusion.141
  125.3 15.2 %collective-permute-done.23 = bf16[256,1024]{1,0:T(8,128)(2,1)} collective-permute-done((bf16[256,1024]{1,0:T(8,128)(2,1)}, bf16[256,1024]{1,0:T(8,128)(2,1)}, u32[]{:S(2)}, u32[]{:S(2)}) %collective-permute-start.23) | collective-permute-done | bytes 524320 | tf_op jit(solution)/shard_map/ppermute | solution.py:51
  140.6 4.5 collective-permute-done.25
  158.7 16.6 %collective-permute-done.26 = bf16[512,512]{1,0:T(8,128)(2,1)} collective-permute-done((bf16[512,512]{1,0:T(8,128)(2,1)}, bf16[512,512]{1,0:T(8,128)(2,1)}, u32[]{:S(2)}, u32[]{:S(2)}) %collective-permute-start.26) | collective-permute-done | bytes 524320 | tf_op jit(solution)/shard_map/ppermute | solution.py:51
  188.8 4.4 collective-permute-done.31
  193.2 6.7 collective-permute-done.32
  200.8 4.5 collective-permute-done.35
  205.9 3.1 collective-permute-start.38
  218.4 6.3 collective-permute-done.37
  238.1 11.9 %attend.1 = (bf16[512,512]{1,0:T(8,128)(2,1)}, f32[512,512]{1,0:T(8,128)}, f32[2,1,512]{2,1,0:T(1,128)}) custom-call(s32[2]{0:T(128)} %pad_add_fusion.place_ref, s32[8]{0:T(128)} %pair_ref.3, s32[4096]{0:T(1024)} %bitcast.302, bf16[512,512]{1,0:T(8,128)(2,1)} %maximum_multiply_fusion.q_ref, bf16[4096,512]{1,0:T(8,128)(2,1)} %constant_dynamic-update-slice_fusion.8.kv_ref, ...), custom_call_target="tpu_custom_call" | custom-call | flops 6000000000 | bytes 6000000 | tf_op jit(solution)/shard_map/attend/pallas_call | solution.py:461
  250.0 4.5 collective-permute-done.41
  273.9 7.3 collective-permute-done.48
  294.9 2.8 collective-permute-start.52
  302.7 5.6 collective-permute-done.50.refs_5_
  327.8 2.9 assemble.2.refs_0_
  334.4 4.1 collective-permute-done.58
  338.5 8.1 %collective-permute-done.59 = bf16[256,1024]{1,0:T(8,128)(2,1)} collective-permute-done((bf16[256,1024]{1,0:T(8,128)(2,1)}, bf16[256,1024]{1,0:T(8,128)(2,1)}, u32[]{:S(2)}, u32[]{:S(2)}) %collective-permute-start.59) | collective-permute-done | bytes 524320 | tf_op jit(solution)/shard_map/ppermute | solution.py:51
  354.8 2.8 collective-permute-done.61
  359.2 6.3 fusion.168
  365.5 4.2 assemble.3
  369.7 7.9 fusion.167
  377.7 7.4 multiply_convert_fusion.2
  385.1 4.8 convolution_convert_fusion.2
  390.0 4.8 convolution_convert_fusion.3
  396.9 7.0 fusion.169
  406.3 9.8 %add_convert_fusion = bf16[1024,2048]{1,0:T(8,128)(2,1)S(1)} fusion(f32[1024,2048]{1,0:T(8,128)} %fusion.169, bf16[1024,1024]{1,0:T(8,128)(2,1)} %get-tuple-element.462, bf16[2048,1024]{1,0:T(8,128)(2,1)} %constant_dynamic-update-slice_fusion.16), kind=kOutput, calls=%fused_computation | convolution fusion | flops 4299161600 | bytes 18874368 | tf_op jit(solution)/shard_map/dot_general | solution.py:908
  417.9 4.9 convolution_convert_fusion
  424.0 5.4 convolution_convert_fusion.1
  437.0 9.6 %collective-permute-done.66 = bf16[2,128,1024]{2,1,0:T(8,128)(2,1)S(1)} collective-permute-done((bf16[2,128,1024]{2,1,0:T(8,128)(2,1)S(1)}, bf16[2,128,1024]{2,1,0:T(8,128)(2,1)S(1)}, u32[]{:S(2)}, u32[]{:S(2)}) %collective-permute-start.66) | collective-permute-done | bytes 524320 | tf_op jit(solution)/shard_map/ppermute | solution.py:51
  451.7 3.2 collective-permute-start.71
  457.5 6.2 collective-permute-done.70
  478.2 12.3 %collective-permute-done.73 = bf16[128,1024]{1,0:T(8,128)(2,1)S(1)} collective-permute-done((bf16[128,1024]{1,0:T(8,128)(2,1)}, bf16[128,1024]{1,0:T(8,128)(2,1)S(1)}, u32[]{:S(2)}, u32[]{:S(2)}) %collective-permute-start.73) | collective-permute-done | bytes 262176 | tf_op jit(solution)/shard_map/ppermute | solution.py:51
  501.6 14.4 %attend_back.1 = (bf16[512,512]{1,0:T(8,128)(2,1)}, bf16[4096,256]{1,0:T(8,128)(2,1)}, bf16[4096,256]{1,0:T(8,128)(2,1)}) custom-call(s32[2]{0:T(128)} %pad_add_fusion.place_ref, s32[8]{0:T(128)} %pair_ref.3, s32[4096]{0:T(1024)} %bitcast.303, bf16[512,512]{1,0:T(8,128)(2,1)} %maximum_multiply_fusion.q_ref, ...), custom_call_target="tpu_custom_call" | custom-call | flops 16000000000 | bytes 12000000 | tf_op jit(solution)/shard_map/attend_back/pallas_call | solution.py:497
  516.0 10.4 %collective-permute-done.79 = bf16[256,1024]{1,0:T(8,128)(2,1)} collective-permute-done((bf16[256,1024]{1,0:T(8,128)(2,1)}, bf16[256,1024]{1,0:T(8,128)(2,1)}, u32[]{:S(2)}, u32[]{:S(2)}) %collective-permute-start.79) | collective-permute-done | bytes 524320 | tf_op jit(solution)/shard_map/ppermute | solution.py:51
  526.4 3.5 collective-permute-done.77
  541.9 18.9 %collective-permute-done.82 = bf16[256,1024]{1,0:T(8,128)(2,1)S(1)} collective-permute-done((bf16[256,1024]{1,0:T(8,128)(2,1)S(1)}, bf16[256,1024]{1,0:T(8,128)(2,1)S(1)}, u32[]{:S(2)}, u32[]{:S(2)}) %collective-permute-start.82) | collective-permute-done | bytes 524320 | tf_op jit(solution)/shard_map/ppermute | solution.py:51
  570.3 18.7 %collective-permute-done.83 = bf16[2,512,256]{2,1,0:T(8,128)(2,1)S(1)} collective-permute-done((bf16[2,512,256]{2,1,0:T(8,128)(2,1)S(1)}, bf16[2,512,256]{2,1,0:T(8,128)(2,1)S(1)}, u32[]{:S(2)}, u32[]{:S(2)}) %collective-permute-start.83) | collective-permute-done | bytes 524320 | tf_op jit(solution)/shard_map/ppermute | solution.py:51
  602.1 6.4 collective-permute-done.87
  608.5 7.5 collective-permute-done.90
  617.3 3.6 collective-permute-start.93
  627.7 7.0 collective-permute-done.92
  648.5 6.6 collective-permute-done.97
  655.1 5.5 collective-permute-done.98
  663.5 3.3 collective-permute-start.101
  670.4 14.5 %collective-permute-done.101 = bf16[1,256,512]{2,1,0:T(8,128)(2,1)S(1)} collective-permute-done((bf16[1,256,512]{2,1,0:T(8,128)(2,1)S(1)}, bf16[1,256,512]{2,1,0:T(8,128)(2,1)S(1)}, u32[]{:S(2)}, u32[]{:S(2)}) %collective-permute-start.101) | collective-permute-done | bytes 262176 | tf_op jit(solution)/shard_map/ppermute | solution.py:51
  685.6 4.0 collective-permute-done.103
  693.9 9.0 %collective-permute-done.104 = bf16[256,1024]{1,0:T(8,128)(2,1)S(1)} collective-permute-done((bf16[256,1024]{1,0:T(8,128)(2,1)S(1)}, bf16[256,1024]{1,0:T(8,128)(2,1)S(1)}, u32[]{:S(2)}, u32[]{:S(2)}) %collective-permute-start.104) | collective-permute-done | bytes 524320 | tf_op jit(solution)/shard_map/ppermute | solution.py:51
  716.9 3.4 collective-permute-start.106
  723.9 5.2 collective-permute-done.106
  739.7 17.1 %collective-permute-done.107 = bf16[1,256,512]{2,1,0:T(8,128)(2,1)S(1)} collective-permute-done((bf16[1,256,512]{2,1,0:T(8,128)(2,1)S(1)}, bf16[1,256,512]{2,1,0:T(8,128)(2,1)S(1)}, u32[]{:S(2)}, u32[]{:S(2)}) %collective-permute-start.107) | collective-permute-done | bytes 262176 | tf_op jit(solution)/shard_map/ppermute | solution.py:51
  766.1 7.9 collective-permute-done.111
  776.3 3.1 reshape.394
  783.7 3.1 reshape.395
  788.4 2.8 collective-permute-start.113
  794.6 6.4 collective-permute-done.113
  801.0 3.6 collective-permute-done.114
  (732 shorter events, 356.1 us)
Async XLA Ops:
  34.5 26.1 %collective-permute-start.7 = (bf16[256,1024]{1,0:T(8,128)(2,1)S(1)}, bf16[256,1024]{1,0:T(8,128)(2,1)}, u32[]{:S(2)}, u32[]{:S(2)}) collective-permute-start(bf16[256,1024]{1,0:T(8,128)(2,1)S(1)} %get-tuple-element.241), channel_id=1, source_target_pairs={{0,4},{1,5},{2,6},{3,7},{4,0},{5,1},{6,2},{7,3},{8,12},{9,13},{10,... | collective-permute-start | bytes 1572872 | tf_op jit(solution)/shard_map/ppermute | solution.py:51
  37.1 23.5 %collective-permute-start.8 = (bf16[256,1024]{1,0:T(8,128)(2,1)S(1)}, bf16[256,1024]{1,0:T(8,128)(2,1)}, u32[]{:S(2)}, u32[]{:S(2)}) collective-permute-start(bf16[256,1024]{1,0:T(8,128)(2,1)S(1)} %get-tuple-element.241), channel_id=1, source_target_pairs={{0,2},{1,3},{2,0},{3,1},{4,6},{5,7},{6,4},{7,5},{8,10},{9,11},{10,... | collective-permute-start | bytes 1572872 | tf_op jit(solution)/shard_map/ppermute | solution.py:51
  38.0 22.6 %collective-permute-start.9 = (bf16[256,1024]{1,0:T(8,128)(2,1)S(1)}, bf16[256,1024]{1,0:T(8,128)(2,1)S(1)}, u32[]{:S(2)}, u32[]{:S(2)}) collective-permute-start(bf16[256,1024]{1,0:T(8,128)(2,1)S(1)} %get-tuple-element.241), channel_id=1, source_target_pairs={{0,16},{1,17},{2,18},{3,19},{4,20},{5,21},{6,22},{7,23},{8,24},{9,... | collective-permute-start | bytes 1572872 | tf_op jit(solution)/shard_map/ppermute | solution.py:51
  39.5 21.1 %collective-permute-start.10 = (bf16[128,2048]{1,0:T(8,128)(2,1)}, bf16[128,2048]{1,0:T(8,128)(2,1)}, u32[]{:S(2)}, u32[]{:S(2)}) collective-permute-start(bf16[128,2048]{1,0:T(8,128)(2,1)} %reshape.371), channel_id=1, source_target_pairs={{0,1},{1,0},{2,3},{3,2},{4,5},{5,4},{6,7},{7,6},{8,9},{9,8},{10,11... | collective-permute-start | bytes 1572872 | tf_op jit(solution)/shard_map/ppermute | solution.py:51
  41.0 19.6 %collective-permute-start.11 = (bf16[2,32,64]{2,1,0:T(8,128)(2,1)S(1)}, bf16[2,32,64]{2,1,0:T(8,128)(2,1)S(1)}, u32[]{:S(2)}, u32[]{:S(2)}) collective-permute-start(bf16[2,32,64]{2,1,0:T(8,128)(2,1)S(1)} %add.437), channel_id=1, source_target_pairs={{0,2},{1,3},{2,0},{3,1},{4,6},{5,7},{6,4},{7,5},{8,10},{9,11},{10,... | collective-permute-start | bytes 24584 | tf_op jit(solution)/shard_map/ppermute | solution.py:51
  64.6 33.5 %collective-permute-start.16 = (bf16[512,1024]{1,0:T(8,128)(2,1)S(1)}, bf16[512,1024]{1,0:T(8,128)(2,1)S(1)}, u32[]{:S(2)}, u32[]{:S(2)}) collective-permute-start(bf16[512,1024]{1,0:T(8,128)(2,1)S(1)} %bitcast.257), channel_id=1, source_target_pairs={{0,1},{1,0},{2,3},{3,2},{4,5},{5,4},{6,7},{7,6},{8,9},{9,8},{10,11... | collective-permute-start | bytes 3145736 | tf_op jit(solution)/shard_map/ppermute | solution.py:51
  70.7 23.9 %collective-permute-start.14 = (bf16[256,1024]{1,0:T(8,128)(2,1)}, bf16[256,1024]{1,0:T(8,128)(2,1)S(1)}, u32[]{:S(2)}, u32[]{:S(2)}) collective-permute-start(bf16[256,1024]{1,0:T(8,128)(2,1)} %collective-permute-done.7), channel_id=1, source_target_pairs={{0,2},{1,3},{2,0},{3,1},{4,6},{5,7},{6,4},{7,5},{8,10},{9,11},{10,... | collective-permute-start | bytes 1572872 | tf_op jit(solution)/shard_map/ppermute | solution.py:51
  72.4 22.2 %collective-permute-start.15 = (bf16[256,1024]{1,0:T(8,128)(2,1)}, bf16[256,1024]{1,0:T(8,128)(2,1)S(1)}, u32[]{:S(2)}, u32[]{:S(2)}) collective-permute-start(bf16[256,1024]{1,0:T(8,128)(2,1)} %collective-permute-done.7), channel_id=1, source_target_pairs={{0,16},{1,17},{2,18},{3,19},{4,20},{5,21},{6,22},{7,23},{8,24},{9,... | collective-permute-start | bytes 1572872 | tf_op jit(solution)/shard_map/ppermute | solution.py:51
  73.0 25.2 %collective-permute-start.17 = (bf16[256,1024]{1,0:T(8,128)(2,1)S(1)}, bf16[256,1024]{1,0:T(8,128)(2,1)}, u32[]{:S(2)}, u32[]{:S(2)}) collective-permute-start(bf16[256,1024]{1,0:T(8,128)(2,1)S(1)} %get-tuple-element.253), channel_id=1, source_target_pairs={{0,4},{1,5},{2,6},{3,7},{4,0},{5,1},{6,2},{7,3},{8,12},{9,13},{10,... | collective-permute-start | bytes 1572872 | tf_op jit(solution)/shard_map/ppermute | solution.py:51
  116.0 24.5 %collective-permute-start.23 = (bf16[256,1024]{1,0:T(8,128)(2,1)}, bf16[256,1024]{1,0:T(8,128)(2,1)}, u32[]{:S(2)}, u32[]{:S(2)}) collective-permute-start(bf16[256,1024]{1,0:T(8,128)(2,1)} %get-tuple-element.267), channel_id=1, source_target_pairs={{0,2},{1,3},{2,0},{3,1},{4,6},{5,7},{6,4},{7,5},{8,10},{9,11},{10,... | collective-permute-start | bytes 1572872 | tf_op jit(solution)/shard_map/ppermute | solution.py:51
  117.9 22.6 %collective-permute-start.24 = (bf16[256,1024]{1,0:T(8,128)(2,1)S(1)}, bf16[256,1024]{1,0:T(8,128)(2,1)}, u32[]{:S(2)}, u32[]{:S(2)}) collective-permute-start(bf16[256,1024]{1,0:T(8,128)(2,1)S(1)} %get-tuple-element.288), channel_id=1, source_target_pairs={{0,1},{1,0},{2,3},{3,2},{4,5},{5,4},{6,7},{7,6},{8,9},{9,8},{10,11... | collective-permute-start | bytes 1572872 | tf_op jit(solution)/shard_map/ppermute | solution.py:51
  118.8 26.2 %collective-permute-start.25 = (bf16[256,1024]{1,0:T(8,128)(2,1)}, bf16[256,1024]{1,0:T(8,128)(2,1)}, u32[]{:S(2)}, u32[]{:S(2)}) collective-permute-start(bf16[256,1024]{1,0:T(8,128)(2,1)} %get-tuple-element.269), channel_id=1, source_target_pairs={{0,4},{1,5},{2,6},{3,7},{4,0},{5,1},{6,2},{7,3},{8,12},{9,13},{10,... | collective-permute-start | bytes 1572872 | tf_op jit(solution)/shard_map/ppermute | solution.py:51
  150.7 24.6 %collective-permute-start.26 = (bf16[512,512]{1,0:T(8,128)(2,1)}, bf16[512,512]{1,0:T(8,128)(2,1)}, u32[]{:S(2)}, u32[]{:S(2)}) collective-permute-start(bf16[512,512]{1,0:T(8,128)(2,1)} %get-tuple-element.276), channel_id=1, source_target_pairs={{0,4},{1,5},{2,6},{3,7},{4,0},{5,1},{6,2},{7,3},{8,12},{9,13},{10,... | collective-permute-start | bytes 1572872 | tf_op jit(solution)/shard_map/ppermute | solution.py:51
  150.7 24.8 %collective-permute-start.27 = (bf16[512,512]{1,0:T(8,128)(2,1)}, bf16[512,512]{1,0:T(8,128)(2,1)}, u32[]{:S(2)}, u32[]{:S(2)}) collective-permute-start(bf16[512,512]{1,0:T(8,128)(2,1)} %get-tuple-element.276), channel_id=1, source_target_pairs={{0,2},{1,3},{2,0},{3,1},{4,6},{5,7},{6,4},{7,5},{8,10},{9,11},{10,... | collective-permute-start | bytes 1572872 | tf_op jit(solution)/shard_map/ppermute | solution.py:51
  153.0 22.5 %collective-permute-start.28 = (bf16[512,512]{1,0:T(8,128)(2,1)}, bf16[512,512]{1,0:T(8,128)(2,1)}, u32[]{:S(2)}, u32[]{:S(2)}) collective-permute-start(bf16[512,512]{1,0:T(8,128)(2,1)} %get-tuple-element.276), channel_id=1, source_target_pairs={{0,16},{1,17},{2,18},{3,19},{4,20},{5,21},{6,22},{7,23},{8,24},{9,... | collective-permute-start | bytes 1572872 | tf_op jit(solution)/shard_map/ppermute | solution.py:51
  154.5 21.0 %collective-permute-start.29 = (bf16[256,1024]{1,0:T(8,128)(2,1)}, bf16[256,1024]{1,0:T(8,128)(2,1)}, u32[]{:S(2)}, u32[]{:S(2)}) collective-permute-start(bf16[256,1024]{1,0:T(8,128)(2,1)} %get-tuple-element.296), channel_id=1, source_target_pairs={{0,1},{1,0},{2,3},{3,2},{4,5},{5,4},{6,7},{7,6},{8,9},{9,8},{10,11... | collective-permute-start | bytes 1572872 | tf_op jit(solution)/shard_map/ppermute | solution.py:51
  155.6 22.5 %collective-permute-start.30 = (bf16[256,1024]{1,0:T(8,128)(2,1)}, bf16[256,1024]{1,0:T(8,128)(2,1)}, u32[]{:S(2)}, u32[]{:S(2)}) collective-permute-start(bf16[256,1024]{1,0:T(8,128)(2,1)} %get-tuple-element.304), channel_id=1, source_target_pairs={{0,1},{1,0},{2,3},{3,2},{4,5},{5,4},{6,7},{7,6},{8,9},{9,8},{10,11... | collective-permute-start | bytes 1572872 | tf_op jit(solution)/shard_map/ppermute | solution.py:51
  178.6 21.3 %collective-permute-start.32 = (bf16[512,512]{1,0:T(8,128)(2,1)}, bf16[512,512]{1,0:T(8,128)(2,1)}, u32[]{:S(2)}, u32[]{:S(2)}) collective-permute-start(bf16[512,512]{1,0:T(8,128)(2,1)} %collective-permute-done.26), channel_id=1, source_target_pairs={{0,2},{1,3},{2,0},{3,1},{4,6},{5,7},{6,4},{7,5},{8,10},{9,11},{10,... | collective-permute-start | bytes 1572872 | tf_op jit(solution)/shard_map/ppermute | solution.py:51
  178.9 21.9 %collective-permute-start.33 = (bf16[512,512]{1,0:T(8,128)(2,1)}, bf16[512,512]{1,0:T(8,128)(2,1)S(1)}, u32[]{:S(2)}, u32[]{:S(2)}) collective-permute-start(bf16[512,512]{1,0:T(8,128)(2,1)} %collective-permute-done.26), channel_id=1, source_target_pairs={{0,16},{1,17},{2,18},{3,19},{4,20},{5,21},{6,22},{7,23},{8,24},{9,... | collective-permute-start | bytes 1572872 | tf_op jit(solution)/shard_map/ppermute | solution.py:51
  180.4 20.4 %collective-permute-start.34 = (bf16[256,1024]{1,0:T(8,128)(2,1)S(1)}, bf16[256,1024]{1,0:T(8,128)(2,1)S(1)}, u32[]{:S(2)}, u32[]{:S(2)}) collective-permute-start(bf16[256,1024]{1,0:T(8,128)(2,1)S(1)} %get-tuple-element.287), channel_id=1, source_target_pairs={{0,1},{1,0},{2,3},{3,2},{4,5},{5,4},{6,7},{7,6},{8,9},{9,8},{10,11... | collective-permute-start | bytes 1572872 | tf_op jit(solution)/shard_map/ppermute | solution.py:51
  181.6 23.8 %collective-permute-start.35 = (bf16[256,1024]{1,0:T(8,128)(2,1)}, bf16[256,1024]{1,0:T(8,128)(2,1)S(1)}, u32[]{:S(2)}, u32[]{:S(2)}) collective-permute-start(bf16[256,1024]{1,0:T(8,128)(2,1)} %copy-done.30), channel_id=1, source_target_pairs={{0,4},{1,5},{2,6},{3,7},{4,0},{5,1},{6,2},{7,3},{8,12},{9,13},{10,... | collective-permute-start | bytes 1572872 | tf_op jit(solution)/shard_map/ppermute | solution.py:51
  205.9 18.8 %collective-permute-start.37 = (bf16[2,256,512]{2,1,0:T(8,128)(2,1)}, bf16[2,256,512]{2,1,0:T(8,128)(2,1)S(1)}, u32[]{:S(2)}, u32[]{:S(2)}) collective-permute-start(bf16[2,256,512]{2,1,0:T(8,128)(2,1)} %pad_maximum_fusion.12), channel_id=1, source_target_pairs={{0,2},{1,3},{2,0},{3,1},{4,6},{5,7},{6,4},{7,5},{8,10},{9,11},{10,... | collective-permute-start | bytes 1572872 | tf_op jit(solution)/shard_map/ppermute | solution.py:51
  205.9 21.1 %collective-permute-start.38 = (bf16[256,1024]{1,0:T(8,128)(2,1)}, bf16[256,1024]{1,0:T(8,128)(2,1)}, u32[]{:S(2)}, u32[]{:S(2)}) collective-permute-start(bf16[256,1024]{1,0:T(8,128)(2,1)} %get-tuple-element.296), channel_id=1, source_target_pairs={{0,4},{1,5},{2,6},{3,7},{4,0},{5,1},{6,2},{7,3},{8,12},{9,13},{10,... | collective-permute-start | bytes 1572872 | tf_op jit(solution)/shard_map/ppermute | solution.py:51
  209.0 18.0 %collective-permute-start.39 = (bf16[256,1024]{1,0:T(8,128)(2,1)}, bf16[256,1024]{1,0:T(8,128)(2,1)S(1)}, u32[]{:S(2)}, u32[]{:S(2)}) collective-permute-start(bf16[256,1024]{1,0:T(8,128)(2,1)} %collective-permute-done.17), channel_id=1, source_target_pairs={{0,1},{1,0},{2,3},{3,2},{4,5},{5,4},{6,7},{7,6},{8,9},{9,8},{10,11... | collective-permute-start | bytes 1572872 | tf_op jit(solution)/shard_map/ppermute | solution.py:51
  228.1 27.5 %collective-permute-start.40 = (bf16[4,256,512]{2,1,0:T(8,128)(2,1)}, bf16[4,256,512]{2,1,0:T(8,128)(2,1)}, u32[]{:S(2)}, u32[]{:S(2)}) collective-permute-start(bf16[4,256,512]{2,1,0:T(8,128)(2,1)} %pad_maximum_fusion.7), channel_id=1, source_target_pairs={{0,16},{1,17},{2,18},{3,19},{4,20},{5,21},{6,22},{7,23},{8,24},{9,... | collective-permute-start | bytes 3145736 | tf_op jit(solution)/shard_map/ppermute | solution.py:51
  232.7 21.8 %collective-permute-start.41 = (bf16[256,1024]{1,0:T(8,128)(2,1)}, bf16[256,1024]{1,0:T(8,128)(2,1)}, u32[]{:S(2)}, u32[]{:S(2)}) collective-permute-start(bf16[256,1024]{1,0:T(8,128)(2,1)} %get-tuple-element.304), channel_id=1, source_target_pairs={{0,4},{1,5},{2,6},{3,7},{4,0},{5,1},{6,2},{7,3},{8,12},{9,13},{10,... | collective-permute-start | bytes 1572872 | tf_op jit(solution)/shard_map/ppermute | solution.py:51
  232.7 21.8 %collective-permute-start.42 = (bf16[256,1024]{1,0:T(8,128)(2,1)}, bf16[256,1024]{1,0:T(8,128)(2,1)}, u32[]{:S(2)}, u32[]{:S(2)}) collective-permute-start(bf16[256,1024]{1,0:T(8,128)(2,1)} %collective-permute-done.25), channel_id=1, source_target_pairs={{0,1},{1,0},{2,3},{3,2},{4,5},{5,4},{6,7},{7,6},{8,9},{9,8},{10,11... | collective-permute-start | bytes 1572872 | tf_op jit(solution)/shard_map/ppermute | solution.py:51
  233.7 21.9 %collective-permute-start.43 = (bf16[128,2048]{1,0:T(8,128)(2,1)S(1)}, bf16[128,2048]{1,0:T(8,128)(2,1)S(1)}, u32[]{:S(2)}, u32[]{:S(2)}) collective-permute-start(bf16[128,2048]{1,0:T(8,128)(2,1)S(1)} %reshape.373), channel_id=1, source_target_pairs={{0,2},{1,3},{2,0},{3,1},{4,6},{5,7},{6,4},{7,5},{8,10},{9,11},{10,... | collective-permute-start | bytes 1572872 | tf_op jit(solution)/shard_map/ppermute | solution.py:51
  263.7 17.5 %collective-permute-start.44 = (bf16[128,2048]{1,0:T(8,128)(2,1)S(1)}, bf16[128,2048]{1,0:T(8,128)(2,1)S(1)}, u32[]{:S(2)}, u32[]{:S(2)}) collective-permute-start(bf16[128,2048]{1,0:T(8,128)(2,1)S(1)} %get-tuple-element.500), channel_id=1, source_target_pairs={{0,8},{1,9},{2,10},{3,11},{4,12},{5,13},{6,14},{7,15},{8,0},{9,1},... | collective-permute-start | bytes 1572872 | tf_op jit(solution)/shard_map/ppermute | solution.py:51
  264.2 16.9 %collective-permute-start.46 = (bf16[128,2048]{1,0:T(8,128)(2,1)S(1)}, bf16[128,2048]{1,0:T(8,128)(2,1)S(1)}, u32[]{:S(2)}, u32[]{:S(2)}) collective-permute-start(bf16[128,2048]{1,0:T(8,128)(2,1)S(1)} %fusion.25), channel_id=1, source_target_pairs={{0,1},{1,0},{2,3},{3,2},{4,5},{5,4},{6,7},{7,6},{8,9},{9,8},{10,11... | collective-permute-start | bytes 1572872 | tf_op jit(solution)/shard_map/ppermute | solution.py:51
  289.0 21.1 %collective-permute-start.51 = (bf16[256,1024]{1,0:T(8,128)(2,1)}, bf16[256,1024]{1,0:T(8,128)(2,1)S(1)}, u32[]{:S(2)}, u32[]{:S(2)}) collective-permute-start(bf16[256,1024]{1,0:T(8,128)(2,1)} %copy-done.70), channel_id=1, source_target_pairs={{0,1},{1,0},{2,3},{3,2},{4,5},{5,4},{6,7},{7,6},{8,9},{9,8},{10,11... | collective-permute-start | bytes 1572872 | tf_op jit(solution)/shard_map/ppermute | solution.py:51
  293.2 65.8 %collective-permute-start.63 = (bf16[512,2048]{1,0:T(8,128)(2,1)}, bf16[512,2048]{1,0:T(8,128)(2,1)S(1)}, u32[]{:S(2)}, u32[]{:S(2)}) collective-permute-start(bf16[512,2048]{1,0:T(8,128)(2,1)} %pad_maximum_fusion.2), channel_id=1, source_target_pairs={{0,8},{1,9},{2,10},{3,11},{4,12},{5,13},{6,14},{7,15},{8,0},{9,1},... | collective-permute-start | bytes 6291464 | tf_op jit(solution)/shard_map/ppermute | solution.py:51
  324.0 22.7 %collective-permute-start.59 = (bf16[256,1024]{1,0:T(8,128)(2,1)}, bf16[256,1024]{1,0:T(8,128)(2,1)}, u32[]{:S(2)}, u32[]{:S(2)}) collective-permute-start(bf16[256,1024]{1,0:T(8,128)(2,1)} %collective-permute-done.41), channel_id=1, source_target_pairs={{0,1},{1,0},{2,3},{3,2},{4,5},{5,4},{6,7},{7,6},{8,9},{9,8},{10,11... | collective-permute-start | bytes 1572872 | tf_op jit(solution)/shard_map/ppermute | solution.py:51
  330.7 34.8 %collective-permute-start.57 = (bf16[512,2048]{1,0:T(8,128)(2,1)}, bf16[512,2048]{1,0:T(8,128)(2,1)}, u32[]{:S(2)}, u32[]{:S(2)}) collective-permute-start(bf16[512,2048]{1,0:T(8,128)(2,1)} %assemble.2.refs_0_), channel_id=1, source_target_pairs={{0,8},{1,9},{2,10},{3,11},{4,12},{5,13},{6,14},{7,15},{8,0},{9,1},... | collective-permute-start | bytes 6291464 | tf_op jit(solution)/shard_map/ppermute | solution.py:51
  406.3 29.8 %collective-permute-start.62 = (bf16[2,2,128,2048]{3,2,1,0:T(8,128)(2,1)}, bf16[2,2,128,2048]{3,2,1,0:T(8,128)(2,1)S(1)}, u32[]{:S(2)}, u32[]{:S(2)}) collective-permute-start(bf16[2,2,128,2048]{3,2,1,0:T(8,128)(2,1)} %bitcast.37), channel_id=1, source_target_pairs={{0,8},{1,9},{2,10},{3,11},{4,12},{5,13},{6,14},{7,15},{8,0},{9,1},... | collective-permute-start | bytes 6291464 | tf_op jit(solution)/shard_map/ppermute | solution.py:51
  473.8 17.1 %collective-permute-start.75 = (bf16[128,2048]{1,0:T(8,128)(2,1)S(1)}, bf16[128,2048]{1,0:T(8,128)(2,1)}, u32[]{:S(2)}, u32[]{:S(2)}) collective-permute-start(bf16[128,2048]{1,0:T(8,128)(2,1)S(1)} %reshape.390), channel_id=1, source_target_pairs={{0,8},{1,9},{2,10},{3,11},{4,12},{5,13},{6,14},{7,15},{8,0},{9,1},... | collective-permute-start | bytes 1572872 | tf_op jit(solution)/shard_map/ppermute | solution.py:51
  473.9 16.6 %collective-permute-start.72 = (bf16[128,2048]{1,0:T(8,128)(2,1)S(1)}, bf16[128,2048]{1,0:T(8,128)(2,1)}, u32[]{:S(2)}, u32[]{:S(2)}) collective-permute-start(bf16[128,2048]{1,0:T(8,128)(2,1)S(1)} %reshape.390), channel_id=1, source_target_pairs={{0,1},{1,0},{2,3},{3,2},{4,5},{5,4},{6,7},{7,6},{8,9},{9,8},{10,11... | collective-permute-start | bytes 1572872 | tf_op jit(solution)/shard_map/ppermute | solution.py:51
  498.5 31.3 %collective-permute-start.77 = (bf16[4,256,640]{2,1,0:T(8,128)(2,1)}, bf16[4,256,640]{2,1,0:T(8,128)(2,1)}, u32[]{:S(2)}, u32[]{:S(2)}) collective-permute-start(bf16[4,256,640]{2,1,0:T(8,128)(2,1)} %bitcast.56), channel_id=1, source_target_pairs={{0,16},{1,17},{2,18},{3,19},{4,20},{5,21},{6,22},{7,23},{8,24},{9,... | collective-permute-start | bytes 3932168 | tf_op jit(solution)/shard_map/ppermute | solution.py:51
  499.7 26.7 %collective-permute-start.78 = (bf16[512,1024]{1,0:T(8,128)(2,1)}, bf16[512,1024]{1,0:T(8,128)(2,1)}, u32[]{:S(2)}, u32[]{:S(2)}) collective-permute-start(bf16[512,1024]{1,0:T(8,128)(2,1)} %get-tuple-element.368), channel_id=1, source_target_pairs={{0,1},{1,0},{2,3},{3,2},{4,5},{5,4},{6,7},{7,6},{8,9},{9,8},{10,11... | collective-permute-start | bytes 3145736 | tf_op jit(solution)/shard_map/ppermute | solution.py:51
  500.3 26.1 %collective-permute-start.79 = (bf16[256,1024]{1,0:T(8,128)(2,1)}, bf16[256,1024]{1,0:T(8,128)(2,1)}, u32[]{:S(2)}, u32[]{:S(2)}) collective-permute-start(bf16[256,1024]{1,0:T(8,128)(2,1)} %slice.531), channel_id=1, source_target_pairs={{0,4},{1,5},{2,6},{3,7},{4,0},{5,1},{6,2},{7,3},{8,12},{9,13},{10,... | collective-permute-start | bytes 1572872 | tf_op jit(solution)/shard_map/ppermute | solution.py:51
  533.6 27.2 %collective-permute-start.80 = (bf16[4,512,256]{2,1,0:T(8,128)(2,1)S(1)}, bf16[4,512,256]{2,1,0:T(8,128)(2,1)S(1)}, u32[]{:S(2)}, u32[]{:S(2)}) collective-permute-start(bf16[4,512,256]{2,1,0:T(8,128)(2,1)S(1)} %bitcast.290), channel_id=1, source_target_pairs={{0,16},{1,17},{2,18},{3,19},{4,20},{5,21},{6,22},{7,23},{8,24},{9,... | collective-permute-start | bytes 3145736 | tf_op jit(solution)/shard_map/ppermute | solution.py:51
  534.8 26.0 %collective-permute-start.81 = (bf16[512,1024]{1,0:T(8,128)(2,1)S(1)}, bf16[512,1024]{1,0:T(8,128)(2,1)S(1)}, u32[]{:S(2)}, u32[]{:S(2)}) collective-permute-start(bf16[512,1024]{1,0:T(8,128)(2,1)S(1)} %copy-done.46), channel_id=1, source_target_pairs={{0,1},{1,0},{2,3},{3,2},{4,5},{5,4},{6,7},{7,6},{8,9},{9,8},{10,11... | collective-permute-start | bytes 3145736 | tf_op jit(solution)/shard_map/ppermute | solution.py:51
  535.8 25.0 %collective-permute-start.82 = (bf16[256,1024]{1,0:T(8,128)(2,1)S(1)}, bf16[256,1024]{1,0:T(8,128)(2,1)S(1)}, u32[]{:S(2)}, u32[]{:S(2)}) collective-permute-start(bf16[256,1024]{1,0:T(8,128)(2,1)S(1)} %get-tuple-element.378), channel_id=1, source_target_pairs={{0,4},{1,5},{2,6},{3,7},{4,0},{5,1},{6,2},{7,3},{8,12},{9,13},{10,... | collective-permute-start | bytes 1572872 | tf_op jit(solution)/shard_map/ppermute | solution.py:51
  561.1 30.6 %collective-permute-start.84 = (bf16[4,512,256]{2,1,0:T(8,128)(2,1)S(1)}, bf16[4,512,256]{2,1,0:T(8,128)(2,1)S(1)}, u32[]{:S(2)}, u32[]{:S(2)}) collective-permute-start(bf16[4,512,256]{2,1,0:T(8,128)(2,1)S(1)} %bitcast.288), channel_id=1, source_target_pairs={{0,16},{1,17},{2,18},{3,19},{4,20},{5,21},{6,22},{7,23},{8,24},{9,... | collective-permute-start | bytes 3145736 | tf_op jit(solution)/shard_map/ppermute | solution.py:51
  562.1 29.7 %collective-permute-start.85 = (bf16[512,1024]{1,0:T(8,128)(2,1)S(1)}, bf16[512,1024]{1,0:T(8,128)(2,1)S(1)}, u32[]{:S(2)}, u32[]{:S(2)}) collective-permute-start(bf16[512,1024]{1,0:T(8,128)(2,1)S(1)} %copy-done.45), channel_id=1, source_target_pairs={{0,1},{1,0},{2,3},{3,2},{4,5},{5,4},{6,7},{7,6},{8,9},{9,8},{10,11... | collective-permute-start | bytes 3145736 | tf_op jit(solution)/shard_map/ppermute | solution.py:51
  566.3 22.8 %collective-permute-start.83 = (bf16[2,512,256]{2,1,0:T(8,128)(2,1)S(1)}, bf16[2,512,256]{2,1,0:T(8,128)(2,1)S(1)}, u32[]{:S(2)}, u32[]{:S(2)}) collective-permute-start(bf16[2,512,256]{2,1,0:T(8,128)(2,1)S(1)} %slice.541), channel_id=1, source_target_pairs={{0,2},{1,3},{2,0},{3,1},{4,6},{5,7},{6,4},{7,5},{8,10},{9,11},{10,... | collective-permute-start | bytes 1572872 | tf_op jit(solution)/shard_map/ppermute | solution.py:51
  568.3 23.5 %collective-permute-start.86 = (bf16[256,1024]{1,0:T(8,128)(2,1)S(1)}, bf16[256,1024]{1,0:T(8,128)(2,1)S(1)}, u32[]{:S(2)}, u32[]{:S(2)}) collective-permute-start(bf16[256,1024]{1,0:T(8,128)(2,1)S(1)} %get-tuple-element.386), channel_id=1, source_target_pairs={{0,4},{1,5},{2,6},{3,7},{4,0},{5,1},{6,2},{7,3},{8,12},{9,13},{10,... | collective-permute-start | bytes 1572872 | tf_op jit(solution)/shard_map/ppermute | solution.py:51
  592.3 24.5 %collective-permute-start.89 = (bf16[4,256,512]{2,1,0:T(8,128)(2,1)S(1)}, bf16[4,256,512]{2,1,0:T(8,128)(2,1)S(1)}, u32[]{:S(2)}, u32[]{:S(2)}) collective-permute-start(bf16[4,256,512]{2,1,0:T(8,128)(2,1)S(1)} %bitcast.287), channel_id=1, source_target_pairs={{0,16},{1,17},{2,18},{3,19},{4,20},{5,21},{6,22},{7,23},{8,24},{9,... | collective-permute-start | bytes 3145736 | tf_op jit(solution)/shard_map/ppermute | solution.py:51
  593.5 23.2 %collective-permute-start.91 = (bf16[512,1024]{1,0:T(8,128)(2,1)S(1)}, bf16[512,1024]{1,0:T(8,128)(2,1)S(1)}, u32[]{:S(2)}, u32[]{:S(2)}) collective-permute-start(bf16[512,1024]{1,0:T(8,128)(2,1)S(1)} %copy-done.54), channel_id=1, source_target_pairs={{0,1},{1,0},{2,3},{3,2},{4,5},{5,4},{6,7},{7,6},{8,9},{9,8},{10,11... | collective-permute-start | bytes 3145736 | tf_op jit(solution)/shard_map/ppermute | solution.py:51
  597.1 19.7 %collective-permute-start.88 = (bf16[2,512,256]{2,1,0:T(8,128)(2,1)S(1)}, bf16[2,512,256]{2,1,0:T(8,128)(2,1)S(1)}, u32[]{:S(2)}, u32[]{:S(2)}) collective-permute-start(bf16[2,512,256]{2,1,0:T(8,128)(2,1)S(1)} %slice.545), channel_id=1, source_target_pairs={{0,2},{1,3},{2,0},{3,1},{4,6},{5,7},{6,4},{7,5},{8,10},{9,11},{10,... | collective-permute-start | bytes 1572872 | tf_op jit(solution)/shard_map/ppermute | solution.py:51
  598.9 17.1 %collective-permute-start.90 = (bf16[128,1024]{1,0:T(8,128)(2,1)S(1)}, bf16[128,1024]{1,0:T(8,128)(2,1)S(1)}, u32[]{:S(2)}, u32[]{:S(2)}) collective-permute-start(bf16[128,1024]{1,0:T(8,128)(2,1)S(1)} %get-tuple-element.394), channel_id=1, source_target_pairs={{0,4},{1,5},{2,6},{3,7},{4,0},{5,1},{6,2},{7,3},{8,12},{9,13},{10,... | collective-permute-start | bytes 786440 | tf_op jit(solution)/shard_map/ppermute | solution.py:51
  617.3 18.1 %collective-permute-start.93 = (bf16[2,256,512]{2,1,0:T(8,128)(2,1)S(1)}, bf16[2,256,512]{2,1,0:T(8,128)(2,1)S(1)}, u32[]{:S(2)}, u32[]{:S(2)}) collective-permute-start(bf16[2,256,512]{2,1,0:T(8,128)(2,1)S(1)} %slice.553), channel_id=1, source_target_pairs={{0,2},{1,3},{2,0},{3,1},{4,6},{5,7},{6,4},{7,5},{8,10},{9,11},{10,... | collective-permute-start | bytes 1572872 | tf_op jit(solution)/shard_map/ppermute | solution.py:51
  638.7 22.0 %collective-permute-start.96 = (bf16[128,2048]{1,0:T(8,128)(2,1)S(1)}, bf16[128,2048]{1,0:T(8,128)(2,1)S(1)}, u32[]{:S(2)}, u32[]{:S(2)}) collective-permute-start(bf16[128,2048]{1,0:T(8,128)(2,1)S(1)} %get-tuple-element.487), channel_id=1, source_target_pairs={{0,8},{1,9},{2,10},{3,11},{4,12},{5,13},{6,14},{7,15},{8,0},{9,1},... | collective-permute-start | bytes 1572872 | tf_op jit(solution)/shard_map/ppermute | solution.py:51
  642.5 18.2 %collective-permute-start.98 = (bf16[256,1024]{1,0:T(8,128)(2,1)S(1)}, bf16[256,1024]{1,0:T(8,128)(2,1)S(1)}, u32[]{:S(2)}, u32[]{:S(2)}) collective-permute-start(bf16[256,1024]{1,0:T(8,128)(2,1)S(1)} %fusion.39), channel_id=1, source_target_pairs={{0,2},{1,3},{2,0},{3,1},{4,6},{5,7},{6,4},{7,5},{8,10},{9,11},{10,... | collective-permute-start | bytes 1572872 | tf_op jit(solution)/shard_map/ppermute | solution.py:51
  660.8 42.8 %collective-permute-start.100 = (bf16[4,256,512]{2,1,0:T(8,128)(2,1)S(1)}, bf16[4,256,512]{2,1,0:T(8,128)(2,1)S(1)}, u32[]{:S(2)}, u32[]{:S(2)}) collective-permute-start(bf16[4,256,512]{2,1,0:T(8,128)(2,1)S(1)} %bitcast.289), channel_id=1, source_target_pairs={{0,16},{1,17},{2,18},{3,19},{4,20},{5,21},{6,22},{7,23},{8,24},{9,... | collective-permute-start | bytes 3145736 | tf_op jit(solution)/shard_map/ppermute | solution.py:51
  663.5 21.4 %collective-permute-start.101 = (bf16[1,256,512]{2,1,0:T(8,128)(2,1)S(1)}, bf16[1,256,512]{2,1,0:T(8,128)(2,1)S(1)}, u32[]{:S(2)}, u32[]{:S(2)}) collective-permute-start(bf16[1,256,512]{2,1,0:T(8,128)(2,1)S(1)} %slice.564), channel_id=1, source_target_pairs={{0,4},{1,5},{2,6},{3,7},{4,0},{5,1},{6,2},{7,3},{8,12},{9,13},{10,... | collective-permute-start | bytes 786440 | tf_op jit(solution)/shard_map/ppermute | solution.py:51
  666.8 22.9 %collective-permute-start.103 = (bf16[128,1024]{1,0:T(8,128)(2,1)S(1)}, bf16[128,1024]{1,0:T(8,128)(2,1)S(1)}, u32[]{:S(2)}, u32[]{:S(2)}) collective-permute-start(bf16[128,1024]{1,0:T(8,128)(2,1)S(1)} %get-tuple-element.417), channel_id=1, source_target_pairs={{0,4},{1,5},{2,6},{3,7},{4,0},{5,1},{6,2},{7,3},{8,12},{9,13},{10,... | collective-permute-start | bytes 786440 | tf_op jit(solution)/shard_map/ppermute | solution.py:51
  668.1 35.5 %collective-permute-start.112 = (bf16[128,2048]{1,0:T(8,128)(2,1)S(1)}, bf16[128,2048]{1,0:T(8,128)(2,1)S(1)}, u32[]{:S(2)}, u32[]{:S(2)}) collective-permute-start(bf16[128,2048]{1,0:T(8,128)(2,1)S(1)} %get-tuple-element.486), channel_id=1, source_target_pairs={{0,8},{1,9},{2,10},{3,11},{4,12},{5,13},{6,14},{7,15},{8,0},{9,1},... | collective-permute-start | bytes 1572872 | tf_op jit(solution)/shard_map/ppermute | solution.py:51
  668.2 25.7 %collective-permute-start.99 = (bf16[128,2048]{1,0:T(8,128)(2,1)S(1)}, bf16[128,2048]{1,0:T(8,128)(2,1)S(1)}, u32[]{:S(2)}, u32[]{:S(2)}) collective-permute-start(bf16[128,2048]{1,0:T(8,128)(2,1)S(1)} %fusion.21), channel_id=1, source_target_pairs={{0,1},{1,0},{2,3},{3,2},{4,5},{5,4},{6,7},{7,6},{8,9},{9,8},{10,11... | collective-permute-start | bytes 1572872 | tf_op jit(solution)/shard_map/ppermute | solution.py:51
  684.9 18.6 %collective-permute-start.102 = (bf16[2,256,640]{2,1,0:T(8,128)(2,1)S(1)}, bf16[2,256,640]{2,1,0:T(8,128)(2,1)S(1)}, u32[]{:S(2)}, u32[]{:S(2)}) collective-permute-start(bf16[2,256,640]{2,1,0:T(8,128)(2,1)S(1)} %slice.565), channel_id=1, source_target_pairs={{0,2},{1,3},{2,0},{3,1},{4,6},{5,7},{6,4},{7,5},{8,10},{9,11},{10,... | collective-permute-start | bytes 1966088 | tf_op jit(solution)/shard_map/ppermute | solution.py:51
  711.1 19.8 %collective-permute-start.105 = (bf16[2,256,512]{2,1,0:T(8,128)(2,1)}, bf16[2,256,512]{2,1,0:T(8,128)(2,1)}, u32[]{:S(2)}, u32[]{:S(2)}) collective-permute-start(bf16[2,256,512]{2,1,0:T(8,128)(2,1)} %slice.572), channel_id=1, source_target_pairs={{0,2},{1,3},{2,0},{3,1},{4,6},{5,7},{6,4},{7,5},{8,10},{9,11},{10,... | collective-permute-start | bytes 1572872 | tf_op jit(solution)/shard_map/ppermute | solution.py:51
  732.3 24.5 %collective-permute-start.108 = (bf16[1,256,640]{2,1,0:T(8,128)(2,1)S(1)}, bf16[1,256,640]{2,1,0:T(8,128)(2,1)S(1)}, u32[]{:S(2)}, u32[]{:S(2)}) collective-permute-start(bf16[1,256,640]{2,1,0:T(8,128)(2,1)S(1)} %slice.577), channel_id=1, source_target_pairs={{0,4},{1,5},{2,6},{3,7},{4,0},{5,1},{6,2},{7,3},{8,12},{9,13},{10,... | collective-permute-start | bytes 983048 | tf_op jit(solution)/shard_map/ppermute | solution.py:51
  733.9 24.7 %collective-permute-start.109 = (bf16[256,1024]{1,0:T(8,128)(2,1)S(1)}, bf16[256,1024]{1,0:T(8,128)(2,1)S(1)}, u32[]{:S(2)}, u32[]{:S(2)}) collective-permute-start(bf16[256,1024]{1,0:T(8,128)(2,1)S(1)} %copy-done.81), channel_id=1, source_target_pairs={{0,2},{1,3},{2,0},{3,1},{4,6},{5,7},{6,4},{7,5},{8,10},{9,11},{10,... | collective-permute-start | bytes 1572872 | tf_op jit(solution)/shard_map/ppermute | solution.py:51
  736.4 20.4 %collective-permute-start.107 = (bf16[1,256,512]{2,1,0:T(8,128)(2,1)S(1)}, bf16[1,256,512]{2,1,0:T(8,128)(2,1)S(1)}, u32[]{:S(2)}, u32[]{:S(2)}) collective-permute-start(bf16[1,256,512]{2,1,0:T(8,128)(2,1)S(1)} %slice.575), channel_id=1, source_target_pairs={{0,4},{1,5},{2,6},{3,7},{4,0},{5,1},{6,2},{7,3},{8,12},{9,13},{10,... | collective-permute-start | bytes 786440 | tf_op jit(solution)/shard_map/ppermute | solution.py:51
  (191 other events, 2429.0 us)

commit v3 on v2

--- a/solution.py
+++ b/solution.py
@@ -655,7 +655,7 @@
     gains = lax.dynamic_update_slice(
         gains, jnp.stack([norm_in, norm_mid])[:, None], (0, head * groups + group, 0)
     )
-    hops = [blk_masks[:1], blk_masks[-1:], blk_masks[1:-1], [None]]
+    hops = [blk_masks[:1], blk_masks[1:-1], blk_masks[-1:], [None]]
 
     def hop():
         nonlocal gains, gain_sent
@@ -683,10 +683,10 @@
         parts, first = [], 0
         for count in (2 * query_local, 2 * key_local, 2 * key_local, 2 * query_local):
             parts.append(
-                lax.dynamic_slice_in_dim(value, first + bit * (count // 2), count // 2, 2)
+                lax.dynamic_slice_in_dim(value, first + bit * (count // 2), count // 2, 1)
             )
             first += count
-        return jnp.concatenate(parts, axis=2)
+        return jnp.concatenate(parts, axis=1)
 
     attention_weights = (w_query, key_weight, value_weight, w_out)
 
@@ -712,18 +712,19 @@
     def high(rows):
         return any([bulk.take(flow, mask, rows, block_rows) for mask in far_masks[:-1]])
 
-    weights_low = flow.send(column_half(attention_weights, 1 - low), 0, 1)
+    own_half, other_half = (column_half(attention_weights, bit) for bit in (low, 1 - low))
+    cols_core = flow.send(core_half(own_half, 1 - core), CORE, 0)
+    cols_low = flow.send(core_half(other_half, core), 0, 1)
+    cols_both = flow.send(core_half(other_half, 1 - core), CORE, 1)
     turned = send_turn(0)
-    cot_far = to_far(cotangent)
-    cot_x = flow.send(cot_far, CROSS, 0)
     hop()
     flow.go()
     end_turn(0, turned)
-    both = pair(column_half(attention_weights, low), weights_low.value, low, 0)
-    weights_core = flow.send(core_half(both, 1 - core), CORE, 0)
-    hop()
-    flow.go()
-    own_cols = pair(core_half(both, core), weights_core.value, core, 0).reshape(4 * shard, -1)
+    own_cols = pair(
+        pair(core_half(own_half, core), cols_low.value, low, 0),
+        pair(cols_core.value, cols_both.value, low, 0),
+        core, 0,
+    ).reshape(4 * shard, -1)
     spread_in = Spread(own_cols[:, :in_cols], wide_masks)
     chain_out = Chain(own_cols[:, in_cols:], wide_masks)
     spread_in.wave(flow, 0)
@@ -731,21 +732,22 @@
     token_low = flow.send(token_x, 0, 1)
     hop()
     flow.go()
-    token_group = jnp.concatenate(
-        [token_x, swap(token_x, CORE, 0), token_low.value, swap(token_low.value, CORE, 0)], axis=0
-    ).astype(F32)
     spread_in.wave(flow, 1)
-    near(block_rows)
     high(ff_rows)
+    hop()
     flow.go()
     for count in range(2, depth):
         if count > 2:
             flow.go()
         spread_in.wave(flow, count)
-    chain_out.advance(flow)
+    token_core = flow.send(token_x, CORE, 0)
+    token_both = flow.send(token_low.value, CORE, 0)
     turned = send_turn(1)
     hop()
     flow.go()
+    token_group = jnp.concatenate(
+        [token_x, token_core.value, token_low.value, token_both.value], axis=0
+    ).astype(F32)
     end_turn(1, turned)
     hop()
     spread_in.settle()
@@ -755,7 +757,9 @@
     gain_in, gain_mid = to_wide(gains[:1]), gains[1:]
     turned = send_turn(2)
     near(ff_rows)
-    high(ff_rows)
+    chain_out.advance(flow)
+    cot_far = to_far(cotangent)
+    cot_x = flow.send(cot_far, CROSS, 0)
     flow.go()
     end_turn(2, turned)
 
@@ -778,7 +782,7 @@
     near(ff_rows)
     flow.go()
     spread_kv.wave(flow, 1)
-    near(ff_rows)
+    near(block_rows)
     high(ff_rows)
     flow.go()
     for count in range(2, depth):
@@ -788,6 +792,7 @@
     chain_out.advance(flow)
     high(ff_rows)
     near(ff_rows)
+    near(ff_rows)
     flow.go()
     spread_kv.settle()
     kv_all = jnp.concatenate(in_fold_order(spread_kv.have, wide_masks), axis=0)
@@ -795,6 +800,7 @@
         chain_out.advance(flow)
         if not chain_out.masks:
             high(ff_rows)
+            near(ff_rows)
             near(ff_rows)
             cot_t = flow.send(cot_far, 0, TURN)
         flow.go()
@@ -831,7 +837,7 @@
     right_x = flow.send(right, CROSS, 0)
     left_xt = flow.send(left_x.value, 0, TURN)
     right_xt = flow.send(right_t.value, CROSS, 0)
-    high(ff_rows)
+    high(ff_rows // 2)
     flow.go()
     def four_rows(parts, first_col):
         return [(part, (i * token_rows, first_col)) for i, part in enumerate(parts)]
@@ -996,12 +1002,15 @@
             near(block_rows)
         else:
             near(ff_rows)
+            high(ff_rows // 2)
             if len(out_parts) == 1:
                 out_parts.append(flow.send(out_four[1, 1], CROSS, 0))
         flow.go()
+    out_two = [add(out_four[0, i], sent.value, BF16) for i, sent in enumerate(out_parts)]
+    out_sent = flow.send(out_two[1], 0, TURN)
     high(ff_rows // 2)
-    take_turn()
-    flow.go()
+    flow.go()
+    layer_out = (middle + from_far(add(out_two[0], out_sent.value, F32))).astype(BF16)
     keys_low, values_low = key_fold.blocks[0].astype(BF16), value_fold.blocks[0].astype(BF16)
     kv_lin = jnp.concatenate(
         [rotate(keys_low.astype(F32), cosine, -sine).astype(BF16), values_low], axis=-1
@@ -1016,21 +1025,17 @@
     kv_fold.advance(flow)
     query_fold.advance(flow)
     out_fold.advance(flow)
-    high(ff_rows // 2)
-    near(ff_rows)
     flow.go()
     kv_fold.advance(flow)
     query_fold.advance(flow)
-    high(ff_rows // 2)
+    out_fold.advance(flow)
     near(ff_rows)
     flow.go()
     kv_fold.advance(flow)
-    out_fold.advance(flow)
     high(ff_rows)
     near(block_rows)
     take_turn()
     flow.go()
-    out_two = [add(out_four[0, i], sent.value, BF16) for i, sent in enumerate(out_parts)]
     while True:
         running = [fold.advance(flow) for fold in (kv_fold, query_fold, out_fold)]
         if not any(running):
@@ -1041,11 +1046,17 @@
     total = jnp.concatenate(
         [fold.blocks[0] for fold in (query_fold, kv_fold, out_fold)], axis=-1
     ).reshape(2, 2, shard, -1)
-    total_core = flow.send(index(total, 1 - core).astype(BF16), CORE, 0)
-    out_sent = flow.send(out_two[1], 0, TURN)
-    flow.go()
-    total = pair(index(total, core), total_core.value.astype(F32), core, 1)
-    total_low = flow.send(index(total, 1 - low).astype(BF16), 0, 1)
+
+    def block_of(core_bit, low_bit):
+        return index(index(total, core_bit), low_bit)
+
+    sent_core = flow.send(block_of(1 - core, low).astype(BF16), CORE, 0)
+    sent_low = flow.send(block_of(core, 1 - low).astype(BF16), 0, 1)
+    sent_both = flow.send(block_of(1 - core, 1 - low).astype(BF16), CORE, 1)
+    for fold in list(turns):
+        if fold.take_turn(flow):
+            turns.remove(fold)
+    flow.go()
     while True:
         near(block_rows), high(block_rows)
         for fold in list(turns):
@@ -1054,10 +1065,12 @@
         if not flow.batch:
             break
         flow.go()
-    total = pair(index(total, low), total_low.value.astype(F32), low, 0).reshape(4, shard, -1)
-    layer_out = (middle + from_far(add(out_two[0], out_sent.value, F32))).astype(BF16)
+    total = pair(
+        pair(block_of(core, low), sent_core.value.astype(F32), core, 0),
+        pair(sent_low.value.astype(F32), sent_both.value.astype(F32), core, 0),
+        low, 0,
+    ).reshape(4, shard, -1)
     scaled = in_own + in_sent.value.astype(F32)
-    tokens_f = tokens.astype(F32)
     inv_in = inv_group[:token_rows]
     normed_in = tokens_f * inv_in
     grad_tokens = grad_middle + rms_back(from_wide(scaled * gain_in), normed_in, inv_in)

time: 816 us -> 787 us (0.964)
  waiting for transfers between devices: 354 us -> 328 us
  starting transfers between devices: 139 us -> 130 us
    ppermute x115 -> x120, waiting for transfers between devices: 354 us -> 328 us  [swap(): return row_major(lax.ppermute(row_major(value), ('head', 'blk'), pairs))]
    unnamed x322 -> x329, local copies, waits for them, and re-layouts: 55 us -> 64.1 us
    ppermute x115 -> x120, starting transfers between devices: 139 us -> 130 us  [swap(): return row_major(lax.ppermute(row_major(value), ('head', 'blk'), pairs))]
  transfers between devices with their start and end apart: 115 -> 120, of which waited for: 67 -> 63; matrix products, arithmetic and copies ran while one was open for 19% -> 22% of each run, Pallas kernels for 4% -> 4%
where the time goes in v3:
time: 787 us; the launch traced here: 779 us
  waiting for transfers between devices  328 us (42%)
  starting transfers between devices  130 us (17%)
  local copies, waits for them, and re-layouts  129 us (16%)
  other arithmetic  77 us (10%)
  matrix products  75.2 us (10%)
  Pallas kernels  35.7 us (5%)
    ppermute x120, waiting for transfers between devices, swap(): return row_major(lax.ppermute(row_major(value), ('head', 'blk'), pairs))  328 us
    ppermute x120, starting transfers between devices, swap(): return row_major(lax.ppermute(row_major(value), ('head', 'blk'), pairs))  130 us
    unnamed x329, local copies, waits for them, and re-layouts  64.1 us
  transfers between devices with their start and end apart: 120, of which 63 were waited for; matrix products, arithmetic and copies ran while one was open for 22% of the time, Pallas kernels for 4%

profile of v3, /device:TPU:0, one launch (start us, length us, event | category | flops | bytes accessed | tf_op | source)
XLA Modules:
  0.0 779.4 jit_solution(3529598826596448076)
XLA Ops:
  12.9 2.6 collective-permute-start.4
  21.4 3.7 collective-permute-done.4
  29.5 2.6 collective-permute-start.5
  41.6 14.0 %collective-permute-done.9 = bf16[2,32,64]{2,1,0:T(8,128)(2,1)S(1)} collective-permute-done((bf16[2,32,64]{2,1,0:T(8,128)(2,1)S(1)}, bf16[2,32,64]{2,1,0:T(8,128)(2,1)S(1)}, u32[]{:S(2)}, u32[]{:S(2)}) %collective-permute-start.9) | collective-permute-done | bytes 8224 | tf_op jit(solution)/shard_map/ppermute | solution.py:51
  59.3 2.6 collective-permute-start.13
  68.1 2.8 collective-permute-done.10
  70.9 9.5 %collective-permute-done.11 = bf16[256,1024]{1,0:T(8,128)(2,1)} collective-permute-done((bf16[256,1024]{1,0:T(8,128)(2,1)}, bf16[256,1024]{1,0:T(8,128)(2,1)}, u32[]{:S(2)}, u32[]{:S(2)}) %collective-permute-start.11) | collective-permute-done | bytes 524320 | tf_op jit(solution)/shard_map/ppermute | solution.py:51
  80.4 3.9 collective-permute-done.13
  96.4 4.0 collective-permute-done.18
  105.8 2.6 collective-permute-start.23
  109.8 4.9 fusion.132
  114.7 7.2 collective-permute-done.23
  136.9 16.5 %collective-permute-done.25 = bf16[512,512]{1,0:T(8,128)(2,1)} collective-permute-done((bf16[512,512]{1,0:T(8,128)(2,1)}, bf16[512,512]{1,0:T(8,128)(2,1)}, u32[]{:S(2)}, u32[]{:S(2)}) %collective-permute-start.25) | collective-permute-done | bytes 524320 | tf_op jit(solution)/shard_map/ppermute | solution.py:51
  161.9 2.6 broadcast_select_fusion.10
  164.5 5.5 collective-permute-done.30
  170.0 7.5 collective-permute-done.31
  178.3 4.1 collective-permute-done.34
  184.2 2.6 collective-permute-start.37
  193.3 8.7 %collective-permute-done.36 = bf16[2,256,512]{2,1,0:T(8,128)(2,1)S(1)} collective-permute-done((bf16[2,256,512]{2,1,0:T(8,128)(2,1)S(1)}, bf16[2,256,512]{2,1,0:T(8,128)(2,1)S(1)}, u32[]{:S(2)}, u32[]{:S(2)}) %collective-permute-start.36) | collective-permute-done | bytes 524320 | tf_op jit(solution)/shard_map/ppermute | solution.py:51
  214.9 13.5 %attend.1 = (bf16[512,512]{1,0:T(8,128)(2,1)}, f32[512,512]{1,0:T(8,128)}, f32[2,1,512]{2,1,0:T(1,128)}) custom-call(s32[2]{0:T(128)} %pad_add_fusion.place_ref, s32[8]{0:T(128)} %pair_ref.3, s32[4096]{0:T(1024)} %bitcast.296, bf16[512,512]{1,0:T(8,128)(2,1)} %maximum_multiply_fusion.q_ref, bf16[4096,512]{1,0:T(8,128)(2,1)} %copy-done.116, ...), custom_call_target="tpu_custom_call" | custom-call | flops 6000000000 | bytes 6000000 | tf_op jit(solution)/shard_map/attend/pallas_call | solution.py:461
  251.9 9.9 %collective-permute-done.49 = bf16[128,1024]{1,0:T(8,128)(2,1)} collective-permute-done((bf16[128,1024]{1,0:T(8,128)(2,1)S(1)}, bf16[128,1024]{1,0:T(8,128)(2,1)}, u32[]{:S(2)}, u32[]{:S(2)}) %collective-permute-start.49) | collective-permute-done | bytes 262176 | tf_op jit(solution)/shard_map/ppermute | solution.py:51
  274.7 2.6 collective-permute-start.53
  281.6 5.6 collective-permute-done.51.refs_5_
  289.2 2.8 pad_maximum_fusion.2
  303.0 4.1 collective-permute-done.56.refs_3_
  308.3 4.1 collective-permute-done.58
  318.6 2.9 assemble.2.refs_0_
  323.4 7.6 collective-permute-done.61
  345.9 3.2 collective-permute-done.65
  351.6 6.1 fusion.159
  357.7 4.2 assemble.3
  362.0 7.9 %fusion.158 = f32[1024,1024]{1,0:T(8,128)S(1)} fusion(bf16[1024,2048]{1,0:T(8,128)(2,1)} %assemble.3, bf16[2048,1024]{1,0:T(8,128)(2,1)} %constant_dynamic-update-slice_fusion.16), kind=kOutput, calls=%fused_computation.434 | convolution fusion | flops 4294967296 | bytes 12582912 | tf_op jit(solution)/shard_map/dot_general | solution.py:878
  370.0 7.4 multiply_convert_fusion.2
  377.4 4.8 convolution_convert_fusion.2
  382.2 4.8 convolution_convert_fusion.3
  389.1 7.0 fusion.160
  399.5 9.8 %add_convert_fusion = bf16[1024,2048]{1,0:T(8,128)(2,1)S(1)} fusion(f32[1024,2048]{1,0:T(8,128)} %fusion.160, bf16[1024,1024]{1,0:T(8,128)(2,1)} %get-tuple-element.490, bf16[2048,1024]{1,0:T(8,128)(2,1)} %constant_dynamic-update-slice_fusion.16), kind=kOutput, calls=%fused_computation | convolution fusion | flops 4299161600 | bytes 18874368 | tf_op jit(solution)/shard_map/dot_general | solution.py:914
  411.1 4.9 convolution_convert_fusion
  417.2 5.4 convolution_convert_fusion.1
  427.4 12.2 %collective-permute-done.70 = bf16[2,128,1024]{2,1,0:T(8,128)(2,1)S(1)} collective-permute-done((bf16[2,128,1024]{2,1,0:T(8,128)(2,1)S(1)}, bf16[2,128,1024]{2,1,0:T(8,128)(2,1)S(1)}, u32[]{:S(2)}, u32[]{:S(2)}) %collective-permute-start.70) | collective-permute-done | bytes 524320 | tf_op jit(solution)/shard_map/ppermute | solution.py:51
  449.5 5.8 collective-permute-done.74
  455.3 2.8 collective-permute-done.75
  469.9 13.1 %collective-permute-done.77 = bf16[128,1024]{1,0:T(8,128)(2,1)S(1)} collective-permute-done((bf16[128,1024]{1,0:T(8,128)(2,1)}, bf16[128,1024]{1,0:T(8,128)(2,1)S(1)}, u32[]{:S(2)}, u32[]{:S(2)}) %collective-permute-start.77) | collective-permute-done | bytes 262176 | tf_op jit(solution)/shard_map/ppermute | solution.py:51
  493.0 2.6 collective-permute-start.83
  495.6 15.0 %attend_back.1 = (bf16[512,512]{1,0:T(8,128)(2,1)}, bf16[4096,256]{1,0:T(8,128)(2,1)}, bf16[4096,256]{1,0:T(8,128)(2,1)}) custom-call(s32[2]{0:T(128)} %pad_add_fusion.place_ref, s32[8]{0:T(128)} %pair_ref.3, s32[4096]{0:T(1024)} %bitcast.297, bf16[512,512]{1,0:T(8,128)(2,1)} %maximum_multiply_fusion.q_ref, bf16[4096,512]{1,0:T(8,128)(2,1)} %copy-done.116, ...), custom_call_target="tpu_custom_call" | custom-call | flops 16000000000 | bytes 12000000 | tf_op jit(solution)/shard_map/attend_back/pallas_call | solution.py:497
  510.6 8.4 %collective-permute-done.83 = bf16[256,1024]{1,0:T(8,128)(2,1)} collective-permute-done((bf16[256,1024]{1,0:T(8,128)(2,1)}, bf16[256,1024]{1,0:T(8,128)(2,1)}, u32[]{:S(2)}, u32[]{:S(2)}) %collective-permute-start.83) | collective-permute-done | bytes 524320 | tf_op jit(solution)/shard_map/ppermute | solution.py:51
  519.1 3.0 collective-permute-done.81
  528.5 2.7 collective-permute-start.86
  535.9 17.6 %collective-permute-done.86 = bf16[256,1024]{1,0:T(8,128)(2,1)S(1)} collective-permute-done((bf16[256,1024]{1,0:T(8,128)(2,1)S(1)}, bf16[256,1024]{1,0:T(8,128)(2,1)S(1)}, u32[]{:S(2)}, u32[]{:S(2)}) %collective-permute-start.86) | collective-permute-done | bytes 524320 | tf_op jit(solution)/shard_map/ppermute | solution.py:51
  562.2 18.7 %collective-permute-done.87 = bf16[2,512,256]{2,1,0:T(8,128)(2,1)S(1)} collective-permute-done((bf16[2,512,256]{2,1,0:T(8,128)(2,1)S(1)}, bf16[2,512,256]{2,1,0:T(8,128)(2,1)S(1)}, u32[]{:S(2)}, u32[]{:S(2)}) %collective-permute-start.87) | collective-permute-done | bytes 524320 | tf_op jit(solution)/shard_map/ppermute | solution.py:51
  595.3 6.9 collective-permute-done.91
  602.1 6.8 collective-permute-done.94
  622.9 4.0 collective-permute-done.96
  626.9 6.4 collective-permute-done.99
  649.1 10.2 %collective-permute-done.102 = bf16[128,1024]{1,0:T(8,128)(2,1)S(1)} collective-permute-done((bf16[128,1024]{1,0:T(8,128)(2,1)S(1)}, bf16[128,1024]{1,0:T(8,128)(2,1)S(1)}, u32[]{:S(2)}, u32[]{:S(2)}) %collective-permute-start.102) | collective-permute-done | bytes 262176 | tf_op jit(solution)/shard_map/ppermute | solution.py:51
  672.8 9.0 %collective-permute-done.107 = bf16[1,256,512]{2,1,0:T(8,128)(2,1)} collective-permute-done((bf16[1,256,512]{2,1,0:T(8,128)(2,1)S(1)}, bf16[1,256,512]{2,1,0:T(8,128)(2,1)}, u32[]{:S(2)}, u32[]{:S(2)}) %collective-permute-start.107) | collective-permute-done | bytes 262176 | tf_op jit(solution)/shard_map/ppermute | solution.py:51
  684.4 2.6 fusion.20
  705.4 7.3 collective-permute-done.110
  714.7 3.2 collective-permute-start.114
  722.3 12.8 %collective-permute-done.112 = bf16[1,256,512]{2,1,0:T(8,128)(2,1)S(1)} collective-permute-done((bf16[1,256,512]{2,1,0:T(8,128)(2,1)S(1)}, bf16[1,256,512]{2,1,0:T(8,128)(2,1)S(1)}, u32[]{:S(2)}, u32[]{:S(2)}) %collective-permute-start.112) | collective-permute-done | bytes 262176 | tf_op jit(solution)/shard_map/ppermute | solution.py:51
  735.1 8.2 %collective-permute-done.113 = bf16[128,1024]{1,0:T(8,128)(2,1)S(1)} collective-permute-done((bf16[128,1024]{1,0:T(8,128)(2,1)S(1)}, bf16[128,1024]{1,0:T(8,128)(2,1)S(1)}, u32[]{:S(2)}, u32[]{:S(2)}) %collective-permute-start.113) | collective-permute-done | bytes 262176 | tf_op jit(solution)/shard_map/ppermute | solution.py:51
  754.1 3.7 collective-permute-done.117
  757.8 4.8 collective-permute-done.118
  762.6 10.7 %collective-permute-done.119 = bf16[256,1024]{1,0:T(8,128)(2,1)S(1)} collective-permute-done((bf16[256,1024]{1,0:T(8,128)(2,1)S(1)}, bf16[256,1024]{1,0:T(8,128)(2,1)S(1)}, u32[]{:S(2)}, u32[]{:S(2)}) %collective-permute-start.119) | collective-permute-done | bytes 524320 | tf_op jit(solution)/shard_map/ppermute | solution.py:51
  (756 shorter events, 350.7 us)
Async XLA Ops:
  8.0 17.1 %collective-permute-start = (bf16[64,1536]{1,0:T(8,128)(2,1)}, bf16[64,1536]{1,0:T(8,128)(2,1)}, u32[]{:S(2)}, u32[]{:S(2)}) collective-permute-start(bf16[64,1536]{1,0:T(8,128)(2,1)} %pad_maximum_fusion.21), channel_id=1, source_target_pairs={{0,8},{1,9},{2,10},{3,11},{4,12},{5,13},{6,14},{7,15},{8,0},{9,1},... | collective-permute-start | bytes 589832 | tf_op jit(solution)/shard_map/ppermute | solution.py:51
  29.5 26.1 %collective-permute-start.5 = (bf16[256,1024]{1,0:T(8,128)(2,1)}, bf16[256,1024]{1,0:T(8,128)(2,1)}, u32[]{:S(2)}, u32[]{:S(2)}) collective-permute-start(bf16[256,1024]{1,0:T(8,128)(2,1)} %get-tuple-element.253), channel_id=1, source_target_pairs={{0,4},{1,5},{2,6},{3,7},{4,0},{5,1},{6,2},{7,3},{8,12},{9,13},{10,... | collective-permute-start | bytes 1572872 | tf_op jit(solution)/shard_map/ppermute | solution.py:51
  32.2 23.4 %collective-permute-start.6 = (bf16[256,1024]{1,0:T(8,128)(2,1)}, bf16[256,1024]{1,0:T(8,128)(2,1)}, u32[]{:S(2)}, u32[]{:S(2)}) collective-permute-start(bf16[256,1024]{1,0:T(8,128)(2,1)} %get-tuple-element.253), channel_id=1, source_target_pairs={{0,2},{1,3},{2,0},{3,1},{4,6},{5,7},{6,4},{7,5},{8,10},{9,11},{10,... | collective-permute-start | bytes 1572872 | tf_op jit(solution)/shard_map/ppermute | solution.py:51
  33.9 21.7 %collective-permute-start.7 = (bf16[256,1024]{1,0:T(8,128)(2,1)}, bf16[256,1024]{1,0:T(8,128)(2,1)}, u32[]{:S(2)}, u32[]{:S(2)}) collective-permute-start(bf16[256,1024]{1,0:T(8,128)(2,1)} %get-tuple-element.253), channel_id=1, source_target_pairs={{0,16},{1,17},{2,18},{3,19},{4,20},{5,21},{6,22},{7,23},{8,24},{9,... | collective-permute-start | bytes 1572872 | tf_op jit(solution)/shard_map/ppermute | solution.py:51
  35.4 20.2 %collective-permute-start.8 = (bf16[128,2048]{1,0:T(8,128)(2,1)S(1)}, bf16[128,2048]{1,0:T(8,128)(2,1)}, u32[]{:S(2)}, u32[]{:S(2)}) collective-permute-start(bf16[128,2048]{1,0:T(8,128)(2,1)S(1)} %reshape.616), channel_id=1, source_target_pairs={{0,1},{1,0},{2,3},{3,2},{4,5},{5,4},{6,7},{7,6},{8,9},{9,8},{10,11... | collective-permute-start | bytes 1572872 | tf_op jit(solution)/shard_map/ppermute | solution.py:51
  38.8 16.8 %collective-permute-start.9 = (bf16[2,32,64]{2,1,0:T(8,128)(2,1)S(1)}, bf16[2,32,64]{2,1,0:T(8,128)(2,1)S(1)}, u32[]{:S(2)}, u32[]{:S(2)}) collective-permute-start(bf16[2,32,64]{2,1,0:T(8,128)(2,1)S(1)} %add.471), channel_id=1, source_target_pairs={{0,2},{1,3},{2,0},{3,1},{4,6},{5,7},{6,4},{7,5},{8,10},{9,11},{10,... | collective-permute-start | bytes 24584 | tf_op jit(solution)/shard_map/ppermute | solution.py:51
  57.4 23.0 %collective-permute-start.11 = (bf16[256,1024]{1,0:T(8,128)(2,1)}, bf16[256,1024]{1,0:T(8,128)(2,1)}, u32[]{:S(2)}, u32[]{:S(2)}) collective-permute-start(bf16[256,1024]{1,0:T(8,128)(2,1)} %collective-permute-done.5), channel_id=1, source_target_pairs={{0,2},{1,3},{2,0},{3,1},{4,6},{5,7},{6,4},{7,5},{8,10},{9,11},{10,... | collective-permute-start | bytes 1572872 | tf_op jit(solution)/shard_map/ppermute | solution.py:51
  58.8 21.6 %collective-permute-start.12 = (bf16[256,1024]{1,0:T(8,128)(2,1)}, bf16[256,1024]{1,0:T(8,128)(2,1)}, u32[]{:S(2)}, u32[]{:S(2)}) collective-permute-start(bf16[256,1024]{1,0:T(8,128)(2,1)} %collective-permute-done.5), channel_id=1, source_target_pairs={{0,16},{1,17},{2,18},{3,19},{4,20},{5,21},{6,22},{7,23},{8,24},{9,... | collective-permute-start | bytes 1572872 | tf_op jit(solution)/shard_map/ppermute | solution.py:51
  59.3 25.0 %collective-permute-start.13 = (bf16[256,1024]{1,0:T(8,128)(2,1)}, bf16[256,1024]{1,0:T(8,128)(2,1)}, u32[]{:S(2)}, u32[]{:S(2)}) collective-permute-start(bf16[256,1024]{1,0:T(8,128)(2,1)} %get-tuple-element.282), channel_id=1, source_target_pairs={{0,4},{1,5},{2,6},{3,7},{4,0},{5,1},{6,2},{7,3},{8,12},{9,13},{10,... | collective-permute-start | bytes 1572872 | tf_op jit(solution)/shard_map/ppermute | solution.py:51
  104.0 20.3 %collective-permute-start.21 = (bf16[256,1024]{1,0:T(8,128)(2,1)}, bf16[256,1024]{1,0:T(8,128)(2,1)}, u32[]{:S(2)}, u32[]{:S(2)}) collective-permute-start(bf16[256,1024]{1,0:T(8,128)(2,1)} %constant_dynamic-slice_fusion), channel_id=1, source_target_pairs={{0,2},{1,3},{2,0},{3,1},{4,6},{5,7},{6,4},{7,5},{8,10},{9,11},{10,... | collective-permute-start | bytes 1572872 | tf_op jit(solution)/shard_map/ppermute | solution.py:51
  104.3 20.0 %collective-permute-start.22 = (bf16[256,1024]{1,0:T(8,128)(2,1)}, bf16[256,1024]{1,0:T(8,128)(2,1)}, u32[]{:S(2)}, u32[]{:S(2)}) collective-permute-start(bf16[256,1024]{1,0:T(8,128)(2,1)} %get-tuple-element.282), channel_id=1, source_target_pairs={{0,1},{1,0},{2,3},{3,2},{4,5},{5,4},{6,7},{7,6},{8,9},{9,8},{10,11... | collective-permute-start | bytes 1572872 | tf_op jit(solution)/shard_map/ppermute | solution.py:51
  127.4 26.0 %collective-permute-start.25 = (bf16[512,512]{1,0:T(8,128)(2,1)}, bf16[512,512]{1,0:T(8,128)(2,1)}, u32[]{:S(2)}, u32[]{:S(2)}) collective-permute-start(bf16[512,512]{1,0:T(8,128)(2,1)} %get-tuple-element.292), channel_id=1, source_target_pairs={{0,4},{1,5},{2,6},{3,7},{4,0},{5,1},{6,2},{7,3},{8,12},{9,13},{10,... | collective-permute-start | bytes 1572872 | tf_op jit(solution)/shard_map/ppermute | solution.py:51
  128.5 24.9 %collective-permute-start.26 = (bf16[512,512]{1,0:T(8,128)(2,1)}, bf16[512,512]{1,0:T(8,128)(2,1)}, u32[]{:S(2)}, u32[]{:S(2)}) collective-permute-start(bf16[512,512]{1,0:T(8,128)(2,1)} %get-tuple-element.292), channel_id=1, source_target_pairs={{0,2},{1,3},{2,0},{3,1},{4,6},{5,7},{6,4},{7,5},{8,10},{9,11},{10,... | collective-permute-start | bytes 1572872 | tf_op jit(solution)/shard_map/ppermute | solution.py:51
  130.3 23.1 %collective-permute-start.27 = (bf16[512,512]{1,0:T(8,128)(2,1)}, bf16[512,512]{1,0:T(8,128)(2,1)}, u32[]{:S(2)}, u32[]{:S(2)}) collective-permute-start(bf16[512,512]{1,0:T(8,128)(2,1)} %get-tuple-element.292), channel_id=1, source_target_pairs={{0,16},{1,17},{2,18},{3,19},{4,20},{5,21},{6,22},{7,23},{8,24},{9,... | collective-permute-start | bytes 1572872 | tf_op jit(solution)/shard_map/ppermute | solution.py:51
  130.9 22.5 %collective-permute-start.28 = (bf16[256,1024]{1,0:T(8,128)(2,1)S(1)}, bf16[256,1024]{1,0:T(8,128)(2,1)}, u32[]{:S(2)}, u32[]{:S(2)}) collective-permute-start(bf16[256,1024]{1,0:T(8,128)(2,1)S(1)} %copy-done.37), channel_id=1, source_target_pairs={{0,1},{1,0},{2,3},{3,2},{4,5},{5,4},{6,7},{7,6},{8,9},{9,8},{10,11... | collective-permute-start | bytes 1572872 | tf_op jit(solution)/shard_map/ppermute | solution.py:51
  132.4 22.5 %collective-permute-start.29 = (bf16[256,1024]{1,0:T(8,128)(2,1)S(1)}, bf16[256,1024]{1,0:T(8,128)(2,1)}, u32[]{:S(2)}, u32[]{:S(2)}) collective-permute-start(bf16[256,1024]{1,0:T(8,128)(2,1)S(1)} %copy-done.40), channel_id=1, source_target_pairs={{0,1},{1,0},{2,3},{3,2},{4,5},{5,4},{6,7},{7,6},{8,9},{9,8},{10,11... | collective-permute-start | bytes 1572872 | tf_op jit(solution)/shard_map/ppermute | solution.py:51
  156.4 21.0 %collective-permute-start.31 = (bf16[512,512]{1,0:T(8,128)(2,1)}, bf16[512,512]{1,0:T(8,128)(2,1)S(1)}, u32[]{:S(2)}, u32[]{:S(2)}) collective-permute-start(bf16[512,512]{1,0:T(8,128)(2,1)} %collective-permute-done.25), channel_id=1, source_target_pairs={{0,2},{1,3},{2,0},{3,1},{4,6},{5,7},{6,4},{7,5},{8,10},{9,11},{10,... | collective-permute-start | bytes 1572872 | tf_op jit(solution)/shard_map/ppermute | solution.py:51
  156.7 21.6 %collective-permute-start.32 = (bf16[512,512]{1,0:T(8,128)(2,1)}, bf16[512,512]{1,0:T(8,128)(2,1)S(1)}, u32[]{:S(2)}, u32[]{:S(2)}) collective-permute-start(bf16[512,512]{1,0:T(8,128)(2,1)} %collective-permute-done.25), channel_id=1, source_target_pairs={{0,16},{1,17},{2,18},{3,19},{4,20},{5,21},{6,22},{7,23},{8,24},{9,... | collective-permute-start | bytes 1572872 | tf_op jit(solution)/shard_map/ppermute | solution.py:51
  157.2 21.0 %collective-permute-start.33 = (bf16[256,1024]{1,0:T(8,128)(2,1)S(1)}, bf16[256,1024]{1,0:T(8,128)(2,1)S(1)}, u32[]{:S(2)}, u32[]{:S(2)}) collective-permute-start(bf16[256,1024]{1,0:T(8,128)(2,1)S(1)} %get-tuple-element.322), channel_id=1, source_target_pairs={{0,1},{1,0},{2,3},{3,2},{4,5},{5,4},{6,7},{7,6},{8,9},{9,8},{10,11... | collective-permute-start | bytes 1572872 | tf_op jit(solution)/shard_map/ppermute | solution.py:51
  158.7 23.6 %collective-permute-start.34 = (bf16[256,1024]{1,0:T(8,128)(2,1)S(1)}, bf16[256,1024]{1,0:T(8,128)(2,1)}, u32[]{:S(2)}, u32[]{:S(2)}) collective-permute-start(bf16[256,1024]{1,0:T(8,128)(2,1)S(1)} %copy-done.37), channel_id=1, source_target_pairs={{0,4},{1,5},{2,6},{3,7},{4,0},{5,1},{6,2},{7,3},{8,12},{9,13},{10,... | collective-permute-start | bytes 1572872 | tf_op jit(solution)/shard_map/ppermute | solution.py:51
  184.2 17.7 %collective-permute-start.36 = (bf16[2,256,512]{2,1,0:T(8,128)(2,1)S(1)}, bf16[2,256,512]{2,1,0:T(8,128)(2,1)S(1)}, u32[]{:S(2)}, u32[]{:S(2)}) collective-permute-start(bf16[2,256,512]{2,1,0:T(8,128)(2,1)S(1)} %pad_maximum_fusion.14), channel_id=1, source_target_pairs={{0,2},{1,3},{2,0},{3,1},{4,6},{5,7},{6,4},{7,5},{8,10},{9,11},{10,... | collective-permute-start | bytes 1572872 | tf_op jit(solution)/shard_map/ppermute | solution.py:51
  184.2 20.2 %collective-permute-start.37 = (bf16[256,1024]{1,0:T(8,128)(2,1)S(1)}, bf16[256,1024]{1,0:T(8,128)(2,1)S(1)}, u32[]{:S(2)}, u32[]{:S(2)}) collective-permute-start(bf16[256,1024]{1,0:T(8,128)(2,1)S(1)} %copy-done.41), channel_id=1, source_target_pairs={{0,4},{1,5},{2,6},{3,7},{4,0},{5,1},{6,2},{7,3},{8,12},{9,13},{10,... | collective-permute-start | bytes 1572872 | tf_op jit(solution)/shard_map/ppermute | solution.py:51
  186.9 17.6 %collective-permute-start.38 = (bf16[256,1024]{1,0:T(8,128)(2,1)S(1)}, bf16[256,1024]{1,0:T(8,128)(2,1)S(1)}, u32[]{:S(2)}, u32[]{:S(2)}) collective-permute-start(bf16[256,1024]{1,0:T(8,128)(2,1)S(1)} %get-tuple-element.313), channel_id=1, source_target_pairs={{0,1},{1,0},{2,3},{3,2},{4,5},{5,4},{6,7},{7,6},{8,9},{9,8},{10,11... | collective-permute-start | bytes 1572872 | tf_op jit(solution)/shard_map/ppermute | solution.py:51
  186.9 17.6 %collective-permute-start.39 = (bf16[256,1024]{1,0:T(8,128)(2,1)S(1)}, bf16[256,1024]{1,0:T(8,128)(2,1)S(1)}, u32[]{:S(2)}, u32[]{:S(2)}) collective-permute-start(bf16[256,1024]{1,0:T(8,128)(2,1)S(1)} %get-tuple-element.314), channel_id=1, source_target_pairs={{0,1},{1,0},{2,3},{3,2},{4,5},{5,4},{6,7},{7,6},{8,9},{9,8},{10,11... | collective-permute-start | bytes 1572872 | tf_op jit(solution)/shard_map/ppermute | solution.py:51
  205.7 27.0 %collective-permute-start.40 = (bf16[4,256,512]{2,1,0:T(8,128)(2,1)}, bf16[4,256,512]{2,1,0:T(8,128)(2,1)}, u32[]{:S(2)}, u32[]{:S(2)}) collective-permute-start(bf16[4,256,512]{2,1,0:T(8,128)(2,1)} %pad_maximum_fusion.6), channel_id=1, source_target_pairs={{0,16},{1,17},{2,18},{3,19},{4,20},{5,21},{6,22},{7,23},{8,24},{9,... | collective-permute-start | bytes 3145736 | tf_op jit(solution)/shard_map/ppermute | solution.py:51
  208.4 22.0 %collective-permute-start.41 = (bf16[256,1024]{1,0:T(8,128)(2,1)S(1)}, bf16[256,1024]{1,0:T(8,128)(2,1)}, u32[]{:S(2)}, u32[]{:S(2)}) collective-permute-start(bf16[256,1024]{1,0:T(8,128)(2,1)S(1)} %copy-done.39), channel_id=1, source_target_pairs={{0,4},{1,5},{2,6},{3,7},{4,0},{5,1},{6,2},{7,3},{8,12},{9,13},{10,... | collective-permute-start | bytes 1572872 | tf_op jit(solution)/shard_map/ppermute | solution.py:51
  208.9 21.5 %collective-permute-start.42 = (bf16[256,1024]{1,0:T(8,128)(2,1)}, bf16[256,1024]{1,0:T(8,128)(2,1)}, u32[]{:S(2)}, u32[]{:S(2)}) collective-permute-start(bf16[256,1024]{1,0:T(8,128)(2,1)} %collective-permute-done.13), channel_id=1, source_target_pairs={{0,1},{1,0},{2,3},{3,2},{4,5},{5,4},{6,7},{7,6},{8,9},{9,8},{10,11... | collective-permute-start | bytes 1572872 | tf_op jit(solution)/shard_map/ppermute | solution.py:51
  210.5 20.9 %collective-permute-start.43 = (bf16[256,1024]{1,0:T(8,128)(2,1)}, bf16[256,1024]{1,0:T(8,128)(2,1)}, u32[]{:S(2)}, u32[]{:S(2)}) collective-permute-start(bf16[256,1024]{1,0:T(8,128)(2,1)} %collective-permute-done.34), channel_id=1, source_target_pairs={{0,1},{1,0},{2,3},{3,2},{4,5},{5,4},{6,7},{7,6},{8,9},{9,8},{10,11... | collective-permute-start | bytes 1572872 | tf_op jit(solution)/shard_map/ppermute | solution.py:51
  210.9 21.8 %collective-permute-start.44 = (bf16[128,2048]{1,0:T(8,128)(2,1)S(1)}, bf16[128,2048]{1,0:T(8,128)(2,1)}, u32[]{:S(2)}, u32[]{:S(2)}) collective-permute-start(bf16[128,2048]{1,0:T(8,128)(2,1)S(1)} %reshape.620), channel_id=1, source_target_pairs={{0,2},{1,3},{2,0},{3,1},{4,6},{5,7},{6,4},{7,5},{8,10},{9,11},{10,... | collective-permute-start | bytes 1572872 | tf_op jit(solution)/shard_map/ppermute | solution.py:51
  238.9 22.9 %collective-permute-start.45 = (bf16[128,2048]{1,0:T(8,128)(2,1)S(1)}, bf16[128,2048]{1,0:T(8,128)(2,1)S(1)}, u32[]{:S(2)}, u32[]{:S(2)}) collective-permute-start(bf16[128,2048]{1,0:T(8,128)(2,1)S(1)} %copy-done.84), channel_id=1, source_target_pairs={{0,8},{1,9},{2,10},{3,11},{4,12},{5,13},{6,14},{7,15},{8,0},{9,1},... | collective-permute-start | bytes 1572872 | tf_op jit(solution)/shard_map/ppermute | solution.py:51
  241.0 20.8 %collective-permute-start.47 = (bf16[128,2048]{1,0:T(8,128)(2,1)S(1)}, bf16[128,2048]{1,0:T(8,128)(2,1)S(1)}, u32[]{:S(2)}, u32[]{:S(2)}) collective-permute-start(bf16[128,2048]{1,0:T(8,128)(2,1)S(1)} %fusion.25), channel_id=1, source_target_pairs={{0,1},{1,0},{2,3},{3,2},{4,5},{5,4},{6,7},{7,6},{8,9},{9,8},{10,11... | collective-permute-start | bytes 1572872 | tf_op jit(solution)/shard_map/ppermute | solution.py:51
  243.0 18.9 %collective-permute-start.48 = (bf16[128,2048]{1,0:T(8,128)(2,1)}, bf16[128,2048]{1,0:T(8,128)(2,1)S(1)}, u32[]{:S(2)}, u32[]{:S(2)}) collective-permute-start(bf16[128,2048]{1,0:T(8,128)(2,1)} %collective-permute-done.44), channel_id=1, source_target_pairs={{0,16},{1,17},{2,18},{3,19},{4,20},{5,21},{6,22},{7,23},{8,24},{9,... | collective-permute-start | bytes 1572872 | tf_op jit(solution)/shard_map/ppermute | solution.py:51
  269.5 19.7 %collective-permute-start.52 = (bf16[256,1024]{1,0:T(8,128)(2,1)}, bf16[256,1024]{1,0:T(8,128)(2,1)S(1)}, u32[]{:S(2)}, u32[]{:S(2)}) collective-permute-start(bf16[256,1024]{1,0:T(8,128)(2,1)} %copy-done.74), channel_id=1, source_target_pairs={{0,1},{1,0},{2,3},{3,2},{4,5},{5,4},{6,7},{7,6},{8,9},{9,8},{10,11... | collective-permute-start | bytes 1572872 | tf_op jit(solution)/shard_map/ppermute | solution.py:51
  292.0 59.2 %collective-permute-start.67 = (bf16[512,2048]{1,0:T(8,128)(2,1)}, bf16[512,2048]{1,0:T(8,128)(2,1)S(1)}, u32[]{:S(2)}, u32[]{:S(2)}) collective-permute-start(bf16[512,2048]{1,0:T(8,128)(2,1)} %pad_maximum_fusion.2), channel_id=1, source_target_pairs={{0,8},{1,9},{2,10},{3,11},{4,12},{5,13},{6,14},{7,15},{8,0},{9,1},... | collective-permute-start | bytes 6291464 | tf_op jit(solution)/shard_map/ppermute | solution.py:51
  312.4 18.6 %collective-permute-start.60 = (bf16[256,1024]{1,0:T(8,128)(2,1)}, bf16[256,1024]{1,0:T(8,128)(2,1)}, u32[]{:S(2)}, u32[]{:S(2)}) collective-permute-start(bf16[256,1024]{1,0:T(8,128)(2,1)} %collective-permute-done.41), channel_id=1, source_target_pairs={{0,1},{1,0},{2,3},{3,2},{4,5},{5,4},{6,7},{7,6},{8,9},{9,8},{10,11... | collective-permute-start | bytes 1572872 | tf_op jit(solution)/shard_map/ppermute | solution.py:51
  321.5 36.2 %collective-permute-start.59 = (bf16[512,2048]{1,0:T(8,128)(2,1)}, bf16[512,2048]{1,0:T(8,128)(2,1)}, u32[]{:S(2)}, u32[]{:S(2)}) collective-permute-start(bf16[512,2048]{1,0:T(8,128)(2,1)} %assemble.2.refs_0_), channel_id=1, source_target_pairs={{0,8},{1,9},{2,10},{3,11},{4,12},{5,13},{6,14},{7,15},{8,0},{9,1},... | collective-permute-start | bytes 6291464 | tf_op jit(solution)/shard_map/ppermute | solution.py:51
  399.5 27.0 %collective-permute-start.66 = (bf16[2,2,128,2048]{3,2,1,0:T(8,128)(2,1)}, bf16[2,2,128,2048]{3,2,1,0:T(8,128)(2,1)S(1)}, u32[]{:S(2)}, u32[]{:S(2)}) collective-permute-start(bf16[2,2,128,2048]{3,2,1,0:T(8,128)(2,1)} %bitcast.37), channel_id=1, source_target_pairs={{0,8},{1,9},{2,10},{3,11},{4,12},{5,13},{6,14},{7,15},{8,0},{9,1},... | collective-permute-start | bytes 6291464 | tf_op jit(solution)/shard_map/ppermute | solution.py:51
  490.7 31.3 %collective-permute-start.81 = (bf16[4,256,640]{2,1,0:T(8,128)(2,1)}, bf16[4,256,640]{2,1,0:T(8,128)(2,1)}, u32[]{:S(2)}, u32[]{:S(2)}) collective-permute-start(bf16[4,256,640]{2,1,0:T(8,128)(2,1)} %bitcast.58), channel_id=1, source_target_pairs={{0,16},{1,17},{2,18},{3,19},{4,20},{5,21},{6,22},{7,23},{8,24},{9,... | collective-permute-start | bytes 3932168 | tf_op jit(solution)/shard_map/ppermute | solution.py:51
  491.4 27.7 %collective-permute-start.82 = (bf16[512,1024]{1,0:T(8,128)(2,1)}, bf16[512,1024]{1,0:T(8,128)(2,1)}, u32[]{:S(2)}, u32[]{:S(2)}) collective-permute-start(bf16[512,1024]{1,0:T(8,128)(2,1)} %get-tuple-element.395), channel_id=1, source_target_pairs={{0,1},{1,0},{2,3},{3,2},{4,5},{5,4},{6,7},{7,6},{8,9},{9,8},{10,11... | collective-permute-start | bytes 3145736 | tf_op jit(solution)/shard_map/ppermute | solution.py:51
  493.0 26.1 %collective-permute-start.83 = (bf16[256,1024]{1,0:T(8,128)(2,1)}, bf16[256,1024]{1,0:T(8,128)(2,1)}, u32[]{:S(2)}, u32[]{:S(2)}) collective-permute-start(bf16[256,1024]{1,0:T(8,128)(2,1)} %slice.543), channel_id=1, source_target_pairs={{0,4},{1,5},{2,6},{3,7},{4,0},{5,1},{6,2},{7,3},{8,12},{9,13},{10,... | collective-permute-start | bytes 1572872 | tf_op jit(solution)/shard_map/ppermute | solution.py:51
  525.8 27.7 %collective-permute-start.84 = (bf16[4,512,256]{2,1,0:T(8,128)(2,1)S(1)}, bf16[4,512,256]{2,1,0:T(8,128)(2,1)S(1)}, u32[]{:S(2)}, u32[]{:S(2)}) collective-permute-start(bf16[4,512,256]{2,1,0:T(8,128)(2,1)S(1)} %bitcast.284), channel_id=1, source_target_pairs={{0,16},{1,17},{2,18},{3,19},{4,20},{5,21},{6,22},{7,23},{8,24},{9,... | collective-permute-start | bytes 3145736 | tf_op jit(solution)/shard_map/ppermute | solution.py:51
  526.5 27.0 %collective-permute-start.85 = (bf16[512,1024]{1,0:T(8,128)(2,1)S(1)}, bf16[512,1024]{1,0:T(8,128)(2,1)S(1)}, u32[]{:S(2)}, u32[]{:S(2)}) collective-permute-start(bf16[512,1024]{1,0:T(8,128)(2,1)S(1)} %copy-done.51), channel_id=1, source_target_pairs={{0,1},{1,0},{2,3},{3,2},{4,5},{5,4},{6,7},{7,6},{8,9},{9,8},{10,11... | collective-permute-start | bytes 3145736 | tf_op jit(solution)/shard_map/ppermute | solution.py:51
  528.5 25.0 %collective-permute-start.86 = (bf16[256,1024]{1,0:T(8,128)(2,1)S(1)}, bf16[256,1024]{1,0:T(8,128)(2,1)S(1)}, u32[]{:S(2)}, u32[]{:S(2)}) collective-permute-start(bf16[256,1024]{1,0:T(8,128)(2,1)S(1)} %get-tuple-element.403), channel_id=1, source_target_pairs={{0,4},{1,5},{2,6},{3,7},{4,0},{5,1},{6,2},{7,3},{8,12},{9,13},{10,... | collective-permute-start | bytes 1572872 | tf_op jit(solution)/shard_map/ppermute | solution.py:51
  553.9 28.7 %collective-permute-start.88 = (bf16[4,512,256]{2,1,0:T(8,128)(2,1)S(1)}, bf16[4,512,256]{2,1,0:T(8,128)(2,1)S(1)}, u32[]{:S(2)}, u32[]{:S(2)}) collective-permute-start(bf16[4,512,256]{2,1,0:T(8,128)(2,1)S(1)} %bitcast.283), channel_id=1, source_target_pairs={{0,16},{1,17},{2,18},{3,19},{4,20},{5,21},{6,22},{7,23},{8,24},{9,... | collective-permute-start | bytes 3145736 | tf_op jit(solution)/shard_map/ppermute | solution.py:51
  555.3 27.3 %collective-permute-start.89 = (bf16[512,1024]{1,0:T(8,128)(2,1)S(1)}, bf16[512,1024]{1,0:T(8,128)(2,1)S(1)}, u32[]{:S(2)}, u32[]{:S(2)}) collective-permute-start(bf16[512,1024]{1,0:T(8,128)(2,1)S(1)} %copy-done.50), channel_id=1, source_target_pairs={{0,1},{1,0},{2,3},{3,2},{4,5},{5,4},{6,7},{7,6},{8,9},{9,8},{10,11... | collective-permute-start | bytes 3145736 | tf_op jit(solution)/shard_map/ppermute | solution.py:51
  558.3 22.6 %collective-permute-start.87 = (bf16[2,512,256]{2,1,0:T(8,128)(2,1)S(1)}, bf16[2,512,256]{2,1,0:T(8,128)(2,1)S(1)}, u32[]{:S(2)}, u32[]{:S(2)}) collective-permute-start(bf16[2,512,256]{2,1,0:T(8,128)(2,1)S(1)} %slice.547), channel_id=1, source_target_pairs={{0,2},{1,3},{2,0},{3,1},{4,6},{5,7},{6,4},{7,5},{8,10},{9,11},{10,... | collective-permute-start | bytes 1572872 | tf_op jit(solution)/shard_map/ppermute | solution.py:51
  558.8 23.7 %collective-permute-start.90 = (bf16[256,1024]{1,0:T(8,128)(2,1)S(1)}, bf16[256,1024]{1,0:T(8,128)(2,1)S(1)}, u32[]{:S(2)}, u32[]{:S(2)}) collective-permute-start(bf16[256,1024]{1,0:T(8,128)(2,1)S(1)} %get-tuple-element.410), channel_id=1, source_target_pairs={{0,4},{1,5},{2,6},{3,7},{4,0},{5,1},{6,2},{7,3},{8,12},{9,13},{10,... | collective-permute-start | bytes 1572872 | tf_op jit(solution)/shard_map/ppermute | solution.py:51
  583.1 28.2 %collective-permute-start.93 = (bf16[4,256,512]{2,1,0:T(8,128)(2,1)S(1)}, bf16[4,256,512]{2,1,0:T(8,128)(2,1)S(1)}, u32[]{:S(2)}, u32[]{:S(2)}) collective-permute-start(bf16[4,256,512]{2,1,0:T(8,128)(2,1)S(1)} %bitcast.282), channel_id=1, source_target_pairs={{0,16},{1,17},{2,18},{3,19},{4,20},{5,21},{6,22},{7,23},{8,24},{9,... | collective-permute-start | bytes 3145736 | tf_op jit(solution)/shard_map/ppermute | solution.py:51
  584.0 27.3 %collective-permute-start.95 = (bf16[512,1024]{1,0:T(8,128)(2,1)S(1)}, bf16[512,1024]{1,0:T(8,128)(2,1)S(1)}, u32[]{:S(2)}, u32[]{:S(2)}) collective-permute-start(bf16[512,1024]{1,0:T(8,128)(2,1)S(1)} %copy-done.61), channel_id=1, source_target_pairs={{0,1},{1,0},{2,3},{3,2},{4,5},{5,4},{6,7},{7,6},{8,9},{9,8},{10,11... | collective-permute-start | bytes 3145736 | tf_op jit(solution)/shard_map/ppermute | solution.py:51
  589.4 21.9 %collective-permute-start.92 = (bf16[2,512,256]{2,1,0:T(8,128)(2,1)S(1)}, bf16[2,512,256]{2,1,0:T(8,128)(2,1)S(1)}, u32[]{:S(2)}, u32[]{:S(2)}) collective-permute-start(bf16[2,512,256]{2,1,0:T(8,128)(2,1)S(1)} %slice.553), channel_id=1, source_target_pairs={{0,2},{1,3},{2,0},{3,1},{4,6},{5,7},{6,4},{7,5},{8,10},{9,11},{10,... | collective-permute-start | bytes 1572872 | tf_op jit(solution)/shard_map/ppermute | solution.py:51
  591.8 17.1 %collective-permute-start.94 = (bf16[128,1024]{1,0:T(8,128)(2,1)S(1)}, bf16[128,1024]{1,0:T(8,128)(2,1)S(1)}, u32[]{:S(2)}, u32[]{:S(2)}) collective-permute-start(bf16[128,1024]{1,0:T(8,128)(2,1)S(1)} %get-tuple-element.420), channel_id=1, source_target_pairs={{0,4},{1,5},{2,6},{3,7},{4,0},{5,1},{6,2},{7,3},{8,12},{9,13},{10,... | collective-permute-start | bytes 786440 | tf_op jit(solution)/shard_map/ppermute | solution.py:51
  614.9 20.5 %collective-permute-start.97 = (bf16[2,256,512]{2,1,0:T(8,128)(2,1)S(1)}, bf16[2,256,512]{2,1,0:T(8,128)(2,1)S(1)}, u32[]{:S(2)}, u32[]{:S(2)}) collective-permute-start(bf16[2,256,512]{2,1,0:T(8,128)(2,1)S(1)} %slice.564), channel_id=1, source_target_pairs={{0,2},{1,3},{2,0},{3,1},{4,6},{5,7},{6,4},{7,5},{8,10},{9,11},{10,... | collective-permute-start | bytes 1572872 | tf_op jit(solution)/shard_map/ppermute | solution.py:51
  616.5 18.8 %collective-permute-start.98 = (bf16[256,1024]{1,0:T(8,128)(2,1)S(1)}, bf16[256,1024]{1,0:T(8,128)(2,1)S(1)}, u32[]{:S(2)}, u32[]{:S(2)}) collective-permute-start(bf16[256,1024]{1,0:T(8,128)(2,1)S(1)} %get-tuple-element.429), channel_id=1, source_target_pairs={{0,1},{1,0},{2,3},{3,2},{4,5},{5,4},{6,7},{7,6},{8,9},{9,8},{10,11... | collective-permute-start | bytes 1572872 | tf_op jit(solution)/shard_map/ppermute | solution.py:51
  617.7 17.6 %collective-permute-start.100 = (bf16[128,2048]{1,0:T(8,128)(2,1)S(1)}, bf16[128,2048]{1,0:T(8,128)(2,1)S(1)}, u32[]{:S(2)}, u32[]{:S(2)}) collective-permute-start(bf16[128,2048]{1,0:T(8,128)(2,1)S(1)} %copy-done.80), channel_id=1, source_target_pairs={{0,16},{1,17},{2,18},{3,19},{4,20},{5,21},{6,22},{7,23},{8,24},{9,... | collective-permute-start | bytes 1572872 | tf_op jit(solution)/shard_map/ppermute | solution.py:51
  639.4 20.5 %collective-permute-start.104 = (bf16[128,2048]{1,0:T(8,128)(2,1)S(1)}, bf16[128,2048]{1,0:T(8,128)(2,1)S(1)}, u32[]{:S(2)}, u32[]{:S(2)}) collective-permute-start(bf16[128,2048]{1,0:T(8,128)(2,1)S(1)} %get-tuple-element.513), channel_id=1, source_target_pairs={{0,8},{1,9},{2,10},{3,11},{4,12},{5,13},{6,14},{7,15},{8,0},{9,1},... | collective-permute-start | bytes 1572872 | tf_op jit(solution)/shard_map/ppermute | solution.py:51
  641.4 18.6 %collective-permute-start.101 = (bf16[128,2048]{1,0:T(8,128)(2,1)S(1)}, bf16[128,2048]{1,0:T(8,128)(2,1)S(1)}, u32[]{:S(2)}, u32[]{:S(2)}) collective-permute-start(bf16[128,2048]{1,0:T(8,128)(2,1)S(1)} %fusion.21), channel_id=1, source_target_pairs={{0,2},{1,3},{2,0},{3,1},{4,6},{5,7},{6,4},{7,5},{8,10},{9,11},{10,... | collective-permute-start | bytes 1572872 | tf_op jit(solution)/shard_map/ppermute | solution.py:51
  645.1 39.3 %collective-permute-start.103 = (bf16[128,2048]{1,0:T(8,128)(2,1)}, bf16[128,2048]{1,0:T(8,128)(2,1)}, u32[]{:S(2)}, u32[]{:S(2)}) collective-permute-start(bf16[128,2048]{1,0:T(8,128)(2,1)} %get-tuple-element.512), channel_id=1, source_target_pairs={{0,8},{1,9},{2,10},{3,11},{4,12},{5,13},{6,14},{7,15},{8,0},{9,1},... | collective-permute-start | bytes 1572872 | tf_op jit(solution)/shard_map/ppermute | solution.py:51
  660.9 23.5 %collective-permute-start.106 = (bf16[4,256,512]{2,1,0:T(8,128)(2,1)}, bf16[4,256,512]{2,1,0:T(8,128)(2,1)}, u32[]{:S(2)}, u32[]{:S(2)}) collective-permute-start(bf16[4,256,512]{2,1,0:T(8,128)(2,1)} %bitcast.74), channel_id=1, source_target_pairs={{0,16},{1,17},{2,18},{3,19},{4,20},{5,21},{6,22},{7,23},{8,24},{9,... | collective-permute-start | bytes 3145736 | tf_op jit(solution)/shard_map/ppermute | solution.py:51
  662.2 20.5 %collective-permute-start.108 = (bf16[2,256,640]{2,1,0:T(8,128)(2,1)}, bf16[2,256,640]{2,1,0:T(8,128)(2,1)}, u32[]{:S(2)}, u32[]{:S(2)}) collective-permute-start(bf16[2,256,640]{2,1,0:T(8,128)(2,1)} %slice.580), channel_id=1, source_target_pairs={{0,2},{1,3},{2,0},{3,1},{4,6},{5,7},{6,4},{7,5},{8,10},{9,11},{10,... | collective-permute-start | bytes 1966088 | tf_op jit(solution)/shard_map/ppermute | solution.py:51
  665.1 16.7 %collective-permute-start.105 = (bf16[128,2048]{1,0:T(8,128)(2,1)}, bf16[128,2048]{1,0:T(8,128)(2,1)}, u32[]{:S(2)}, u32[]{:S(2)}) collective-permute-start(bf16[128,2048]{1,0:T(8,128)(2,1)} %fusion.18), channel_id=1, source_target_pairs={{0,1},{1,0},{2,3},{3,2},{4,5},{5,4},{6,7},{7,6},{8,9},{9,8},{10,11... | collective-permute-start | bytes 1572872 | tf_op jit(solution)/shard_map/ppermute | solution.py:51
  694.8 18.5 %collective-permute-start.109 = (bf16[2,256,512]{2,1,0:T(8,128)(2,1)}, bf16[2,256,512]{2,1,0:T(8,128)(2,1)}, u32[]{:S(2)}, u32[]{:S(2)}) collective-permute-start(bf16[2,256,512]{2,1,0:T(8,128)(2,1)} %slice.584), channel_id=1, source_target_pairs={{0,2},{1,3},{2,0},{3,1},{4,6},{5,7},{6,4},{7,5},{8,10},{9,11},{10,... | collective-permute-start | bytes 1572872 | tf_op jit(solution)/shard_map/ppermute | solution.py:51
  714.7 28.5 %collective-permute-start.114 = (bf16[256,1024]{1,0:T(8,128)(2,1)}, bf16[256,1024]{1,0:T(8,128)(2,1)S(1)}, u32[]{:S(2)}, u32[]{:S(2)}) collective-permute-start(bf16[256,1024]{1,0:T(8,128)(2,1)} %fusion.33), channel_id=1, source_target_pairs={{0,2},{1,3},{2,0},{3,1},{4,6},{5,7},{6,4},{7,5},{8,10},{9,11},{10,... | collective-permute-start | bytes 1572872 | tf_op jit(solution)/shard_map/ppermute | solution.py:51
  721.1 22.1 %collective-permute-start.113 = (bf16[128,1024]{1,0:T(8,128)(2,1)S(1)}, bf16[128,1024]{1,0:T(8,128)(2,1)S(1)}, u32[]{:S(2)}, u32[]{:S(2)}) collective-permute-start(bf16[128,1024]{1,0:T(8,128)(2,1)S(1)} %copy-done.111), channel_id=1, source_target_pairs={{0,4},{1,5},{2,6},{3,7},{4,0},{5,1},{6,2},{7,3},{8,12},{9,13},{10,... | collective-permute-start | bytes 786440 | tf_op jit(solution)/shard_map/ppermute | solution.py:51
  747.9 25.4 %collective-permute-start.119 = (bf16[256,1024]{1,0:T(8,128)(2,1)S(1)}, bf16[256,1024]{1,0:T(8,128)(2,1)S(1)}, u32[]{:S(2)}, u32[]{:S(2)}) collective-permute-start(bf16[256,1024]{1,0:T(8,128)(2,1)S(1)} %fusion.35), channel_id=1, source_target_pairs={{0,2},{1,3},{2,0},{3,1},{4,6},{5,7},{6,4},{7,5},{8,10},{9,11},{10,... | collective-permute-start | bytes 1572872 | tf_op jit(solution)/shard_map/ppermute | solution.py:51
  (198 other events, 2895.2 us)

commit v4 on v3

--- a/solution.py
+++ b/solution.py
@@ -142,7 +142,10 @@
 
 
     def join(self, value):
-        return after(value, *(sent.value for sent in self.before))
+        value, *arrived = lax.optimization_barrier((value, *(sent.value for sent in self.before)))
+        for sent, one in zip(self.before, arrived):
+            sent.value = one
+        return value
 
 
 class Spread:
@@ -254,52 +257,83 @@
     def __init__(self, total, masks, turn):
         count = 1 << len(masks)
         blocks = total.reshape(count, -1, total.shape[1])
-        self.blocks = [blocks[i] for i in range(count)]
-        self.rows, self.turn = blocks.shape[1], turn
-        self.missing, self.tasks, self.sent_rows = [len(masks)] + [0] * (count - 1), {}, {}
+        self.rows, self.half = blocks.shape[1], blocks.shape[1] // 2
+        self.raw, self.halves = [blocks[i] for i in range(count)], {}
+        self.turn, self.turning = turn, None
+        self.missing = [[len(masks)] * 2] + [[0, 0] for _ in range(count - 1)]
+        self.tasks, self.sent_rows = {}, {}
         for stage, mask in enumerate(masks):
             half = count >> (stage + 1)
             self.tasks[mask] = [(block, half) for block in range(2 * half - 1, half - 1, -1)]
             for block in range(half, 2 * half):
-                self.missing[block] = stage
-        self.got, self.sents, self.turning = {}, [], None
+                self.missing[block] = [stage, stage]
+        self.got, self.sents = {}, []
+
+    def half_of(self, block, part):
+        if (block, part) not in self.halves:
+            first = part * self.half
+            self.halves[block, part] = self.raw[block][first : first + self.half]
+        return self.halves[block, part]
 
     def settle(self):
         waiting = []
-        for block, half, sent in self.sents:
+        for block, half, first, sent in self.sents:
             if sent.value is None:
-                waiting.append((block, half, sent))
+                waiting.append((block, half, first, sent))
                 continue
-            parts = self.got.setdefault(block, [])
-            parts.append(sent.value)
-            if sum(part.shape[0] for part in parts) == self.rows:
-                into = block - half
-                self.missing[into] -= 1
-                received = jnp.concatenate(parts, axis=0)
-                self.blocks[into] = add(self.blocks[into], received, BF16 if into else F32)
+            value = sent.value
+            while value.shape[0]:
+                part = first // self.half
+                rows = min(value.shape[0], (part + 1) * self.half - first)
+                parts = self.got.setdefault((block, part), [])
+                parts.append(value[:rows])
+                value, first = value[rows:], first + rows
+                if sum(one.shape[0] for one in parts) == self.half:
+                    into = block - half
+                    self.missing[into][part] -= 1
+                    received = jnp.concatenate(parts, axis=0) if len(parts) > 1 else parts[0]
+                    self.halves[into, part] = add(
+                        self.half_of(into, part), received, BF16 if into else F32
+                    )
         self.sents = waiting
 
-    def take(self, flow, mask, rows):
+    def ready(self, block):
+        if self.missing[block][0]:
+            return 0
+        return self.half if self.missing[block][1] else self.rows
+
+    def next(self, mask):
         self.settle()
         for block, half in self.tasks[mask]:
-            if self.missing[block]:
-                continue
-            first = self.sent_rows.get(block, 0)
-            piece = self.blocks[block][first : first + rows]
-            self.sent_rows[block] = first + piece.shape[0]
-            if self.sent_rows[block] == self.rows:
-                self.tasks[mask].remove((block, half))
-            self.sents.append((block, half, flow.send(piece, 0, mask)))
-            return True
-        return False
+            if self.ready(block) > self.sent_rows.get(block, 0):
+                return block, half
+        return None
+
+    def take(self, flow, mask, rows):
+        found = self.next(mask)
+        if found is None:
+            return False
+        block, half = found
+        first = self.sent_rows.get(block, 0)
+        if (block, 0) in self.halves or (block, 1) in self.halves:
+            part = first // self.half
+            start = first - part * self.half
+            piece = self.half_of(block, part)[start : start + rows]
+        else:
+            piece = self.raw[block][first : min(first + rows, self.ready(block))]
+        self.sent_rows[block] = first + piece.shape[0]
+        if self.sent_rows[block] == self.rows:
+            self.tasks[mask].remove(found)
+        self.sents.append((block, half, first, flow.send(piece, 0, mask)))
+        return True
 
     def take_turn(self, flow):
         self.settle()
-        if self.missing[0] or self.turning is not None:
+        if any(self.missing[0]) or self.turning is not None:
             return False
-        total = self.blocks[0].reshape(2, self.rows // 2, -1)
-        self.mine = lax.dynamic_index_in_dim(total, self.turn, 0, keepdims=False)
-        other = lax.dynamic_index_in_dim(total, 1 - self.turn, 0, keepdims=False)
+        parts = [self.half_of(0, part) for part in (0, 1)]
+        self.mine = jnp.where(self.turn == 0, parts[0], parts[1])
+        other = jnp.where(self.turn == 0, parts[1], parts[0])
         self.turning = flow.send(other.astype(BF16), 0, TURN)
         return True
 
@@ -845,15 +879,8 @@
     placed = four_rows([left, left_t.value, left_x.value, left_xt.value], 0)
     placed += four_rows([right, right_t.value, right_x.value, right_xt.value], half)
     mid_four = assemble([part for part, _ in placed], [where for _, where in placed])
-    early = [near(block_rows) for _ in range(2)] + [high(block_rows)]
-    flow.go()
-
     def eight(four):
         return stack_rows([four, swap(four, CORE, 0)])
-
-    mid_group = eight(mid_four)
-    cot_four = jnp.concatenate([cot_far, cot_t.value, cot_x.value, cot_xt.value], axis=0)
-    grad_group = jnp.concatenate([cot_four, swap(cot_four, CORE, 0)], axis=0)
 
     def weight_of(which):
         have = bulk.parts(which)
@@ -861,20 +888,25 @@
             [part for parts in in_fold_order(have, far_masks) for part in parts], axis=0
         )
 
+    cot_four = jnp.concatenate([cot_far, cot_t.value, cot_x.value, cot_xt.value], axis=0)
+    grad_group = jnp.concatenate([cot_four, swap(cot_four, CORE, 0)], axis=0)
     while bulk.left(None, 0):
         near(block_rows), high(block_rows)
         flow.go()
     down = weight_of(0)
+    near(block_rows), near(block_rows), high(block_rows)
+    flow.go()
+    mid_group = eight(mid_four)
     grad_hidden = flow.join(jnp.dot(grad_group, down, preferred_element_type=F32))
-    while bulk.left(1, 1):
-        near(block_rows), high(block_rows)
+    while bulk.left(None, 1):
+        near(block_rows), near(block_rows), high(block_rows)
         flow.go()
-    while True:
-        more = [near(block_rows) for _ in range(4)] + [high(block_rows)]
+    gate = weight_of(1)
+    while bulk.left(None, 2):
+        for _ in range(4):
+            near(block_rows)
+        high(block_rows)
         flow.go()
-        if not bulk.left(None, 2):
-            break
-    gate = weight_of(1)
     gate_lin = flow.join(jnp.dot(mid_group, gate, preferred_element_type=F32))
     up = weight_of(2)
     up_proj = jnp.dot(mid_group, up, preferred_element_type=F32)
@@ -891,16 +923,11 @@
         total = row_major(total.astype(BF16))
         return FfnFold(total, far_masks[::-1], turn)
 
-    down_fold = ffn_fold(grad_group, hidden_act)
-    ffn_folds = [down_fold]
+    ffn_folds = []
 
     def near(rows):
-        found = [
-            (-block, i)
-            for i, fold in enumerate(ffn_folds)
-            for block, _ in fold.tasks[1][:1]
-            if not fold.missing[block]
-        ]
+        found = [(fold.next(1), i) for i, fold in enumerate(ffn_folds)]
+        found = [(-block[0], i) for block, i in found if block is not None]
         return bool(found) and ffn_folds[min(found)[1]].take(flow, 1, rows)
 
     def high(rows):
@@ -909,26 +936,31 @@
             found = any(fold.take(flow, mask, rows) for fold in ffn_folds) or found
         return found
 
-    near(ff_rows)
-    flow.go()
     mid_partial = lax.dot_general(
         grad_gate_lin, gate, COLS, preferred_element_type=F32
     ) + lax.dot_general(grad_up_proj, up, COLS, preferred_element_type=F32)
-    mid_partial = flow.join(row_major(mid_partial.astype(BF16))).reshape(2, 2, 2, token_rows, width)
+    mid_partial = row_major(mid_partial.astype(BF16))
+    down_fold = ffn_fold(grad_group, after(hidden_act, mid_partial))
+    ffn_folds.append(down_fold)
+    mid_partial = mid_partial.reshape(2, 2, 2, token_rows, width)
     four = add(mid_partial[0], swap(mid_partial[1], CORE, 0), BF16)
     left, right = four[..., :half], four[..., half:]
     left_sent = flow.send(left[:, 1], 0, TURN)
     right_sent = flow.send(right[1], CROSS, 0)
     near(ff_rows)
     flow.go()
-    gate_fold = ffn_fold(mid_group, grad_gate_lin)
-    ffn_partial = lax.dot_general(hidden_act, down, COLS, preferred_element_type=F32)
+    gate_fold = ffn_fold(mid_group, after(grad_gate_lin, four))
+    first_step = left_sent.value
+    ffn_partial = lax.dot_general(
+        after(hidden_act, four), down, COLS, preferred_element_type=F32
+    )
     ffn_partial = row_major(ffn_partial.astype(BF16)).reshape(2, 2, 2, token_rows, width)
     out_four = add(ffn_partial[0], swap(ffn_partial[1], CORE, 0), BF16)
     left = add(left[:, 0], left_sent.value, BF16)
     right = add(right[0], right_sent.value, BF16)
     left_sent = flow.send(left[1], CROSS, 0)
     right_sent = flow.send(right[1], 0, TURN)
+    near(ff_rows)
     high(ff_rows // 2)
     flow.go()
     ffn_folds.append(gate_fold)
@@ -944,7 +976,7 @@
     high(ff_rows // 2)
     out_parts = [flow.send(out_four[1, 0], CROSS, 0)]
     flow.go()
-    up_fold = ffn_fold(mid_group, grad_up_proj)
+    up_fold = ffn_fold(mid_group, after(grad_up_proj, first_step))
     ffn_folds.append(up_fold)
     branch_group = jnp.concatenate(
         [grad_branch, swap(grad_branch, CORE, 0), branch_low.value, swap(branch_low.value, CORE, 0)],

time: 787 us -> 763 us (0.970)
  waiting for transfers between devices: 328 us -> 273 us
  other arithmetic: 77 us -> 88.7 us
  matrix products: 75.2 us -> 83.3 us
    ppermute x120, waiting for transfers between devices: 328 us -> 273 us  [swap(): return row_major(lax.ppermute(row_major(value), ('head', 'blk'), pairs))]
    dynamic_update_slice x0 -> x3, other arithmetic: none -> 7.87 us  [result(): out = lax.dynamic_update_slice(out, self.mine, (0, self.turn * cols))]
    convert_element_type x19 -> x20, other arithmetic: 14.1 us -> 21.5 us  [add(): return (a.astype(F32) + b.astype(F32)).astype(dtype)]
    unnamed x329 -> x331, local copies, waits for them, and re-layouts: 64.1 us -> 67.5 us
  transfers between devices with their start and end apart: 120 -> 120, of which waited for: 63 -> 54; matrix products, arithmetic and copies ran while one was open for 22% -> 27% of each run, Pallas kernels for 4% -> 4%
where the time goes in v4:
time: 763 us; the launch traced here: 750 us
  waiting for transfers between devices  273 us (36%)
  local copies, waits for them, and re-layouts  136 us (18%)
  starting transfers between devices  130 us (17%)
  other arithmetic  88.7 us (12%)
  matrix products  83.3 us (11%)
  Pallas kernels  36.3 us (5%)
    ppermute x120, waiting for transfers between devices, swap(): return row_major(lax.ppermute(row_major(value), ('head', 'blk'), pairs))  273 us
    ppermute x120, starting transfers between devices, swap(): return row_major(lax.ppermute(row_major(value), ('head', 'blk'), pairs))  130 us
    unnamed x331, local copies, waits for them, and re-layouts  67.5 us
    convert_element_type x20, other arithmetic, add(): return (a.astype(F32) + b.astype(F32)).astype(dtype)  21.5 us
    dot_general x3, matrix products, ffn_fold(): total = lax.dot_general(lhs, rhs, ROWS, preferred_element_type=F32)  17.4 us
    pallas_call x1, Pallas kernels, attend_back(): pl.pallas_call(functools.partial(backward_kernel, per_seq), grid_spec=plt...  15.6 us
  transfers between devices with their start and end apart: 120, of which 54 were waited for; matrix products, arithmetic and copies ran while one was open for 27% of the time, Pallas kernels for 4%

profile of v4, /device:TPU:0, one launch (start us, length us, event | category | flops | bytes accessed | tf_op | source)
XLA Modules:
  0.0 750.4 jit_solution(3924309850367399856)
XLA Ops:
  10.1 3.0 collective-permute-start.3
  29.3 2.6 collective-permute-start.5
  42.6 12.7 %collective-permute-done.9 = bf16[2,32,64]{2,1,0:T(8,128)(2,1)S(1)} collective-permute-done((bf16[2,32,64]{2,1,0:T(8,128)(2,1)S(1)}, bf16[2,32,64]{2,1,0:T(8,128)(2,1)S(1)}, u32[]{:S(2)}, u32[]{:S(2)}) %collective-permute-start.9) | collective-permute-done | bytes 8224 | tf_op jit(solution)/shard_map/ppermute | solution.py:51
  67.6 3.0 collective-permute-done.10
  70.6 9.5 %collective-permute-done.11 = bf16[256,1024]{1,0:T(8,128)(2,1)} collective-permute-done((bf16[256,1024]{1,0:T(8,128)(2,1)}, bf16[256,1024]{1,0:T(8,128)(2,1)}, u32[]{:S(2)}, u32[]{:S(2)}) %collective-permute-start.11) | collective-permute-done | bytes 524320 | tf_op jit(solution)/shard_map/ppermute | solution.py:51
  80.1 3.7 collective-permute-done.13
  96.0 4.0 collective-permute-done.18
  108.6 4.9 fusion.129
  113.6 5.0 collective-permute-done.23
  133.2 15.0 %collective-permute-done.25 = bf16[512,512]{1,0:T(8,128)(2,1)} collective-permute-done((bf16[512,512]{1,0:T(8,128)(2,1)}, bf16[512,512]{1,0:T(8,128)(2,1)}, u32[]{:S(2)}, u32[]{:S(2)}) %collective-permute-start.25) | collective-permute-done | bytes 524320 | tf_op jit(solution)/shard_map/ppermute | solution.py:51
  156.8 7.9 %collective-permute-done.30 = bf16[512,512]{1,0:T(8,128)(2,1)S(1)} collective-permute-done((bf16[512,512]{1,0:T(8,128)(2,1)}, bf16[512,512]{1,0:T(8,128)(2,1)S(1)}, u32[]{:S(2)}, u32[]{:S(2)}) %collective-permute-start.30) | collective-permute-done | bytes 524320 | tf_op jit(solution)/shard_map/ppermute | solution.py:51
  164.7 5.1 collective-permute-done.31
  169.9 3.1 collective-permute-done.32
  173.0 4.4 collective-permute-done.34
  177.8 2.9 collective-permute-start.37
  187.5 11.8 %collective-permute-done.36 = bf16[2,256,512]{2,1,0:T(8,128)(2,1)S(1)} collective-permute-done((bf16[2,256,512]{2,1,0:T(8,128)(2,1)S(1)}, bf16[2,256,512]{2,1,0:T(8,128)(2,1)S(1)}, u32[]{:S(2)}, u32[]{:S(2)}) %collective-permute-start.36) | collective-permute-done | bytes 524320 | tf_op jit(solution)/shard_map/ppermute | solution.py:51
  208.0 2.7 collective-permute-start.44
  212.8 13.6 %attend.1 = (bf16[512,512]{1,0:T(8,128)(2,1)}, f32[512,512]{1,0:T(8,128)}, f32[2,1,512]{2,1,0:T(1,128)}) custom-call(s32[2]{0:T(128)} %pad_add_fusion.place_ref, s32[8]{0:T(128)} %pair_ref.3, s32[4096]{0:T(1024)} %bitcast.274, bf16[512,512]{1,0:T(8,128)(2,1)} %maximum_multiply_fusion.q_ref, bf16[4096,512]{1,0:T(8,128)(2,1)} %copy-done.119, ...), custom_call_target="tpu_custom_call" | custom-call | flops 6000000000 | bytes 6000000 | tf_op jit(solution)/shard_map/attend/pallas_call | solution.py:495
  245.7 8.8 %collective-permute-done.49 = bf16[128,1024]{1,0:T(8,128)(2,1)} collective-permute-done((bf16[128,1024]{1,0:T(8,128)(2,1)S(1)}, bf16[128,1024]{1,0:T(8,128)(2,1)}, u32[]{:S(2)}, u32[]{:S(2)}) %collective-permute-start.49) | collective-permute-done | bytes 262176 | tf_op jit(solution)/shard_map/ppermute | solution.py:51
  271.5 3.0 collective-permute-start.53
  280.2 4.8 collective-permute-done.51.refs_5_
  299.2 4.7 collective-permute-done.56.refs_3_
  303.9 2.9 collective-permute-done.58
  312.5 2.9 assemble.2.refs_0_
  318.1 4.3 collective-permute-done.62
  323.9 8.5 %fusion.155 = f32[1024,1024]{1,0:T(8,128)} fusion(bf16[1024,2048]{1,0:T(8,128)(2,1)} %constant_dynamic-update-slice_fusion.16, bf16[2048,1024]{1,0:T(8,128)(2,1)S(1)} %copy-done.105), kind=kOutput, calls=%fused_computation.440 | convolution fusion | flops 4294967296 | bytes 12582912 | tf_op jit(solution)/shard_map/dot_general | solution.py:900
  344.1 2.9 collective-permute-done.65
  347.0 2.8 collective-permute-done.66
  349.8 4.2 assemble.3
  354.0 7.9 %fusion.156 = f32[1024,1024]{1,0:T(8,128)S(1)} fusion(bf16[1024,2048]{1,0:T(8,128)(2,1)} %assemble.3, bf16[2048,1024]{1,0:T(8,128)(2,1)} %constant_dynamic-update-slice_fusion.28), kind=kOutput, calls=%fused_computation.441 | convolution fusion | flops 4294967296 | bytes 12582912 | tf_op jit(solution)/shard_map/dot_general | solution.py:910
  364.1 9.2 %multiply_convert_fusion.2 = (bf16[1024,1024]{1,0:T(8,128)(2,1)}, bf16[1024,1024]{1,0:T(8,128)(2,1)S(1)}, bf16[1024,1024]{1,0:T(8,128)(2,1)S(1)}) fusion(f32[1024,1024]{1,0:T(8,128)S(1)} %fusion.156, f32[1024,1024]{1,0:T(8,128)S(1)} %copy-done.137, bf16[1024,2048]{1,0:T(8,128)(2,1)S(1)} %copy-done.14, ...), kind=kOutput, calls=%fused_computation.12 | convolution fusion | flops 4310695936 | bytes 23068672 | tf_op jit(solution)/shard_map/dot_general | solution.py:912
  373.3 7.9 %fusion.157 = f32[1024,2048]{1,0:T(8,128)S(1)} fusion(bf16[1024,1024]{1,0:T(8,128)(2,1)S(1)} %get-tuple-element.434, bf16[2048,1024]{1,0:T(8,128)(2,1)} %constant_dynamic-update-slice_fusion.28), kind=kOutput, calls=%fused_computation.442 | convolution fusion | flops 4294967296 | bytes 14680064 | tf_op jit(solution)/shard_map/dot_general | solution.py:939
  381.2 7.5 add_convert_fusion
  390.3 7.4 convolution_convert_fusion.2
  399.0 2.9 fusion.4
  406.6 4.9 convolution_convert_fusion.1
  411.5 8.5 %convolution_convert_fusion.3 = bf16[1024,2048]{1,0:T(8,128)(2,1)S(1)} fusion(bf16[1024,1024]{1,0:T(8,128)(2,1)S(1)} %copy-done.140, bf16[2048,1024]{1,0:T(8,128)(2,1)} %constant_dynamic-update-slice_fusion.21), kind=kOutput, calls=%fused_computation.18 | convolution fusion | flops 4297064448 | bytes 10485760 | tf_op jit(solution)/shard_map/dot_general | solution.py:954
  428.2 5.1 convolution_convert_fusion
  452.1 3.0 fusion.3
  462.6 11.3 %collective-permute-done.77 = bf16[128,1024]{1,0:T(8,128)(2,1)S(1)} collective-permute-done((bf16[128,1024]{1,0:T(8,128)(2,1)S(1)}, bf16[128,1024]{1,0:T(8,128)(2,1)S(1)}, u32[]{:S(2)}, u32[]{:S(2)}) %collective-permute-start.77) | collective-permute-done | bytes 262176 | tf_op jit(solution)/shard_map/ppermute | solution.py:51
  478.8 3.0 convolution_convert_fusion.7
  487.5 15.6 %attend_back.1 = (bf16[512,512]{1,0:T(8,128)(2,1)}, bf16[4096,256]{1,0:T(8,128)(2,1)}, bf16[4096,256]{1,0:T(8,128)(2,1)}) custom-call(s32[2]{0:T(128)} %pad_add_fusion.place_ref, s32[8]{0:T(128)} %pair_ref.3, s32[4096]{0:T(1024)} %bitcast.275, bf16[512,512]{1,0:T(8,128)(2,1)} %maximum_multiply_fusion.q_ref, bf16[4096,512]{1,0:T(8,128)(2,1)} %copy-done.119, ...), custom_call_target="tpu_custom_call" | custom-call | flops 16000000000 | bytes 12000000 | tf_op jit(solution)/shard_map/attend_back/pallas_call | solution.py:531
  503.1 9.6 %collective-permute-done.83 = bf16[256,1024]{1,0:T(8,128)(2,1)} collective-permute-done((bf16[256,1024]{1,0:T(8,128)(2,1)}, bf16[256,1024]{1,0:T(8,128)(2,1)}, u32[]{:S(2)}, u32[]{:S(2)}) %collective-permute-start.83) | collective-permute-done | bytes 524320 | tf_op jit(solution)/shard_map/ppermute | solution.py:51
  512.7 4.3 collective-permute-done.81
  527.7 19.3 %collective-permute-done.86 = bf16[256,1024]{1,0:T(8,128)(2,1)S(1)} collective-permute-done((bf16[256,1024]{1,0:T(8,128)(2,1)S(1)}, bf16[256,1024]{1,0:T(8,128)(2,1)S(1)}, u32[]{:S(2)}, u32[]{:S(2)}) %collective-permute-start.86) | collective-permute-done | bytes 524320 | tf_op jit(solution)/shard_map/ppermute | solution.py:51
  554.3 20.7 %collective-permute-done.87 = bf16[2,512,256]{2,1,0:T(8,128)(2,1)S(1)} collective-permute-done((bf16[2,512,256]{2,1,0:T(8,128)(2,1)S(1)}, bf16[2,512,256]{2,1,0:T(8,128)(2,1)S(1)}, u32[]{:S(2)}, u32[]{:S(2)}) %collective-permute-start.87) | collective-permute-done | bytes 524320 | tf_op jit(solution)/shard_map/ppermute | solution.py:51
  586.6 2.8 select_dynamic-update-slice_fusion
  589.4 10.9 %collective-permute-done.91 = bf16[1,512,256]{2,1,0:T(8,128)(2,1)S(1)} collective-permute-done((bf16[1,512,256]{2,1,0:T(8,128)(2,1)S(1)}, bf16[1,512,256]{2,1,0:T(8,128)(2,1)S(1)}, u32[]{:S(2)}, u32[]{:S(2)}) %collective-permute-start.91) | collective-permute-done | bytes 262176 | tf_op jit(solution)/shard_map/ppermute | solution.py:51
  600.3 6.7 collective-permute-done.94
  613.4 2.8 select_dynamic-update-slice_fusion.2
  618.8 6.6 collective-permute-done.96
  625.4 8.1 %collective-permute-done.99 = bf16[128,1024]{1,0:T(8,128)(2,1)S(1)} collective-permute-done((bf16[128,1024]{1,0:T(8,128)(2,1)S(1)}, bf16[128,1024]{1,0:T(8,128)(2,1)S(1)}, u32[]{:S(2)}, u32[]{:S(2)}) %collective-permute-start.99) | collective-permute-done | bytes 262176 | tf_op jit(solution)/shard_map/ppermute | solution.py:51
  642.4 2.7 collective-permute-done.102
  659.0 3.0 reshape.625
  662.0 3.4 collective-permute-done.107
  671.6 2.8 fusion.7
  678.7 4.5 collective-permute-start.110
  696.0 2.9 collective-permute-start.114
  703.3 11.8 %collective-permute-done.112 = bf16[1,256,512]{2,1,0:T(8,128)(2,1)S(1)} collective-permute-done((bf16[1,256,512]{2,1,0:T(8,128)(2,1)S(1)}, bf16[1,256,512]{2,1,0:T(8,128)(2,1)S(1)}, u32[]{:S(2)}, u32[]{:S(2)}) %collective-permute-start.112) | collective-permute-done | bytes 262176 | tf_op jit(solution)/shard_map/ppermute | solution.py:51
  715.1 7.2 collective-permute-done.113
  727.2 4.4 collective-permute-start.116
  733.4 4.3 collective-permute-done.116
  737.7 4.2 collective-permute-done.117
  741.9 2.7 collective-permute-done.119
  (752 shorter events, 341.8 us)
Async XLA Ops:
  29.3 26.0 %collective-permute-start.5 = (bf16[256,1024]{1,0:T(8,128)(2,1)}, bf16[256,1024]{1,0:T(8,128)(2,1)}, u32[]{:S(2)}, u32[]{:S(2)}) collective-permute-start(bf16[256,1024]{1,0:T(8,128)(2,1)} %get-tuple-element.277), channel_id=1, source_target_pairs={{0,4},{1,5},{2,6},{3,7},{4,0},{5,1},{6,2},{7,3},{8,12},{9,13},{10,... | collective-permute-start | bytes 1572872 | tf_op jit(solution)/shard_map/ppermute | solution.py:51
  32.0 23.3 %collective-permute-start.6 = (bf16[256,1024]{1,0:T(8,128)(2,1)}, bf16[256,1024]{1,0:T(8,128)(2,1)}, u32[]{:S(2)}, u32[]{:S(2)}) collective-permute-start(bf16[256,1024]{1,0:T(8,128)(2,1)} %get-tuple-element.277), channel_id=1, source_target_pairs={{0,2},{1,3},{2,0},{3,1},{4,6},{5,7},{6,4},{7,5},{8,10},{9,11},{10,... | collective-permute-start | bytes 1572872 | tf_op jit(solution)/shard_map/ppermute | solution.py:51
  33.7 21.6 %collective-permute-start.7 = (bf16[256,1024]{1,0:T(8,128)(2,1)}, bf16[256,1024]{1,0:T(8,128)(2,1)}, u32[]{:S(2)}, u32[]{:S(2)}) collective-permute-start(bf16[256,1024]{1,0:T(8,128)(2,1)} %get-tuple-element.277), channel_id=1, source_target_pairs={{0,16},{1,17},{2,18},{3,19},{4,20},{5,21},{6,22},{7,23},{8,24},{9,... | collective-permute-start | bytes 1572872 | tf_op jit(solution)/shard_map/ppermute | solution.py:51
  35.2 20.1 %collective-permute-start.8 = (bf16[128,2048]{1,0:T(8,128)(2,1)S(1)}, bf16[128,2048]{1,0:T(8,128)(2,1)S(1)}, u32[]{:S(2)}, u32[]{:S(2)}) collective-permute-start(bf16[128,2048]{1,0:T(8,128)(2,1)S(1)} %reshape.604), channel_id=1, source_target_pairs={{0,1},{1,0},{2,3},{3,2},{4,5},{5,4},{6,7},{7,6},{8,9},{9,8},{10,11... | collective-permute-start | bytes 1572872 | tf_op jit(solution)/shard_map/ppermute | solution.py:51
  56.9 23.2 %collective-permute-start.11 = (bf16[256,1024]{1,0:T(8,128)(2,1)}, bf16[256,1024]{1,0:T(8,128)(2,1)}, u32[]{:S(2)}, u32[]{:S(2)}) collective-permute-start(bf16[256,1024]{1,0:T(8,128)(2,1)} %collective-permute-done.5), channel_id=1, source_target_pairs={{0,2},{1,3},{2,0},{3,1},{4,6},{5,7},{6,4},{7,5},{8,10},{9,11},{10,... | collective-permute-start | bytes 1572872 | tf_op jit(solution)/shard_map/ppermute | solution.py:51
  58.6 21.5 %collective-permute-start.12 = (bf16[256,1024]{1,0:T(8,128)(2,1)}, bf16[256,1024]{1,0:T(8,128)(2,1)}, u32[]{:S(2)}, u32[]{:S(2)}) collective-permute-start(bf16[256,1024]{1,0:T(8,128)(2,1)} %collective-permute-done.5), channel_id=1, source_target_pairs={{0,16},{1,17},{2,18},{3,19},{4,20},{5,21},{6,22},{7,23},{8,24},{9,... | collective-permute-start | bytes 1572872 | tf_op jit(solution)/shard_map/ppermute | solution.py:51
  59.2 24.7 %collective-permute-start.13 = (bf16[256,1024]{1,0:T(8,128)(2,1)}, bf16[256,1024]{1,0:T(8,128)(2,1)}, u32[]{:S(2)}, u32[]{:S(2)}) collective-permute-start(bf16[256,1024]{1,0:T(8,128)(2,1)} %get-tuple-element.306), channel_id=1, source_target_pairs={{0,4},{1,5},{2,6},{3,7},{4,0},{5,1},{6,2},{7,3},{8,12},{9,13},{10,... | collective-permute-start | bytes 1572872 | tf_op jit(solution)/shard_map/ppermute | solution.py:51
  101.6 19.0 %collective-permute-start.21 = (bf16[256,1024]{1,0:T(8,128)(2,1)}, bf16[256,1024]{1,0:T(8,128)(2,1)}, u32[]{:S(2)}, u32[]{:S(2)}) collective-permute-start(bf16[256,1024]{1,0:T(8,128)(2,1)} %constant_dynamic-slice_fusion), channel_id=1, source_target_pairs={{0,2},{1,3},{2,0},{3,1},{4,6},{5,7},{6,4},{7,5},{8,10},{9,11},{10,... | collective-permute-start | bytes 1572872 | tf_op jit(solution)/shard_map/ppermute | solution.py:51
  101.9 18.6 %collective-permute-start.22 = (bf16[256,1024]{1,0:T(8,128)(2,1)}, bf16[256,1024]{1,0:T(8,128)(2,1)}, u32[]{:S(2)}, u32[]{:S(2)}) collective-permute-start(bf16[256,1024]{1,0:T(8,128)(2,1)} %get-tuple-element.306), channel_id=1, source_target_pairs={{0,1},{1,0},{2,3},{3,2},{4,5},{5,4},{6,7},{7,6},{8,9},{9,8},{10,11... | collective-permute-start | bytes 1572872 | tf_op jit(solution)/shard_map/ppermute | solution.py:51
  103.5 17.1 %collective-permute-start.24 = (bf16[128,2048]{1,0:T(8,128)(2,1)S(1)}, bf16[128,2048]{1,0:T(8,128)(2,1)}, u32[]{:S(2)}, u32[]{:S(2)}) collective-permute-start(bf16[128,2048]{1,0:T(8,128)(2,1)S(1)} %reshape.608), channel_id=1, source_target_pairs={{0,16},{1,17},{2,18},{3,19},{4,20},{5,21},{6,22},{7,23},{8,24},{9,... | collective-permute-start | bytes 1572872 | tf_op jit(solution)/shard_map/ppermute | solution.py:51
  123.7 24.5 %collective-permute-start.25 = (bf16[512,512]{1,0:T(8,128)(2,1)}, bf16[512,512]{1,0:T(8,128)(2,1)}, u32[]{:S(2)}, u32[]{:S(2)}) collective-permute-start(bf16[512,512]{1,0:T(8,128)(2,1)} %get-tuple-element.319), channel_id=1, source_target_pairs={{0,4},{1,5},{2,6},{3,7},{4,0},{5,1},{6,2},{7,3},{8,12},{9,13},{10,... | collective-permute-start | bytes 1572872 | tf_op jit(solution)/shard_map/ppermute | solution.py:51
  125.1 23.1 %collective-permute-start.26 = (bf16[512,512]{1,0:T(8,128)(2,1)}, bf16[512,512]{1,0:T(8,128)(2,1)}, u32[]{:S(2)}, u32[]{:S(2)}) collective-permute-start(bf16[512,512]{1,0:T(8,128)(2,1)} %get-tuple-element.319), channel_id=1, source_target_pairs={{0,2},{1,3},{2,0},{3,1},{4,6},{5,7},{6,4},{7,5},{8,10},{9,11},{10,... | collective-permute-start | bytes 1572872 | tf_op jit(solution)/shard_map/ppermute | solution.py:51
  126.6 21.6 %collective-permute-start.27 = (bf16[512,512]{1,0:T(8,128)(2,1)}, bf16[512,512]{1,0:T(8,128)(2,1)}, u32[]{:S(2)}, u32[]{:S(2)}) collective-permute-start(bf16[512,512]{1,0:T(8,128)(2,1)} %get-tuple-element.319), channel_id=1, source_target_pairs={{0,16},{1,17},{2,18},{3,19},{4,20},{5,21},{6,22},{7,23},{8,24},{9,... | collective-permute-start | bytes 1572872 | tf_op jit(solution)/shard_map/ppermute | solution.py:51
  127.1 21.1 %collective-permute-start.28 = (bf16[256,1024]{1,0:T(8,128)(2,1)S(1)}, bf16[256,1024]{1,0:T(8,128)(2,1)}, u32[]{:S(2)}, u32[]{:S(2)}) collective-permute-start(bf16[256,1024]{1,0:T(8,128)(2,1)S(1)} %copy-done.35), channel_id=1, source_target_pairs={{0,1},{1,0},{2,3},{3,2},{4,5},{5,4},{6,7},{7,6},{8,9},{9,8},{10,11... | collective-permute-start | bytes 1572872 | tf_op jit(solution)/shard_map/ppermute | solution.py:51
  128.6 21.0 %collective-permute-start.29 = (bf16[256,1024]{1,0:T(8,128)(2,1)S(1)}, bf16[256,1024]{1,0:T(8,128)(2,1)}, u32[]{:S(2)}, u32[]{:S(2)}) collective-permute-start(bf16[256,1024]{1,0:T(8,128)(2,1)S(1)} %copy-done.36), channel_id=1, source_target_pairs={{0,1},{1,0},{2,3},{3,2},{4,5},{5,4},{6,7},{7,6},{8,9},{9,8},{10,11... | collective-permute-start | bytes 1572872 | tf_op jit(solution)/shard_map/ppermute | solution.py:51
  151.2 18.7 %collective-permute-start.31 = (bf16[512,512]{1,0:T(8,128)(2,1)}, bf16[512,512]{1,0:T(8,128)(2,1)S(1)}, u32[]{:S(2)}, u32[]{:S(2)}) collective-permute-start(bf16[512,512]{1,0:T(8,128)(2,1)} %collective-permute-done.25), channel_id=1, source_target_pairs={{0,2},{1,3},{2,0},{3,1},{4,6},{5,7},{6,4},{7,5},{8,10},{9,11},{10,... | collective-permute-start | bytes 1572872 | tf_op jit(solution)/shard_map/ppermute | solution.py:51
  152.0 21.0 %collective-permute-start.32 = (bf16[512,512]{1,0:T(8,128)(2,1)}, bf16[512,512]{1,0:T(8,128)(2,1)S(1)}, u32[]{:S(2)}, u32[]{:S(2)}) collective-permute-start(bf16[512,512]{1,0:T(8,128)(2,1)} %collective-permute-done.25), channel_id=1, source_target_pairs={{0,16},{1,17},{2,18},{3,19},{4,20},{5,21},{6,22},{7,23},{8,24},{9,... | collective-permute-start | bytes 1572872 | tf_op jit(solution)/shard_map/ppermute | solution.py:51
  152.3 20.7 %collective-permute-start.33 = (bf16[256,1024]{1,0:T(8,128)(2,1)S(1)}, bf16[256,1024]{1,0:T(8,128)(2,1)S(1)}, u32[]{:S(2)}, u32[]{:S(2)}) collective-permute-start(bf16[256,1024]{1,0:T(8,128)(2,1)S(1)} %get-tuple-element.349), channel_id=1, source_target_pairs={{0,1},{1,0},{2,3},{3,2},{4,5},{5,4},{6,7},{7,6},{8,9},{9,8},{10,11... | collective-permute-start | bytes 1572872 | tf_op jit(solution)/shard_map/ppermute | solution.py:51
  153.9 23.6 %collective-permute-start.34 = (bf16[256,1024]{1,0:T(8,128)(2,1)S(1)}, bf16[256,1024]{1,0:T(8,128)(2,1)}, u32[]{:S(2)}, u32[]{:S(2)}) collective-permute-start(bf16[256,1024]{1,0:T(8,128)(2,1)S(1)} %copy-done.35), channel_id=1, source_target_pairs={{0,4},{1,5},{2,6},{3,7},{4,0},{5,1},{6,2},{7,3},{8,12},{9,13},{10,... | collective-permute-start | bytes 1572872 | tf_op jit(solution)/shard_map/ppermute | solution.py:51
  177.8 21.5 %collective-permute-start.36 = (bf16[2,256,512]{2,1,0:T(8,128)(2,1)S(1)}, bf16[2,256,512]{2,1,0:T(8,128)(2,1)S(1)}, u32[]{:S(2)}, u32[]{:S(2)}) collective-permute-start(bf16[2,256,512]{2,1,0:T(8,128)(2,1)S(1)} %pad_maximum_fusion.14), channel_id=1, source_target_pairs={{0,2},{1,3},{2,0},{3,1},{4,6},{5,7},{6,4},{7,5},{8,10},{9,11},{10,... | collective-permute-start | bytes 1572872 | tf_op jit(solution)/shard_map/ppermute | solution.py:51
  177.8 22.3 %collective-permute-start.37 = (bf16[256,1024]{1,0:T(8,128)(2,1)S(1)}, bf16[256,1024]{1,0:T(8,128)(2,1)S(1)}, u32[]{:S(2)}, u32[]{:S(2)}) collective-permute-start(bf16[256,1024]{1,0:T(8,128)(2,1)S(1)} %copy-done.36), channel_id=1, source_target_pairs={{0,4},{1,5},{2,6},{3,7},{4,0},{5,1},{6,2},{7,3},{8,12},{9,13},{10,... | collective-permute-start | bytes 1572872 | tf_op jit(solution)/shard_map/ppermute | solution.py:51
  180.7 19.4 %collective-permute-start.38 = (bf16[256,1024]{1,0:T(8,128)(2,1)S(1)}, bf16[256,1024]{1,0:T(8,128)(2,1)S(1)}, u32[]{:S(2)}, u32[]{:S(2)}) collective-permute-start(bf16[256,1024]{1,0:T(8,128)(2,1)S(1)} %get-tuple-element.340), channel_id=1, source_target_pairs={{0,1},{1,0},{2,3},{3,2},{4,5},{5,4},{6,7},{7,6},{8,9},{9,8},{10,11... | collective-permute-start | bytes 1572872 | tf_op jit(solution)/shard_map/ppermute | solution.py:51
  181.0 20.7 %collective-permute-start.39 = (bf16[256,1024]{1,0:T(8,128)(2,1)S(1)}, bf16[256,1024]{1,0:T(8,128)(2,1)}, u32[]{:S(2)}, u32[]{:S(2)}) collective-permute-start(bf16[256,1024]{1,0:T(8,128)(2,1)S(1)} %get-tuple-element.341), channel_id=1, source_target_pairs={{0,1},{1,0},{2,3},{3,2},{4,5},{5,4},{6,7},{7,6},{8,9},{9,8},{10,11... | collective-permute-start | bytes 1572872 | tf_op jit(solution)/shard_map/ppermute | solution.py:51
  202.8 26.6 %collective-permute-start.40 = (bf16[4,256,512]{2,1,0:T(8,128)(2,1)}, bf16[4,256,512]{2,1,0:T(8,128)(2,1)}, u32[]{:S(2)}, u32[]{:S(2)}) collective-permute-start(bf16[4,256,512]{2,1,0:T(8,128)(2,1)} %pad_maximum_fusion.6), channel_id=1, source_target_pairs={{0,16},{1,17},{2,18},{3,19},{4,20},{5,21},{6,22},{7,23},{8,24},{9,... | collective-permute-start | bytes 3145736 | tf_op jit(solution)/shard_map/ppermute | solution.py:51
  205.7 22.1 %collective-permute-start.41 = (bf16[256,1024]{1,0:T(8,128)(2,1)S(1)}, bf16[256,1024]{1,0:T(8,128)(2,1)}, u32[]{:S(2)}, u32[]{:S(2)}) collective-permute-start(bf16[256,1024]{1,0:T(8,128)(2,1)S(1)} %get-tuple-element.349), channel_id=1, source_target_pairs={{0,4},{1,5},{2,6},{3,7},{4,0},{5,1},{6,2},{7,3},{8,12},{9,13},{10,... | collective-permute-start | bytes 1572872 | tf_op jit(solution)/shard_map/ppermute | solution.py:51
  206.0 21.8 %collective-permute-start.42 = (bf16[256,1024]{1,0:T(8,128)(2,1)}, bf16[256,1024]{1,0:T(8,128)(2,1)}, u32[]{:S(2)}, u32[]{:S(2)}) collective-permute-start(bf16[256,1024]{1,0:T(8,128)(2,1)} %collective-permute-done.13), channel_id=1, source_target_pairs={{0,1},{1,0},{2,3},{3,2},{4,5},{5,4},{6,7},{7,6},{8,9},{9,8},{10,11... | collective-permute-start | bytes 1572872 | tf_op jit(solution)/shard_map/ppermute | solution.py:51
  206.3 21.9 %collective-permute-start.43 = (bf16[256,1024]{1,0:T(8,128)(2,1)}, bf16[256,1024]{1,0:T(8,128)(2,1)}, u32[]{:S(2)}, u32[]{:S(2)}) collective-permute-start(bf16[256,1024]{1,0:T(8,128)(2,1)} %collective-permute-done.34), channel_id=1, source_target_pairs={{0,1},{1,0},{2,3},{3,2},{4,5},{5,4},{6,7},{7,6},{8,9},{9,8},{10,11... | collective-permute-start | bytes 1572872 | tf_op jit(solution)/shard_map/ppermute | solution.py:51
  208.0 21.3 %collective-permute-start.44 = (bf16[128,2048]{1,0:T(8,128)(2,1)S(1)}, bf16[128,2048]{1,0:T(8,128)(2,1)S(1)}, u32[]{:S(2)}, u32[]{:S(2)}) collective-permute-start(bf16[128,2048]{1,0:T(8,128)(2,1)S(1)} %reshape.608), channel_id=1, source_target_pairs={{0,2},{1,3},{2,0},{3,1},{4,6},{5,7},{6,4},{7,5},{8,10},{9,11},{10,... | collective-permute-start | bytes 1572872 | tf_op jit(solution)/shard_map/ppermute | solution.py:51
  235.4 20.0 %collective-permute-start.45 = (bf16[128,2048]{1,0:T(8,128)(2,1)}, bf16[128,2048]{1,0:T(8,128)(2,1)}, u32[]{:S(2)}, u32[]{:S(2)}) collective-permute-start(bf16[128,2048]{1,0:T(8,128)(2,1)} %get-tuple-element.582), channel_id=1, source_target_pairs={{0,8},{1,9},{2,10},{3,11},{4,12},{5,13},{6,14},{7,15},{8,0},{9,1},... | collective-permute-start | bytes 1572872 | tf_op jit(solution)/shard_map/ppermute | solution.py:51
  236.3 18.2 %collective-permute-start.47 = (bf16[128,2048]{1,0:T(8,128)(2,1)}, bf16[128,2048]{1,0:T(8,128)(2,1)}, u32[]{:S(2)}, u32[]{:S(2)}) collective-permute-start(bf16[128,2048]{1,0:T(8,128)(2,1)} %fusion.25), channel_id=1, source_target_pairs={{0,1},{1,0},{2,3},{3,2},{4,5},{5,4},{6,7},{7,6},{8,9},{9,8},{10,11... | collective-permute-start | bytes 1572872 | tf_op jit(solution)/shard_map/ppermute | solution.py:51
  236.9 17.6 %collective-permute-start.48 = (bf16[128,2048]{1,0:T(8,128)(2,1)S(1)}, bf16[128,2048]{1,0:T(8,128)(2,1)S(1)}, u32[]{:S(2)}, u32[]{:S(2)}) collective-permute-start(bf16[128,2048]{1,0:T(8,128)(2,1)S(1)} %copy-done.42), channel_id=1, source_target_pairs={{0,16},{1,17},{2,18},{3,19},{4,20},{5,21},{6,22},{7,23},{8,24},{9,... | collective-permute-start | bytes 1572872 | tf_op jit(solution)/shard_map/ppermute | solution.py:51
  267.1 55.3 %collective-permute-start.60 = (bf16[512,2048]{1,0:T(8,128)(2,1)}, bf16[512,2048]{1,0:T(8,128)(2,1)S(1)}, u32[]{:S(2)}, u32[]{:S(2)}) collective-permute-start(bf16[512,2048]{1,0:T(8,128)(2,1)} %pad_maximum_fusion.2), channel_id=1, source_target_pairs={{0,8},{1,9},{2,10},{3,11},{4,12},{5,13},{6,14},{7,15},{8,0},{9,1},... | collective-permute-start | bytes 6291464 | tf_op jit(solution)/shard_map/ppermute | solution.py:51
  267.2 19.1 %collective-permute-start.52 = (bf16[256,1024]{1,0:T(8,128)(2,1)S(1)}, bf16[256,1024]{1,0:T(8,128)(2,1)S(1)}, u32[]{:S(2)}, u32[]{:S(2)}) collective-permute-start(bf16[256,1024]{1,0:T(8,128)(2,1)S(1)} %copy-done.80), channel_id=1, source_target_pairs={{0,1},{1,0},{2,3},{3,2},{4,5},{5,4},{6,7},{7,6},{8,9},{9,8},{10,11... | collective-permute-start | bytes 1572872 | tf_op jit(solution)/shard_map/ppermute | solution.py:51
  315.4 34.3 %collective-permute-start.59 = (bf16[512,2048]{1,0:T(8,128)(2,1)}, bf16[512,2048]{1,0:T(8,128)(2,1)}, u32[]{:S(2)}, u32[]{:S(2)}) collective-permute-start(bf16[512,2048]{1,0:T(8,128)(2,1)} %assemble.2.refs_0_), channel_id=1, source_target_pairs={{0,8},{1,9},{2,10},{3,11},{4,12},{5,13},{6,14},{7,15},{8,0},{9,1},... | collective-permute-start | bytes 6291464 | tf_op jit(solution)/shard_map/ppermute | solution.py:51
  402.1 21.8 %collective-permute-start.69 = (bf16[2,128,1024]{2,1,0:T(8,128)(2,1)S(1)}, bf16[2,128,1024]{2,1,0:T(8,128)(2,1)S(1)}, u32[]{:S(2)}, u32[]{:S(2)}) collective-permute-start(bf16[2,128,1024]{2,1,0:T(8,128)(2,1)S(1)} %slice_bitcast_fusion.11), channel_id=1, source_target_pairs={{0,2},{1,3},{2,0},{3,1},{4,6},{5,7},{6,4},{7,5},{8,10},{9,11},{10,... | collective-permute-start | bytes 1572872 | tf_op jit(solution)/shard_map/ppermute | solution.py:51
  403.7 20.1 %collective-permute-start.70 = (bf16[2,128,1024]{2,1,0:T(8,128)(2,1)S(1)}, bf16[2,128,1024]{2,1,0:T(8,128)(2,1)S(1)}, u32[]{:S(2)}, u32[]{:S(2)}) collective-permute-start(bf16[2,128,1024]{2,1,0:T(8,128)(2,1)S(1)} %slice_bitcast_fusion.10), channel_id=1, source_target_pairs={{0,16},{1,17},{2,18},{3,19},{4,20},{5,21},{6,22},{7,23},{8,24},{9,... | collective-permute-start | bytes 1572872 | tf_op jit(solution)/shard_map/ppermute | solution.py:51
  405.8 18.0 %collective-permute-start.71 = (bf16[256,1024]{1,0:T(8,128)(2,1)S(1)}, bf16[256,1024]{1,0:T(8,128)(2,1)S(1)}, u32[]{:S(2)}, u32[]{:S(2)}) collective-permute-start(bf16[256,1024]{1,0:T(8,128)(2,1)S(1)} %get-tuple-element.412), channel_id=1, source_target_pairs={{0,1},{1,0},{2,3},{3,2},{4,5},{5,4},{6,7},{7,6},{8,9},{9,8},{10,11... | collective-permute-start | bytes 1572872 | tf_op jit(solution)/shard_map/ppermute | solution.py:51
  422.4 29.7 %collective-permute-start.68 = (bf16[2,2,128,2048]{3,2,1,0:T(8,128)(2,1)}, bf16[2,2,128,2048]{3,2,1,0:T(8,128)(2,1)}, u32[]{:S(2)}, u32[]{:S(2)}) collective-permute-start(bf16[2,2,128,2048]{3,2,1,0:T(8,128)(2,1)} %bitcast.39), channel_id=1, source_target_pairs={{0,8},{1,9},{2,10},{3,11},{4,12},{5,13},{6,14},{7,15},{8,0},{9,1},... | collective-permute-start | bytes 6291464 | tf_op jit(solution)/shard_map/ppermute | solution.py:51
  451.2 22.9 %collective-permute-start.79 = (bf16[128,2048]{1,0:T(8,128)(2,1)S(1)}, bf16[128,2048]{1,0:T(8,128)(2,1)}, u32[]{:S(2)}, u32[]{:S(2)}) collective-permute-start(bf16[128,2048]{1,0:T(8,128)(2,1)S(1)} %reshape.623), channel_id=1, source_target_pairs={{0,8},{1,9},{2,10},{3,11},{4,12},{5,13},{6,14},{7,15},{8,0},{9,1},... | collective-permute-start | bytes 1572872 | tf_op jit(solution)/shard_map/ppermute | solution.py:51
  485.6 31.3 %collective-permute-start.81 = (bf16[4,256,640]{2,1,0:T(8,128)(2,1)}, bf16[4,256,640]{2,1,0:T(8,128)(2,1)}, u32[]{:S(2)}, u32[]{:S(2)}) collective-permute-start(bf16[4,256,640]{2,1,0:T(8,128)(2,1)} %bitcast.58), channel_id=1, source_target_pairs={{0,16},{1,17},{2,18},{3,19},{4,20},{5,21},{6,22},{7,23},{8,24},{9,... | collective-permute-start | bytes 3932168 | tf_op jit(solution)/shard_map/ppermute | solution.py:51
  485.9 26.8 %collective-permute-start.82 = (bf16[512,1024]{1,0:T(8,128)(2,1)}, bf16[512,1024]{1,0:T(8,128)(2,1)}, u32[]{:S(2)}, u32[]{:S(2)}) collective-permute-start(bf16[512,1024]{1,0:T(8,128)(2,1)} %get-tuple-element.437), channel_id=1, source_target_pairs={{0,1},{1,0},{2,3},{3,2},{4,5},{5,4},{6,7},{7,6},{8,9},{9,8},{10,11... | collective-permute-start | bytes 3145736 | tf_op jit(solution)/shard_map/ppermute | solution.py:51
  487.1 25.6 %collective-permute-start.83 = (bf16[256,1024]{1,0:T(8,128)(2,1)}, bf16[256,1024]{1,0:T(8,128)(2,1)}, u32[]{:S(2)}, u32[]{:S(2)}) collective-permute-start(bf16[256,1024]{1,0:T(8,128)(2,1)} %add_convert_fusion.11), channel_id=1, source_target_pairs={{0,4},{1,5},{2,6},{3,7},{4,0},{5,1},{6,2},{7,3},{8,12},{9,13},{10,... | collective-permute-start | bytes 1572872 | tf_op jit(solution)/shard_map/ppermute | solution.py:51
  520.6 26.4 %collective-permute-start.84 = (bf16[4,512,256]{2,1,0:T(8,128)(2,1)S(1)}, bf16[4,512,256]{2,1,0:T(8,128)(2,1)S(1)}, u32[]{:S(2)}, u32[]{:S(2)}) collective-permute-start(bf16[4,512,256]{2,1,0:T(8,128)(2,1)S(1)} %bitcast.262), channel_id=1, source_target_pairs={{0,16},{1,17},{2,18},{3,19},{4,20},{5,21},{6,22},{7,23},{8,24},{9,... | collective-permute-start | bytes 3145736 | tf_op jit(solution)/shard_map/ppermute | solution.py:51
  521.0 26.0 %collective-permute-start.85 = (bf16[512,1024]{1,0:T(8,128)(2,1)S(1)}, bf16[512,1024]{1,0:T(8,128)(2,1)S(1)}, u32[]{:S(2)}, u32[]{:S(2)}) collective-permute-start(bf16[512,1024]{1,0:T(8,128)(2,1)S(1)} %copy-done.50), channel_id=1, source_target_pairs={{0,1},{1,0},{2,3},{3,2},{4,5},{5,4},{6,7},{7,6},{8,9},{9,8},{10,11... | collective-permute-start | bytes 3145736 | tf_op jit(solution)/shard_map/ppermute | solution.py:51
  522.4 24.6 %collective-permute-start.86 = (bf16[256,1024]{1,0:T(8,128)(2,1)S(1)}, bf16[256,1024]{1,0:T(8,128)(2,1)S(1)}, u32[]{:S(2)}, u32[]{:S(2)}) collective-permute-start(bf16[256,1024]{1,0:T(8,128)(2,1)S(1)} %get-tuple-element.452), channel_id=1, source_target_pairs={{0,4},{1,5},{2,6},{3,7},{4,0},{5,1},{6,2},{7,3},{8,12},{9,13},{10,... | collective-permute-start | bytes 1572872 | tf_op jit(solution)/shard_map/ppermute | solution.py:51
  547.3 29.6 %collective-permute-start.88 = (bf16[4,512,256]{2,1,0:T(8,128)(2,1)S(1)}, bf16[4,512,256]{2,1,0:T(8,128)(2,1)S(1)}, u32[]{:S(2)}, u32[]{:S(2)}) collective-permute-start(bf16[4,512,256]{2,1,0:T(8,128)(2,1)S(1)} %bitcast.261), channel_id=1, source_target_pairs={{0,16},{1,17},{2,18},{3,19},{4,20},{5,21},{6,22},{7,23},{8,24},{9,... | collective-permute-start | bytes 3145736 | tf_op jit(solution)/shard_map/ppermute | solution.py:51
  549.1 27.8 %collective-permute-start.89 = (bf16[512,1024]{1,0:T(8,128)(2,1)S(1)}, bf16[512,1024]{1,0:T(8,128)(2,1)S(1)}, u32[]{:S(2)}, u32[]{:S(2)}) collective-permute-start(bf16[512,1024]{1,0:T(8,128)(2,1)S(1)} %copy-done.49), channel_id=1, source_target_pairs={{0,1},{1,0},{2,3},{3,2},{4,5},{5,4},{6,7},{7,6},{8,9},{9,8},{10,11... | collective-permute-start | bytes 3145736 | tf_op jit(solution)/shard_map/ppermute | solution.py:51
  551.3 23.7 %collective-permute-start.87 = (bf16[2,512,256]{2,1,0:T(8,128)(2,1)S(1)}, bf16[2,512,256]{2,1,0:T(8,128)(2,1)S(1)}, u32[]{:S(2)}, u32[]{:S(2)}) collective-permute-start(bf16[2,512,256]{2,1,0:T(8,128)(2,1)S(1)} %slice.616), channel_id=1, source_target_pairs={{0,2},{1,3},{2,0},{3,1},{4,6},{5,7},{6,4},{7,5},{8,10},{9,11},{10,... | collective-permute-start | bytes 1572872 | tf_op jit(solution)/shard_map/ppermute | solution.py:51
  551.4 25.5 %collective-permute-start.90 = (bf16[256,1024]{1,0:T(8,128)(2,1)S(1)}, bf16[256,1024]{1,0:T(8,128)(2,1)S(1)}, u32[]{:S(2)}, u32[]{:S(2)}) collective-permute-start(bf16[256,1024]{1,0:T(8,128)(2,1)S(1)} %get-tuple-element.459), channel_id=1, source_target_pairs={{0,4},{1,5},{2,6},{3,7},{4,0},{5,1},{6,2},{7,3},{8,12},{9,13},{10,... | collective-permute-start | bytes 1572872 | tf_op jit(solution)/shard_map/ppermute | solution.py:51
  577.4 29.6 %collective-permute-start.93 = (bf16[4,256,512]{2,1,0:T(8,128)(2,1)S(1)}, bf16[4,256,512]{2,1,0:T(8,128)(2,1)S(1)}, u32[]{:S(2)}, u32[]{:S(2)}) collective-permute-start(bf16[4,256,512]{2,1,0:T(8,128)(2,1)S(1)} %bitcast.260), channel_id=1, source_target_pairs={{0,16},{1,17},{2,18},{3,19},{4,20},{5,21},{6,22},{7,23},{8,24},{9,... | collective-permute-start | bytes 3145736 | tf_op jit(solution)/shard_map/ppermute | solution.py:51
  578.3 28.7 %collective-permute-start.95 = (bf16[512,1024]{1,0:T(8,128)(2,1)S(1)}, bf16[512,1024]{1,0:T(8,128)(2,1)S(1)}, u32[]{:S(2)}, u32[]{:S(2)}) collective-permute-start(bf16[512,1024]{1,0:T(8,128)(2,1)S(1)} %copy-done.60), channel_id=1, source_target_pairs={{0,1},{1,0},{2,3},{3,2},{4,5},{5,4},{6,7},{7,6},{8,9},{9,8},{10,11... | collective-permute-start | bytes 3145736 | tf_op jit(solution)/shard_map/ppermute | solution.py:51
  582.7 24.3 %collective-permute-start.92 = (bf16[2,512,256]{2,1,0:T(8,128)(2,1)S(1)}, bf16[2,512,256]{2,1,0:T(8,128)(2,1)S(1)}, u32[]{:S(2)}, u32[]{:S(2)}) collective-permute-start(bf16[2,512,256]{2,1,0:T(8,128)(2,1)S(1)} %slice.622), channel_id=1, source_target_pairs={{0,2},{1,3},{2,0},{3,1},{4,6},{5,7},{6,4},{7,5},{8,10},{9,11},{10,... | collective-permute-start | bytes 1572872 | tf_op jit(solution)/shard_map/ppermute | solution.py:51
  585.7 21.3 %collective-permute-start.94 = (bf16[128,1024]{1,0:T(8,128)(2,1)S(1)}, bf16[128,1024]{1,0:T(8,128)(2,1)S(1)}, u32[]{:S(2)}, u32[]{:S(2)}) collective-permute-start(bf16[128,1024]{1,0:T(8,128)(2,1)S(1)} %get-tuple-element.468), channel_id=1, source_target_pairs={{0,4},{1,5},{2,6},{3,7},{4,0},{5,1},{6,2},{7,3},{8,12},{9,13},{10,... | collective-permute-start | bytes 786440 | tf_op jit(solution)/shard_map/ppermute | solution.py:51
  607.6 26.0 %collective-permute-start.100 = (bf16[128,2048]{1,0:T(8,128)(2,1)S(1)}, bf16[128,2048]{1,0:T(8,128)(2,1)S(1)}, u32[]{:S(2)}, u32[]{:S(2)}) collective-permute-start(bf16[128,2048]{1,0:T(8,128)(2,1)S(1)} %copy-done.84), channel_id=1, source_target_pairs={{0,16},{1,17},{2,18},{3,19},{4,20},{5,21},{6,22},{7,23},{8,24},{9,... | collective-permute-start | bytes 1572872 | tf_op jit(solution)/shard_map/ppermute | solution.py:51
  609.1 24.5 %collective-permute-start.97 = (bf16[2,256,512]{2,1,0:T(8,128)(2,1)S(1)}, bf16[2,256,512]{2,1,0:T(8,128)(2,1)S(1)}, u32[]{:S(2)}, u32[]{:S(2)}) collective-permute-start(bf16[2,256,512]{2,1,0:T(8,128)(2,1)S(1)} %slice.633), channel_id=1, source_target_pairs={{0,2},{1,3},{2,0},{3,1},{4,6},{5,7},{6,4},{7,5},{8,10},{9,11},{10,... | collective-permute-start | bytes 1572872 | tf_op jit(solution)/shard_map/ppermute | solution.py:51
  609.1 24.5 %collective-permute-start.98 = (bf16[256,1024]{1,0:T(8,128)(2,1)S(1)}, bf16[256,1024]{1,0:T(8,128)(2,1)S(1)}, u32[]{:S(2)}, u32[]{:S(2)}) collective-permute-start(bf16[256,1024]{1,0:T(8,128)(2,1)S(1)} %get-tuple-element.477), channel_id=1, source_target_pairs={{0,1},{1,0},{2,3},{3,2},{4,5},{5,4},{6,7},{7,6},{8,9},{9,8},{10,11... | collective-permute-start | bytes 1572872 | tf_op jit(solution)/shard_map/ppermute | solution.py:51
  612.8 20.8 %collective-permute-start.99 = (bf16[128,1024]{1,0:T(8,128)(2,1)S(1)}, bf16[128,1024]{1,0:T(8,128)(2,1)S(1)}, u32[]{:S(2)}, u32[]{:S(2)}) collective-permute-start(bf16[128,1024]{1,0:T(8,128)(2,1)S(1)} %get-tuple-element.478), channel_id=1, source_target_pairs={{0,4},{1,5},{2,6},{3,7},{4,0},{5,1},{6,2},{7,3},{8,12},{9,13},{10,... | collective-permute-start | bytes 786440 | tf_op jit(solution)/shard_map/ppermute | solution.py:51
  638.9 44.3 %collective-permute-start.103 = (bf16[128,2048]{1,0:T(8,128)(2,1)}, bf16[128,2048]{1,0:T(8,128)(2,1)}, u32[]{:S(2)}, u32[]{:S(2)}) collective-permute-start(bf16[128,2048]{1,0:T(8,128)(2,1)} %get-tuple-element.570), channel_id=1, source_target_pairs={{0,8},{1,9},{2,10},{3,11},{4,12},{5,13},{6,14},{7,15},{8,0},{9,1},... | collective-permute-start | bytes 1572872 | tf_op jit(solution)/shard_map/ppermute | solution.py:51
  647.8 20.9 %collective-permute-start.106 = (bf16[4,256,512]{2,1,0:T(8,128)(2,1)}, bf16[4,256,512]{2,1,0:T(8,128)(2,1)}, u32[]{:S(2)}, u32[]{:S(2)}) collective-permute-start(bf16[4,256,512]{2,1,0:T(8,128)(2,1)} %bitcast.74), channel_id=1, source_target_pairs={{0,16},{1,17},{2,18},{3,19},{4,20},{5,21},{6,22},{7,23},{8,24},{9,... | collective-permute-start | bytes 3145736 | tf_op jit(solution)/shard_map/ppermute | solution.py:51
  648.6 18.4 %collective-permute-start.108 = (bf16[2,256,640]{2,1,0:T(8,128)(2,1)}, bf16[2,256,640]{2,1,0:T(8,128)(2,1)}, u32[]{:S(2)}, u32[]{:S(2)}) collective-permute-start(bf16[2,256,640]{2,1,0:T(8,128)(2,1)} %slice.650), channel_id=1, source_target_pairs={{0,2},{1,3},{2,0},{3,1},{4,6},{5,7},{6,4},{7,5},{8,10},{9,11},{10,... | collective-permute-start | bytes 1966088 | tf_op jit(solution)/shard_map/ppermute | solution.py:51
  676.2 18.3 %collective-permute-start.109 = (bf16[2,256,512]{2,1,0:T(8,128)(2,1)}, bf16[2,256,512]{2,1,0:T(8,128)(2,1)}, u32[]{:S(2)}, u32[]{:S(2)}) collective-permute-start(bf16[2,256,512]{2,1,0:T(8,128)(2,1)} %slice.654), channel_id=1, source_target_pairs={{0,2},{1,3},{2,0},{3,1},{4,6},{5,7},{6,4},{7,5},{8,10},{9,11},{10,... | collective-permute-start | bytes 1572872 | tf_op jit(solution)/shard_map/ppermute | solution.py:51
  696.0 26.3 %collective-permute-start.114 = (bf16[256,1024]{1,0:T(8,128)(2,1)}, bf16[256,1024]{1,0:T(8,128)(2,1)S(1)}, u32[]{:S(2)}, u32[]{:S(2)}) collective-permute-start(bf16[256,1024]{1,0:T(8,128)(2,1)} %get-tuple-element.505), channel_id=1, source_target_pairs={{0,2},{1,3},{2,0},{3,1},{4,6},{5,7},{6,4},{7,5},{8,10},{9,11},{10,... | collective-permute-start | bytes 1572872 | tf_op jit(solution)/shard_map/ppermute | solution.py:51
  702.1 20.2 %collective-permute-start.113 = (bf16[128,1024]{1,0:T(8,128)(2,1)S(1)}, bf16[128,1024]{1,0:T(8,128)(2,1)S(1)}, u32[]{:S(2)}, u32[]{:S(2)}) collective-permute-start(bf16[128,1024]{1,0:T(8,128)(2,1)S(1)} %copy-done.110), channel_id=1, source_target_pairs={{0,4},{1,5},{2,6},{3,7},{4,0},{5,1},{6,2},{7,3},{8,12},{9,13},{10,... | collective-permute-start | bytes 786440 | tf_op jit(solution)/shard_map/ppermute | solution.py:51
  725.2 19.4 %collective-permute-start.119 = (bf16[256,1024]{1,0:T(8,128)(2,1)S(1)}, bf16[256,1024]{1,0:T(8,128)(2,1)S(1)}, u32[]{:S(2)}, u32[]{:S(2)}) collective-permute-start(bf16[256,1024]{1,0:T(8,128)(2,1)S(1)} %get-tuple-element.513), channel_id=1, source_target_pairs={{0,2},{1,3},{2,0},{3,1},{4,6},{5,7},{6,4},{7,5},{8,10},{9,11},{10,... | collective-permute-start | bytes 1572872 | tf_op jit(solution)/shard_map/ppermute | solution.py:51
  (199 other events, 2696.8 us)

commit v5 on v4

--- a/solution.py
+++ b/solution.py
@@ -396,28 +396,30 @@
         sum_ref[...] = jnp.zeros(sum_ref.shape, F32)
         acc_ref[...] = jnp.zeros(acc_ref.shape, F32)
 
-    for part in range(2):
-        visible, place_k, place_q = tile_visible(
-            place_ref, pair_ref, seg_ref, step, part, per_seq, seq_len
-        )
-
-        @pl.when(visible)
-        def _():
-            keys = kv_ref[:, :HEAD_WIDTH]
-            values = kv_ref[:, HEAD_WIDTH:]
-            queries = stack_heads(q_ref, part)
-            scores = lax.dot_general(keys, queries, COLS, preferred_element_type=F32)
-            mask = tile_mask(row_ref, col_ref, place_k, place_q)
-            scores = jnp.where(mask, scores, NEGATIVE)
-            old_max = max_ref[part]
-            new_max = jnp.maximum(old_max, jnp.max(scores, axis=0, keepdims=True))
-            weights = jnp.where(mask, jnp.exp(scores - new_max), 0.0)
-            factor = jnp.exp(old_max - new_max)
-            max_ref[part] = new_max
-            sum_ref[part] = sum_ref[part] * factor + jnp.sum(weights, axis=0, keepdims=True)
-            acc_ref[part] = acc_ref[part] * factor + lax.dot_general(
-                values, weights.astype(BF16), ROWS, preferred_element_type=F32
+    for sub in range(2):
+        rows = pl.ds(sub * BLOCK, BLOCK)
+        for part in range(2):
+            visible, place_k, place_q = tile_visible(
+                place_ref, pair_ref, seg_ref, 2 * step + sub, part, per_seq, seq_len
             )
+
+            @pl.when(visible)
+            def _():
+                keys = kv_ref[rows, :HEAD_WIDTH]
+                values = kv_ref[rows, HEAD_WIDTH:]
+                queries = stack_heads(q_ref, part)
+                scores = lax.dot_general(keys, queries, COLS, preferred_element_type=F32)
+                mask = tile_mask(row_ref, col_ref, place_k, place_q)
+                scores = jnp.where(mask, scores, NEGATIVE)
+                old_max = max_ref[part]
+                new_max = jnp.maximum(old_max, jnp.max(scores, axis=0, keepdims=True))
+                weights = jnp.where(mask, jnp.exp(scores - new_max), 0.0)
+                factor = jnp.exp(old_max - new_max)
+                max_ref[part] = new_max
+                sum_ref[part] = sum_ref[part] * factor + jnp.sum(weights, axis=0, keepdims=True)
+                acc_ref[part] = acc_ref[part] * factor + lax.dot_general(
+                    values, weights.astype(BF16), ROWS, preferred_element_type=F32
+                )
 
     @pl.when(step == pl.num_programs(0) - 1)
     def _():
@@ -447,32 +449,34 @@
             product = stack_heads(out_ref, part) * stack_heads(do_ref, part).astype(F32)
             delta_ref[part] = jnp.sum(product.T, axis=0, keepdims=True)
 
-    dk_acc[...] = jnp.zeros(dk_acc.shape, F32)
-    dv_acc[...] = jnp.zeros(dv_acc.shape, F32)
-    for part in range(2):
-        visible, place_k, place_q = tile_visible(
-            place_ref, pair_ref, seg_ref, step, part, per_seq, seq_len
-        )
-
-        @pl.when(visible)
-        def _():
-            keys = kv_ref[:, :HEAD_WIDTH]
-            values = kv_ref[:, HEAD_WIDTH:]
-            queries = stack_heads(q_ref, part)
-            grads = stack_heads(do_ref, part)
-            scores = lax.dot_general(keys, queries, COLS, preferred_element_type=F32)
-            mask = tile_mask(row_ref, col_ref, place_k, place_q)
-            probs = jnp.where(mask, jnp.exp(scores - lse_ref[part]), 0.0)
-            grad_probs = lax.dot_general(values, grads, COLS, preferred_element_type=F32)
-            grad_scores = (probs * (grad_probs - delta_ref[part])).astype(BF16)
-            dv_acc[...] += jnp.dot(probs.astype(BF16), grads, preferred_element_type=F32)
-            dk_acc[...] += jnp.dot(grad_scores, queries, preferred_element_type=F32)
-            dq_acc[part] += lax.dot_general(
-                grad_scores, keys, ROWS, preferred_element_type=F32
+    for sub in range(2):
+        key_rows = pl.ds(sub * BLOCK, BLOCK)
+        dk_acc[...] = jnp.zeros(dk_acc.shape, F32)
+        dv_acc[...] = jnp.zeros(dv_acc.shape, F32)
+        for part in range(2):
+            visible, place_k, place_q = tile_visible(
+                place_ref, pair_ref, seg_ref, 2 * step + sub, part, per_seq, seq_len
             )
 
-    dk_ref[...] = dk_acc[...].astype(BF16)
-    dv_ref[...] = dv_acc[...].astype(BF16)
+            @pl.when(visible)
+            def _():
+                keys = kv_ref[key_rows, :HEAD_WIDTH]
+                values = kv_ref[key_rows, HEAD_WIDTH:]
+                queries = stack_heads(q_ref, part)
+                grads = stack_heads(do_ref, part)
+                scores = lax.dot_general(keys, queries, COLS, preferred_element_type=F32)
+                mask = tile_mask(row_ref, col_ref, place_k, place_q)
+                probs = jnp.where(mask, jnp.exp(scores - lse_ref[part]), 0.0)
+                grad_probs = lax.dot_general(values, grads, COLS, preferred_element_type=F32)
+                grad_scores = (probs * (grad_probs - delta_ref[part])).astype(BF16)
+                dv_acc[...] += jnp.dot(probs.astype(BF16), grads, preferred_element_type=F32)
+                dk_acc[...] += jnp.dot(grad_scores, queries, preferred_element_type=F32)
+                dq_acc[part] += lax.dot_general(
+                    grad_scores, keys, ROWS, preferred_element_type=F32
+                )
+
+        dk_ref[key_rows, :] = dk_acc[...].astype(BF16)
+        dv_ref[key_rows, :] = dv_acc[...].astype(BF16)
 
     @pl.when(step == pl.num_programs(0) - 1)
     def _():
@@ -490,7 +494,7 @@
 
 
 def attend(place, pair_order, seg_flat, queries, keys_values, seg_row, seg_col, per_seq):
-    steps = keys_values.shape[0] // BLOCK
+    steps = keys_values.shape[0] // (2 * BLOCK)
     rows, width = queries.shape
     return pl.pallas_call(
         functools.partial(forward_kernel, per_seq),
@@ -499,7 +503,7 @@
             grid=(steps,),
             in_specs=[
                 whole(queries.shape),
-                pl.BlockSpec((BLOCK, 2 * HEAD_WIDTH), lambda step, *refs: (step, 0)),
+                pl.BlockSpec((2 * BLOCK, 2 * HEAD_WIDTH), lambda step, *refs: (step, 0)),
                 whole(seg_row.shape),
                 whole(seg_col.shape),
             ],
@@ -526,7 +530,7 @@
 def attend_back(
     place, pair_order, seg_flat, queries, keys_values, seg_row, seg_col, lse, out, grads, per_seq
 ):
-    steps = keys_values.shape[0] // BLOCK
+    steps = keys_values.shape[0] // (2 * BLOCK)
     rows, width = queries.shape
     return pl.pallas_call(
         functools.partial(backward_kernel, per_seq),
@@ -535,7 +539,7 @@
             grid=(steps,),
             in_specs=[
                 whole(queries.shape),
-                pl.BlockSpec((BLOCK, 2 * HEAD_WIDTH), lambda step, *refs: (step, 0)),
+                pl.BlockSpec((2 * BLOCK, 2 * HEAD_WIDTH), lambda step, *refs: (step, 0)),
                 whole(seg_row.shape),
                 whole(seg_col.shape),
                 whole(lse.shape),
@@ -544,8 +548,8 @@
             ],
             out_specs=[
                 whole((rows, width)),
-                pl.BlockSpec((BLOCK, HEAD_WIDTH), lambda step, *refs: (step, 0)),
-                pl.BlockSpec((BLOCK, HEAD_WIDTH), lambda step, *refs: (step, 0)),
+                pl.BlockSpec((2 * BLOCK, HEAD_WIDTH), lambda step, *refs: (step, 0)),
+                pl.BlockSpec((2 * BLOCK, HEAD_WIDTH), lambda step, *refs: (step, 0)),
             ],
             scratch_shapes=[
                 pltpu.VMEM((2, 1, rows), F32),
@@ -896,8 +900,9 @@
     down = weight_of(0)
     near(block_rows), near(block_rows), high(block_rows)
     flow.go()
+    bulk.settle()
     mid_group = eight(mid_four)
-    grad_hidden = flow.join(jnp.dot(grad_group, down, preferred_element_type=F32))
+    grad_hidden = jnp.dot(grad_group, down, preferred_element_type=F32)
     while bulk.left(None, 1):
         near(block_rows), near(block_rows), high(block_rows)
         flow.go()
@@ -907,6 +912,7 @@
             near(block_rows)
         high(block_rows)
         flow.go()
+    grad_hidden = flow.join(grad_hidden)
     gate_lin = flow.join(jnp.dot(mid_group, gate, preferred_element_type=F32))
     up = weight_of(2)
     up_proj = jnp.dot(mid_group, up, preferred_element_type=F32)

time: 763 us -> 757 us (level)
  waiting for transfers between devices: 273 us -> 292 us
  starting transfers between devices: 130 us -> 119 us
    ppermute x120, waiting for transfers between devices: 273 us -> 292 us  [swap(): return row_major(lax.ppermute(row_major(value), ('head', 'blk'), pairs))]
    ppermute x120, starting transfers between devices: 130 us -> 119 us  [swap(): return row_major(lax.ppermute(row_major(value), ('head', 'blk'), pairs))]
    unnamed x331 -> x309, local copies, waits for them, and re-layouts: 67.5 us -> 69.4 us
  transfers between devices with their start and end apart: 120 -> 120, of which waited for: 54 -> 56; matrix products, arithmetic and copies ran while one was open for 27% -> 29% of each run, Pallas kernels for 4% -> 4%
where the time goes in v5:
time: 757 us; the launch traced here: 749 us
  waiting for transfers between devices  292 us (39%)
  local copies, waits for them, and re-layouts  137 us (18%)
  starting transfers between devices  119 us (16%)
  other arithmetic  89 us (12%)
  matrix products  78 us (10%)
  Pallas kernels  30.7 us (4%)
    ppermute x120, waiting for transfers between devices, swap(): return row_major(lax.ppermute(row_major(value), ('head', 'blk'), pairs))  292 us
    ppermute x120, starting transfers between devices, swap(): return row_major(lax.ppermute(row_major(value), ('head', 'blk'), pairs))  119 us
    unnamed x309, local copies, waits for them, and re-layouts  69.4 us
    convert_element_type x20, other arithmetic, add(): return (a.astype(F32) + b.astype(F32)).astype(dtype)  20.5 us
    dot_general x3, matrix products, ffn_fold(): total = lax.dot_general(lhs, rhs, ROWS, preferred_element_type=F32)  17.4 us
  transfers between devices with their start and end apart: 120, of which 56 were waited for; matrix products, arithmetic and copies ran while one was open for 29% of the time, Pallas kernels for 4%

profile of v5, /device:TPU:0, one launch (start us, length us, event | category | flops | bytes accessed | tf_op | source)
XLA Modules:
  0.0 749.0 jit_solution(8708655938514261546)
XLA Ops:
  10.1 3.0 collective-permute-start.3
  29.4 2.6 collective-permute-start.5
  41.9 13.5 %collective-permute-done.9 = bf16[2,32,64]{2,1,0:T(8,128)(2,1)S(1)} collective-permute-done((bf16[2,32,64]{2,1,0:T(8,128)(2,1)S(1)}, bf16[2,32,64]{2,1,0:T(8,128)(2,1)S(1)}, u32[]{:S(2)}, u32[]{:S(2)}) %collective-permute-start.9) | collective-permute-done | bytes 8224 | tf_op jit(solution)/shard_map/ppermute | solution.py:51
  67.2 3.5 collective-permute-done.10
  70.7 9.5 %collective-permute-done.11 = bf16[256,1024]{1,0:T(8,128)(2,1)} collective-permute-done((bf16[256,1024]{1,0:T(8,128)(2,1)}, bf16[256,1024]{1,0:T(8,128)(2,1)}, u32[]{:S(2)}, u32[]{:S(2)}) %collective-permute-start.11) | collective-permute-done | bytes 524320 | tf_op jit(solution)/shard_map/ppermute | solution.py:51
  80.2 3.7 collective-permute-done.13
  96.0 4.0 collective-permute-done.18
  105.0 2.6 collective-permute-start.23
  109.7 5.1 fusion.129
  114.8 4.9 collective-permute-done.23
  134.6 14.7 %collective-permute-done.25 = bf16[512,512]{1,0:T(8,128)(2,1)} collective-permute-done((bf16[512,512]{1,0:T(8,128)(2,1)}, bf16[512,512]{1,0:T(8,128)(2,1)}, u32[]{:S(2)}, u32[]{:S(2)}) %collective-permute-start.25) | collective-permute-done | bytes 524320 | tf_op jit(solution)/shard_map/ppermute | solution.py:51
  159.6 6.2 collective-permute-done.30
  165.8 5.3 collective-permute-done.31
  171.1 2.8 collective-permute-done.32
  173.9 4.6 collective-permute-done.34
  178.9 2.9 collective-permute-start.37
  192.6 8.2 %collective-permute-done.36 = bf16[2,256,512]{2,1,0:T(8,128)(2,1)S(1)} collective-permute-done((bf16[2,256,512]{2,1,0:T(8,128)(2,1)}, bf16[2,256,512]{2,1,0:T(8,128)(2,1)S(1)}, u32[]{:S(2)}, u32[]{:S(2)}) %collective-permute-start.36) | collective-permute-done | bytes 524320 | tf_op jit(solution)/shard_map/ppermute | solution.py:51
  214.6 10.9 %attend.1 = (bf16[512,512]{1,0:T(8,128)(2,1)}, f32[512,512]{1,0:T(8,128)}, f32[2,1,512]{2,1,0:T(1,128)}) custom-call(s32[2]{0:T(128)} %pad_add_fusion.place_ref, s32[8]{0:T(128)} %pair_ref.3, s32[4096]{0:T(1024)} %bitcast.272, bf16[512,512]{1,0:T(8,128)(2,1)} %maximum_multiply_fusion.q_ref, bf16[4096,512]{1,0:T(8,128)(2,1)} %constant_dynamic-update-slice_fusion.8.kv_ref, ...), custom_call_target="tpu_custom_call" | custom-call | flops 6000000000 | bytes 6000000 | tf_op jit(solution)/shard_map/attend/pallas_call | solution.py:499
  225.5 4.7 collective-permute-done.41
  251.7 7.2 collective-permute-done.49
  270.5 2.9 collective-permute-start.53
  273.4 2.7 pad_maximum_fusion.2
  278.0 5.2 collective-permute-done.51.refs_5_
  291.8 5.0 collective-permute-done.54.refs_1_
  299.9 6.3 collective-permute-done.58
  311.6 2.9 assemble.2.refs_0_
  334.3 2.8 collective-permute-done.66
  338.0 6.3 fusion.156
  344.3 4.3 assemble.3
  348.6 7.7 %fusion.155 = f32[1024,1024]{1,0:T(8,128)S(1)} fusion(bf16[1024,2048]{1,0:T(8,128)(2,1)} %assemble.3, bf16[2048,1024]{1,0:T(8,128)(2,1)} %constant_dynamic-update-slice_fusion.16), kind=kOutput, calls=%fused_computation.440 | convolution fusion | flops 4294967296 | bytes 12582912 | tf_op jit(solution)/shard_map/dot_general | solution.py:916
  356.4 7.4 multiply_convert_fusion.2
  363.8 4.5 fusion.157
  368.3 7.5 add_convert_fusion
  377.5 7.4 convolution_convert_fusion.2
  386.2 2.8 fusion.4
  394.3 4.9 convolution_convert_fusion.1
  399.3 8.5 %convolution_convert_fusion.3 = bf16[1024,2048]{1,0:T(8,128)(2,1)S(1)} fusion(bf16[1024,1024]{1,0:T(8,128)(2,1)S(1)} %copy-done.129, bf16[2048,1024]{1,0:T(8,128)(2,1)} %constant_dynamic-update-slice_fusion.28), kind=kOutput, calls=%fused_computation.18 | convolution fusion | flops 4297064448 | bytes 10485760 | tf_op jit(solution)/shard_map/dot_general | solution.py:960
  416.3 5.1 convolution_convert_fusion
  439.7 3.0 fusion.3
  450.4 11.0 %collective-permute-done.77 = bf16[128,1024]{1,0:T(8,128)(2,1)S(1)} collective-permute-done((bf16[128,1024]{1,0:T(8,128)(2,1)S(1)}, bf16[128,1024]{1,0:T(8,128)(2,1)S(1)}, u32[]{:S(2)}, u32[]{:S(2)}) %collective-permute-start.77) | collective-permute-done | bytes 262176 | tf_op jit(solution)/shard_map/ppermute | solution.py:51
  466.2 3.0 convolution_convert_fusion.7
  474.9 12.7 %attend_back.1 = (bf16[512,512]{1,0:T(8,128)(2,1)}, bf16[4096,256]{1,0:T(8,128)(2,1)}, bf16[4096,256]{1,0:T(8,128)(2,1)}) custom-call(s32[2]{0:T(128)} %pad_add_fusion.place_ref, s32[8]{0:T(128)} %pair_ref.3, s32[4096]{0:T(1024)} %bitcast.273, bf16[512,512]{1,0:T(8,128)(2,1)} %maximum_multiply_fusion.q_ref, ...), custom_call_target="tpu_custom_call" | custom-call | flops 16000000000 | bytes 12000000 | tf_op jit(solution)/shard_map/attend_back/pallas_call | solution.py:535
  487.6 12.7 %collective-permute-done.83 = bf16[256,1024]{1,0:T(8,128)(2,1)} collective-permute-done((bf16[256,1024]{1,0:T(8,128)(2,1)}, bf16[256,1024]{1,0:T(8,128)(2,1)}, u32[]{:S(2)}, u32[]{:S(2)}) %collective-permute-start.83) | collective-permute-done | bytes 524320 | tf_op jit(solution)/shard_map/ppermute | solution.py:51
  500.3 4.0 collective-permute-done.81
  515.2 19.3 %collective-permute-done.86 = bf16[256,1024]{1,0:T(8,128)(2,1)S(1)} collective-permute-done((bf16[256,1024]{1,0:T(8,128)(2,1)S(1)}, bf16[256,1024]{1,0:T(8,128)(2,1)S(1)}, u32[]{:S(2)}, u32[]{:S(2)}) %collective-permute-start.86) | collective-permute-done | bytes 524320 | tf_op jit(solution)/shard_map/ppermute | solution.py:51
  542.7 20.7 %collective-permute-done.87 = bf16[2,512,256]{2,1,0:T(8,128)(2,1)S(1)} collective-permute-done((bf16[2,512,256]{2,1,0:T(8,128)(2,1)S(1)}, bf16[2,512,256]{2,1,0:T(8,128)(2,1)S(1)}, u32[]{:S(2)}, u32[]{:S(2)}) %collective-permute-start.87) | collective-permute-done | bytes 524320 | tf_op jit(solution)/shard_map/ppermute | solution.py:51
  575.2 2.8 select_dynamic-update-slice_fusion
  578.0 11.1 %collective-permute-done.91 = bf16[1,512,256]{2,1,0:T(8,128)(2,1)S(1)} collective-permute-done((bf16[1,512,256]{2,1,0:T(8,128)(2,1)S(1)}, bf16[1,512,256]{2,1,0:T(8,128)(2,1)S(1)}, u32[]{:S(2)}, u32[]{:S(2)}) %collective-permute-start.91) | collective-permute-done | bytes 262176 | tf_op jit(solution)/shard_map/ppermute | solution.py:51
  589.1 6.8 collective-permute-done.94
  598.6 3.0 collective-permute-start.96
  601.8 2.8 select_dynamic-update-slice_fusion.2
  607.3 10.6 %collective-permute-done.96 = bf16[1,512,256]{2,1,0:T(8,128)(2,1)S(1)} collective-permute-done((bf16[1,512,256]{2,1,0:T(8,128)(2,1)S(1)}, bf16[1,512,256]{2,1,0:T(8,128)(2,1)S(1)}, u32[]{:S(2)}, u32[]{:S(2)}) %collective-permute-start.96) | collective-permute-done | bytes 262176 | tf_op jit(solution)/shard_map/ppermute | solution.py:51
  617.9 8.4 %collective-permute-done.99 = bf16[128,1024]{1,0:T(8,128)(2,1)S(1)} collective-permute-done((bf16[128,1024]{1,0:T(8,128)(2,1)S(1)}, bf16[128,1024]{1,0:T(8,128)(2,1)S(1)}, u32[]{:S(2)}, u32[]{:S(2)}) %collective-permute-start.99) | collective-permute-done | bytes 262176 | tf_op jit(solution)/shard_map/ppermute | solution.py:51
  647.8 3.1 reshape.625
  650.9 7.6 %collective-permute-done.107 = bf16[1,256,512]{2,1,0:T(8,128)(2,1)} collective-permute-done((bf16[1,256,512]{2,1,0:T(8,128)(2,1)}, bf16[1,256,512]{2,1,0:T(8,128)(2,1)}, u32[]{:S(2)}, u32[]{:S(2)}) %collective-permute-start.107) | collective-permute-done | bytes 262176 | tf_op jit(solution)/shard_map/ppermute | solution.py:51
  664.7 2.8 fusion.7
  671.3 2.9 collective-permute-start.110
  685.6 2.7 collective-permute-done.110
  690.4 3.7 collective-permute-start.114
  698.5 13.9 %collective-permute-done.112 = bf16[1,256,512]{2,1,0:T(8,128)(2,1)S(1)} collective-permute-done((bf16[1,256,512]{2,1,0:T(8,128)(2,1)S(1)}, bf16[1,256,512]{2,1,0:T(8,128)(2,1)S(1)}, u32[]{:S(2)}, u32[]{:S(2)}) %collective-permute-start.112) | collective-permute-done | bytes 262176 | tf_op jit(solution)/shard_map/ppermute | solution.py:51
  712.4 7.3 collective-permute-done.113
  728.1 4.5 collective-permute-done.116
  732.7 3.8 collective-permute-done.117
  737.5 5.8 collective-permute-done.119
  (730 shorter events, 341.3 us)
Async XLA Ops:
  29.4 26.0 %collective-permute-start.5 = (bf16[256,1024]{1,0:T(8,128)(2,1)}, bf16[256,1024]{1,0:T(8,128)(2,1)}, u32[]{:S(2)}, u32[]{:S(2)}) collective-permute-start(bf16[256,1024]{1,0:T(8,128)(2,1)} %get-tuple-element.277), channel_id=1, source_target_pairs={{0,4},{1,5},{2,6},{3,7},{4,0},{5,1},{6,2},{7,3},{8,12},{9,13},{10,... | collective-permute-start | bytes 1572872 | tf_op jit(solution)/shard_map/ppermute | solution.py:51
  32.0 23.4 %collective-permute-start.6 = (bf16[256,1024]{1,0:T(8,128)(2,1)}, bf16[256,1024]{1,0:T(8,128)(2,1)}, u32[]{:S(2)}, u32[]{:S(2)}) collective-permute-start(bf16[256,1024]{1,0:T(8,128)(2,1)} %get-tuple-element.277), channel_id=1, source_target_pairs={{0,2},{1,3},{2,0},{3,1},{4,6},{5,7},{6,4},{7,5},{8,10},{9,11},{10,... | collective-permute-start | bytes 1572872 | tf_op jit(solution)/shard_map/ppermute | solution.py:51
  33.8 21.6 %collective-permute-start.7 = (bf16[256,1024]{1,0:T(8,128)(2,1)}, bf16[256,1024]{1,0:T(8,128)(2,1)}, u32[]{:S(2)}, u32[]{:S(2)}) collective-permute-start(bf16[256,1024]{1,0:T(8,128)(2,1)} %get-tuple-element.277), channel_id=1, source_target_pairs={{0,16},{1,17},{2,18},{3,19},{4,20},{5,21},{6,22},{7,23},{8,24},{9,... | collective-permute-start | bytes 1572872 | tf_op jit(solution)/shard_map/ppermute | solution.py:51
  35.3 20.1 %collective-permute-start.8 = (bf16[128,2048]{1,0:T(8,128)(2,1)S(1)}, bf16[128,2048]{1,0:T(8,128)(2,1)}, u32[]{:S(2)}, u32[]{:S(2)}) collective-permute-start(bf16[128,2048]{1,0:T(8,128)(2,1)S(1)} %reshape.604), channel_id=1, source_target_pairs={{0,1},{1,0},{2,3},{3,2},{4,5},{5,4},{6,7},{7,6},{8,9},{9,8},{10,11... | collective-permute-start | bytes 1572872 | tf_op jit(solution)/shard_map/ppermute | solution.py:51
  57.0 23.2 %collective-permute-start.11 = (bf16[256,1024]{1,0:T(8,128)(2,1)}, bf16[256,1024]{1,0:T(8,128)(2,1)}, u32[]{:S(2)}, u32[]{:S(2)}) collective-permute-start(bf16[256,1024]{1,0:T(8,128)(2,1)} %collective-permute-done.5), channel_id=1, source_target_pairs={{0,2},{1,3},{2,0},{3,1},{4,6},{5,7},{6,4},{7,5},{8,10},{9,11},{10,... | collective-permute-start | bytes 1572872 | tf_op jit(solution)/shard_map/ppermute | solution.py:51
  58.7 21.5 %collective-permute-start.12 = (bf16[256,1024]{1,0:T(8,128)(2,1)}, bf16[256,1024]{1,0:T(8,128)(2,1)}, u32[]{:S(2)}, u32[]{:S(2)}) collective-permute-start(bf16[256,1024]{1,0:T(8,128)(2,1)} %collective-permute-done.5), channel_id=1, source_target_pairs={{0,16},{1,17},{2,18},{3,19},{4,20},{5,21},{6,22},{7,23},{8,24},{9,... | collective-permute-start | bytes 1572872 | tf_op jit(solution)/shard_map/ppermute | solution.py:51
  59.2 24.7 %collective-permute-start.13 = (bf16[256,1024]{1,0:T(8,128)(2,1)}, bf16[256,1024]{1,0:T(8,128)(2,1)}, u32[]{:S(2)}, u32[]{:S(2)}) collective-permute-start(bf16[256,1024]{1,0:T(8,128)(2,1)} %get-tuple-element.306), channel_id=1, source_target_pairs={{0,4},{1,5},{2,6},{3,7},{4,0},{5,1},{6,2},{7,3},{8,12},{9,13},{10,... | collective-permute-start | bytes 1572872 | tf_op jit(solution)/shard_map/ppermute | solution.py:51
  102.7 19.0 %collective-permute-start.21 = (bf16[256,1024]{1,0:T(8,128)(2,1)}, bf16[256,1024]{1,0:T(8,128)(2,1)}, u32[]{:S(2)}, u32[]{:S(2)}) collective-permute-start(bf16[256,1024]{1,0:T(8,128)(2,1)} %constant_dynamic-slice_fusion), channel_id=1, source_target_pairs={{0,2},{1,3},{2,0},{3,1},{4,6},{5,7},{6,4},{7,5},{8,10},{9,11},{10,... | collective-permute-start | bytes 1572872 | tf_op jit(solution)/shard_map/ppermute | solution.py:51
  103.0 18.6 %collective-permute-start.22 = (bf16[256,1024]{1,0:T(8,128)(2,1)}, bf16[256,1024]{1,0:T(8,128)(2,1)}, u32[]{:S(2)}, u32[]{:S(2)}) collective-permute-start(bf16[256,1024]{1,0:T(8,128)(2,1)} %get-tuple-element.306), channel_id=1, source_target_pairs={{0,1},{1,0},{2,3},{3,2},{4,5},{5,4},{6,7},{7,6},{8,9},{9,8},{10,11... | collective-permute-start | bytes 1572872 | tf_op jit(solution)/shard_map/ppermute | solution.py:51
  124.8 24.5 %collective-permute-start.25 = (bf16[512,512]{1,0:T(8,128)(2,1)}, bf16[512,512]{1,0:T(8,128)(2,1)}, u32[]{:S(2)}, u32[]{:S(2)}) collective-permute-start(bf16[512,512]{1,0:T(8,128)(2,1)} %get-tuple-element.319), channel_id=1, source_target_pairs={{0,4},{1,5},{2,6},{3,7},{4,0},{5,1},{6,2},{7,3},{8,12},{9,13},{10,... | collective-permute-start | bytes 1572872 | tf_op jit(solution)/shard_map/ppermute | solution.py:51
  126.2 23.1 %collective-permute-start.26 = (bf16[512,512]{1,0:T(8,128)(2,1)}, bf16[512,512]{1,0:T(8,128)(2,1)}, u32[]{:S(2)}, u32[]{:S(2)}) collective-permute-start(bf16[512,512]{1,0:T(8,128)(2,1)} %get-tuple-element.319), channel_id=1, source_target_pairs={{0,2},{1,3},{2,0},{3,1},{4,6},{5,7},{6,4},{7,5},{8,10},{9,11},{10,... | collective-permute-start | bytes 1572872 | tf_op jit(solution)/shard_map/ppermute | solution.py:51
  127.7 21.6 %collective-permute-start.27 = (bf16[512,512]{1,0:T(8,128)(2,1)}, bf16[512,512]{1,0:T(8,128)(2,1)}, u32[]{:S(2)}, u32[]{:S(2)}) collective-permute-start(bf16[512,512]{1,0:T(8,128)(2,1)} %get-tuple-element.319), channel_id=1, source_target_pairs={{0,16},{1,17},{2,18},{3,19},{4,20},{5,21},{6,22},{7,23},{8,24},{9,... | collective-permute-start | bytes 1572872 | tf_op jit(solution)/shard_map/ppermute | solution.py:51
  128.2 21.1 %collective-permute-start.28 = (bf16[256,1024]{1,0:T(8,128)(2,1)S(1)}, bf16[256,1024]{1,0:T(8,128)(2,1)}, u32[]{:S(2)}, u32[]{:S(2)}) collective-permute-start(bf16[256,1024]{1,0:T(8,128)(2,1)S(1)} %get-tuple-element.331), channel_id=1, source_target_pairs={{0,1},{1,0},{2,3},{3,2},{4,5},{5,4},{6,7},{7,6},{8,9},{9,8},{10,11... | collective-permute-start | bytes 1572872 | tf_op jit(solution)/shard_map/ppermute | solution.py:51
  129.7 21.0 %collective-permute-start.29 = (bf16[256,1024]{1,0:T(8,128)(2,1)S(1)}, bf16[256,1024]{1,0:T(8,128)(2,1)}, u32[]{:S(2)}, u32[]{:S(2)}) collective-permute-start(bf16[256,1024]{1,0:T(8,128)(2,1)S(1)} %copy-done.33), channel_id=1, source_target_pairs={{0,1},{1,0},{2,3},{3,2},{4,5},{5,4},{6,7},{7,6},{8,9},{9,8},{10,11... | collective-permute-start | bytes 1572872 | tf_op jit(solution)/shard_map/ppermute | solution.py:51
  152.3 18.8 %collective-permute-start.31 = (bf16[512,512]{1,0:T(8,128)(2,1)}, bf16[512,512]{1,0:T(8,128)(2,1)}, u32[]{:S(2)}, u32[]{:S(2)}) collective-permute-start(bf16[512,512]{1,0:T(8,128)(2,1)} %collective-permute-done.25), channel_id=1, source_target_pairs={{0,2},{1,3},{2,0},{3,1},{4,6},{5,7},{6,4},{7,5},{8,10},{9,11},{10,... | collective-permute-start | bytes 1572872 | tf_op jit(solution)/shard_map/ppermute | solution.py:51
  153.1 20.8 %collective-permute-start.32 = (bf16[512,512]{1,0:T(8,128)(2,1)}, bf16[512,512]{1,0:T(8,128)(2,1)S(1)}, u32[]{:S(2)}, u32[]{:S(2)}) collective-permute-start(bf16[512,512]{1,0:T(8,128)(2,1)} %collective-permute-done.25), channel_id=1, source_target_pairs={{0,16},{1,17},{2,18},{3,19},{4,20},{5,21},{6,22},{7,23},{8,24},{9,... | collective-permute-start | bytes 1572872 | tf_op jit(solution)/shard_map/ppermute | solution.py:51
  153.4 20.5 %collective-permute-start.33 = (bf16[256,1024]{1,0:T(8,128)(2,1)S(1)}, bf16[256,1024]{1,0:T(8,128)(2,1)S(1)}, u32[]{:S(2)}, u32[]{:S(2)}) collective-permute-start(bf16[256,1024]{1,0:T(8,128)(2,1)S(1)} %get-tuple-element.349), channel_id=1, source_target_pairs={{0,1},{1,0},{2,3},{3,2},{4,5},{5,4},{6,7},{7,6},{8,9},{9,8},{10,11... | collective-permute-start | bytes 1572872 | tf_op jit(solution)/shard_map/ppermute | solution.py:51
  155.0 23.6 %collective-permute-start.34 = (bf16[256,1024]{1,0:T(8,128)(2,1)S(1)}, bf16[256,1024]{1,0:T(8,128)(2,1)}, u32[]{:S(2)}, u32[]{:S(2)}) collective-permute-start(bf16[256,1024]{1,0:T(8,128)(2,1)S(1)} %get-tuple-element.331), channel_id=1, source_target_pairs={{0,4},{1,5},{2,6},{3,7},{4,0},{5,1},{6,2},{7,3},{8,12},{9,13},{10,... | collective-permute-start | bytes 1572872 | tf_op jit(solution)/shard_map/ppermute | solution.py:51
  178.9 21.9 %collective-permute-start.36 = (bf16[2,256,512]{2,1,0:T(8,128)(2,1)}, bf16[2,256,512]{2,1,0:T(8,128)(2,1)S(1)}, u32[]{:S(2)}, u32[]{:S(2)}) collective-permute-start(bf16[2,256,512]{2,1,0:T(8,128)(2,1)} %pad_maximum_fusion.14), channel_id=1, source_target_pairs={{0,2},{1,3},{2,0},{3,1},{4,6},{5,7},{6,4},{7,5},{8,10},{9,11},{10,... | collective-permute-start | bytes 1572872 | tf_op jit(solution)/shard_map/ppermute | solution.py:51
  178.9 21.9 %collective-permute-start.37 = (bf16[256,1024]{1,0:T(8,128)(2,1)S(1)}, bf16[256,1024]{1,0:T(8,128)(2,1)}, u32[]{:S(2)}, u32[]{:S(2)}) collective-permute-start(bf16[256,1024]{1,0:T(8,128)(2,1)S(1)} %copy-done.33), channel_id=1, source_target_pairs={{0,4},{1,5},{2,6},{3,7},{4,0},{5,1},{6,2},{7,3},{8,12},{9,13},{10,... | collective-permute-start | bytes 1572872 | tf_op jit(solution)/shard_map/ppermute | solution.py:51
  181.8 19.0 %collective-permute-start.38 = (bf16[256,1024]{1,0:T(8,128)(2,1)}, bf16[256,1024]{1,0:T(8,128)(2,1)}, u32[]{:S(2)}, u32[]{:S(2)}) collective-permute-start(bf16[256,1024]{1,0:T(8,128)(2,1)} %get-tuple-element.340), channel_id=1, source_target_pairs={{0,1},{1,0},{2,3},{3,2},{4,5},{5,4},{6,7},{7,6},{8,9},{9,8},{10,11... | collective-permute-start | bytes 1572872 | tf_op jit(solution)/shard_map/ppermute | solution.py:51
  182.1 20.9 %collective-permute-start.39 = (bf16[256,1024]{1,0:T(8,128)(2,1)}, bf16[256,1024]{1,0:T(8,128)(2,1)}, u32[]{:S(2)}, u32[]{:S(2)}) collective-permute-start(bf16[256,1024]{1,0:T(8,128)(2,1)} %get-tuple-element.341), channel_id=1, source_target_pairs={{0,1},{1,0},{2,3},{3,2},{4,5},{5,4},{6,7},{7,6},{8,9},{9,8},{10,11... | collective-permute-start | bytes 1572872 | tf_op jit(solution)/shard_map/ppermute | solution.py:51
  204.1 27.5 %collective-permute-start.40 = (bf16[4,256,512]{2,1,0:T(8,128)(2,1)}, bf16[4,256,512]{2,1,0:T(8,128)(2,1)}, u32[]{:S(2)}, u32[]{:S(2)}) collective-permute-start(bf16[4,256,512]{2,1,0:T(8,128)(2,1)} %pad_maximum_fusion.6), channel_id=1, source_target_pairs={{0,16},{1,17},{2,18},{3,19},{4,20},{5,21},{6,22},{7,23},{8,24},{9,... | collective-permute-start | bytes 3145736 | tf_op jit(solution)/shard_map/ppermute | solution.py:51
  209.4 20.9 %collective-permute-start.41 = (bf16[256,1024]{1,0:T(8,128)(2,1)S(1)}, bf16[256,1024]{1,0:T(8,128)(2,1)}, u32[]{:S(2)}, u32[]{:S(2)}) collective-permute-start(bf16[256,1024]{1,0:T(8,128)(2,1)S(1)} %get-tuple-element.349), channel_id=1, source_target_pairs={{0,4},{1,5},{2,6},{3,7},{4,0},{5,1},{6,2},{7,3},{8,12},{9,13},{10,... | collective-permute-start | bytes 1572872 | tf_op jit(solution)/shard_map/ppermute | solution.py:51
  209.6 20.6 %collective-permute-start.42 = (bf16[256,1024]{1,0:T(8,128)(2,1)}, bf16[256,1024]{1,0:T(8,128)(2,1)}, u32[]{:S(2)}, u32[]{:S(2)}) collective-permute-start(bf16[256,1024]{1,0:T(8,128)(2,1)} %collective-permute-done.13), channel_id=1, source_target_pairs={{0,1},{1,0},{2,3},{3,2},{4,5},{5,4},{6,7},{7,6},{8,9},{9,8},{10,11... | collective-permute-start | bytes 1572872 | tf_op jit(solution)/shard_map/ppermute | solution.py:51
  209.9 20.6 %collective-permute-start.43 = (bf16[256,1024]{1,0:T(8,128)(2,1)}, bf16[256,1024]{1,0:T(8,128)(2,1)}, u32[]{:S(2)}, u32[]{:S(2)}) collective-permute-start(bf16[256,1024]{1,0:T(8,128)(2,1)} %collective-permute-done.34), channel_id=1, source_target_pairs={{0,1},{1,0},{2,3},{3,2},{4,5},{5,4},{6,7},{7,6},{8,9},{9,8},{10,11... | collective-permute-start | bytes 1572872 | tf_op jit(solution)/shard_map/ppermute | solution.py:51
  211.7 19.9 %collective-permute-start.44 = (bf16[128,2048]{1,0:T(8,128)(2,1)S(1)}, bf16[128,2048]{1,0:T(8,128)(2,1)S(1)}, u32[]{:S(2)}, u32[]{:S(2)}) collective-permute-start(bf16[128,2048]{1,0:T(8,128)(2,1)S(1)} %reshape.608), channel_id=1, source_target_pairs={{0,2},{1,3},{2,0},{3,1},{4,6},{5,7},{6,4},{7,5},{8,10},{9,11},{10,... | collective-permute-start | bytes 1572872 | tf_op jit(solution)/shard_map/ppermute | solution.py:51
  238.0 21.7 %collective-permute-start.45 = (bf16[128,2048]{1,0:T(8,128)(2,1)S(1)}, bf16[128,2048]{1,0:T(8,128)(2,1)S(1)}, u32[]{:S(2)}, u32[]{:S(2)}) collective-permute-start(bf16[128,2048]{1,0:T(8,128)(2,1)S(1)} %get-tuple-element.582), channel_id=1, source_target_pairs={{0,8},{1,9},{2,10},{3,11},{4,12},{5,13},{6,14},{7,15},{8,0},{9,1},... | collective-permute-start | bytes 1572872 | tf_op jit(solution)/shard_map/ppermute | solution.py:51
  238.7 20.2 %collective-permute-start.47 = (bf16[128,2048]{1,0:T(8,128)(2,1)S(1)}, bf16[128,2048]{1,0:T(8,128)(2,1)S(1)}, u32[]{:S(2)}, u32[]{:S(2)}) collective-permute-start(bf16[128,2048]{1,0:T(8,128)(2,1)S(1)} %fusion.25), channel_id=1, source_target_pairs={{0,1},{1,0},{2,3},{3,2},{4,5},{5,4},{6,7},{7,6},{8,9},{9,8},{10,11... | collective-permute-start | bytes 1572872 | tf_op jit(solution)/shard_map/ppermute | solution.py:51
  239.1 19.7 %collective-permute-start.48 = (bf16[128,2048]{1,0:T(8,128)(2,1)S(1)}, bf16[128,2048]{1,0:T(8,128)(2,1)S(1)}, u32[]{:S(2)}, u32[]{:S(2)}) collective-permute-start(bf16[128,2048]{1,0:T(8,128)(2,1)S(1)} %collective-permute-done.44), channel_id=1, source_target_pairs={{0,16},{1,17},{2,18},{3,19},{4,20},{5,21},{6,22},{7,23},{8,24},{9,... | collective-permute-start | bytes 1572872 | tf_op jit(solution)/shard_map/ppermute | solution.py:51
  276.1 61.7 %collective-permute-start.63 = (bf16[512,2048]{1,0:T(8,128)(2,1)}, bf16[512,2048]{1,0:T(8,128)(2,1)S(1)}, u32[]{:S(2)}, u32[]{:S(2)}) collective-permute-start(bf16[512,2048]{1,0:T(8,128)(2,1)} %pad_maximum_fusion.2), channel_id=1, source_target_pairs={{0,8},{1,9},{2,10},{3,11},{4,12},{5,13},{6,14},{7,15},{8,0},{9,1},... | collective-permute-start | bytes 6291464 | tf_op jit(solution)/shard_map/ppermute | solution.py:51
  314.6 29.7 %collective-permute-start.59 = (bf16[512,2048]{1,0:T(8,128)(2,1)}, bf16[512,2048]{1,0:T(8,128)(2,1)}, u32[]{:S(2)}, u32[]{:S(2)}) collective-permute-start(bf16[512,2048]{1,0:T(8,128)(2,1)} %assemble.2.refs_0_), channel_id=1, source_target_pairs={{0,8},{1,9},{2,10},{3,11},{4,12},{5,13},{6,14},{7,15},{8,0},{9,1},... | collective-permute-start | bytes 6291464 | tf_op jit(solution)/shard_map/ppermute | solution.py:51
  389.2 22.4 %collective-permute-start.69 = (bf16[2,128,1024]{2,1,0:T(8,128)(2,1)S(1)}, bf16[2,128,1024]{2,1,0:T(8,128)(2,1)S(1)}, u32[]{:S(2)}, u32[]{:S(2)}) collective-permute-start(bf16[2,128,1024]{2,1,0:T(8,128)(2,1)S(1)} %slice_bitcast_fusion.11), channel_id=1, source_target_pairs={{0,2},{1,3},{2,0},{3,1},{4,6},{5,7},{6,4},{7,5},{8,10},{9,11},{10,... | collective-permute-start | bytes 1572872 | tf_op jit(solution)/shard_map/ppermute | solution.py:51
  391.8 19.8 %collective-permute-start.70 = (bf16[2,128,1024]{2,1,0:T(8,128)(2,1)S(1)}, bf16[2,128,1024]{2,1,0:T(8,128)(2,1)S(1)}, u32[]{:S(2)}, u32[]{:S(2)}) collective-permute-start(bf16[2,128,1024]{2,1,0:T(8,128)(2,1)S(1)} %slice_bitcast_fusion.10), channel_id=1, source_target_pairs={{0,16},{1,17},{2,18},{3,19},{4,20},{5,21},{6,22},{7,23},{8,24},{9,... | collective-permute-start | bytes 1572872 | tf_op jit(solution)/shard_map/ppermute | solution.py:51
  392.6 19.0 %collective-permute-start.71 = (bf16[256,1024]{1,0:T(8,128)(2,1)S(1)}, bf16[256,1024]{1,0:T(8,128)(2,1)S(1)}, u32[]{:S(2)}, u32[]{:S(2)}) collective-permute-start(bf16[256,1024]{1,0:T(8,128)(2,1)S(1)} %get-tuple-element.412), channel_id=1, source_target_pairs={{0,1},{1,0},{2,3},{3,2},{4,5},{5,4},{6,7},{7,6},{8,9},{9,8},{10,11... | collective-permute-start | bytes 1572872 | tf_op jit(solution)/shard_map/ppermute | solution.py:51
  410.1 29.7 %collective-permute-start.68 = (bf16[2,2,128,2048]{3,2,1,0:T(8,128)(2,1)}, bf16[2,2,128,2048]{3,2,1,0:T(8,128)(2,1)}, u32[]{:S(2)}, u32[]{:S(2)}) collective-permute-start(bf16[2,2,128,2048]{3,2,1,0:T(8,128)(2,1)} %bitcast.39), channel_id=1, source_target_pairs={{0,8},{1,9},{2,10},{3,11},{4,12},{5,13},{6,14},{7,15},{8,0},{9,1},... | collective-permute-start | bytes 6291464 | tf_op jit(solution)/shard_map/ppermute | solution.py:51
  438.8 22.6 %collective-permute-start.79 = (bf16[128,2048]{1,0:T(8,128)(2,1)S(1)}, bf16[128,2048]{1,0:T(8,128)(2,1)}, u32[]{:S(2)}, u32[]{:S(2)}) collective-permute-start(bf16[128,2048]{1,0:T(8,128)(2,1)S(1)} %reshape.623), channel_id=1, source_target_pairs={{0,8},{1,9},{2,10},{3,11},{4,12},{5,13},{6,14},{7,15},{8,0},{9,1},... | collective-permute-start | bytes 1572872 | tf_op jit(solution)/shard_map/ppermute | solution.py:51
  473.0 31.3 %collective-permute-start.81 = (bf16[4,256,640]{2,1,0:T(8,128)(2,1)}, bf16[4,256,640]{2,1,0:T(8,128)(2,1)}, u32[]{:S(2)}, u32[]{:S(2)}) collective-permute-start(bf16[4,256,640]{2,1,0:T(8,128)(2,1)} %bitcast.58), channel_id=1, source_target_pairs={{0,16},{1,17},{2,18},{3,19},{4,20},{5,21},{6,22},{7,23},{8,24},{9,... | collective-permute-start | bytes 3932168 | tf_op jit(solution)/shard_map/ppermute | solution.py:51
  473.9 26.4 %collective-permute-start.82 = (bf16[512,1024]{1,0:T(8,128)(2,1)}, bf16[512,1024]{1,0:T(8,128)(2,1)}, u32[]{:S(2)}, u32[]{:S(2)}) collective-permute-start(bf16[512,1024]{1,0:T(8,128)(2,1)} %get-tuple-element.437), channel_id=1, source_target_pairs={{0,1},{1,0},{2,3},{3,2},{4,5},{5,4},{6,7},{7,6},{8,9},{9,8},{10,11... | collective-permute-start | bytes 3145736 | tf_op jit(solution)/shard_map/ppermute | solution.py:51
  474.9 25.4 %collective-permute-start.83 = (bf16[256,1024]{1,0:T(8,128)(2,1)}, bf16[256,1024]{1,0:T(8,128)(2,1)}, u32[]{:S(2)}, u32[]{:S(2)}) collective-permute-start(bf16[256,1024]{1,0:T(8,128)(2,1)} %add_convert_fusion.11), channel_id=1, source_target_pairs={{0,4},{1,5},{2,6},{3,7},{4,0},{5,1},{6,2},{7,3},{8,12},{9,13},{10,... | collective-permute-start | bytes 1572872 | tf_op jit(solution)/shard_map/ppermute | solution.py:51
  508.0 26.5 %collective-permute-start.84 = (bf16[4,512,256]{2,1,0:T(8,128)(2,1)S(1)}, bf16[4,512,256]{2,1,0:T(8,128)(2,1)S(1)}, u32[]{:S(2)}, u32[]{:S(2)}) collective-permute-start(bf16[4,512,256]{2,1,0:T(8,128)(2,1)S(1)} %bitcast.260), channel_id=1, source_target_pairs={{0,16},{1,17},{2,18},{3,19},{4,20},{5,21},{6,22},{7,23},{8,24},{9,... | collective-permute-start | bytes 3145736 | tf_op jit(solution)/shard_map/ppermute | solution.py:51
  509.0 25.5 %collective-permute-start.85 = (bf16[512,1024]{1,0:T(8,128)(2,1)S(1)}, bf16[512,1024]{1,0:T(8,128)(2,1)S(1)}, u32[]{:S(2)}, u32[]{:S(2)}) collective-permute-start(bf16[512,1024]{1,0:T(8,128)(2,1)S(1)} %copy-done.40), channel_id=1, source_target_pairs={{0,1},{1,0},{2,3},{3,2},{4,5},{5,4},{6,7},{7,6},{8,9},{9,8},{10,11... | collective-permute-start | bytes 3145736 | tf_op jit(solution)/shard_map/ppermute | solution.py:51
  510.2 24.3 %collective-permute-start.86 = (bf16[256,1024]{1,0:T(8,128)(2,1)S(1)}, bf16[256,1024]{1,0:T(8,128)(2,1)S(1)}, u32[]{:S(2)}, u32[]{:S(2)}) collective-permute-start(bf16[256,1024]{1,0:T(8,128)(2,1)S(1)} %get-tuple-element.452), channel_id=1, source_target_pairs={{0,4},{1,5},{2,6},{3,7},{4,0},{5,1},{6,2},{7,3},{8,12},{9,13},{10,... | collective-permute-start | bytes 1572872 | tf_op jit(solution)/shard_map/ppermute | solution.py:51
  534.9 30.7 %collective-permute-start.88 = (bf16[4,512,256]{2,1,0:T(8,128)(2,1)S(1)}, bf16[4,512,256]{2,1,0:T(8,128)(2,1)S(1)}, u32[]{:S(2)}, u32[]{:S(2)}) collective-permute-start(bf16[4,512,256]{2,1,0:T(8,128)(2,1)S(1)} %bitcast.259), channel_id=1, source_target_pairs={{0,16},{1,17},{2,18},{3,19},{4,20},{5,21},{6,22},{7,23},{8,24},{9,... | collective-permute-start | bytes 3145736 | tf_op jit(solution)/shard_map/ppermute | solution.py:51
  535.9 29.8 %collective-permute-start.89 = (bf16[512,1024]{1,0:T(8,128)(2,1)S(1)}, bf16[512,1024]{1,0:T(8,128)(2,1)S(1)}, u32[]{:S(2)}, u32[]{:S(2)}) collective-permute-start(bf16[512,1024]{1,0:T(8,128)(2,1)S(1)} %copy-done.39), channel_id=1, source_target_pairs={{0,1},{1,0},{2,3},{3,2},{4,5},{5,4},{6,7},{7,6},{8,9},{9,8},{10,11... | collective-permute-start | bytes 3145736 | tf_op jit(solution)/shard_map/ppermute | solution.py:51
  540.0 23.4 %collective-permute-start.87 = (bf16[2,512,256]{2,1,0:T(8,128)(2,1)S(1)}, bf16[2,512,256]{2,1,0:T(8,128)(2,1)S(1)}, u32[]{:S(2)}, u32[]{:S(2)}) collective-permute-start(bf16[2,512,256]{2,1,0:T(8,128)(2,1)S(1)} %slice.616), channel_id=1, source_target_pairs={{0,2},{1,3},{2,0},{3,1},{4,6},{5,7},{6,4},{7,5},{8,10},{9,11},{10,... | collective-permute-start | bytes 1572872 | tf_op jit(solution)/shard_map/ppermute | solution.py:51
  540.1 25.5 %collective-permute-start.90 = (bf16[256,1024]{1,0:T(8,128)(2,1)S(1)}, bf16[256,1024]{1,0:T(8,128)(2,1)S(1)}, u32[]{:S(2)}, u32[]{:S(2)}) collective-permute-start(bf16[256,1024]{1,0:T(8,128)(2,1)S(1)} %get-tuple-element.459), channel_id=1, source_target_pairs={{0,4},{1,5},{2,6},{3,7},{4,0},{5,1},{6,2},{7,3},{8,12},{9,13},{10,... | collective-permute-start | bytes 1572872 | tf_op jit(solution)/shard_map/ppermute | solution.py:51
  566.1 29.7 %collective-permute-start.93 = (bf16[4,256,512]{2,1,0:T(8,128)(2,1)S(1)}, bf16[4,256,512]{2,1,0:T(8,128)(2,1)S(1)}, u32[]{:S(2)}, u32[]{:S(2)}) collective-permute-start(bf16[4,256,512]{2,1,0:T(8,128)(2,1)S(1)} %bitcast.258), channel_id=1, source_target_pairs={{0,16},{1,17},{2,18},{3,19},{4,20},{5,21},{6,22},{7,23},{8,24},{9,... | collective-permute-start | bytes 3145736 | tf_op jit(solution)/shard_map/ppermute | solution.py:51
  567.1 28.7 %collective-permute-start.95 = (bf16[512,1024]{1,0:T(8,128)(2,1)S(1)}, bf16[512,1024]{1,0:T(8,128)(2,1)S(1)}, u32[]{:S(2)}, u32[]{:S(2)}) collective-permute-start(bf16[512,1024]{1,0:T(8,128)(2,1)S(1)} %copy-done.49), channel_id=1, source_target_pairs={{0,1},{1,0},{2,3},{3,2},{4,5},{5,4},{6,7},{7,6},{8,9},{9,8},{10,11... | collective-permute-start | bytes 3145736 | tf_op jit(solution)/shard_map/ppermute | solution.py:51
  571.3 24.6 %collective-permute-start.92 = (bf16[2,512,256]{2,1,0:T(8,128)(2,1)S(1)}, bf16[2,512,256]{2,1,0:T(8,128)(2,1)S(1)}, u32[]{:S(2)}, u32[]{:S(2)}) collective-permute-start(bf16[2,512,256]{2,1,0:T(8,128)(2,1)S(1)} %slice.622), channel_id=1, source_target_pairs={{0,2},{1,3},{2,0},{3,1},{4,6},{5,7},{6,4},{7,5},{8,10},{9,11},{10,... | collective-permute-start | bytes 1572872 | tf_op jit(solution)/shard_map/ppermute | solution.py:51
  574.5 21.4 %collective-permute-start.94 = (bf16[128,1024]{1,0:T(8,128)(2,1)S(1)}, bf16[128,1024]{1,0:T(8,128)(2,1)S(1)}, u32[]{:S(2)}, u32[]{:S(2)}) collective-permute-start(bf16[128,1024]{1,0:T(8,128)(2,1)S(1)} %get-tuple-element.468), channel_id=1, source_target_pairs={{0,4},{1,5},{2,6},{3,7},{4,0},{5,1},{6,2},{7,3},{8,12},{9,13},{10,... | collective-permute-start | bytes 786440 | tf_op jit(solution)/shard_map/ppermute | solution.py:51
  596.4 29.9 %collective-permute-start.100 = (bf16[128,2048]{1,0:T(8,128)(2,1)S(1)}, bf16[128,2048]{1,0:T(8,128)(2,1)S(1)}, u32[]{:S(2)}, u32[]{:S(2)}) collective-permute-start(bf16[128,2048]{1,0:T(8,128)(2,1)S(1)} %copy-done.70), channel_id=1, source_target_pairs={{0,16},{1,17},{2,18},{3,19},{4,20},{5,21},{6,22},{7,23},{8,24},{9,... | collective-permute-start | bytes 1572872 | tf_op jit(solution)/shard_map/ppermute | solution.py:51
  596.9 29.4 %collective-permute-start.97 = (bf16[2,256,512]{2,1,0:T(8,128)(2,1)S(1)}, bf16[2,256,512]{2,1,0:T(8,128)(2,1)S(1)}, u32[]{:S(2)}, u32[]{:S(2)}) collective-permute-start(bf16[2,256,512]{2,1,0:T(8,128)(2,1)S(1)} %slice.633), channel_id=1, source_target_pairs={{0,2},{1,3},{2,0},{3,1},{4,6},{5,7},{6,4},{7,5},{8,10},{9,11},{10,... | collective-permute-start | bytes 1572872 | tf_op jit(solution)/shard_map/ppermute | solution.py:51
  596.9 29.4 %collective-permute-start.98 = (bf16[256,1024]{1,0:T(8,128)(2,1)S(1)}, bf16[256,1024]{1,0:T(8,128)(2,1)S(1)}, u32[]{:S(2)}, u32[]{:S(2)}) collective-permute-start(bf16[256,1024]{1,0:T(8,128)(2,1)S(1)} %get-tuple-element.477), channel_id=1, source_target_pairs={{0,1},{1,0},{2,3},{3,2},{4,5},{5,4},{6,7},{7,6},{8,9},{9,8},{10,11... | collective-permute-start | bytes 1572872 | tf_op jit(solution)/shard_map/ppermute | solution.py:51
  598.6 19.3 %collective-permute-start.96 = (bf16[1,512,256]{2,1,0:T(8,128)(2,1)S(1)}, bf16[1,512,256]{2,1,0:T(8,128)(2,1)S(1)}, u32[]{:S(2)}, u32[]{:S(2)}) collective-permute-start(bf16[1,512,256]{2,1,0:T(8,128)(2,1)S(1)} %slice.631), channel_id=1, source_target_pairs={{0,4},{1,5},{2,6},{3,7},{4,0},{5,1},{6,2},{7,3},{8,12},{9,13},{10,... | collective-permute-start | bytes 786440 | tf_op jit(solution)/shard_map/ppermute | solution.py:51
  601.6 24.7 %collective-permute-start.99 = (bf16[128,1024]{1,0:T(8,128)(2,1)S(1)}, bf16[128,1024]{1,0:T(8,128)(2,1)S(1)}, u32[]{:S(2)}, u32[]{:S(2)}) collective-permute-start(bf16[128,1024]{1,0:T(8,128)(2,1)S(1)} %get-tuple-element.478), channel_id=1, source_target_pairs={{0,4},{1,5},{2,6},{3,7},{4,0},{5,1},{6,2},{7,3},{8,12},{9,13},{10,... | collective-permute-start | bytes 786440 | tf_op jit(solution)/shard_map/ppermute | solution.py:51
  631.0 43.2 %collective-permute-start.103 = (bf16[128,2048]{1,0:T(8,128)(2,1)}, bf16[128,2048]{1,0:T(8,128)(2,1)}, u32[]{:S(2)}, u32[]{:S(2)}) collective-permute-start(bf16[128,2048]{1,0:T(8,128)(2,1)} %get-tuple-element.570), channel_id=1, source_target_pairs={{0,8},{1,9},{2,10},{3,11},{4,12},{5,13},{6,14},{7,15},{8,0},{9,1},... | collective-permute-start | bytes 1572872 | tf_op jit(solution)/shard_map/ppermute | solution.py:51
  639.6 22.2 %collective-permute-start.106 = (bf16[4,256,512]{2,1,0:T(8,128)(2,1)}, bf16[4,256,512]{2,1,0:T(8,128)(2,1)}, u32[]{:S(2)}, u32[]{:S(2)}) collective-permute-start(bf16[4,256,512]{2,1,0:T(8,128)(2,1)} %bitcast.74), channel_id=1, source_target_pairs={{0,16},{1,17},{2,18},{3,19},{4,20},{5,21},{6,22},{7,23},{8,24},{9,... | collective-permute-start | bytes 3145736 | tf_op jit(solution)/shard_map/ppermute | solution.py:51
  639.6 19.6 %collective-permute-start.108 = (bf16[2,256,640]{2,1,0:T(8,128)(2,1)}, bf16[2,256,640]{2,1,0:T(8,128)(2,1)}, u32[]{:S(2)}, u32[]{:S(2)}) collective-permute-start(bf16[2,256,640]{2,1,0:T(8,128)(2,1)} %slice.650), channel_id=1, source_target_pairs={{0,2},{1,3},{2,0},{3,1},{4,6},{5,7},{6,4},{7,5},{8,10},{9,11},{10,... | collective-permute-start | bytes 1966088 | tf_op jit(solution)/shard_map/ppermute | solution.py:51
  639.9 18.6 %collective-permute-start.105 = (bf16[128,2048]{1,0:T(8,128)(2,1)}, bf16[128,2048]{1,0:T(8,128)(2,1)}, u32[]{:S(2)}, u32[]{:S(2)}) collective-permute-start(bf16[128,2048]{1,0:T(8,128)(2,1)} %fusion.18), channel_id=1, source_target_pairs={{0,1},{1,0},{2,3},{3,2},{4,5},{5,4},{6,7},{7,6},{8,9},{9,8},{10,11... | collective-permute-start | bytes 1572872 | tf_op jit(solution)/shard_map/ppermute | solution.py:51
  669.4 19.7 %collective-permute-start.109 = (bf16[2,256,512]{2,1,0:T(8,128)(2,1)}, bf16[2,256,512]{2,1,0:T(8,128)(2,1)}, u32[]{:S(2)}, u32[]{:S(2)}) collective-permute-start(bf16[2,256,512]{2,1,0:T(8,128)(2,1)} %slice.654), channel_id=1, source_target_pairs={{0,2},{1,3},{2,0},{3,1},{4,6},{5,7},{6,4},{7,5},{8,10},{9,11},{10,... | collective-permute-start | bytes 1572872 | tf_op jit(solution)/shard_map/ppermute | solution.py:51
  690.4 29.3 %collective-permute-start.114 = (bf16[256,1024]{1,0:T(8,128)(2,1)}, bf16[256,1024]{1,0:T(8,128)(2,1)S(1)}, u32[]{:S(2)}, u32[]{:S(2)}) collective-permute-start(bf16[256,1024]{1,0:T(8,128)(2,1)} %get-tuple-element.505), channel_id=1, source_target_pairs={{0,2},{1,3},{2,0},{3,1},{4,6},{5,7},{6,4},{7,5},{8,10},{9,11},{10,... | collective-permute-start | bytes 1572872 | tf_op jit(solution)/shard_map/ppermute | solution.py:51
  697.4 22.3 %collective-permute-start.113 = (bf16[128,1024]{1,0:T(8,128)(2,1)S(1)}, bf16[128,1024]{1,0:T(8,128)(2,1)S(1)}, u32[]{:S(2)}, u32[]{:S(2)}) collective-permute-start(bf16[128,1024]{1,0:T(8,128)(2,1)S(1)} %copy-done.100), channel_id=1, source_target_pairs={{0,4},{1,5},{2,6},{3,7},{4,0},{5,1},{6,2},{7,3},{8,12},{9,13},{10,... | collective-permute-start | bytes 786440 | tf_op jit(solution)/shard_map/ppermute | solution.py:51
  722.6 20.6 %collective-permute-start.119 = (bf16[256,1024]{1,0:T(8,128)(2,1)S(1)}, bf16[256,1024]{1,0:T(8,128)(2,1)S(1)}, u32[]{:S(2)}, u32[]{:S(2)}) collective-permute-start(bf16[256,1024]{1,0:T(8,128)(2,1)S(1)} %get-tuple-element.513), channel_id=1, source_target_pairs={{0,2},{1,3},{2,0},{3,1},{4,6},{5,7},{6,4},{7,5},{8,10},{9,11},{10,... | collective-permute-start | bytes 1572872 | tf_op jit(solution)/shard_map/ppermute | solution.py:51
  (188 other events, 2545.5 us)

commit v6 on v5

--- a/solution.py
+++ b/solution.py
@@ -998,7 +998,9 @@
         total = row_major(total.astype(BF16))
         return Fold(total.reshape(groups, 4 * shard, -1), wide_masks[::-1])
 
-    out_fold = weight_fold(branch_group, attention_low, norm_mid_sum)
+    out_blocks = weight_fold(branch_group, attention_low, norm_mid_sum).blocks
+    out_fold = Fold(out_blocks[..., : query_local - 128], wide_masks[::-1])
+    out_rest = Fold(out_blocks[..., query_local - 128 :], wide_masks[::-1])
     out_fold.advance(flow)
     near(block_rows)
     high(ff_rows)
@@ -1046,6 +1048,7 @@
         flow.go()
     out_two = [add(out_four[0, i], sent.value, BF16) for i, sent in enumerate(out_parts)]
     out_sent = flow.send(out_two[1], 0, TURN)
+    out_rest.advance(flow)
     high(ff_rows // 2)
     flow.go()
     layer_out = (middle + from_far(add(out_two[0], out_sent.value, F32))).astype(BF16)
@@ -1063,10 +1066,12 @@
     kv_fold.advance(flow)
     query_fold.advance(flow)
     out_fold.advance(flow)
+    out_rest.advance(flow)
     flow.go()
     kv_fold.advance(flow)
     query_fold.advance(flow)
     out_fold.advance(flow)
+    out_rest.advance(flow)
     near(ff_rows)
     flow.go()
     kv_fold.advance(flow)
@@ -1075,14 +1080,14 @@
     take_turn()
     flow.go()
     while True:
-        running = [fold.advance(flow) for fold in (kv_fold, query_fold, out_fold)]
+        running = [fold.advance(flow) for fold in (kv_fold, query_fold, out_fold, out_rest)]
         if not any(running):
             break
         near(block_rows), high(block_rows)
         flow.go()
 
     total = jnp.concatenate(
-        [fold.blocks[0] for fold in (query_fold, kv_fold, out_fold)], axis=-1
+        [fold.blocks[0] for fold in (query_fold, kv_fold, out_fold, out_rest)], axis=-1
     ).reshape(2, 2, shard, -1)
 
     def block_of(core_bit, low_bit):

time: 757 us -> 753 us (level)
  waiting for transfers between devices: 292 us -> 278 us
    ppermute x120 -> x123, waiting for transfers between devices: 292 us -> 278 us  [swap(): return row_major(lax.ppermute(row_major(value), ('head', 'blk'), pairs))]
    ppermute x120 -> x123, starting transfers between devices: 119 us -> 122 us  [swap(): return row_major(lax.ppermute(row_major(value), ('head', 'blk'), pairs))]
    unnamed x309 -> x325, local copies, waits for them, and re-layouts: 69.4 us -> 71.3 us
    convert_element_type x20 -> x22, other arithmetic: 20.5 us -> 20.9 us  [add(): return (a.astype(F32) + b.astype(F32)).astype(dtype)]
  transfers between devices with their start and end apart: 120 -> 123, of which waited for: 56 -> 54; matrix products, arithmetic and copies ran while one was open for 29% -> 29% of each run, Pallas kernels for 4% -> 4%
where the time goes in v6:
time: 753 us; the launch traced here: 745 us
  waiting for transfers between devices  278 us (37%)
  local copies, waits for them, and re-layouts  142 us (19%)
  starting transfers between devices  122 us (16%)
  other arithmetic  90.3 us (12%)
  matrix products  78 us (10%)
  Pallas kernels  31 us (4%)
    ppermute x123, waiting for transfers between devices, swap(): return row_major(lax.ppermute(row_major(value), ('head', 'blk'), pairs))  278 us
    ppermute x123, starting transfers between devices, swap(): return row_major(lax.ppermute(row_major(value), ('head', 'blk'), pairs))  122 us
    unnamed x325, local copies, waits for them, and re-layouts  71.3 us
    convert_element_type x22, other arithmetic, add(): return (a.astype(F32) + b.astype(F32)).astype(dtype)  20.9 us
    dot_general x3, matrix products, ffn_fold(): total = lax.dot_general(lhs, rhs, ROWS, preferred_element_type=F32)  17.4 us
  transfers between devices with their start and end apart: 123, of which 54 were waited for; matrix products, arithmetic and copies ran while one was open for 29% of the time, Pallas kernels for 4%

profile of v6, /device:TPU:0, one launch (start us, length us, event | category | flops | bytes accessed | tf_op | source)
XLA Modules:
  0.0 744.9 jit_solution(14164735042863701449)
XLA Ops:
  10.1 3.0 collective-permute-start.3
  15.0 2.6 collective-permute-start.4
  29.3 2.6 collective-permute-start.5
  41.8 13.5 %collective-permute-done.9 = bf16[2,32,64]{2,1,0:T(8,128)(2,1)S(1)} collective-permute-done((bf16[2,32,64]{2,1,0:T(8,128)(2,1)S(1)}, bf16[2,32,64]{2,1,0:T(8,128)(2,1)S(1)}, u32[]{:S(2)}, u32[]{:S(2)}) %collective-permute-start.9) | collective-permute-done | bytes 8224 | tf_op jit(solution)/shard_map/ppermute | solution.py:51
  67.2 3.5 collective-permute-done.10
  70.6 9.5 %collective-permute-done.11 = bf16[256,1024]{1,0:T(8,128)(2,1)} collective-permute-done((bf16[256,1024]{1,0:T(8,128)(2,1)}, bf16[256,1024]{1,0:T(8,128)(2,1)}, u32[]{:S(2)}, u32[]{:S(2)}) %collective-permute-start.11) | collective-permute-done | bytes 524320 | tf_op jit(solution)/shard_map/ppermute | solution.py:51
  80.1 3.7 collective-permute-done.13
  96.0 4.0 collective-permute-done.18
  105.0 2.6 collective-permute-start.23
  109.6 5.1 fusion.127
  114.7 4.9 collective-permute-done.23
  134.5 14.7 %collective-permute-done.25 = bf16[512,512]{1,0:T(8,128)(2,1)} collective-permute-done((bf16[512,512]{1,0:T(8,128)(2,1)}, bf16[512,512]{1,0:T(8,128)(2,1)}, u32[]{:S(2)}, u32[]{:S(2)}) %collective-permute-start.25) | collective-permute-done | bytes 524320 | tf_op jit(solution)/shard_map/ppermute | solution.py:51
  159.6 6.2 collective-permute-done.30
  165.8 5.3 collective-permute-done.31
  171.0 2.8 collective-permute-done.32
  173.9 4.6 collective-permute-done.34
  178.8 2.9 collective-permute-start.37
  193.2 7.5 %collective-permute-done.36 = bf16[2,256,512]{2,1,0:T(8,128)(2,1)S(1)} collective-permute-done((bf16[2,256,512]{2,1,0:T(8,128)(2,1)}, bf16[2,256,512]{2,1,0:T(8,128)(2,1)S(1)}, u32[]{:S(2)}, u32[]{:S(2)}) %collective-permute-start.36) | collective-permute-done | bytes 524320 | tf_op jit(solution)/shard_map/ppermute | solution.py:51
  214.6 10.8 %attend.1 = (bf16[512,512]{1,0:T(8,128)(2,1)}, f32[512,512]{1,0:T(8,128)}, f32[2,1,512]{2,1,0:T(1,128)}) custom-call(s32[2]{0:T(128)} %pad_add_fusion.place_ref, s32[8]{0:T(128)} %pair_ref.3, s32[4096]{0:T(1024)} %bitcast.275, bf16[512,512]{1,0:T(8,128)(2,1)} %maximum_multiply_fusion.q_ref, bf16[4096,512]{1,0:T(8,128)(2,1)} %constant_dynamic-update-slice_fusion.8.kv_ref, ...), custom_call_target="tpu_custom_call" | custom-call | flops 6000000000 | bytes 6000000 | tf_op jit(solution)/shard_map/attend/pallas_call | solution.py:499
  225.4 4.8 collective-permute-done.41
  251.5 7.2 collective-permute-done.49
  270.4 2.9 collective-permute-start.53
  273.3 2.7 pad_maximum_fusion.3
  277.9 5.2 collective-permute-done.51.refs_5_
  291.7 5.0 collective-permute-done.54.refs_1_
  299.8 6.3 collective-permute-done.58
  311.6 2.9 assemble.2.refs_0_
  334.2 2.8 collective-permute-done.66
  337.9 6.3 fusion.154
  344.2 4.3 assemble.3
  348.5 7.7 %fusion.153 = f32[1024,1024]{1,0:T(8,128)S(1)} fusion(bf16[1024,2048]{1,0:T(8,128)(2,1)} %assemble.3, bf16[2048,1024]{1,0:T(8,128)(2,1)} %constant_dynamic-update-slice_fusion.16), kind=kOutput, calls=%fused_computation.439 | convolution fusion | flops 4294967296 | bytes 12582912 | tf_op jit(solution)/shard_map/dot_general | solution.py:916
  356.4 7.4 multiply_convert_fusion.2
  363.7 4.5 fusion.155
  368.3 7.5 %add_convert_fusion = bf16[1024,2048]{1,0:T(8,128)(2,1)S(1)} fusion(f32[1024,2048]{1,0:T(8,128)S(1)} %fusion.155, bf16[1024,1024]{1,0:T(8,128)(2,1)S(1)} %get-tuple-element.440, bf16[2048,1024]{1,0:T(8,128)(2,1)} %constant_dynamic-update-slice_fusion.16), kind=kOutput, calls=%fused_computation | convolution fusion | flops 4299161600 | bytes 18874368 | tf_op jit(solution)/shard_map/dot_general | solution.py:945
  377.9 7.4 convolution_convert_fusion.2
  386.6 2.9 fusion.4
  389.7 2.6 collective-permute-start.69
  394.8 4.9 convolution_convert_fusion.1
  399.7 8.5 %convolution_convert_fusion.3 = bf16[1024,2048]{1,0:T(8,128)(2,1)S(1)} fusion(bf16[1024,1024]{1,0:T(8,128)(2,1)S(1)} %copy-done.137, bf16[2048,1024]{1,0:T(8,128)(2,1)} %constant_dynamic-update-slice_fusion.28), kind=kOutput, calls=%fused_computation.18 | convolution fusion | flops 4297064448 | bytes 10485760 | tf_op jit(solution)/shard_map/dot_general | solution.py:960
  416.8 5.1 convolution_convert_fusion
  440.2 3.0 fusion.3
  450.8 10.9 %collective-permute-done.77 = bf16[128,1024]{1,0:T(8,128)(2,1)S(1)} collective-permute-done((bf16[128,1024]{1,0:T(8,128)(2,1)S(1)}, bf16[128,1024]{1,0:T(8,128)(2,1)S(1)}, u32[]{:S(2)}, u32[]{:S(2)}) %collective-permute-start.77) | collective-permute-done | bytes 262176 | tf_op jit(solution)/shard_map/ppermute | solution.py:51
  466.7 3.0 convolution_convert_fusion.7
  476.8 13.0 %attend_back.1 = (bf16[512,512]{1,0:T(8,128)(2,1)}, bf16[4096,256]{1,0:T(8,128)(2,1)}, bf16[4096,256]{1,0:T(8,128)(2,1)}) custom-call(s32[2]{0:T(128)} %pad_add_fusion.place_ref, s32[8]{0:T(128)} %pair_ref.3, s32[4096]{0:T(1024)} %bitcast.276, bf16[512,512]{1,0:T(8,128)(2,1)} %maximum_multiply_fusion.q_ref, ...), custom_call_target="tpu_custom_call" | custom-call | flops 16000000000 | bytes 12000000 | tf_op jit(solution)/shard_map/attend_back/pallas_call | solution.py:535
  489.7 12.4 %collective-permute-done.83 = bf16[256,1024]{1,0:T(8,128)(2,1)} collective-permute-done((bf16[256,1024]{1,0:T(8,128)(2,1)}, bf16[256,1024]{1,0:T(8,128)(2,1)}, u32[]{:S(2)}, u32[]{:S(2)}) %collective-permute-start.83) | collective-permute-done | bytes 524320 | tf_op jit(solution)/shard_map/ppermute | solution.py:51
  513.3 19.3 %collective-permute-done.86 = bf16[256,1024]{1,0:T(8,128)(2,1)S(1)} collective-permute-done((bf16[256,1024]{1,0:T(8,128)(2,1)S(1)}, bf16[256,1024]{1,0:T(8,128)(2,1)S(1)}, u32[]{:S(2)}, u32[]{:S(2)}) %collective-permute-start.86) | collective-permute-done | bytes 524320 | tf_op jit(solution)/shard_map/ppermute | solution.py:51
  537.5 2.5 collective-permute-start.90
  540.7 20.7 %collective-permute-done.87 = bf16[2,512,256]{2,1,0:T(8,128)(2,1)S(1)} collective-permute-done((bf16[2,512,256]{2,1,0:T(8,128)(2,1)S(1)}, bf16[2,512,256]{2,1,0:T(8,128)(2,1)S(1)}, u32[]{:S(2)}, u32[]{:S(2)}) %collective-permute-start.87) | collective-permute-done | bytes 524320 | tf_op jit(solution)/shard_map/ppermute | solution.py:51
  569.3 2.7 collective-permute-start.91
  572.4 2.8 select_dynamic-update-slice_fusion
  575.3 11.3 %collective-permute-done.91 = bf16[1,512,256]{2,1,0:T(8,128)(2,1)S(1)} collective-permute-done((bf16[1,512,256]{2,1,0:T(8,128)(2,1)S(1)}, bf16[1,512,256]{2,1,0:T(8,128)(2,1)S(1)}, u32[]{:S(2)}, u32[]{:S(2)}) %collective-permute-start.91) | collective-permute-done | bytes 262176 | tf_op jit(solution)/shard_map/ppermute | solution.py:51
  586.5 6.8 collective-permute-done.94
  598.6 2.8 select_dynamic-update-slice_fusion.2
  604.1 5.4 collective-permute-done.96
  609.5 6.9 collective-permute-done.99
  630.1 2.7 collective-permute-done.101
  646.2 3.0 reshape.626
  649.2 3.5 collective-permute-done.108
  652.7 5.3 collective-permute-done.110
  694.4 12.6 %collective-permute-done.115 = bf16[1,256,512]{2,1,0:T(8,128)(2,1)S(1)} collective-permute-done((bf16[1,256,512]{2,1,0:T(8,128)(2,1)S(1)}, bf16[1,256,512]{2,1,0:T(8,128)(2,1)S(1)}, u32[]{:S(2)}, u32[]{:S(2)}) %collective-permute-start.115) | collective-permute-done | bytes 262176 | tf_op jit(solution)/shard_map/ppermute | solution.py:51
  707.0 5.8 collective-permute-done.116
  721.4 4.5 collective-permute-done.119
  725.9 3.8 collective-permute-done.120
  730.7 8.5 %collective-permute-done.122 = bf16[256,1024]{1,0:T(8,128)(2,1)S(1)} collective-permute-done((bf16[256,1024]{1,0:T(8,128)(2,1)S(1)}, bf16[256,1024]{1,0:T(8,128)(2,1)S(1)}, u32[]{:S(2)}, u32[]{:S(2)}) %collective-permute-start.122) | collective-permute-done | bytes 524320 | tf_op jit(solution)/shard_map/ppermute | solution.py:51
  (759 shorter events, 349.2 us)
Async XLA Ops:
  29.3 26.0 %collective-permute-start.5 = (bf16[256,1024]{1,0:T(8,128)(2,1)}, bf16[256,1024]{1,0:T(8,128)(2,1)}, u32[]{:S(2)}, u32[]{:S(2)}) collective-permute-start(bf16[256,1024]{1,0:T(8,128)(2,1)} %get-tuple-element.283), channel_id=1, source_target_pairs={{0,4},{1,5},{2,6},{3,7},{4,0},{5,1},{6,2},{7,3},{8,12},{9,13},{10,... | collective-permute-start | bytes 1572872 | tf_op jit(solution)/shard_map/ppermute | solution.py:51
  32.0 23.4 %collective-permute-start.6 = (bf16[256,1024]{1,0:T(8,128)(2,1)}, bf16[256,1024]{1,0:T(8,128)(2,1)}, u32[]{:S(2)}, u32[]{:S(2)}) collective-permute-start(bf16[256,1024]{1,0:T(8,128)(2,1)} %get-tuple-element.283), channel_id=1, source_target_pairs={{0,2},{1,3},{2,0},{3,1},{4,6},{5,7},{6,4},{7,5},{8,10},{9,11},{10,... | collective-permute-start | bytes 1572872 | tf_op jit(solution)/shard_map/ppermute | solution.py:51
  33.7 21.6 %collective-permute-start.7 = (bf16[256,1024]{1,0:T(8,128)(2,1)}, bf16[256,1024]{1,0:T(8,128)(2,1)}, u32[]{:S(2)}, u32[]{:S(2)}) collective-permute-start(bf16[256,1024]{1,0:T(8,128)(2,1)} %get-tuple-element.283), channel_id=1, source_target_pairs={{0,16},{1,17},{2,18},{3,19},{4,20},{5,21},{6,22},{7,23},{8,24},{9,... | collective-permute-start | bytes 1572872 | tf_op jit(solution)/shard_map/ppermute | solution.py:51
  35.2 20.1 %collective-permute-start.8 = (bf16[128,2048]{1,0:T(8,128)(2,1)S(1)}, bf16[128,2048]{1,0:T(8,128)(2,1)}, u32[]{:S(2)}, u32[]{:S(2)}) collective-permute-start(bf16[128,2048]{1,0:T(8,128)(2,1)S(1)} %reshape.604), channel_id=1, source_target_pairs={{0,1},{1,0},{2,3},{3,2},{4,5},{5,4},{6,7},{7,6},{8,9},{9,8},{10,11... | collective-permute-start | bytes 1572872 | tf_op jit(solution)/shard_map/ppermute | solution.py:51
  56.9 23.2 %collective-permute-start.11 = (bf16[256,1024]{1,0:T(8,128)(2,1)}, bf16[256,1024]{1,0:T(8,128)(2,1)}, u32[]{:S(2)}, u32[]{:S(2)}) collective-permute-start(bf16[256,1024]{1,0:T(8,128)(2,1)} %collective-permute-done.5), channel_id=1, source_target_pairs={{0,2},{1,3},{2,0},{3,1},{4,6},{5,7},{6,4},{7,5},{8,10},{9,11},{10,... | collective-permute-start | bytes 1572872 | tf_op jit(solution)/shard_map/ppermute | solution.py:51
  58.6 21.5 %collective-permute-start.12 = (bf16[256,1024]{1,0:T(8,128)(2,1)}, bf16[256,1024]{1,0:T(8,128)(2,1)}, u32[]{:S(2)}, u32[]{:S(2)}) collective-permute-start(bf16[256,1024]{1,0:T(8,128)(2,1)} %collective-permute-done.5), channel_id=1, source_target_pairs={{0,16},{1,17},{2,18},{3,19},{4,20},{5,21},{6,22},{7,23},{8,24},{9,... | collective-permute-start | bytes 1572872 | tf_op jit(solution)/shard_map/ppermute | solution.py:51
  59.2 24.7 %collective-permute-start.13 = (bf16[256,1024]{1,0:T(8,128)(2,1)}, bf16[256,1024]{1,0:T(8,128)(2,1)}, u32[]{:S(2)}, u32[]{:S(2)}) collective-permute-start(bf16[256,1024]{1,0:T(8,128)(2,1)} %get-tuple-element.312), channel_id=1, source_target_pairs={{0,4},{1,5},{2,6},{3,7},{4,0},{5,1},{6,2},{7,3},{8,12},{9,13},{10,... | collective-permute-start | bytes 1572872 | tf_op jit(solution)/shard_map/ppermute | solution.py:51
  102.6 19.0 %collective-permute-start.21 = (bf16[256,1024]{1,0:T(8,128)(2,1)}, bf16[256,1024]{1,0:T(8,128)(2,1)}, u32[]{:S(2)}, u32[]{:S(2)}) collective-permute-start(bf16[256,1024]{1,0:T(8,128)(2,1)} %constant_dynamic-slice_fusion), channel_id=1, source_target_pairs={{0,2},{1,3},{2,0},{3,1},{4,6},{5,7},{6,4},{7,5},{8,10},{9,11},{10,... | collective-permute-start | bytes 1572872 | tf_op jit(solution)/shard_map/ppermute | solution.py:51
  103.0 18.6 %collective-permute-start.22 = (bf16[256,1024]{1,0:T(8,128)(2,1)}, bf16[256,1024]{1,0:T(8,128)(2,1)}, u32[]{:S(2)}, u32[]{:S(2)}) collective-permute-start(bf16[256,1024]{1,0:T(8,128)(2,1)} %get-tuple-element.312), channel_id=1, source_target_pairs={{0,1},{1,0},{2,3},{3,2},{4,5},{5,4},{6,7},{7,6},{8,9},{9,8},{10,11... | collective-permute-start | bytes 1572872 | tf_op jit(solution)/shard_map/ppermute | solution.py:51
  124.7 24.5 %collective-permute-start.25 = (bf16[512,512]{1,0:T(8,128)(2,1)}, bf16[512,512]{1,0:T(8,128)(2,1)}, u32[]{:S(2)}, u32[]{:S(2)}) collective-permute-start(bf16[512,512]{1,0:T(8,128)(2,1)} %get-tuple-element.325), channel_id=1, source_target_pairs={{0,4},{1,5},{2,6},{3,7},{4,0},{5,1},{6,2},{7,3},{8,12},{9,13},{10,... | collective-permute-start | bytes 1572872 | tf_op jit(solution)/shard_map/ppermute | solution.py:51
  126.1 23.1 %collective-permute-start.26 = (bf16[512,512]{1,0:T(8,128)(2,1)}, bf16[512,512]{1,0:T(8,128)(2,1)}, u32[]{:S(2)}, u32[]{:S(2)}) collective-permute-start(bf16[512,512]{1,0:T(8,128)(2,1)} %get-tuple-element.325), channel_id=1, source_target_pairs={{0,2},{1,3},{2,0},{3,1},{4,6},{5,7},{6,4},{7,5},{8,10},{9,11},{10,... | collective-permute-start | bytes 1572872 | tf_op jit(solution)/shard_map/ppermute | solution.py:51
  127.6 21.6 %collective-permute-start.27 = (bf16[512,512]{1,0:T(8,128)(2,1)}, bf16[512,512]{1,0:T(8,128)(2,1)}, u32[]{:S(2)}, u32[]{:S(2)}) collective-permute-start(bf16[512,512]{1,0:T(8,128)(2,1)} %get-tuple-element.325), channel_id=1, source_target_pairs={{0,16},{1,17},{2,18},{3,19},{4,20},{5,21},{6,22},{7,23},{8,24},{9,... | collective-permute-start | bytes 1572872 | tf_op jit(solution)/shard_map/ppermute | solution.py:51
  128.2 21.1 %collective-permute-start.28 = (bf16[256,1024]{1,0:T(8,128)(2,1)S(1)}, bf16[256,1024]{1,0:T(8,128)(2,1)}, u32[]{:S(2)}, u32[]{:S(2)}) collective-permute-start(bf16[256,1024]{1,0:T(8,128)(2,1)S(1)} %get-tuple-element.337), channel_id=1, source_target_pairs={{0,1},{1,0},{2,3},{3,2},{4,5},{5,4},{6,7},{7,6},{8,9},{9,8},{10,11... | collective-permute-start | bytes 1572872 | tf_op jit(solution)/shard_map/ppermute | solution.py:51
  129.7 21.0 %collective-permute-start.29 = (bf16[256,1024]{1,0:T(8,128)(2,1)S(1)}, bf16[256,1024]{1,0:T(8,128)(2,1)}, u32[]{:S(2)}, u32[]{:S(2)}) collective-permute-start(bf16[256,1024]{1,0:T(8,128)(2,1)S(1)} %copy-done.36), channel_id=1, source_target_pairs={{0,1},{1,0},{2,3},{3,2},{4,5},{5,4},{6,7},{7,6},{8,9},{9,8},{10,11... | collective-permute-start | bytes 1572872 | tf_op jit(solution)/shard_map/ppermute | solution.py:51
  152.2 18.8 %collective-permute-start.31 = (bf16[512,512]{1,0:T(8,128)(2,1)}, bf16[512,512]{1,0:T(8,128)(2,1)}, u32[]{:S(2)}, u32[]{:S(2)}) collective-permute-start(bf16[512,512]{1,0:T(8,128)(2,1)} %collective-permute-done.25), channel_id=1, source_target_pairs={{0,2},{1,3},{2,0},{3,1},{4,6},{5,7},{6,4},{7,5},{8,10},{9,11},{10,... | collective-permute-start | bytes 1572872 | tf_op jit(solution)/shard_map/ppermute | solution.py:51
  153.0 20.8 %collective-permute-start.32 = (bf16[512,512]{1,0:T(8,128)(2,1)}, bf16[512,512]{1,0:T(8,128)(2,1)S(1)}, u32[]{:S(2)}, u32[]{:S(2)}) collective-permute-start(bf16[512,512]{1,0:T(8,128)(2,1)} %collective-permute-done.25), channel_id=1, source_target_pairs={{0,16},{1,17},{2,18},{3,19},{4,20},{5,21},{6,22},{7,23},{8,24},{9,... | collective-permute-start | bytes 1572872 | tf_op jit(solution)/shard_map/ppermute | solution.py:51
  153.4 20.5 %collective-permute-start.33 = (bf16[256,1024]{1,0:T(8,128)(2,1)S(1)}, bf16[256,1024]{1,0:T(8,128)(2,1)S(1)}, u32[]{:S(2)}, u32[]{:S(2)}) collective-permute-start(bf16[256,1024]{1,0:T(8,128)(2,1)S(1)} %get-tuple-element.355), channel_id=1, source_target_pairs={{0,1},{1,0},{2,3},{3,2},{4,5},{5,4},{6,7},{7,6},{8,9},{9,8},{10,11... | collective-permute-start | bytes 1572872 | tf_op jit(solution)/shard_map/ppermute | solution.py:51
  154.9 23.6 %collective-permute-start.34 = (bf16[256,1024]{1,0:T(8,128)(2,1)S(1)}, bf16[256,1024]{1,0:T(8,128)(2,1)}, u32[]{:S(2)}, u32[]{:S(2)}) collective-permute-start(bf16[256,1024]{1,0:T(8,128)(2,1)S(1)} %get-tuple-element.337), channel_id=1, source_target_pairs={{0,4},{1,5},{2,6},{3,7},{4,0},{5,1},{6,2},{7,3},{8,12},{9,13},{10,... | collective-permute-start | bytes 1572872 | tf_op jit(solution)/shard_map/ppermute | solution.py:51
  178.8 21.9 %collective-permute-start.36 = (bf16[2,256,512]{2,1,0:T(8,128)(2,1)}, bf16[2,256,512]{2,1,0:T(8,128)(2,1)S(1)}, u32[]{:S(2)}, u32[]{:S(2)}) collective-permute-start(bf16[2,256,512]{2,1,0:T(8,128)(2,1)} %pad_maximum_fusion.14), channel_id=1, source_target_pairs={{0,2},{1,3},{2,0},{3,1},{4,6},{5,7},{6,4},{7,5},{8,10},{9,11},{10,... | collective-permute-start | bytes 1572872 | tf_op jit(solution)/shard_map/ppermute | solution.py:51
  178.8 21.9 %collective-permute-start.37 = (bf16[256,1024]{1,0:T(8,128)(2,1)S(1)}, bf16[256,1024]{1,0:T(8,128)(2,1)}, u32[]{:S(2)}, u32[]{:S(2)}) collective-permute-start(bf16[256,1024]{1,0:T(8,128)(2,1)S(1)} %copy-done.36), channel_id=1, source_target_pairs={{0,4},{1,5},{2,6},{3,7},{4,0},{5,1},{6,2},{7,3},{8,12},{9,13},{10,... | collective-permute-start | bytes 1572872 | tf_op jit(solution)/shard_map/ppermute | solution.py:51
  181.7 19.0 %collective-permute-start.38 = (bf16[256,1024]{1,0:T(8,128)(2,1)}, bf16[256,1024]{1,0:T(8,128)(2,1)}, u32[]{:S(2)}, u32[]{:S(2)}) collective-permute-start(bf16[256,1024]{1,0:T(8,128)(2,1)} %get-tuple-element.346), channel_id=1, source_target_pairs={{0,1},{1,0},{2,3},{3,2},{4,5},{5,4},{6,7},{7,6},{8,9},{9,8},{10,11... | collective-permute-start | bytes 1572872 | tf_op jit(solution)/shard_map/ppermute | solution.py:51
  182.1 20.9 %collective-permute-start.39 = (bf16[256,1024]{1,0:T(8,128)(2,1)}, bf16[256,1024]{1,0:T(8,128)(2,1)}, u32[]{:S(2)}, u32[]{:S(2)}) collective-permute-start(bf16[256,1024]{1,0:T(8,128)(2,1)} %get-tuple-element.347), channel_id=1, source_target_pairs={{0,1},{1,0},{2,3},{3,2},{4,5},{5,4},{6,7},{7,6},{8,9},{9,8},{10,11... | collective-permute-start | bytes 1572872 | tf_op jit(solution)/shard_map/ppermute | solution.py:51
  204.0 27.6 %collective-permute-start.40 = (bf16[4,256,512]{2,1,0:T(8,128)(2,1)}, bf16[4,256,512]{2,1,0:T(8,128)(2,1)}, u32[]{:S(2)}, u32[]{:S(2)}) collective-permute-start(bf16[4,256,512]{2,1,0:T(8,128)(2,1)} %pad_maximum_fusion.6), channel_id=1, source_target_pairs={{0,16},{1,17},{2,18},{3,19},{4,20},{5,21},{6,22},{7,23},{8,24},{9,... | collective-permute-start | bytes 3145736 | tf_op jit(solution)/shard_map/ppermute | solution.py:51
  209.3 20.9 %collective-permute-start.41 = (bf16[256,1024]{1,0:T(8,128)(2,1)S(1)}, bf16[256,1024]{1,0:T(8,128)(2,1)}, u32[]{:S(2)}, u32[]{:S(2)}) collective-permute-start(bf16[256,1024]{1,0:T(8,128)(2,1)S(1)} %get-tuple-element.355), channel_id=1, source_target_pairs={{0,4},{1,5},{2,6},{3,7},{4,0},{5,1},{6,2},{7,3},{8,12},{9,13},{10,... | collective-permute-start | bytes 1572872 | tf_op jit(solution)/shard_map/ppermute | solution.py:51
  209.6 20.6 %collective-permute-start.42 = (bf16[256,1024]{1,0:T(8,128)(2,1)}, bf16[256,1024]{1,0:T(8,128)(2,1)}, u32[]{:S(2)}, u32[]{:S(2)}) collective-permute-start(bf16[256,1024]{1,0:T(8,128)(2,1)} %collective-permute-done.13), channel_id=1, source_target_pairs={{0,1},{1,0},{2,3},{3,2},{4,5},{5,4},{6,7},{7,6},{8,9},{9,8},{10,11... | collective-permute-start | bytes 1572872 | tf_op jit(solution)/shard_map/ppermute | solution.py:51
  209.9 20.6 %collective-permute-start.43 = (bf16[256,1024]{1,0:T(8,128)(2,1)}, bf16[256,1024]{1,0:T(8,128)(2,1)}, u32[]{:S(2)}, u32[]{:S(2)}) collective-permute-start(bf16[256,1024]{1,0:T(8,128)(2,1)} %collective-permute-done.34), channel_id=1, source_target_pairs={{0,1},{1,0},{2,3},{3,2},{4,5},{5,4},{6,7},{7,6},{8,9},{9,8},{10,11... | collective-permute-start | bytes 1572872 | tf_op jit(solution)/shard_map/ppermute | solution.py:51
  211.6 19.9 %collective-permute-start.44 = (bf16[128,2048]{1,0:T(8,128)(2,1)S(1)}, bf16[128,2048]{1,0:T(8,128)(2,1)S(1)}, u32[]{:S(2)}, u32[]{:S(2)}) collective-permute-start(bf16[128,2048]{1,0:T(8,128)(2,1)S(1)} %reshape.608), channel_id=1, source_target_pairs={{0,2},{1,3},{2,0},{3,1},{4,6},{5,7},{6,4},{7,5},{8,10},{9,11},{10,... | collective-permute-start | bytes 1572872 | tf_op jit(solution)/shard_map/ppermute | solution.py:51
  237.9 21.7 %collective-permute-start.45 = (bf16[128,2048]{1,0:T(8,128)(2,1)S(1)}, bf16[128,2048]{1,0:T(8,128)(2,1)S(1)}, u32[]{:S(2)}, u32[]{:S(2)}) collective-permute-start(bf16[128,2048]{1,0:T(8,128)(2,1)S(1)} %get-tuple-element.592), channel_id=1, source_target_pairs={{0,8},{1,9},{2,10},{3,11},{4,12},{5,13},{6,14},{7,15},{8,0},{9,1},... | collective-permute-start | bytes 1572872 | tf_op jit(solution)/shard_map/ppermute | solution.py:51
  238.6 20.2 %collective-permute-start.47 = (bf16[128,2048]{1,0:T(8,128)(2,1)S(1)}, bf16[128,2048]{1,0:T(8,128)(2,1)S(1)}, u32[]{:S(2)}, u32[]{:S(2)}) collective-permute-start(bf16[128,2048]{1,0:T(8,128)(2,1)S(1)} %fusion.23), channel_id=1, source_target_pairs={{0,1},{1,0},{2,3},{3,2},{4,5},{5,4},{6,7},{7,6},{8,9},{9,8},{10,11... | collective-permute-start | bytes 1572872 | tf_op jit(solution)/shard_map/ppermute | solution.py:51
  239.0 19.7 %collective-permute-start.48 = (bf16[128,2048]{1,0:T(8,128)(2,1)S(1)}, bf16[128,2048]{1,0:T(8,128)(2,1)S(1)}, u32[]{:S(2)}, u32[]{:S(2)}) collective-permute-start(bf16[128,2048]{1,0:T(8,128)(2,1)S(1)} %collective-permute-done.44), channel_id=1, source_target_pairs={{0,16},{1,17},{2,18},{3,19},{4,20},{5,21},{6,22},{7,23},{8,24},{9,... | collective-permute-start | bytes 1572872 | tf_op jit(solution)/shard_map/ppermute | solution.py:51
  276.0 61.7 %collective-permute-start.63 = (bf16[512,2048]{1,0:T(8,128)(2,1)}, bf16[512,2048]{1,0:T(8,128)(2,1)S(1)}, u32[]{:S(2)}, u32[]{:S(2)}) collective-permute-start(bf16[512,2048]{1,0:T(8,128)(2,1)} %pad_maximum_fusion.3), channel_id=1, source_target_pairs={{0,8},{1,9},{2,10},{3,11},{4,12},{5,13},{6,14},{7,15},{8,0},{9,1},... | collective-permute-start | bytes 6291464 | tf_op jit(solution)/shard_map/ppermute | solution.py:51
  314.5 29.7 %collective-permute-start.59 = (bf16[512,2048]{1,0:T(8,128)(2,1)}, bf16[512,2048]{1,0:T(8,128)(2,1)}, u32[]{:S(2)}, u32[]{:S(2)}) collective-permute-start(bf16[512,2048]{1,0:T(8,128)(2,1)} %assemble.2.refs_0_), channel_id=1, source_target_pairs={{0,8},{1,9},{2,10},{3,11},{4,12},{5,13},{6,14},{7,15},{8,0},{9,1},... | collective-permute-start | bytes 6291464 | tf_op jit(solution)/shard_map/ppermute | solution.py:51
  389.7 22.4 %collective-permute-start.69 = (bf16[2,128,1024]{2,1,0:T(8,128)(2,1)S(1)}, bf16[2,128,1024]{2,1,0:T(8,128)(2,1)S(1)}, u32[]{:S(2)}, u32[]{:S(2)}) collective-permute-start(bf16[2,128,1024]{2,1,0:T(8,128)(2,1)S(1)} %slice_bitcast_fusion.11), channel_id=1, source_target_pairs={{0,2},{1,3},{2,0},{3,1},{4,6},{5,7},{6,4},{7,5},{8,10},{9,11},{10,... | collective-permute-start | bytes 1572872 | tf_op jit(solution)/shard_map/ppermute | solution.py:51
  392.2 19.8 %collective-permute-start.70 = (bf16[2,128,1024]{2,1,0:T(8,128)(2,1)S(1)}, bf16[2,128,1024]{2,1,0:T(8,128)(2,1)S(1)}, u32[]{:S(2)}, u32[]{:S(2)}) collective-permute-start(bf16[2,128,1024]{2,1,0:T(8,128)(2,1)S(1)} %slice_bitcast_fusion.10), channel_id=1, source_target_pairs={{0,16},{1,17},{2,18},{3,19},{4,20},{5,21},{6,22},{7,23},{8,24},{9,... | collective-permute-start | bytes 1572872 | tf_op jit(solution)/shard_map/ppermute | solution.py:51
  393.1 19.0 %collective-permute-start.71 = (bf16[256,1024]{1,0:T(8,128)(2,1)S(1)}, bf16[256,1024]{1,0:T(8,128)(2,1)S(1)}, u32[]{:S(2)}, u32[]{:S(2)}) collective-permute-start(bf16[256,1024]{1,0:T(8,128)(2,1)S(1)} %get-tuple-element.418), channel_id=1, source_target_pairs={{0,1},{1,0},{2,3},{3,2},{4,5},{5,4},{6,7},{7,6},{8,9},{9,8},{10,11... | collective-permute-start | bytes 1572872 | tf_op jit(solution)/shard_map/ppermute | solution.py:51
  410.5 29.7 %collective-permute-start.68 = (bf16[2,2,128,2048]{3,2,1,0:T(8,128)(2,1)}, bf16[2,2,128,2048]{3,2,1,0:T(8,128)(2,1)}, u32[]{:S(2)}, u32[]{:S(2)}) collective-permute-start(bf16[2,2,128,2048]{3,2,1,0:T(8,128)(2,1)} %bitcast.39), channel_id=1, source_target_pairs={{0,8},{1,9},{2,10},{3,11},{4,12},{5,13},{6,14},{7,15},{8,0},{9,1},... | collective-permute-start | bytes 6291464 | tf_op jit(solution)/shard_map/ppermute | solution.py:51
  439.3 22.6 %collective-permute-start.79 = (bf16[128,2048]{1,0:T(8,128)(2,1)S(1)}, bf16[128,2048]{1,0:T(8,128)(2,1)}, u32[]{:S(2)}, u32[]{:S(2)}) collective-permute-start(bf16[128,2048]{1,0:T(8,128)(2,1)S(1)} %reshape.623), channel_id=1, source_target_pairs={{0,8},{1,9},{2,10},{3,11},{4,12},{5,13},{6,14},{7,15},{8,0},{9,1},... | collective-permute-start | bytes 1572872 | tf_op jit(solution)/shard_map/ppermute | solution.py:51
  474.8 27.3 %collective-permute-start.82 = (bf16[512,1024]{1,0:T(8,128)(2,1)}, bf16[512,1024]{1,0:T(8,128)(2,1)S(1)}, u32[]{:S(2)}, u32[]{:S(2)}) collective-permute-start(bf16[512,1024]{1,0:T(8,128)(2,1)} %get-tuple-element.443), channel_id=1, source_target_pairs={{0,1},{1,0},{2,3},{3,2},{4,5},{5,4},{6,7},{7,6},{8,9},{9,8},{10,11... | collective-permute-start | bytes 3145736 | tf_op jit(solution)/shard_map/ppermute | solution.py:51
  475.2 27.0 %collective-permute-start.81 = (bf16[4,256,384]{2,1,0:T(8,128)(2,1)}, bf16[4,256,384]{2,1,0:T(8,128)(2,1)}, u32[]{:S(2)}, u32[]{:S(2)}) collective-permute-start(bf16[4,256,384]{2,1,0:T(8,128)(2,1)} %slice.635), channel_id=1, source_target_pairs={{0,16},{1,17},{2,18},{3,19},{4,20},{5,21},{6,22},{7,23},{8,24},{9,... | collective-permute-start | bytes 2359304 | tf_op jit(solution)/shard_map/ppermute | solution.py:51
  476.7 25.4 %collective-permute-start.83 = (bf16[256,1024]{1,0:T(8,128)(2,1)}, bf16[256,1024]{1,0:T(8,128)(2,1)}, u32[]{:S(2)}, u32[]{:S(2)}) collective-permute-start(bf16[256,1024]{1,0:T(8,128)(2,1)} %add_convert_fusion.12), channel_id=1, source_target_pairs={{0,4},{1,5},{2,6},{3,7},{4,0},{5,1},{6,2},{7,3},{8,12},{9,13},{10,... | collective-permute-start | bytes 1572872 | tf_op jit(solution)/shard_map/ppermute | solution.py:51
  505.5 27.1 %collective-permute-start.84 = (bf16[4,512,256]{2,1,0:T(8,128)(2,1)S(1)}, bf16[4,512,256]{2,1,0:T(8,128)(2,1)S(1)}, u32[]{:S(2)}, u32[]{:S(2)}) collective-permute-start(bf16[4,512,256]{2,1,0:T(8,128)(2,1)S(1)} %bitcast.262), channel_id=1, source_target_pairs={{0,16},{1,17},{2,18},{3,19},{4,20},{5,21},{6,22},{7,23},{8,24},{9,... | collective-permute-start | bytes 3145736 | tf_op jit(solution)/shard_map/ppermute | solution.py:51
  506.5 26.1 %collective-permute-start.85 = (bf16[512,1024]{1,0:T(8,128)(2,1)S(1)}, bf16[512,1024]{1,0:T(8,128)(2,1)S(1)}, u32[]{:S(2)}, u32[]{:S(2)}) collective-permute-start(bf16[512,1024]{1,0:T(8,128)(2,1)S(1)} %copy-done.44), channel_id=1, source_target_pairs={{0,1},{1,0},{2,3},{3,2},{4,5},{5,4},{6,7},{7,6},{8,9},{9,8},{10,11... | collective-permute-start | bytes 3145736 | tf_op jit(solution)/shard_map/ppermute | solution.py:51
  508.3 24.3 %collective-permute-start.86 = (bf16[256,1024]{1,0:T(8,128)(2,1)S(1)}, bf16[256,1024]{1,0:T(8,128)(2,1)S(1)}, u32[]{:S(2)}, u32[]{:S(2)}) collective-permute-start(bf16[256,1024]{1,0:T(8,128)(2,1)S(1)} %get-tuple-element.458), channel_id=1, source_target_pairs={{0,4},{1,5},{2,6},{3,7},{4,0},{5,1},{6,2},{7,3},{8,12},{9,13},{10,... | collective-permute-start | bytes 1572872 | tf_op jit(solution)/shard_map/ppermute | solution.py:51
  532.9 30.1 %collective-permute-start.88 = (bf16[4,512,256]{2,1,0:T(8,128)(2,1)S(1)}, bf16[4,512,256]{2,1,0:T(8,128)(2,1)S(1)}, u32[]{:S(2)}, u32[]{:S(2)}) collective-permute-start(bf16[4,512,256]{2,1,0:T(8,128)(2,1)S(1)} %bitcast.261), channel_id=1, source_target_pairs={{0,16},{1,17},{2,18},{3,19},{4,20},{5,21},{6,22},{7,23},{8,24},{9,... | collective-permute-start | bytes 3145736 | tf_op jit(solution)/shard_map/ppermute | solution.py:51
  533.9 29.1 %collective-permute-start.89 = (bf16[512,1024]{1,0:T(8,128)(2,1)S(1)}, bf16[512,1024]{1,0:T(8,128)(2,1)S(1)}, u32[]{:S(2)}, u32[]{:S(2)}) collective-permute-start(bf16[512,1024]{1,0:T(8,128)(2,1)S(1)} %copy-done.43), channel_id=1, source_target_pairs={{0,1},{1,0},{2,3},{3,2},{4,5},{5,4},{6,7},{7,6},{8,9},{9,8},{10,11... | collective-permute-start | bytes 3145736 | tf_op jit(solution)/shard_map/ppermute | solution.py:51
  537.4 23.9 %collective-permute-start.87 = (bf16[2,512,256]{2,1,0:T(8,128)(2,1)S(1)}, bf16[2,512,256]{2,1,0:T(8,128)(2,1)S(1)}, u32[]{:S(2)}, u32[]{:S(2)}) collective-permute-start(bf16[2,512,256]{2,1,0:T(8,128)(2,1)S(1)} %slice.640), channel_id=1, source_target_pairs={{0,2},{1,3},{2,0},{3,1},{4,6},{5,7},{6,4},{7,5},{8,10},{9,11},{10,... | collective-permute-start | bytes 1572872 | tf_op jit(solution)/shard_map/ppermute | solution.py:51
  537.5 25.5 %collective-permute-start.90 = (bf16[256,1024]{1,0:T(8,128)(2,1)S(1)}, bf16[256,1024]{1,0:T(8,128)(2,1)S(1)}, u32[]{:S(2)}, u32[]{:S(2)}) collective-permute-start(bf16[256,1024]{1,0:T(8,128)(2,1)S(1)} %get-tuple-element.465), channel_id=1, source_target_pairs={{0,4},{1,5},{2,6},{3,7},{4,0},{5,1},{6,2},{7,3},{8,12},{9,13},{10,... | collective-permute-start | bytes 1572872 | tf_op jit(solution)/shard_map/ppermute | solution.py:51
  563.6 29.8 %collective-permute-start.93 = (bf16[4,256,512]{2,1,0:T(8,128)(2,1)S(1)}, bf16[4,256,512]{2,1,0:T(8,128)(2,1)S(1)}, u32[]{:S(2)}, u32[]{:S(2)}) collective-permute-start(bf16[4,256,512]{2,1,0:T(8,128)(2,1)S(1)} %bitcast.260), channel_id=1, source_target_pairs={{0,16},{1,17},{2,18},{3,19},{4,20},{5,21},{6,22},{7,23},{8,24},{9,... | collective-permute-start | bytes 3145736 | tf_op jit(solution)/shard_map/ppermute | solution.py:51
  564.1 29.3 %collective-permute-start.95 = (bf16[512,1024]{1,0:T(8,128)(2,1)S(1)}, bf16[512,1024]{1,0:T(8,128)(2,1)S(1)}, u32[]{:S(2)}, u32[]{:S(2)}) collective-permute-start(bf16[512,1024]{1,0:T(8,128)(2,1)S(1)} %copy-done.53), channel_id=1, source_target_pairs={{0,1},{1,0},{2,3},{3,2},{4,5},{5,4},{6,7},{7,6},{8,9},{9,8},{10,11... | collective-permute-start | bytes 3145736 | tf_op jit(solution)/shard_map/ppermute | solution.py:51
  568.1 25.2 %collective-permute-start.92 = (bf16[2,512,256]{2,1,0:T(8,128)(2,1)S(1)}, bf16[2,512,256]{2,1,0:T(8,128)(2,1)S(1)}, u32[]{:S(2)}, u32[]{:S(2)}) collective-permute-start(bf16[2,512,256]{2,1,0:T(8,128)(2,1)S(1)} %slice.646), channel_id=1, source_target_pairs={{0,2},{1,3},{2,0},{3,1},{4,6},{5,7},{6,4},{7,5},{8,10},{9,11},{10,... | collective-permute-start | bytes 1572872 | tf_op jit(solution)/shard_map/ppermute | solution.py:51
  571.9 21.4 %collective-permute-start.94 = (bf16[128,1024]{1,0:T(8,128)(2,1)S(1)}, bf16[128,1024]{1,0:T(8,128)(2,1)S(1)}, u32[]{:S(2)}, u32[]{:S(2)}) collective-permute-start(bf16[128,1024]{1,0:T(8,128)(2,1)S(1)} %get-tuple-element.474), channel_id=1, source_target_pairs={{0,4},{1,5},{2,6},{3,7},{4,0},{5,1},{6,2},{7,3},{8,12},{9,13},{10,... | collective-permute-start | bytes 786440 | tf_op jit(solution)/shard_map/ppermute | solution.py:51
  593.9 22.6 %collective-permute-start.100 = (bf16[128,2048]{1,0:T(8,128)(2,1)S(1)}, bf16[128,2048]{1,0:T(8,128)(2,1)S(1)}, u32[]{:S(2)}, u32[]{:S(2)}) collective-permute-start(bf16[128,2048]{1,0:T(8,128)(2,1)S(1)} %copy-done.74), channel_id=1, source_target_pairs={{0,16},{1,17},{2,18},{3,19},{4,20},{5,21},{6,22},{7,23},{8,24},{9,... | collective-permute-start | bytes 1572872 | tf_op jit(solution)/shard_map/ppermute | solution.py:51
  594.9 21.6 %collective-permute-start.97 = (bf16[2,256,512]{2,1,0:T(8,128)(2,1)S(1)}, bf16[2,256,512]{2,1,0:T(8,128)(2,1)S(1)}, u32[]{:S(2)}, u32[]{:S(2)}) collective-permute-start(bf16[2,256,512]{2,1,0:T(8,128)(2,1)S(1)} %slice.657), channel_id=1, source_target_pairs={{0,2},{1,3},{2,0},{3,1},{4,6},{5,7},{6,4},{7,5},{8,10},{9,11},{10,... | collective-permute-start | bytes 1572872 | tf_op jit(solution)/shard_map/ppermute | solution.py:51
  594.9 21.6 %collective-permute-start.98 = (bf16[256,1024]{1,0:T(8,128)(2,1)S(1)}, bf16[256,1024]{1,0:T(8,128)(2,1)S(1)}, u32[]{:S(2)}, u32[]{:S(2)}) collective-permute-start(bf16[256,1024]{1,0:T(8,128)(2,1)S(1)} %get-tuple-element.483), channel_id=1, source_target_pairs={{0,1},{1,0},{2,3},{3,2},{4,5},{5,4},{6,7},{7,6},{8,9},{9,8},{10,11... | collective-permute-start | bytes 1572872 | tf_op jit(solution)/shard_map/ppermute | solution.py:51
  597.9 18.6 %collective-permute-start.99 = (bf16[128,1024]{1,0:T(8,128)(2,1)S(1)}, bf16[128,1024]{1,0:T(8,128)(2,1)S(1)}, u32[]{:S(2)}, u32[]{:S(2)}) collective-permute-start(bf16[128,1024]{1,0:T(8,128)(2,1)S(1)} %get-tuple-element.484), channel_id=1, source_target_pairs={{0,4},{1,5},{2,6},{3,7},{4,0},{5,1},{6,2},{7,3},{8,12},{9,13},{10,... | collective-permute-start | bytes 786440 | tf_op jit(solution)/shard_map/ppermute | solution.py:51
  635.4 24.1 %collective-permute-start.107 = (bf16[4,256,512]{2,1,0:T(8,128)(2,1)}, bf16[4,256,512]{2,1,0:T(8,128)(2,1)}, u32[]{:S(2)}, u32[]{:S(2)}) collective-permute-start(bf16[4,256,512]{2,1,0:T(8,128)(2,1)} %bitcast.74), channel_id=1, source_target_pairs={{0,16},{1,17},{2,18},{3,19},{4,20},{5,21},{6,22},{7,23},{8,24},{9,... | collective-permute-start | bytes 3145736 | tf_op jit(solution)/shard_map/ppermute | solution.py:51
  637.0 21.0 %collective-permute-start.106 = (bf16[128,2048]{1,0:T(8,128)(2,1)}, bf16[128,2048]{1,0:T(8,128)(2,1)}, u32[]{:S(2)}, u32[]{:S(2)}) collective-permute-start(bf16[128,2048]{1,0:T(8,128)(2,1)} %fusion.16), channel_id=1, source_target_pairs={{0,1},{1,0},{2,3},{3,2},{4,5},{5,4},{6,7},{7,6},{8,9},{9,8},{10,11... | collective-permute-start | bytes 1572872 | tf_op jit(solution)/shard_map/ppermute | solution.py:51
  637.0 21.0 %collective-permute-start.109 = (bf16[2,256,384]{2,1,0:T(8,128)(2,1)S(1)}, bf16[2,256,384]{2,1,0:T(8,128)(2,1)}, u32[]{:S(2)}, u32[]{:S(2)}) collective-permute-start(bf16[2,256,384]{2,1,0:T(8,128)(2,1)S(1)} %slice.676), channel_id=1, source_target_pairs={{0,2},{1,3},{2,0},{3,1},{4,6},{5,7},{6,4},{7,5},{8,10},{9,11},{10,... | collective-permute-start | bytes 1179656 | tf_op jit(solution)/shard_map/ppermute | solution.py:51
  652.7 21.1 %collective-permute-start.104 = (bf16[128,2048]{1,0:T(8,128)(2,1)}, bf16[128,2048]{1,0:T(8,128)(2,1)S(1)}, u32[]{:S(2)}, u32[]{:S(2)}) collective-permute-start(bf16[128,2048]{1,0:T(8,128)(2,1)} %get-tuple-element.580), channel_id=1, source_target_pairs={{0,8},{1,9},{2,10},{3,11},{4,12},{5,13},{6,14},{7,15},{8,0},{9,1},... | collective-permute-start | bytes 1572872 | tf_op jit(solution)/shard_map/ppermute | solution.py:51
  668.2 19.0 %collective-permute-start.111 = (bf16[2,256,512]{2,1,0:T(8,128)(2,1)}, bf16[2,256,512]{2,1,0:T(8,128)(2,1)}, u32[]{:S(2)}, u32[]{:S(2)}) collective-permute-start(bf16[2,256,512]{2,1,0:T(8,128)(2,1)} %slice.682), channel_id=1, source_target_pairs={{0,2},{1,3},{2,0},{3,1},{4,6},{5,7},{6,4},{7,5},{8,10},{9,11},{10,... | collective-permute-start | bytes 1572872 | tf_op jit(solution)/shard_map/ppermute | solution.py:51
  668.2 19.0 %collective-permute-start.114 = (bf16[256,1024]{1,0:T(8,128)(2,1)}, bf16[256,1024]{1,0:T(8,128)(2,1)}, u32[]{:S(2)}, u32[]{:S(2)}) collective-permute-start(bf16[256,1024]{1,0:T(8,128)(2,1)} %get-tuple-element.510), channel_id=1, source_target_pairs={{0,1},{1,0},{2,3},{3,2},{4,5},{5,4},{6,7},{7,6},{8,9},{9,8},{10,11... | collective-permute-start | bytes 1572872 | tf_op jit(solution)/shard_map/ppermute | solution.py:51
  688.6 24.3 %collective-permute-start.117 = (bf16[256,1024]{1,0:T(8,128)(2,1)}, bf16[256,1024]{1,0:T(8,128)(2,1)S(1)}, u32[]{:S(2)}, u32[]{:S(2)}) collective-permute-start(bf16[256,1024]{1,0:T(8,128)(2,1)} %get-tuple-element.517), channel_id=1, source_target_pairs={{0,2},{1,3},{2,0},{3,1},{4,6},{5,7},{6,4},{7,5},{8,10},{9,11},{10,... | collective-permute-start | bytes 1572872 | tf_op jit(solution)/shard_map/ppermute | solution.py:51
  691.2 21.7 %collective-permute-start.116 = (bf16[128,1024]{1,0:T(8,128)(2,1)}, bf16[128,1024]{1,0:T(8,128)(2,1)S(1)}, u32[]{:S(2)}, u32[]{:S(2)}) collective-permute-start(bf16[128,1024]{1,0:T(8,128)(2,1)} %get-tuple-element.516), channel_id=1, source_target_pairs={{0,4},{1,5},{2,6},{3,7},{4,0},{5,1},{6,2},{7,3},{8,12},{9,13},{10,... | collective-permute-start | bytes 786440 | tf_op jit(solution)/shard_map/ppermute | solution.py:51
  716.4 22.8 %collective-permute-start.122 = (bf16[256,1024]{1,0:T(8,128)(2,1)S(1)}, bf16[256,1024]{1,0:T(8,128)(2,1)S(1)}, u32[]{:S(2)}, u32[]{:S(2)}) collective-permute-start(bf16[256,1024]{1,0:T(8,128)(2,1)S(1)} %get-tuple-element.525), channel_id=1, source_target_pairs={{0,2},{1,3},{2,0},{3,1},{4,6},{5,7},{6,4},{7,5},{8,10},{9,11},{10,... | collective-permute-start | bytes 1572872 | tf_op jit(solution)/shard_map/ppermute | solution.py:51
  (199 other events, 2714.3 us)
